TPU v7x, 32 devices: a whole 2x2x4 slice. The times are simulated.
32 devices in a mesh: gen: 4 (over y, x), fit: 8 (over z, core).
Axes of the slice: x: 2, y: 2, z: 4, core: 2. Of those that a mesh axis runs over, the one named last changes fastest.
Arguments:
- raw_columns: bfloat16 [8, 2000, 2000], P(None, 'gen', 'fit'), as said below
- pivot_pairs: int32 [8], replicated, may hold values from 0 to 3999999, as said below
- collocation: bfloat16 [2000, 4096], P('gen', 'fit'), may hold values from -0.125 to 0.125
- metric_factor: float32 [4096, 4096], P('fit', 'gen'), as said below
Outputs:
- panel: float32 [8, 4096], P('gen', 'fit')
Inputs may be any that keep to these rules, and one draw needn't show every extreme that they name: `pivot_pairs`: 8 distinct orbital-pair indices p * 2000 + q. The entries at the pivots, raw_columns[P, pivot_pairs[Q] // 2000, pivot_pairs[Q] % 2000], form a symmetric positive definite matrix. `metric_factor`: lower triangular with a positive diagonal.
All inputs are finite; a program needn't handle non-finite values.
Results may differ from a plain program's by a relative error of at most 0.0029.
Values may be sent and summed in bfloat16 or wider, within the bound.
No kernel may reach another device: no remote copies, remote signals or barrier semaphores. Data moves between devices by JAX's collectives and lax.ppermute only.
A program may use at most 64 MiB of HBM per device.

v0:
```python
import math

import jax
import jax.numpy as jnp
from jax import lax
from jax.sharding import PartitionSpec as P

NORB = 2000


def spread(value, axis, source):
    kept = jnp.where(lax.axis_index(axis) == source, value, 0).astype(value.dtype)
    return lax.psum(kept, axis)


def project_block(vectors, stacked, orbital_count):
    point_count = stacked.shape[1]
    block_width = math.gcd(point_count, 512)
    block_count = point_count // block_width
    pair_count = stacked.shape[0] - orbital_count
    orbital_part = (
        stacked[:orbital_count].reshape(orbital_count, block_count, block_width).transpose(1, 0, 2)
    )
    pair_part = (
        stacked[orbital_count:].reshape(pair_count, block_count, block_width).transpose(1, 0, 2)
    )

    def one_block(pieces):
        mixed_terms = jnp.einsum(
            "apq,pn->aqn", vectors, pieces[0], preferred_element_type=jnp.float32
        )
        return jnp.sum(mixed_terms * pieces[1].astype(jnp.float32)[None], axis=1)

    blocks = lax.map(one_block, (orbital_part, pair_part))
    return blocks.transpose(1, 0, 2).reshape(vectors.shape[0], point_count)


def on_device(raw_columns, pivot_pairs, collocation, metric_factor):
    vec_total, orb_block, pair_block = raw_columns.shape
    gen_count = lax.axis_size("gen")
    fit_count = lax.axis_size("fit")
    gen_index = lax.axis_index("gen")
    fit_index = lax.axis_index("fit")
    point_dev = metric_factor.shape[0]
    vec_dev = vec_total // gen_count
    pair_first = pivot_pairs // NORB
    pair_second = pivot_pairs % NORB
    row_hits = (
        pair_first[:, None] == gen_index * orb_block + jnp.arange(orb_block)[None, :]
    ).astype(jnp.bfloat16)
    col_hits = (
        pair_second[:, None] == fit_index * pair_block + jnp.arange(pair_block)[None, :]
    ).astype(jnp.float32)
    picked = jnp.einsum("apq,bp->abq", raw_columns, row_hits, preferred_element_type=jnp.float32)
    own_entries = jnp.sum(picked * col_hits[None], axis=2)
    pivot_block = lax.psum(own_entries, ("gen", "fit"))
    factor = jnp.linalg.cholesky(pivot_block)
    flat_columns = raw_columns.reshape(vec_total, orb_block * pair_block).astype(jnp.float32)
    vectors = jax.scipy.linalg.solve_triangular(factor, flat_columns, lower=True)
    vectors = vectors.astype(jnp.bfloat16).reshape(vec_total, orb_block, pair_block)
    group_ratio = fit_count // gen_count
    owner_index = fit_index // group_ratio
    portion = fit_index % group_ratio
    orbital_side = lax.all_gather(collocation, "fit", axis=1, tiled=True)
    wide_slice = lax.dynamic_slice_in_dim(orbital_side, portion * pair_block, pair_block, 0)
    pair_side = spread(wide_slice, "gen", owner_index)
    partial_panel = project_block(
        vectors, jnp.concatenate([orbital_side, pair_side], axis=0), orb_block
    )
    arranged = partial_panel.reshape(gen_count, vec_dev, fit_count, point_dev).transpose(0, 2, 1, 3)
    arranged = arranged.reshape(gen_count * fit_count * vec_dev, point_dev)
    summed = lax.psum_scatter(arranged, ("gen", "fit"), scatter_dimension=0, tiled=True)
    remaining_start = jnp.zeros((vec_total, point_dev), jnp.float32)
    remaining_start = lax.dynamic_update_slice_in_dim(
        remaining_start, summed, gen_index * vec_dev, 0
    )

    def advance(turn_index, carried):
        remaining, solved = carried
        turn_owner = turn_index // group_ratio
        local_start = turn_index % group_ratio * point_dev
        whole_rest = lax.psum(remaining, "gen")
        column_part = lax.dynamic_slice_in_dim(metric_factor, local_start, point_dev, 1)
        candidate = jax.scipy.linalg.solve_triangular(column_part, whole_rest.T, lower=True).T
        holder = jnp.logical_and(fit_index == turn_index, gen_index == turn_owner)
        candidate = jnp.where(holder, candidate, 0.0)
        arrived = spread(candidate, ("gen", "fit"), turn_owner * fit_count + turn_index)
        update = jnp.dot(arrived, column_part.T, precision=lax.Precision.HIGHEST)
        remaining = remaining - jnp.where(gen_index == turn_owner, update, 0.0)
        own_rows = lax.dynamic_slice_in_dim(arrived, gen_index * vec_dev, vec_dev, 0)
        solved = jnp.where(fit_index == turn_index, own_rows, solved)
        return (remaining, solved)

    initial = jnp.zeros((vec_dev, point_dev), jnp.float32)
    remaining, solved = lax.fori_loop(0, fit_count, advance, (remaining_start, initial))
    return solved


def solution(mesh):
    in_specs = (P(None, "gen", "fit"), P(), P("gen", "fit"), P("fit", "gen"))
    out_specs = P("gen", "fit")
    return jax.shard_map(
        on_device, mesh=mesh, in_specs=in_specs, out_specs=out_specs, check_vma=False
    )
```

profile of v0, /device:TPU:24, one launch (start us, length us, event | category | flops | bytes accessed | tf_op | source)
XLA Modules:
  0.0 1172.6 jit_solution(14042528507513244858)
XLA Ops:
  7.3 47.1 %all-gather.2.cloned.1.call-done = bf16[500,4096]{1,0:T(8,128)(2,1)} async-done(((bf16[500,512]{1,0:T(8,128)(2,1)}), bf16[500,4096]{1,0:T(8,128)(2,1)}) %all-gather.2.cloned.1.call-update) | async-done | bytes 4096016 | tf_op jit(solution)/shard_map/all_gather | solution.py:64
  63.2 40.1 %psum.42 = f32[8,8]{0,1:T(8,128)S(1)} all-reduce(f32[8,8]{0,1:T(8,128)S(1)} %bitcast.108), channel_id=1, replica_groups=mesh['gen'=4,'fit'=8] {'gen','fit'}, use_global_device_ids=true, to_apply=%region_2.3 | all-reduce | flops 64 | bytes 512 | tf_op jit(solution)/shard_map/psum | solution.py:56
  143.4 35.0 %while.31 = (s32[]{:T(128)}, f32[8,8,512]{2,1,0:T(8,128)S(1)}, bf16[8,500,512]{2,1,0:T(8,128)(2,1)}, bf16[8,500,250]{2,1,0:T(8,128)(2,1)}, bf16[8,250,512]{1,2,0:T(8,128)(2,1)}, /*index=5*/s32[]{:T(128)}) while((s32[]{:T(128)}, f32[8,8,512]{2,1,0:T(8,128)S(1)}, bf16[8,500,512]{2,1,0:T(8,128)(2,1)}, bf16[8,500,250]{2,1,0:T(8,128)(2,1)}, ...), condition=%wide.region_7.8_spmd, body=%wide.region_5.7_spmd.sunk | while | flops 1026171904 | bytes 4934221 | solution.py:34
  179.2 122.5 %all-reduce.6.cloned.1.call-done = f32[64,512]{1,0:T(8,128)} async-done(((f32[64,512]{1,0:T(8,128)}), f32[64,512]{1,0:T(8,128)}) %all-reduce.6.cloned.1.call-update) | async-done | bytes 131088
  302.4 863.1 %while.33 = (s32[]{:T(128)}, f32[8,512]{1,0:T(8,128)S(1)}, f32[2,512]{1,0:T(2,128)S(1)}, s32[]{:T(128)}, s32[]{:T(128)}, /*index=5*/f32[512,1024]{1,0:T(8,128)S(...) while((s32[]{:T(128)}, f32[8,512]{1,0:T(8,128)S(1)}, ...), condition=%wide.region_12.13_spmd.clone, body=%wide.region_9.12_spmd.clone.sunk | while | flops 41468964 | bytes 4176043 | solution.py:95
  302.8 10.0 while.34
  312.9 40.1 %custom-call.26 = f32[4,128,128]{1,2,0:T(8,128)S(1)} custom-call(f32[4,128,128]{2,1,0:T(8,128)} %get-tuple-element.386), custom_call_target="InvertDiagBlocksLowerTriangular" | custom-call | tf_op jit(solution)/shard_map/while/body/eval_jaxpr/jit(_solve_triangular)/triangular_solve | solution.py:84
  353.0 15.1 %psum.48 = f32[512,8]{0,1:T(8,128)S(1)} all-reduce(f32[512,8]{0,1:T(8,128)S(1)} %bitcast.105), channel_id=1, replica_groups=mesh['gen'=4,'fit'=8] {'gen'}, use_global_device_ids=true, to_apply=%region_10.10 | all-reduce | flops 4096 | bytes 32768 | tf_op jit(solution)/shard_map/while/body/eval_jaxpr/psum | solution.py:82
  369.6 39.2 %psum.49 = f32[8,512]{1,0:T(8,128)S(1)} all-reduce(f32[8,512]{1,0:T(8,128)S(1)} %fusion.88), channel_id=1, replica_groups=mesh['gen'=4,'fit'=8] {'gen','fit'}, use_global_device_ids=true, to_apply=%region_11.11 | all-reduce | flops 4096 | bytes 32768 | tf_op jit(solution)/shard_map/while/body/eval_jaxpr/psum | solution.py:13
  410.0 10.0 while.34
  420.0 40.1 %custom-call.26 = f32[4,128,128]{1,2,0:T(8,128)S(1)} custom-call(f32[4,128,128]{2,1,0:T(8,128)} %get-tuple-element.386), custom_call_target="InvertDiagBlocksLowerTriangular" | custom-call | tf_op jit(solution)/shard_map/while/body/eval_jaxpr/jit(_solve_triangular)/triangular_solve | solution.py:84
  460.1 16.0 %psum.48 = f32[512,8]{0,1:T(8,128)S(1)} all-reduce(f32[512,8]{0,1:T(8,128)S(1)} %bitcast.105), channel_id=1, replica_groups=mesh['gen'=4,'fit'=8] {'gen'}, use_global_device_ids=true, to_apply=%region_10.10 | all-reduce | flops 4096 | bytes 32768 | tf_op jit(solution)/shard_map/while/body/eval_jaxpr/psum | solution.py:82
  477.6 39.2 %psum.49 = f32[8,512]{1,0:T(8,128)S(1)} all-reduce(f32[8,512]{1,0:T(8,128)S(1)} %fusion.88), channel_id=1, replica_groups=mesh['gen'=4,'fit'=8] {'gen','fit'}, use_global_device_ids=true, to_apply=%region_11.11 | all-reduce | flops 4096 | bytes 32768 | tf_op jit(solution)/shard_map/while/body/eval_jaxpr/psum | solution.py:13
  517.9 10.0 while.34
  528.0 40.1 %custom-call.26 = f32[4,128,128]{1,2,0:T(8,128)S(1)} custom-call(f32[4,128,128]{2,1,0:T(8,128)} %get-tuple-element.386), custom_call_target="InvertDiagBlocksLowerTriangular" | custom-call | tf_op jit(solution)/shard_map/while/body/eval_jaxpr/jit(_solve_triangular)/triangular_solve | solution.py:84
  568.1 16.0 %psum.48 = f32[512,8]{0,1:T(8,128)S(1)} all-reduce(f32[512,8]{0,1:T(8,128)S(1)} %bitcast.105), channel_id=1, replica_groups=mesh['gen'=4,'fit'=8] {'gen'}, use_global_device_ids=true, to_apply=%region_10.10 | all-reduce | flops 4096 | bytes 32768 | tf_op jit(solution)/shard_map/while/body/eval_jaxpr/psum | solution.py:82
  585.5 39.2 %psum.49 = f32[8,512]{1,0:T(8,128)S(1)} all-reduce(f32[8,512]{1,0:T(8,128)S(1)} %fusion.88), channel_id=1, replica_groups=mesh['gen'=4,'fit'=8] {'gen','fit'}, use_global_device_ids=true, to_apply=%region_11.11 | all-reduce | flops 4096 | bytes 32768 | tf_op jit(solution)/shard_map/while/body/eval_jaxpr/psum | solution.py:13
  635.9 40.1 %custom-call.26 = f32[4,128,128]{1,2,0:T(8,128)S(1)} custom-call(f32[4,128,128]{2,1,0:T(8,128)} %get-tuple-element.386), custom_call_target="InvertDiagBlocksLowerTriangular" | custom-call | tf_op jit(solution)/shard_map/while/body/eval_jaxpr/jit(_solve_triangular)/triangular_solve | solution.py:84
  676.1 16.0 %psum.48 = f32[512,8]{0,1:T(8,128)S(1)} all-reduce(f32[512,8]{0,1:T(8,128)S(1)} %bitcast.105), channel_id=1, replica_groups=mesh['gen'=4,'fit'=8] {'gen'}, use_global_device_ids=true, to_apply=%region_10.10 | all-reduce | flops 4096 | bytes 32768 | tf_op jit(solution)/shard_map/while/body/eval_jaxpr/psum | solution.py:82
  693.5 39.2 %psum.49 = f32[8,512]{1,0:T(8,128)S(1)} all-reduce(f32[8,512]{1,0:T(8,128)S(1)} %fusion.88), channel_id=1, replica_groups=mesh['gen'=4,'fit'=8] {'gen','fit'}, use_global_device_ids=true, to_apply=%region_11.11 | all-reduce | flops 4096 | bytes 32768 | tf_op jit(solution)/shard_map/while/body/eval_jaxpr/psum | solution.py:13
  743.9 40.1 %custom-call.26 = f32[4,128,128]{1,2,0:T(8,128)S(1)} custom-call(f32[4,128,128]{2,1,0:T(8,128)} %get-tuple-element.386), custom_call_target="InvertDiagBlocksLowerTriangular" | custom-call | tf_op jit(solution)/shard_map/while/body/eval_jaxpr/jit(_solve_triangular)/triangular_solve | solution.py:84
  784.0 16.0 %psum.48 = f32[512,8]{0,1:T(8,128)S(1)} all-reduce(f32[512,8]{0,1:T(8,128)S(1)} %bitcast.105), channel_id=1, replica_groups=mesh['gen'=4,'fit'=8] {'gen'}, use_global_device_ids=true, to_apply=%region_10.10 | all-reduce | flops 4096 | bytes 32768 | tf_op jit(solution)/shard_map/while/body/eval_jaxpr/psum | solution.py:82
  801.5 39.2 %psum.49 = f32[8,512]{1,0:T(8,128)S(1)} all-reduce(f32[8,512]{1,0:T(8,128)S(1)} %fusion.88), channel_id=1, replica_groups=mesh['gen'=4,'fit'=8] {'gen','fit'}, use_global_device_ids=true, to_apply=%region_11.11 | all-reduce | flops 4096 | bytes 32768 | tf_op jit(solution)/shard_map/while/body/eval_jaxpr/psum | solution.py:13
  851.9 40.1 %custom-call.26 = f32[4,128,128]{1,2,0:T(8,128)S(1)} custom-call(f32[4,128,128]{2,1,0:T(8,128)} %get-tuple-element.386), custom_call_target="InvertDiagBlocksLowerTriangular" | custom-call | tf_op jit(solution)/shard_map/while/body/eval_jaxpr/jit(_solve_triangular)/triangular_solve | solution.py:84
  892.0 16.0 %psum.48 = f32[512,8]{0,1:T(8,128)S(1)} all-reduce(f32[512,8]{0,1:T(8,128)S(1)} %bitcast.105), channel_id=1, replica_groups=mesh['gen'=4,'fit'=8] {'gen'}, use_global_device_ids=true, to_apply=%region_10.10 | all-reduce | flops 4096 | bytes 32768 | tf_op jit(solution)/shard_map/while/body/eval_jaxpr/psum | solution.py:82
  909.5 39.1 %psum.49 = f32[8,512]{1,0:T(8,128)S(1)} all-reduce(f32[8,512]{1,0:T(8,128)S(1)} %fusion.88), channel_id=1, replica_groups=mesh['gen'=4,'fit'=8] {'gen','fit'}, use_global_device_ids=true, to_apply=%region_11.11 | all-reduce | flops 4096 | bytes 32768 | tf_op jit(solution)/shard_map/while/body/eval_jaxpr/psum | solution.py:13
  959.8 40.1 %custom-call.26 = f32[4,128,128]{1,2,0:T(8,128)S(1)} custom-call(f32[4,128,128]{2,1,0:T(8,128)} %get-tuple-element.386), custom_call_target="InvertDiagBlocksLowerTriangular" | custom-call | tf_op jit(solution)/shard_map/while/body/eval_jaxpr/jit(_solve_triangular)/triangular_solve | solution.py:84
  999.9 16.0 %psum.48 = f32[512,8]{0,1:T(8,128)S(1)} all-reduce(f32[512,8]{0,1:T(8,128)S(1)} %bitcast.105), channel_id=1, replica_groups=mesh['gen'=4,'fit'=8] {'gen'}, use_global_device_ids=true, to_apply=%region_10.10 | all-reduce | flops 4096 | bytes 32768 | tf_op jit(solution)/shard_map/while/body/eval_jaxpr/psum | solution.py:82
  1017.4 39.2 %psum.49 = f32[8,512]{1,0:T(8,128)S(1)} all-reduce(f32[8,512]{1,0:T(8,128)S(1)} %fusion.88), channel_id=1, replica_groups=mesh['gen'=4,'fit'=8] {'gen','fit'}, use_global_device_ids=true, to_apply=%region_11.11 | all-reduce | flops 4096 | bytes 32768 | tf_op jit(solution)/shard_map/while/body/eval_jaxpr/psum | solution.py:13
  1067.8 40.1 %custom-call.26 = f32[4,128,128]{1,2,0:T(8,128)S(1)} custom-call(f32[4,128,128]{2,1,0:T(8,128)} %get-tuple-element.386), custom_call_target="InvertDiagBlocksLowerTriangular" | custom-call | tf_op jit(solution)/shard_map/while/body/eval_jaxpr/jit(_solve_triangular)/triangular_solve | solution.py:84
  1107.9 16.0 %psum.48 = f32[512,8]{0,1:T(8,128)S(1)} all-reduce(f32[512,8]{0,1:T(8,128)S(1)} %bitcast.105), channel_id=1, replica_groups=mesh['gen'=4,'fit'=8] {'gen'}, use_global_device_ids=true, to_apply=%region_10.10 | all-reduce | flops 4096 | bytes 32768 | tf_op jit(solution)/shard_map/while/body/eval_jaxpr/psum | solution.py:82
  1125.4 39.1 %psum.49 = f32[8,512]{1,0:T(8,128)S(1)} all-reduce(f32[8,512]{1,0:T(8,128)S(1)} %fusion.88), channel_id=1, replica_groups=mesh['gen'=4,'fit'=8] {'gen','fit'}, use_global_device_ids=true, to_apply=%region_11.11 | all-reduce | flops 4096 | bytes 32768 | tf_op jit(solution)/shard_map/while/body/eval_jaxpr/psum | solution.py:13
  (298 shorter events, 237.2 us)
Async XLA Ops:
  6.5 47.9 %all-gather.2.cloned.1.call-start = ((), (), s32[]{:S(2)}) async-start(), calls=%async_computation | async-start | bytes 4644864 | tf_op jit(solution)/shard_map/all_gather | solution.py:64
  7.3 136.1 %all-reduce.4.cloned.1.call-start = ((), (), s32[]{:S(2)}) async-start(), calls=%async_computation.1 | async-start | bytes 4194304 | tf_op jit(solution)/shard_map/psum | solution.py:13
  59.1 1.6 copy-start.1
  59.2 3.3 copy-start.3
  59.2 242.5 %all-reduce.6.cloned.1.call-start = ((), (), s32[]{:S(2)}) async-start(), calls=%async_computation.2 | async-start | bytes 262144
  143.4 159.1 %copy-start = (f32[512,1024]{1,0:T(8,128)S(1)}, f32[512,1024]{1,0:T(8,128)}, u32[]{:S(2)}) copy-start(f32[512,1024]{1,0:T(8,128)} %param.11) | copy-start | bytes 6291460
  1165.5 0.6 copy-start.2
Sparse Core Ops, SparseCore 0:
  9.0 45.3 all-gather.1
  59.3 71.2 all-reduce.3
  179.3 122.3 all-reduce.5
where the time goes:
time: 1180 us; the launch traced here: 1170 us
  blocking collectives  481 us (41%)
  other arithmetic  328 us (28%)
  waiting for transfers between devices  170 us (14%)
  local copies, waits for them, and re-layouts  132 us (11%)
  matrix products  47.8 us (4%)
  between operations  13.3 us (1%)
    another operation x24, other arithmetic, advance(): jax.scipy.linalg.solve_triangular(column_part, whole_rest.T, lower=True)  322 us
    psum x8, blocking collectives, spread(): return lax.psum(kept, axis)  313 us
    psum x8, blocking collectives, advance(): whole_rest = lax.psum(remaining, 'gen')  127 us
    unnamed x4, waiting for transfers between devices  123 us
    another operation x96, local copies, waits for them, and re-layouts  80.2 us
    all_gather x1, waiting for transfers between devices, on_device(): orbital_side = lax.all_gather(collocation, 'fit', axis=1, tiled=True)  47.1 us
    psum x1, blocking collectives, on_device(): pivot_block = lax.psum(own_entries, ('gen', 'fit'))  40.1 us
    dot_general x8, matrix products, one_block(): jnp.einsum('apq,pn->aqn', vectors, pieces[0], preferred_element_type=jnp....  25.1 us
  transfers between devices with their start and end apart: 3, of which 2 were waited for; matrix products, arithmetic and copies ran while one was open for 4% of the time, Pallas kernels for 0%

commit v1 on v0

v1 whole, which is shorter than its diff:
```python
import functools

import jax
import jax.numpy as jnp
from jax import lax
from jax.experimental import pallas as pl
from jax.experimental.pallas import tpu as pltpu
from jax.sharding import PartitionSpec as P

NORB = 2000
F32 = jnp.float32
BF16 = jnp.bfloat16
BOTH = ("gen", "fit")
HIGHEST = lax.Precision.HIGHEST


def mover(gen_count):
    fit_count = 2 * gen_count

    def move(value, target):
        pairs = []
        for g in range(gen_count):
            for j in range(gen_count):
                for c in range(2):
                    to = target(g, j, c)
                    if to is not None:
                        pairs.append(
                            (g * fit_count + 2 * j + c, to[0] * fit_count + 2 * to[1] + to[2])
                        )
        return lax.ppermute(value, BOTH, pairs)

    return move


def split_hi_lo(x):
    hi = lax.reduce_precision(x, 8, 7)
    return hi.astype(BF16), (x - hi).astype(BF16)


def pivot_kernel(raw_ref, rows_ref, cols_ref, out_ref):
    i = pl.program_id(0)
    picked = jnp.dot(rows_ref[...], raw_ref[0], preferred_element_type=F32)
    entries = jnp.sum(picked * cols_ref[...], axis=1, keepdims=True)
    out_ref[pl.ds(i, 1), :] = entries.T


def pivot_entries(raw, row_hits, col_hits):
    vec_total, orb, pair = raw.shape
    return pl.pallas_call(
        pivot_kernel,
        grid=(vec_total,),
        in_specs=[
            pl.BlockSpec((1, orb, pair), lambda i: (i, 0, 0)),
            pl.BlockSpec((vec_total, orb), lambda i: (0, 0)),
            pl.BlockSpec((vec_total, pair), lambda i: (0, 0)),
        ],
        out_specs=pl.BlockSpec((vec_total, vec_total), lambda i: (0, 0)),
        out_shape=jax.ShapeDtypeStruct((vec_total, vec_total), F32),
        name="pivot_entries",
    )(raw, row_hits, col_hits)


def factor_inverse_kernel(block_ref, out_ref):
    a = block_ref[...]
    n = a.shape[0]
    row = lax.broadcasted_iota(jnp.int32, (n, n), 0)
    col = lax.broadcasted_iota(jnp.int32, (n, n), 1)
    w = (row == col).astype(F32)
    for i in range(n):
        pivot = a[i : i + 1, i : i + 1]
        scale = jnp.where(row[:, :1] > i, a[:, i : i + 1] / pivot, 0.0)
        w = w - scale * w[i : i + 1, :]
        a = a - scale * a[i : i + 1, :]
    diag = jnp.sum(jnp.where(row == col, a, 0.0), axis=1, keepdims=True)
    out_ref[...] = w / jnp.sqrt(diag)


def factor_inverse(block):
    return pl.pallas_call(
        factor_inverse_kernel,
        out_shape=jax.ShapeDtypeStruct(block.shape, F32),
        name="factor_inverse",
    )(block)


def project_kernel(where_ref, own_ref, sib_ref, cq_ref, cp_ref, out_ref):
    i = pl.program_id(0)
    core = where_ref[1]
    mixed = jnp.dot(own_ref[0], cq_ref[0, core], preferred_element_type=F32)
    mixed += jnp.dot(sib_ref[0], cq_ref[0, 1 - core], preferred_element_type=F32)
    out_ref[pl.ds(i, 1), :] = jnp.sum(mixed * cp_ref[...].astype(F32), axis=0, keepdims=True)


def project(where, own, sib, cq, cp):
    vec_total, orb, pair = own.shape
    points = cp.shape[1]
    return pl.pallas_call(
        project_kernel,
        grid_spec=pltpu.PrefetchScalarGridSpec(
            num_scalar_prefetch=1,
            grid=(vec_total,),
            in_specs=[
                pl.BlockSpec((1, orb, pair), lambda i, s: (i, 0, 0)),
                pl.BlockSpec((1, orb, pair), lambda i, s: (i, 0, 0)),
                pl.BlockSpec((1, 2, pair, points), lambda i, s: (s[0], 0, 0, 0)),
                pl.BlockSpec((orb, points), lambda i, s: (0, 0)),
            ],
            out_specs=pl.BlockSpec((vec_total, points), lambda i, s: (0, 0)),
        ),
        out_shape=jax.ShapeDtypeStruct((vec_total, points), F32),
        compiler_params=pltpu.CompilerParams(vmem_limit_bytes=32 << 20),
        name="project",
    )(where, own, sib, cq, cp)


def invert_kernel(where_ref, block_ref, out_ref):
    n = block_ref.shape[0]
    tile = 128
    count = n // tile
    holds = where_ref[1] == 1
    row = lax.broadcasted_iota(jnp.int32, (tile, tile), 0)
    col = lax.broadcasted_iota(jnp.int32, (tile, tile), 1)
    eye = (row == col).astype(F32)
    dot = functools.partial(jnp.dot, precision=HIGHEST, preferred_element_type=F32)
    parts, xs = [], []
    for b in range(count):
        part = block_ref[b * tile : (b + 1) * tile, b * tile : (b + 1) * tile]
        part = jnp.where(holds, part, eye)
        diag = jnp.sum(part * eye, axis=1, keepdims=True)
        parts.append(part)
        xs.append(eye / diag)
    size = 1
    while size < tile:
        pick = (row // (2 * size) == col // (2 * size)) & (row // size != col // size) & (row > col)
        for b in range(count):
            off = jnp.where(pick, parts[b], 0.0)
            xs[b] = xs[b] - dot(xs[b], dot(off, xs[b]))
        size *= 2
    out_ref[...] = jnp.zeros_like(out_ref)
    for b in range(count):
        out_ref[b * tile : (b + 1) * tile, b * tile : (b + 1) * tile] = xs[b]
    size = tile
    while size < n:
        for b in range(0, n, 2 * size):
            mid, end = b + size, b + 2 * size
            lower = jnp.where(holds, block_ref[mid:end, b:mid], 0.0)
            inner = dot(lower, out_ref[b:mid, b:mid])
            out_ref[mid:end, b:mid] = -dot(out_ref[mid:end, mid:end], inner)
        size *= 2


def invert_block(where, metric):
    n = metric.shape[0]
    return pl.pallas_call(
        invert_kernel,
        grid_spec=pltpu.PrefetchScalarGridSpec(
            num_scalar_prefetch=1,
            grid=(1,),
            in_specs=[pl.BlockSpec((n, n), lambda i, s: (0, s[0]))],
            out_specs=pl.BlockSpec((n, n), lambda i, s: (0, 0)),
        ),
        out_shape=jax.ShapeDtypeStruct((n, n), F32),
        compiler_params=pltpu.CompilerParams(vmem_limit_bytes=32 << 20),
        name="invert_block",
    )(where, metric)


def apply_kernel(sign, where_ref, hi_ref, lo_ref, xa_ref, xb_ref, bias_ref, out_ref):
    core = where_ref[0]
    total = jnp.zeros(out_ref.shape, F32)
    n = out_ref.shape[0]
    dims = (((1,), (1,)), ((), ()))
    for x_ref, half in ((xa_ref, core), (xb_ref, 1 - core)):
        hi = x_ref[...].astype(BF16)
        lo = (x_ref[...] - hi.astype(F32)).astype(BF16)
        hi_w = hi_ref[half]
        total += lax.dot_general(hi, hi_w, dims, preferred_element_type=F32)
        total += lax.dot_general(lo, hi_w, dims, preferred_element_type=F32)
        total += lax.dot_general(hi, lo_ref[half], dims, preferred_element_type=F32)
    if sign < 0:
        total = -total
    out_ref[...] = bias_ref[...] + total


def apply_weights(where, weights, xa, xb, bias, sign):
    hi, lo = weights
    return pl.pallas_call(
        functools.partial(apply_kernel, sign),
        in_specs=[pl.BlockSpec(memory_space=pltpu.SMEM)] + [pl.BlockSpec(memory_space=pltpu.VMEM)] * 5,
        out_specs=pl.BlockSpec(memory_space=pltpu.VMEM),
        out_shape=jax.ShapeDtypeStruct(xa.shape, F32),
        compiler_params=pltpu.CompilerParams(vmem_limit_bytes=32 << 20),
        name="apply_weights",
    )(where, hi, lo, xa, xb, bias)


def on_device(raw_columns, pivot_pairs, collocation, metric_factor):
    vec_total, orb_block, pair_block = raw_columns.shape
    gen_count = lax.axis_size("gen")
    gen_index = lax.axis_index("gen")
    fit_index = lax.axis_index("fit")
    chip = fit_index // 2
    core = fit_index % 2
    points = metric_factor.shape[0]
    vec_dev = vec_total // gen_count
    move = mover(gen_count)
    others = range(1, gen_count)
    diagonal = gen_index == chip
    swap = lambda g, j, c: (g, j, 1 - c)

    first_side = [collocation] + [
        move(collocation, lambda g, j, c, k=k: (g, j ^ k, c)) for k in others
    ]
    part = points // gen_count
    halves = collocation.reshape(2, orb_block // 2, points)
    pieces = []
    for m in range(gen_count):
        start = lax.rem(m - chip + gen_count, gen_count) * part
        piece = lax.dynamic_slice_in_dim(halves, start, part, 2)
        pieces.append(move(piece, lambda g, j, c, m=m: ((m - j) % gen_count, g, c)))
    pieces = jnp.stack(pieces + pieces)
    pieces = lax.dynamic_slice_in_dim(pieces, gen_index, gen_count, 0)
    second_side = lax.all_gather(pieces, "gen", axis=3, tiled=True)
    sibling = move(raw_columns, swap)

    pair_first = pivot_pairs // NORB
    pair_second = pivot_pairs % NORB
    row_hits = (
        pair_first[:, None] == gen_index * orb_block + jnp.arange(orb_block)[None, :]
    ).astype(BF16)
    col_hits = (
        pair_second[:, None] == fit_index * pair_block + jnp.arange(pair_block)[None, :]
    ).astype(F32)
    entries = pivot_entries(raw_columns, row_hits, col_hits)
    entries = entries + move(entries, swap)
    entries = sum([move(entries, lambda g, j, c, k=k: (g, j ^ k, c)) for k in others], entries)
    entries = sum([move(entries, lambda g, j, c, k=k: (g ^ k, j, c)) for k in others], entries)
    inverse_factor = factor_inverse(entries)

    own_inverse = invert_block(jnp.stack([core, diagonal.astype(jnp.int32)]), metric_factor)
    upper = move(own_inverse, swap)
    corner = jnp.dot(metric_factor[:, :points], upper, precision=HIGHEST)
    corner = -jnp.dot(own_inverse, corner, precision=HIGHEST)
    zeros = jnp.zeros_like(own_inverse)
    inverse_rows = jnp.stack(
        [jnp.where(core == 0, own_inverse, corner), jnp.where(core == 0, zeros, own_inverse)]
    )
    left = move(metric_factor, lambda g, j, c: (g + 1, j, c) if j == g + 1 else None)
    left_sib = move(left, swap)
    top = jnp.where(core == 0, left, left_sib)
    bottom = jnp.where(core == 0, left_sib, left)
    step_rows = jnp.dot(inverse_rows[0], top, precision=HIGHEST) + jnp.dot(
        inverse_rows[1], bottom, precision=HIGHEST
    )
    step_rows = jnp.stack([step_rows[:, :points], step_rows[:, points:]])
    own_rows = jnp.stack([metric_factor[:, :points], metric_factor[:, points:]])
    inverse_rows = split_hi_lo(inverse_rows)
    step_rows = split_hi_lo(step_rows)
    own_rows = split_hi_lo(own_rows)

    total = None
    for k in range(gen_count):
        where = jnp.stack([chip ^ k, core])
        share = project(where, raw_columns, sibling, second_side, first_side[k])
        if k:
            share = move(share, lambda g, j, c, k=k: (g, j ^ k, c))
        total = share if total is None else total + share
    total = sum([move(total, lambda g, j, c, k=k: (g ^ k, j, c)) for k in others], total)
    rest = jnp.dot(inverse_factor, total, precision=HIGHEST)

    at_core = core[None]
    nothing = jnp.zeros_like(rest)
    solved = apply_weights(at_core, inverse_rows, rest, move(rest, swap), nothing, 1)
    kept = solved
    for t in range(gen_count - 1):
        near = move(kept, lambda g, j, c: (t + 1, t + 1, c) if g == j == t else None)
        near_sib = move(kept, lambda g, j, c: (t + 1, t + 1, 1 - c) if g == j == t else None)
        if t + 2 < gen_count:
            far, far_sib = nothing, nothing
            for z in range(t + 2, gen_count):
                far += move(kept, lambda g, j, c: (t, z, c) if g == j == t else None)
                far_sib += move(kept, lambda g, j, c: (t, z, 1 - c) if g == j == t else None)
            brought = apply_weights(at_core, own_rows, far, far_sib, nothing, 1)
            brought = move(brought, lambda g, j, c: (j, j, c) if g == t and j >= t + 2 else None)
        if t > 0:
            base = apply_weights(at_core, inverse_rows, rest, move(rest, swap), nothing, 1)
        else:
            base = solved
        stepped = apply_weights(at_core, step_rows, near, near_sib, base, -1)
        kept = jnp.where(jnp.logical_and(diagonal, gen_index == t + 1), stepped, kept)
        if t + 2 < gen_count:
            rest = rest - brought

    def rows_of(index):
        return lax.dynamic_slice_in_dim(kept, index * vec_dev, vec_dev, 0)

    result = jnp.where(diagonal, rows_of(gen_index), 0.0)
    for k in others:
        result += move(
            rows_of(gen_index ^ k), lambda g, j, c, k=k: (g ^ k, j, c) if g == j else None
        )
    return result


def solution(mesh):
    in_specs = (P(None, "gen", "fit"), P(), P("gen", "fit"), P("fit", "gen"))
    out_specs = P("gen", "fit")
    return jax.shard_map(
        on_device, mesh=mesh, in_specs=in_specs, out_specs=out_specs, check_vma=False
    )
```

time: 1180 us -> 211 us (0.18)
  blocking collectives: 481 us -> 0 us
  other arithmetic: 328 us -> 5.08 us
  local copies, waits for them, and re-layouts: 132 us -> 14.3 us
  waiting for transfers between devices: 170 us -> 64.7 us
  starting transfers between devices: 0.08 us -> 51.9 us
  Pallas kernels: 0 us -> 40.9 us
  matrix products: 47.8 us -> 17.7 us
    psum x17 -> x0, blocking collectives: 481 us -> none  [the longest x8 313 us: spread(): return lax.psum(kept, axis)]
    another operation x29 -> x6, other arithmetic: 324 us -> 1.46 us  [the longest x1 1.08 us: on_device(): jnp.stack([jnp.where(core == 0, own_inverse, corner), jnp.where(core == 0...]
    unnamed x4 -> x1, waiting for transfers between devices: 123 us -> 0.02 us
    another operation x106 -> x3, local copies, waits for them, and re-layouts: 80.3 us -> 1.69 us  [the longest x1 1.5 us: on_device(): own_rows = jnp.stack([metric_factor[:, :points], metric_factor[:, points:]])]
    ppermute x0 -> x44, waiting for transfers between devices: none -> 64.7 us  [move(): return lax.ppermute(value, BOTH, pairs)]
    ppermute x0 -> x44, starting transfers between devices: none -> 51.9 us  [move(): return lax.ppermute(value, BOTH, pairs)]
    all_gather x1, waiting for transfers between devices: 47.1 us -> 0.01 us  [on_device(): second_side = lax.all_gather(pieces, 'gen', axis=3, tiled=True)]
    pallas_call x0 -> x15, Pallas kernels: none -> 40.9 us  [the longest x4 20.2 us: project(): pl.pallas_call(project_kernel, grid_spec=pltpu.PrefetchScalarGridSpec(num...]
  transfers between devices with their start and end apart: 3 -> 45, of which waited for: 2 -> 10; matrix products, arithmetic and copies ran while one was open for 4% -> 15% of each run, Pallas kernels for 0% -> 19%
where the time goes in v1:
time: 211 us; the launch traced here: 209 us
  waiting for transfers between devices  64.7 us (31%)
  starting transfers between devices  51.9 us (25%)
  Pallas kernels  40.9 us (19%)
  matrix products  17.7 us (8%)
  local copies, waits for them, and re-layouts  14.3 us (7%)
  between operations  14.1 us (7%)
  other arithmetic  5.08 us (2%)
    ppermute x44, waiting for transfers between devices, move(): return lax.ppermute(value, BOTH, pairs)  64.7 us
    ppermute x44, starting transfers between devices, move(): return lax.ppermute(value, BOTH, pairs)  51.9 us
    pallas_call x4, Pallas kernels, project(): pl.pallas_call(project_kernel, grid_spec=pltpu.PrefetchScalarGridSpec(num...  20.2 us
    pallas_call x8, Pallas kernels, apply_weights(): pl.pallas_call(functools.partial(apply_kernel, sign), in_specs=[pl.BlockS...  7.29 us
    unnamed x38, local copies, waits for them, and re-layouts  7.04 us
    pallas_call x1, Pallas kernels, pivot_entries(): pl.pallas_call(pivot_kernel, grid=(vec_total,), in_specs=[pl.BlockSpec((1...  5.99 us
    dot_general x1, matrix products, on_device(): jnp.dot(inverse_rows[0], top, precision=HIGHEST)  5.52 us
    dot_general x1, matrix products, on_device(): jnp.dot(inverse_rows[1], bottom, precision=HIGHEST)  5.47 us
  transfers between devices with their start and end apart: 45, of which 10 were waited for; matrix products, arithmetic and copies ran while one was open for 15% of the time, Pallas kernels for 19%

profile of v1, /device:TPU:24, one launch (start us, length us, event | category | flops | bytes accessed | tf_op | source)
XLA Modules:
  0.0 208.7 jit_solution(14851090183438517265)
XLA Ops:
  8.0 3.1 %collective-permute-start.11 = (bf16[2,250,128]{2,1,0:T(8,128)(2,1)S(1)}, bf16[2,250,128]{2,1,0:T(8,128)(2,1)S(1)}, u32[]{:S(2)}, u32[]{:S(2)}) collective-permute-start(bf16[2,250,128]{2,1,0:T(8,128)(2,1)S(1)} %get-tuple-element.20), channel_id=1, source_target_pairs={{0,0},{1,1},{2,24},{3,25},{4,16},{5,17},{6,8},{7,9},{8,2},{9,3},{1... | collective-permute-start | bytes 384008 | tf_op jit(solution)/shard_map/ppermute | solution.py:30
  11.0 2.0 collective-permute-start.1
  13.1 2.6 %collective-permute-start.12 = (bf16[2,250,128]{2,1,0:T(8,128)(2,1)S(1)}, bf16[2,250,128]{2,1,0:T(8,128)(2,1)S(1)}, u32[]{:S(2)}, u32[]{:S(2)}) collective-permute-start(bf16[2,250,128]{2,1,0:T(8,128)(2,1)S(1)} %get-tuple-element.19), channel_id=1, source_target_pairs={{0,8},{1,9},{2,0},{3,1},{4,24},{5,25},{6,16},{7,17},{8,10},{9,11},... | collective-permute-start | bytes 384008 | tf_op jit(solution)/shard_map/ppermute | solution.py:30
  15.6 4.2 %collective-permute-start.13 = (bf16[2,250,128]{2,1,0:T(8,128)(2,1)S(1)}, bf16[2,250,128]{2,1,0:T(8,128)(2,1)S(1)}, u32[]{:S(2)}, u32[]{:S(2)}) collective-permute-start(bf16[2,250,128]{2,1,0:T(8,128)(2,1)S(1)} %get-tuple-element.18), channel_id=1, source_target_pairs={{0,16},{1,17},{2,8},{3,9},{4,0},{5,1},{6,24},{7,25},{8,18},{9,19},... | collective-permute-start | bytes 384008 | tf_op jit(solution)/shard_map/ppermute | solution.py:30
  21.1 11.9 %collective-permute-done.12 = bf16[2,250,128]{2,1,0:T(8,128)(2,1)S(1)} collective-permute-done((bf16[2,250,128]{2,1,0:T(8,128)(2,1)S(1)}, bf16[2,250,128]{2,1,0:T(8,128)(2,1)S(1)}, u32[]{:S(2)}, u32[]{:S(2)}) %collective-permute-start.12) | collective-permute-done | bytes 128032 | tf_op jit(solution)/shard_map/ppermute | solution.py:30
  33.0 13.1 %collective-permute-done.13 = bf16[2,250,128]{2,1,0:T(8,128)(2,1)S(1)} collective-permute-done((bf16[2,250,128]{2,1,0:T(8,128)(2,1)S(1)}, bf16[2,250,128]{2,1,0:T(8,128)(2,1)S(1)}, u32[]{:S(2)}, u32[]{:S(2)}) %collective-permute-start.13) | collective-permute-done | bytes 128032 | tf_op jit(solution)/shard_map/ppermute | solution.py:30
  47.2 3.4 %copy.17.raw_ref.own_ref = bf16[8,500,250]{2,1,0:T(8,128)(2,1)} copy(bf16[8,500,250]{2,0,1:T(8,128)(2,1)} %param.4) | data formatting | bytes 4000000 | tf_op args[0]
  51.9 6.0 %pivot_entries.1 = f32[8,8]{1,0:T(8,128)} custom-call(bf16[8,500,250]{2,1,0:T(8,128)(2,1)} %copy.17.raw_ref.own_ref, bf16[8,500]{1,0:T(8,128)(2,1)} %compare_convert_fusion.rows_ref, f32[8,250]{1,0:T(8,128)} %compare_convert_fusion.1.cols_ref), custom_call_target="tpu_custom_call" | custom-call | tf_op jit(solution)/shard_map/pivot_entries/pallas_call | solution.py:49
  58.4 1.5 slice_bitcast_fusion.3
  60.2 5.4 %invert_block.1 = f32[512,512]{1,0:T(8,128)S(1)} custom-call(s32[2]{0:T(128)S(1)} %pad_add_fusion.where_ref, f32[512,1024]{1,0:T(8,128)S(1)} %copy-done.6), custom_call_target="tpu_custom_call" | custom-call | tf_op jit(solution)/shard_map/invert_block/pallas_call | solution.py:154
  65.7 4.3 %collective-permute-start.4 = (f32[8,8]{1,0:T(8,128)S(1)}, f32[8,8]{1,0:T(8,128)S(1)}, u32[]{:S(2)}, u32[]{:S(2)}) collective-permute-start(f32[8,8]{1,0:T(8,128)S(1)} %add.141), channel_id=1, source_target_pairs={{0,2},{1,3},{2,0},{3,1},{4,6},{5,7},{6,4},{7,5},{8,10},{9,11},{10,... | collective-permute-start | bytes 776 | tf_op jit(solution)/shard_map/ppermute | solution.py:30
  72.7 2.8 %collective-permute-start.8 = (f32[8,8]{1,0:T(8,128)S(1)}, f32[8,8]{1,0:T(8,128)S(1)}, u32[]{:S(2)}, u32[]{:S(2)}) collective-permute-start(f32[8,8]{1,0:T(8,128)S(1)} %add_add_fusion.3), channel_id=1, source_target_pairs={{0,16},{1,17},{2,18},{3,19},{4,20},{5,21},{6,22},{7,23},{8,24},{9,... | collective-permute-start | bytes 776 | tf_op jit(solution)/shard_map/ppermute | solution.py:30
  76.3 2.3 %collective-permute-start.7 = (f32[8,8]{1,0:T(8,128)S(1)}, f32[8,8]{1,0:T(8,128)S(1)}, u32[]{:S(2)}, u32[]{:S(2)}) collective-permute-start(f32[8,8]{1,0:T(8,128)S(1)} %add_add_fusion.3), channel_id=1, source_target_pairs={{0,8},{1,9},{2,10},{3,11},{4,12},{5,13},{6,14},{7,15},{8,0},{9,1},... | collective-permute-start | bytes 776 | tf_op jit(solution)/shard_map/ppermute | solution.py:30
  78.6 2.4 %collective-permute-start.19 = (bf16[500,512]{1,0:T(8,128)(2,1)}, bf16[500,512]{1,0:T(8,128)(2,1)}, u32[]{:S(2)}, u32[]{:S(2)}) collective-permute-start(bf16[500,512]{1,0:T(8,128)(2,1)} %cp_ref.1), channel_id=1, source_target_pairs={{0,6},{1,7},{2,4},{3,5},{4,2},{5,3},{6,0},{7,1},{8,14},{9,15},{10,... | collective-permute-start | bytes 1536008 | tf_op jit(solution)/shard_map/ppermute | solution.py:30
  84.9 1.9 factor_inverse.1
  86.9 3.3 %copy.19.sib_ref = bf16[8,500,250]{2,1,0:T(8,128)(2,1)} copy(bf16[8,500,250]{2,0,1:T(8,128)(2,1)} %collective-permute-done.10) | data formatting | bytes 4000000 | tf_op jit(solution)/shard_map/ppermute | solution.py:30
  90.2 5.3 %collective-permute-done.19.cp_ref = bf16[500,512]{1,0:T(8,128)(2,1)} collective-permute-done((bf16[500,512]{1,0:T(8,128)(2,1)}, bf16[500,512]{1,0:T(8,128)(2,1)}, u32[]{:S(2)}, u32[]{:S(2)}) %collective-permute-start.19) | collective-permute-done | bytes 512032 | tf_op jit(solution)/shard_map/ppermute | solution.py:30
  95.5 1.6 copy-done.1
  97.1 1.6 copy-done.2
  98.7 5.3 %project.7 = f32[8,512]{1,0:T(8,128)S(1)} custom-call(s32[2]{0:T(128)S(1)} %pad_add_fusion.4.where_ref, bf16[8,500,250]{2,1,0:T(8,128)(2,1)S(1)} %copy-done, bf16[8,500,250]{2,1,0:T(8,128)(2,1)S(1)} %copy-done.1, bf16[4,2,250,512]{3,2,1,0:T(8,128)(2,1)S(1)} %copy-done.2, bf16[500,512]{1,0:T(8,128)(2,1)} %collective-permute-done.19.cp_ref), custom_call_target="tpu_custom_call" | custom-call | tf_op jit(solution)/shard_map/project/pallas_call | solution.py:97
  103.9 2.5 %collective-permute-start.20 = (f32[8,512]{1,0:T(8,128)S(1)}, f32[8,512]{1,0:T(8,128)S(1)}, u32[]{:S(2)}, u32[]{:S(2)}) collective-permute-start(f32[8,512]{1,0:T(8,128)S(1)} %project.7), channel_id=1, source_target_pairs={{0,6},{1,7},{2,4},{3,5},{4,2},{5,3},{6,0},{7,1},{8,14},{9,15},{10,... | collective-permute-start | bytes 49160 | tf_op jit(solution)/shard_map/ppermute | solution.py:30
  106.4 18.2 %collective-permute-done.17.cp_ref = bf16[500,512]{1,0:T(8,128)(2,1)} collective-permute-done((bf16[500,512]{1,0:T(8,128)(2,1)}, bf16[500,512]{1,0:T(8,128)(2,1)}, u32[]{:S(2)}, u32[]{:S(2)}) %collective-permute-start.17) | collective-permute-done | bytes 512032 | tf_op jit(solution)/shard_map/ppermute | solution.py:30
  124.7 5.3 %project.6 = f32[8,512]{1,0:T(8,128)S(1)} custom-call(s32[2]{0:T(128)S(1)} %pad_add_fusion.3.where_ref, bf16[8,500,250]{2,1,0:T(8,128)(2,1)S(1)} %copy-done, bf16[8,500,250]{2,1,0:T(8,128)(2,1)S(1)} %copy-done.1, bf16[4,2,250,512]{3,2,1,0:T(8,128)(2,1)S(1)} %copy-done.2, bf16[500,512]{1,0:T(8,128)(2,1)} %collective-permute-done.17.cp_ref), custom_call_target="tpu_custom_call" | custom-call | tf_op jit(solution)/shard_map/project/pallas_call | solution.py:97
  130.6 5.3 %project.5 = f32[8,512]{1,0:T(8,128)S(1)} custom-call(s32[2]{0:T(128)S(1)} %pad_add_fusion.2.where_ref, bf16[8,500,250]{2,1,0:T(8,128)(2,1)S(1)} %copy-done, bf16[8,500,250]{2,1,0:T(8,128)(2,1)S(1)} %copy-done.1, bf16[4,2,250,512]{3,2,1,0:T(8,128)(2,1)S(1)} %copy-done.2, bf16[500,512]{1,0:T(8,128)(2,1)} %collective-permute-done.15.cp_ref), custom_call_target="tpu_custom_call" | custom-call | tf_op jit(solution)/shard_map/project/pallas_call | solution.py:97
  137.1 4.7 %fusion.14 = f32[512,512]{1,0:T(8,128)S(1)} fusion(f32[512,512]{1,0:T(8,128)} %collective-permute-done, f32[512,1024]{1,0:T(8,128)S(1)} %copy-done.7), kind=kOutput, calls=%fused_computation.27 | convolution fusion | flops 1610612736 | bytes 3145728 | tf_op jit(solution)/shard_map/dot_general | solution.py:242
  141.9 4.4 %project.4 = f32[8,512]{1,0:T(8,128)S(1)} custom-call(s32[2]{0:T(128)S(1)} %pad_add_fusion.1.where_ref, bf16[8,500,250]{2,1,0:T(8,128)(2,1)S(1)} %copy-done, bf16[8,500,250]{2,1,0:T(8,128)(2,1)S(1)} %copy-done.1, bf16[4,2,250,512]{3,2,1,0:T(8,128)(2,1)S(1)} %copy-done.2, bf16[500,512]{1,0:T(8,128)(2,1)S(1)} %copy-done.8), custom_call_target="tpu_custom_call" | custom-call | tf_op jit(solution)/shard_map/project/pallas_call | solution.py:97
  149.9 1.9 fusion.10
  158.7 5.5 %fusion.3 = f32[512,1024]{1,0:T(8,128)S(1)} fusion(f32[512,1024]{1,0:T(8,128)} %collective-permute-done.2, f32[512,1024]{1,0:T(8,128)} %collective-permute-done.1, pred[]{:T(512)S(6)} %eq.50, f32[512,512]{1,0:T(8,128)S(1)} %invert_block.1), kind=kOutput, calls=%fused_computation.12 | convolution fusion | flops 3222011904 | bytes 7340033 | tf_op jit(solution)/shard_map/dot_general | solution.py:252
  164.2 5.5 %fusion.7 = f32[512,1024]{1,0:T(8,128)S(1)} fusion(f32[512,1024]{1,0:T(8,128)S(1)} %fusion.3, f32[512,512]{1,0:T(8,128)S(1)} %fusion.10, f32[512,1024]{1,0:T(8,128)} %collective-permute-done.1, f32[512,1024]{1,0:T(8,128)} %collective-permute-done.2, pred[]{:T(512)S(6)} %eq.50), kind=kOutput, calls=%fused_computation.16 | convolution fusion | flops 3222274048 | bytes 9437185 | tf_op jit(solution)/shard_map/dot_general | solution.py:252
  170.3 1.6 collective-permute-start.32
  174.6 4.9 %collective-permute-done.32 = f32[8,512]{1,0:T(8,128)S(1)} collective-permute-done((f32[8,512]{1,0:T(8,128)S(1)}, f32[8,512]{1,0:T(8,128)S(1)}, u32[]{:S(2)}, u32[]{:S(2)}) %collective-permute-start.32) | collective-permute-done | bytes 16416 | tf_op jit(solution)/shard_map/ppermute | solution.py:30
  193.4 7.8 %collective-permute-done.43 = f32[2,512]{1,0:T(2,128)S(1)} collective-permute-done((f32[2,512]{1,0:T(2,128)S(1)}, f32[2,512]{1,0:T(2,128)S(1)}, u32[]{:S(2)}, u32[]{:S(2)}) %collective-permute-start.43) | collective-permute-done | bytes 4128 | tf_op jit(solution)/shard_map/ppermute | solution.py:30
  (151 shorter events, 43.3 us)
Async XLA Ops:
  6.5 88.9 %all-gather.2.cloned.1.call-start = ((), (), s32[]{:S(2)}) async-start(), calls=%async_computation | async-start | bytes 2621440 | tf_op jit(solution)/shard_map/all_gather | solution.py:223
  8.0 13.1 %collective-permute-start.11 = (bf16[2,250,128]{2,1,0:T(8,128)(2,1)S(1)}, bf16[2,250,128]{2,1,0:T(8,128)(2,1)S(1)}, u32[]{:S(2)}, u32[]{:S(2)}) collective-permute-start(bf16[2,250,128]{2,1,0:T(8,128)(2,1)S(1)} %get-tuple-element.20), channel_id=1, source_target_pairs={{0,0},{1,1},{2,24},{3,25},{4,16},{5,17},{6,8},{7,9},{8,2},{9,3},{1... | collective-permute-start | bytes 384008 | tf_op jit(solution)/shard_map/ppermute | solution.py:30
  11.0 59.0 %collective-permute-start.1 = (f32[512,1024]{1,0:T(8,128)S(1)}, f32[512,1024]{1,0:T(8,128)}, u32[]{:S(2)}, u32[]{:S(2)}) collective-permute-start(f32[512,1024]{1,0:T(8,128)S(1)} %copy-done.6), channel_id=1, source_target_pairs={{2,10},{3,11},{12,20},{13,21},{22,30},{23,31}} | collective-permute-start | bytes 6291464 | tf_op jit(solution)/shard_map/ppermute | solution.py:30
  13.1 19.9 %collective-permute-start.12 = (bf16[2,250,128]{2,1,0:T(8,128)(2,1)S(1)}, bf16[2,250,128]{2,1,0:T(8,128)(2,1)S(1)}, u32[]{:S(2)}, u32[]{:S(2)}) collective-permute-start(bf16[2,250,128]{2,1,0:T(8,128)(2,1)S(1)} %get-tuple-element.19), channel_id=1, source_target_pairs={{0,8},{1,9},{2,0},{3,1},{4,24},{5,25},{6,16},{7,17},{8,10},{9,11},... | collective-permute-start | bytes 384008 | tf_op jit(solution)/shard_map/ppermute | solution.py:30
  15.6 30.5 %collective-permute-start.13 = (bf16[2,250,128]{2,1,0:T(8,128)(2,1)S(1)}, bf16[2,250,128]{2,1,0:T(8,128)(2,1)S(1)}, u32[]{:S(2)}, u32[]{:S(2)}) collective-permute-start(bf16[2,250,128]{2,1,0:T(8,128)(2,1)S(1)} %get-tuple-element.18), channel_id=1, source_target_pairs={{0,16},{1,17},{2,8},{3,9},{4,0},{5,1},{6,24},{7,25},{8,18},{9,19},... | collective-permute-start | bytes 384008 | tf_op jit(solution)/shard_map/ppermute | solution.py:30
  19.8 26.3 %collective-permute-start.14 = (bf16[2,250,128]{2,1,0:T(8,128)(2,1)S(1)}, bf16[2,250,128]{2,1,0:T(8,128)(2,1)S(1)}, u32[]{:S(2)}, u32[]{:S(2)}) collective-permute-start(bf16[2,250,128]{2,1,0:T(8,128)(2,1)S(1)} %get-tuple-element.17), channel_id=1, source_target_pairs={{0,24},{1,25},{2,16},{3,17},{4,8},{5,9},{6,0},{7,1},{8,26},{9,27},... | collective-permute-start | bytes 384008 | tf_op jit(solution)/shard_map/ppermute | solution.py:30
  47.2 35.0 %collective-permute-start.10 = (bf16[8,500,250]{2,0,1:T(8,128)(2,1)}, bf16[8,500,250]{2,0,1:T(8,128)(2,1)}, u32[]{:S(2)}, u32[]{:S(2)}) collective-permute-start(bf16[8,500,250]{2,0,1:T(8,128)(2,1)} %param.4), channel_id=1, source_target_pairs={{0,1},{1,0},{2,3},{3,2},{4,5},{5,4},{6,7},{7,6},{8,9},{9,8},{10,11... | collective-permute-start | bytes 6000008 | tf_op jit(solution)/shard_map/ppermute | solution.py:30
  60.0 10.0 %collective-permute-start.6 = (f32[8,8]{1,0:T(8,128)S(1)}, f32[8,8]{1,0:T(8,128)S(1)}, u32[]{:S(2)}, u32[]{:S(2)}) collective-permute-start(f32[8,8]{1,0:T(8,128)S(1)} %add.141), channel_id=1, source_target_pairs={{0,6},{1,7},{2,4},{3,5},{4,2},{5,3},{6,0},{7,1},{8,14},{9,15},{10,... | collective-permute-start | bytes 776 | tf_op jit(solution)/shard_map/ppermute | solution.py:30
  65.6 5.0 %collective-permute-start.5 = (f32[8,8]{1,0:T(8,128)S(1)}, f32[8,8]{1,0:T(8,128)S(1)}, u32[]{:S(2)}, u32[]{:S(2)}) collective-permute-start(f32[8,8]{1,0:T(8,128)S(1)} %add.141), channel_id=1, source_target_pairs={{0,4},{1,5},{2,6},{3,7},{4,0},{5,1},{6,2},{7,3},{8,12},{9,13},{10,... | collective-permute-start | bytes 776 | tf_op jit(solution)/shard_map/ppermute | solution.py:30
  65.7 5.9 %collective-permute-start.4 = (f32[8,8]{1,0:T(8,128)S(1)}, f32[8,8]{1,0:T(8,128)S(1)}, u32[]{:S(2)}, u32[]{:S(2)}) collective-permute-start(f32[8,8]{1,0:T(8,128)S(1)} %add.141), channel_id=1, source_target_pairs={{0,2},{1,3},{2,0},{3,1},{4,6},{5,7},{6,4},{7,5},{8,10},{9,11},{10,... | collective-permute-start | bytes 776 | tf_op jit(solution)/shard_map/ppermute | solution.py:30
  70.1 67.1 %collective-permute-start = (f32[512,512]{1,0:T(8,128)S(1)}, f32[512,512]{1,0:T(8,128)}, u32[]{:S(2)}, u32[]{:S(2)}) collective-permute-start(f32[512,512]{1,0:T(8,128)S(1)} %invert_block.1), channel_id=1, source_target_pairs={{0,1},{1,0},{2,3},{3,2},{4,5},{5,4},{6,7},{7,6},{8,9},{9,8},{10,11... | collective-permute-start | bytes 3145736 | tf_op jit(solution)/shard_map/ppermute | solution.py:30
  70.1 88.0 %collective-permute-start.2 = (f32[512,1024]{1,0:T(8,128)}, f32[512,1024]{1,0:T(8,128)}, u32[]{:S(2)}, u32[]{:S(2)}) collective-permute-start(f32[512,1024]{1,0:T(8,128)} %collective-permute-done.1), channel_id=1, source_target_pairs={{0,1},{1,0},{2,3},{3,2},{4,5},{5,4},{6,7},{7,6},{8,9},{9,8},{10,11... | collective-permute-start | bytes 6291464 | tf_op jit(solution)/shard_map/ppermute | solution.py:30
  72.7 6.0 %collective-permute-start.8 = (f32[8,8]{1,0:T(8,128)S(1)}, f32[8,8]{1,0:T(8,128)S(1)}, u32[]{:S(2)}, u32[]{:S(2)}) collective-permute-start(f32[8,8]{1,0:T(8,128)S(1)} %add_add_fusion.3), channel_id=1, source_target_pairs={{0,16},{1,17},{2,18},{3,19},{4,20},{5,21},{6,22},{7,23},{8,24},{9,... | collective-permute-start | bytes 776 | tf_op jit(solution)/shard_map/ppermute | solution.py:30
  76.3 4.8 %collective-permute-start.7 = (f32[8,8]{1,0:T(8,128)S(1)}, f32[8,8]{1,0:T(8,128)S(1)}, u32[]{:S(2)}, u32[]{:S(2)}) collective-permute-start(f32[8,8]{1,0:T(8,128)S(1)} %add_add_fusion.3), channel_id=1, source_target_pairs={{0,8},{1,9},{2,10},{3,11},{4,12},{5,13},{6,14},{7,15},{8,0},{9,1},... | collective-permute-start | bytes 776 | tf_op jit(solution)/shard_map/ppermute | solution.py:30
  78.6 16.9 %collective-permute-start.19 = (bf16[500,512]{1,0:T(8,128)(2,1)}, bf16[500,512]{1,0:T(8,128)(2,1)}, u32[]{:S(2)}, u32[]{:S(2)}) collective-permute-start(bf16[500,512]{1,0:T(8,128)(2,1)} %cp_ref.1), channel_id=1, source_target_pairs={{0,6},{1,7},{2,4},{3,5},{4,2},{5,3},{6,0},{7,1},{8,14},{9,15},{10,... | collective-permute-start | bytes 1536008 | tf_op jit(solution)/shard_map/ppermute | solution.py:30
  81.0 43.6 %collective-permute-start.17 = (bf16[500,512]{1,0:T(8,128)(2,1)}, bf16[500,512]{1,0:T(8,128)(2,1)}, u32[]{:S(2)}, u32[]{:S(2)}) collective-permute-start(bf16[500,512]{1,0:T(8,128)(2,1)} %cp_ref.1), channel_id=1, source_target_pairs={{0,4},{1,5},{2,6},{3,7},{4,0},{5,1},{6,2},{7,3},{8,12},{9,13},{10,... | collective-permute-start | bytes 1536008 | tf_op jit(solution)/shard_map/ppermute | solution.py:30
  82.1 48.5 %collective-permute-start.15 = (bf16[500,512]{1,0:T(8,128)(2,1)}, bf16[500,512]{1,0:T(8,128)(2,1)}, u32[]{:S(2)}, u32[]{:S(2)}) collective-permute-start(bf16[500,512]{1,0:T(8,128)(2,1)} %cp_ref.1), channel_id=1, source_target_pairs={{0,2},{1,3},{2,0},{3,1},{4,6},{5,7},{6,4},{7,5},{8,10},{9,11},{10,... | collective-permute-start | bytes 1536008 | tf_op jit(solution)/shard_map/ppermute | solution.py:30
  103.9 42.4 %collective-permute-start.20 = (f32[8,512]{1,0:T(8,128)S(1)}, f32[8,512]{1,0:T(8,128)S(1)}, u32[]{:S(2)}, u32[]{:S(2)}) collective-permute-start(f32[8,512]{1,0:T(8,128)S(1)} %project.7), channel_id=1, source_target_pairs={{0,6},{1,7},{2,4},{3,5},{4,2},{5,3},{6,0},{7,1},{8,14},{9,15},{10,... | collective-permute-start | bytes 49160 | tf_op jit(solution)/shard_map/ppermute | solution.py:30
  130.0 16.3 %collective-permute-start.18 = (f32[8,512]{1,0:T(8,128)S(1)}, f32[8,512]{1,0:T(8,128)S(1)}, u32[]{:S(2)}, u32[]{:S(2)}) collective-permute-start(f32[8,512]{1,0:T(8,128)S(1)} %project.6), channel_id=1, source_target_pairs={{0,4},{1,5},{2,6},{3,7},{4,0},{5,1},{6,2},{7,3},{8,12},{9,13},{10,... | collective-permute-start | bytes 49160 | tf_op jit(solution)/shard_map/ppermute | solution.py:30
  135.9 10.4 %collective-permute-start.16 = (f32[8,512]{1,0:T(8,128)S(1)}, f32[8,512]{1,0:T(8,128)S(1)}, u32[]{:S(2)}, u32[]{:S(2)}) collective-permute-start(f32[8,512]{1,0:T(8,128)S(1)} %project.5), channel_id=1, source_target_pairs={{0,2},{1,3},{2,0},{3,1},{4,6},{5,7},{6,4},{7,5},{8,10},{9,11},{10,... | collective-permute-start | bytes 49160 | tf_op jit(solution)/shard_map/ppermute | solution.py:30
  146.3 5.4 %collective-permute-start.23 = (f32[8,512]{1,0:T(8,128)S(1)}, f32[8,512]{1,0:T(8,128)S(1)}, u32[]{:S(2)}, u32[]{:S(2)}) collective-permute-start(f32[8,512]{1,0:T(8,128)S(1)} %add_add_fusion), channel_id=1, source_target_pairs={{0,24},{1,25},{2,26},{3,27},{4,28},{5,29},{6,30},{7,31},{8,16},{9,... | collective-permute-start | bytes 49160 | tf_op jit(solution)/shard_map/ppermute | solution.py:30
  154.7 15.6 %collective-permute-start.25 = (f32[8,512]{1,0:T(8,128)S(1)}, f32[8,512]{1,0:T(8,128)S(1)}, u32[]{:S(2)}, u32[]{:S(2)}) collective-permute-start(f32[8,512]{1,0:T(8,128)S(1)} %apply_weights.8.bias_ref), channel_id=1, source_target_pairs={{0,10},{1,11}} | collective-permute-start | bytes 49160 | tf_op jit(solution)/shard_map/ppermute | solution.py:30
  155.4 16.5 %collective-permute-start.26 = (f32[8,512]{1,0:T(8,128)S(1)}, f32[8,512]{1,0:T(8,128)S(1)}, u32[]{:S(2)}, u32[]{:S(2)}) collective-permute-start(f32[8,512]{1,0:T(8,128)S(1)} %apply_weights.8.bias_ref), channel_id=1, source_target_pairs={{0,11},{1,10}} | collective-permute-start | bytes 49160 | tf_op jit(solution)/shard_map/ppermute | solution.py:30
  156.1 17.4 %collective-permute-start.29 = (f32[8,512]{1,0:T(8,128)S(1)}, f32[8,512]{1,0:T(8,128)S(1)}, u32[]{:S(2)}, u32[]{:S(2)}) collective-permute-start(f32[8,512]{1,0:T(8,128)S(1)} %apply_weights.8.bias_ref), channel_id=1, source_target_pairs={{0,4},{1,5}} | collective-permute-start | bytes 49160 | tf_op jit(solution)/shard_map/ppermute | solution.py:30
  156.7 17.8 %collective-permute-start.30 = (f32[8,512]{1,0:T(8,128)S(1)}, f32[8,512]{1,0:T(8,128)S(1)}, u32[]{:S(2)}, u32[]{:S(2)}) collective-permute-start(f32[8,512]{1,0:T(8,128)S(1)} %apply_weights.8.bias_ref), channel_id=1, source_target_pairs={{0,6},{1,7}} | collective-permute-start | bytes 49160 | tf_op jit(solution)/shard_map/ppermute | solution.py:30
  158.1 16.5 %collective-permute-start.31 = (f32[8,512]{1,0:T(8,128)S(1)}, f32[8,512]{1,0:T(8,128)S(1)}, u32[]{:S(2)}, u32[]{:S(2)}) collective-permute-start(f32[8,512]{1,0:T(8,128)S(1)} %apply_weights.8.bias_ref), channel_id=1, source_target_pairs={{0,5},{1,4}} | collective-permute-start | bytes 49160 | tf_op jit(solution)/shard_map/ppermute | solution.py:30
  170.3 9.1 %collective-permute-start.32 = (f32[8,512]{1,0:T(8,128)S(1)}, f32[8,512]{1,0:T(8,128)S(1)}, u32[]{:S(2)}, u32[]{:S(2)}) collective-permute-start(f32[8,512]{1,0:T(8,128)S(1)} %apply_weights.8.bias_ref), channel_id=1, source_target_pairs={{0,7},{1,6}} | collective-permute-start | bytes 49160 | tf_op jit(solution)/shard_map/ppermute | solution.py:30
  172.8 8.9 %collective-permute-start.37 = (f32[8,512]{1,0:T(8,128)S(1)}, f32[8,512]{1,0:T(8,128)S(1)}, u32[]{:S(2)}, u32[]{:S(2)}) collective-permute-start(f32[8,512]{1,0:T(8,128)S(1)} %broadcast_select_fusion), channel_id=1, source_target_pairs={{10,14},{11,15}} | collective-permute-start | bytes 49160 | tf_op jit(solution)/shard_map/ppermute | solution.py:30
  173.5 8.2 %collective-permute-start.38 = (f32[8,512]{1,0:T(8,128)S(1)}, f32[8,512]{1,0:T(8,128)S(1)}, u32[]{:S(2)}, u32[]{:S(2)}) collective-permute-start(f32[8,512]{1,0:T(8,128)S(1)} %broadcast_select_fusion), channel_id=1, source_target_pairs={{10,15},{11,14}} | collective-permute-start | bytes 49160 | tf_op jit(solution)/shard_map/ppermute | solution.py:30
  190.8 10.4 %collective-permute-start.43 = (f32[2,512]{1,0:T(2,128)S(1)}, f32[2,512]{1,0:T(2,128)S(1)}, u32[]{:S(2)}, u32[]{:S(2)}) collective-permute-start(f32[2,512]{1,0:T(2,128)S(1)} %get-tuple-element.22), channel_id=1, source_target_pairs={{0,24},{1,25},{10,18},{11,19},{20,12},{21,13},{30,6},{31,7}} | collective-permute-start | bytes 12296 | tf_op jit(solution)/shard_map/ppermute | solution.py:30
  192.1 9.2 %collective-permute-start.42 = (f32[2,512]{1,0:T(2,128)S(1)}, f32[2,512]{1,0:T(2,128)S(1)}, u32[]{:S(2)}, u32[]{:S(2)}) collective-permute-start(f32[2,512]{1,0:T(2,128)S(1)} %get-tuple-element.23), channel_id=1, source_target_pairs={{0,16},{1,17},{10,26},{11,27},{20,4},{21,5},{30,14},{31,15}} | collective-permute-start | bytes 12296 | tf_op jit(solution)/shard_map/ppermute | solution.py:30
  192.7 8.5 %collective-permute-start.41 = (f32[2,512]{1,0:T(2,128)S(1)}, f32[2,512]{1,0:T(2,128)S(1)}, u32[]{:S(2)}, u32[]{:S(2)}) collective-permute-start(f32[2,512]{1,0:T(2,128)S(1)} %get-tuple-element.21), channel_id=1, source_target_pairs={{0,8},{1,9},{10,2},{11,3},{20,28},{21,29},{30,22},{31,23}} | collective-permute-start | bytes 12296 | tf_op jit(solution)/shard_map/ppermute | solution.py:30
  (28 other events, 97.0 us)
Sparse Core Ops, SparseCore 0:
  47.3 37.9 all-gather.1

commit v2 on v1

--- a/solution.py
+++ b/solution.py
@@ -37,27 +37,46 @@
     return hi.astype(BF16), (x - hi).astype(BF16)
 
 
-def pivot_kernel(raw_ref, rows_ref, cols_ref, out_ref):
-    i = pl.program_id(0)
-    picked = jnp.dot(rows_ref[...], raw_ref[0], preferred_element_type=F32)
-    entries = jnp.sum(picked * cols_ref[...], axis=1, keepdims=True)
-    out_ref[pl.ds(i, 1), :] = entries.T
-
-
-def pivot_entries(raw, row_hits, col_hits):
-    vec_total, orb, pair = raw.shape
+def pivot_kernel(row_ref, own_ref, sib_ref, own_col_ref, sib_col_ref, out_ref, buffer, sems):
+    count, orb = out_ref.shape[1], own_ref.shape[0]
+    copies = []
+    for i in range(count):
+        row = jnp.clip(row_ref[i], 0, orb - 1)
+        for n, ref in enumerate((own_ref, sib_ref)):
+            copies.append(
+                pltpu.make_async_copy(ref.at[row], buffer.at[2 * i + n], sems.at[2 * i + n])
+            )
+            copies[-1].start()
+    lane = lax.broadcasted_iota(jnp.int32, buffer.shape[1:], 1)
+    for i in range(count):
+        copies[2 * i].wait()
+        copies[2 * i + 1].wait()
+        local = jnp.logical_and(row_ref[i] >= 0, row_ref[i] < orb)
+        kept = jnp.where(lane == own_col_ref[i], buffer[2 * i].astype(F32), 0.0)
+        kept += jnp.where(lane == sib_col_ref[i], buffer[2 * i + 1].astype(F32), 0.0)
+        kept = jnp.where(local, kept, 0.0)
+        out_ref[:, i : i + 1] = jnp.sum(kept, axis=1, keepdims=True)
+
+
+def pivot_entries(own, sib, rows, own_cols, sib_cols):
+    vec_total, pair = own.shape[1:]
     return pl.pallas_call(
         pivot_kernel,
-        grid=(vec_total,),
         in_specs=[
-            pl.BlockSpec((1, orb, pair), lambda i: (i, 0, 0)),
-            pl.BlockSpec((vec_total, orb), lambda i: (0, 0)),
-            pl.BlockSpec((vec_total, pair), lambda i: (0, 0)),
+            pl.BlockSpec(memory_space=pltpu.SMEM),
+            pl.BlockSpec(memory_space=pl.ANY),
+            pl.BlockSpec(memory_space=pl.ANY),
+            pl.BlockSpec(memory_space=pltpu.SMEM),
+            pl.BlockSpec(memory_space=pltpu.SMEM),
         ],
-        out_specs=pl.BlockSpec((vec_total, vec_total), lambda i: (0, 0)),
+        out_specs=pl.BlockSpec(memory_space=pltpu.VMEM),
         out_shape=jax.ShapeDtypeStruct((vec_total, vec_total), F32),
+        scratch_shapes=[
+            pltpu.VMEM((2 * vec_total, vec_total, pair), BF16),
+            pltpu.SemaphoreType.DMA((2 * vec_total,)),
+        ],
         name="pivot_entries",
-    )(raw, row_hits, col_hits)
+    )(rows, own, sib, own_cols, sib_cols)
 
 
 def factor_inverse_kernel(block_ref, out_ref):
@@ -83,34 +102,63 @@
     )(block)
 
 
-def project_kernel(where_ref, own_ref, sib_ref, cq_ref, cp_ref, out_ref):
-    i = pl.program_id(0)
-    core = where_ref[1]
-    mixed = jnp.dot(own_ref[0], cq_ref[0, core], preferred_element_type=F32)
-    mixed += jnp.dot(sib_ref[0], cq_ref[0, 1 - core], preferred_element_type=F32)
-    out_ref[pl.ds(i, 1), :] = jnp.sum(mixed * cp_ref[...].astype(F32), axis=0, keepdims=True)
-
-
-def project(where, own, sib, cq, cp):
-    vec_total, orb, pair = own.shape
-    points = cp.shape[1]
-    return pl.pallas_call(
-        project_kernel,
+def project_kernel(vec_total, chunk, group, where_ref, own_ref, sib_ref, cp_ref, *rest):
+    part_refs, (out_ref, cq, cp) = rest[:-3], rest[-3:]
+    part = part_refs[0].shape[-1]
+    step = pl.program_id(0)
+    core = where_ref[0]
+
+    @pl.when(step == 0)
+    def _():
+        for n, ref in enumerate(part_refs):
+            start = 0
+            if len(part_refs) > 1:
+                start = pl.multiple_of(where_ref[1 + n] * part, part)
+            cq[:, :, pl.ds(start, part)] = ref[...]
+        cp[...] = cp_ref[...].astype(F32)
+        out_ref[...] = jnp.zeros_like(out_ref)
+
+    rows = group * vec_total
+
+    def one_group(i, total):
+        start = pl.multiple_of(i * rows, 8)
+        mixed = jnp.dot(own_ref[pl.ds(start, rows), :], cq[core], preferred_element_type=F32)
+        mixed += jnp.dot(sib_ref[pl.ds(start, rows), :], cq[1 - core], preferred_element_type=F32)
+        for p in range(group):
+            at = step * chunk + i * group + p
+            total += mixed[p * vec_total : (p + 1) * vec_total] * cp[pl.ds(at, 1), :]
+        return total
+
+    out_ref[...] = lax.fori_loop(0, chunk // group, one_group, out_ref[...])
+
+
+def project(where, own, sib, cp, parts):
+    orb, points = cp.shape
+    pair = own.shape[1]
+    vec_total = own.shape[0] // orb
+    chunk, group = 125, 25
+    part_shape = parts[0].shape
+    return pl.pallas_call(
+        functools.partial(project_kernel, vec_total, chunk, group),
         grid_spec=pltpu.PrefetchScalarGridSpec(
             num_scalar_prefetch=1,
-            grid=(vec_total,),
+            grid=(orb // chunk,),
             in_specs=[
-                pl.BlockSpec((1, orb, pair), lambda i, s: (i, 0, 0)),
-                pl.BlockSpec((1, orb, pair), lambda i, s: (i, 0, 0)),
-                pl.BlockSpec((1, 2, pair, points), lambda i, s: (s[0], 0, 0, 0)),
+                pl.BlockSpec((chunk * vec_total, pair), lambda i, s: (i, 0)),
+                pl.BlockSpec((chunk * vec_total, pair), lambda i, s: (i, 0)),
                 pl.BlockSpec((orb, points), lambda i, s: (0, 0)),
+            ]
+            + [pl.BlockSpec(part_shape, lambda i, s: (0, 0, 0))] * len(parts),
+            out_specs=pl.BlockSpec((vec_total, points), lambda i, s: (0, 0)),
+            scratch_shapes=[
+                pltpu.VMEM((2, pair, points), BF16),
+                pltpu.VMEM((orb, points), F32),
             ],
-            out_specs=pl.BlockSpec((vec_total, points), lambda i, s: (0, 0)),
         ),
         out_shape=jax.ShapeDtypeStruct((vec_total, points), F32),
         compiler_params=pltpu.CompilerParams(vmem_limit_bytes=32 << 20),
         name="project",
-    )(where, own, sib, cq, cp)
+    )(where, own, sib, cp, *parts)
 
 
 def invert_kernel(where_ref, block_ref, out_ref):
@@ -208,31 +256,51 @@
     diagonal = gen_index == chip
     swap = lambda g, j, c: (g, j, 1 - c)
 
-    first_side = [collocation] + [
-        move(collocation, lambda g, j, c, k=k: (g, j ^ k, c)) for k in others
-    ]
+    from_left, from_right = [collocation], [collocation]
+    for _ in others:
+        from_left.append(move(from_left[-1], lambda g, j, c: (g, j + 1, c) if j + 1 < gen_count else None))
+        from_right.append(move(from_right[-1], lambda g, j, c: (g, j - 1, c) if j > 0 else None))
+
+    def first_side(k):
+        block = None
+        for j in range(gen_count):
+            away = j - (j ^ k)
+            held = from_left[away] if away > 0 else from_right[-away]
+            block = held if block is None else jnp.where(chip == j, held, block)
+        return block
+
     part = points // gen_count
     halves = collocation.reshape(2, orb_block // 2, points)
-    pieces = []
-    for m in range(gen_count):
-        start = lax.rem(m - chip + gen_count, gen_count) * part
-        piece = lax.dynamic_slice_in_dim(halves, start, part, 2)
-        pieces.append(move(piece, lambda g, j, c, m=m: ((m - j) % gen_count, g, c)))
-    pieces = jnp.stack(pieces + pieces)
-    pieces = lax.dynamic_slice_in_dim(pieces, gen_index, gen_count, 0)
-    second_side = lax.all_gather(pieces, "gen", axis=3, tiled=True)
+    spread = []
+    for k in range(gen_count):
+        piece = lax.dynamic_slice_in_dim(halves, (gen_index ^ k) * part, part, 2)
+        spread.append(move(piece, lambda g, j, c, k=k: (g ^ k, j, c)) if k else piece)
+    spread = jnp.stack(spread)
+    own_parts = []
+    for k in range(gen_count):
+        piece = lax.dynamic_index_in_dim(spread, gen_index ^ chip ^ k, 0, keepdims=False)
+        own_parts.append(move(piece, lambda g, j, c, k=k: (g, j ^ k, c)) if k else piece)
+    near_parts, far_parts = [own_parts[0]], [jnp.stack(own_parts[1:])]
+    for k in others:
+        near_parts.append(move(near_parts[0], lambda g, j, c, k=k: (g ^ k, j, c)))
+        far_parts.append(move(far_parts[0], lambda g, j, c, k=k: (g ^ k, j, c)))
+
+    def second_side(k):
+        parts = near_parts if k == 0 else [x[k - 1] for x in far_parts]
+        if part % 128 == 0:
+            return parts
+        whole = jnp.zeros(halves.shape, BF16)
+        for n, x in enumerate(parts):
+            whole = lax.dynamic_update_slice_in_dim(whole, x, (gen_index ^ n) * part, 2)
+        return [whole]
+
     sibling = move(raw_columns, swap)
-
-    pair_first = pivot_pairs // NORB
-    pair_second = pivot_pairs % NORB
-    row_hits = (
-        pair_first[:, None] == gen_index * orb_block + jnp.arange(orb_block)[None, :]
-    ).astype(BF16)
-    col_hits = (
-        pair_second[:, None] == fit_index * pair_block + jnp.arange(pair_block)[None, :]
-    ).astype(F32)
-    entries = pivot_entries(raw_columns, row_hits, col_hits)
-    entries = entries + move(entries, swap)
+    own_raw = raw_columns.transpose(1, 0, 2)
+    sib_raw = sibling.transpose(1, 0, 2)
+    pivot_rows = pivot_pairs // NORB - gen_index * orb_block
+    own_cols = pivot_pairs % NORB - fit_index * pair_block
+    sib_cols = pivot_pairs % NORB - (fit_index ^ 1) * pair_block
+    entries = pivot_entries(own_raw, sib_raw, pivot_rows, own_cols, sib_cols)
     entries = sum([move(entries, lambda g, j, c, k=k: (g, j ^ k, c)) for k in others], entries)
     entries = sum([move(entries, lambda g, j, c, k=k: (g ^ k, j, c)) for k in others], entries)
     inverse_factor = factor_inverse(entries)
@@ -258,10 +326,17 @@
     step_rows = split_hi_lo(step_rows)
     own_rows = split_hi_lo(own_rows)
 
+    own_raw = own_raw.reshape(orb_block * vec_total, pair_block)
+    sib_raw = sib_raw.reshape(orb_block * vec_total, pair_block)
+    where = jnp.stack([core] + [gen_index ^ k for k in range(gen_count)])
     total = None
     for k in range(gen_count):
-        where = jnp.stack([chip ^ k, core])
-        share = project(where, raw_columns, sibling, second_side, first_side[k])
+        block = first_side(k)
+        if k == gen_count - 1:
+            block, step_rows, inverse_rows, own_rows = lax.optimization_barrier(
+                (block, step_rows, inverse_rows, own_rows)
+            )
+        share = project(where, own_raw, sib_raw, block, second_side(k))
         if k:
             share = move(share, lambda g, j, c, k=k: (g, j ^ k, c))
         total = share if total is None else total + share

time: 211 us -> 245 us (1.16)
  starting transfers between devices: 51.9 us -> 109 us
  waiting for transfers between devices: 64.7 us -> 31.1 us
  between operations: 14.1 us -> 0.76 us
  local copies, waits for them, and re-layouts: 14.3 us -> 22.5 us
  other arithmetic: 5.08 us -> 12.1 us
  Pallas kernels: 40.9 us -> 47.7 us
    ppermute x44 -> x54, starting transfers between devices: 51.9 us -> 109 us  [move(): return lax.ppermute(value, BOTH, pairs)]
    ppermute x44 -> x54, waiting for transfers between devices: 64.7 us -> 31.1 us  [move(): return lax.ppermute(value, BOTH, pairs)]
    pallas_call x5, Pallas kernels: 26.2 us -> 33 us  [the longest x4 30.2 us: project(): pl.pallas_call(functools.partial(project_kernel, vec_total, chunk, group)...]
    squeeze x0 -> x4, local copies, waits for them, and re-layouts: none -> 6.22 us  [the longest x3 5.38 us: second_side(): parts = near_parts if k == 0 else [x[k - 1] for x in far_parts]]
    unnamed x38 -> x52, local copies, waits for them, and re-layouts: 7.04 us -> 13 us
    convert_element_type x3 -> x2, other arithmetic: 1.01 us -> 4.97 us  [split_hi_lo(): return (hi.astype(BF16), (x - hi).astype(BF16))]
    ppermute x1 -> x0, local copies, waits for them, and re-layouts: 3.28 us -> none  [move(): return lax.ppermute(value, BOTH, pairs)]
    select_n x1 -> x2, other arithmetic: 0.01 us -> 3.16 us  [first_side(): block = held if block is None else jnp.where(chip == j, held, block)]
  transfers between devices with their start and end apart: 45 -> 54, of which waited for: 10 -> 11; matrix products, arithmetic and copies ran while one was open for 15% -> 16% of each run, Pallas kernels for 19% -> 19%
where the time goes in v2:
time: 245 us; the launch traced here: 242 us
  starting transfers between devices  109 us (44%)
  Pallas kernels  47.7 us (19%)
  waiting for transfers between devices  31.1 us (13%)
  local copies, waits for them, and re-layouts  22.5 us (9%)
  matrix products  19.3 us (8%)
  other arithmetic  12.1 us (5%)
    ppermute x54, starting transfers between devices, move(): return lax.ppermute(value, BOTH, pairs)  109 us
    ppermute x54, waiting for transfers between devices, move(): return lax.ppermute(value, BOTH, pairs)  31.1 us
    pallas_call x4, Pallas kernels, project(): pl.pallas_call(functools.partial(project_kernel, vec_total, chunk, group)...  30.2 us
    unnamed x52, local copies, waits for them, and re-layouts  13 us
    pallas_call x8, Pallas kernels, apply_weights(): pl.pallas_call(functools.partial(apply_kernel, sign), in_specs=[pl.BlockS...  7.3 us
    dot_general x1, matrix products, on_device(): jnp.dot(inverse_rows[0], top, precision=HIGHEST)  5.49 us
    dot_general x1, matrix products, on_device(): jnp.dot(inverse_rows[1], bottom, precision=HIGHEST)  5.44 us
    pallas_call x1, Pallas kernels, invert_block(): pl.pallas_call(invert_kernel, grid_spec=pltpu.PrefetchScalarGridSpec(num_...  5.42 us
  transfers between devices with their start and end apart: 54, of which 11 were waited for; matrix products, arithmetic and copies ran while one was open for 16% of the time, Pallas kernels for 19%

profile of v2, /device:TPU:24, one launch (start us, length us, event | category | flops | bytes accessed | tf_op | source)
XLA Modules:
  0.0 242.2 jit_solution(14854734053288836321)
XLA Ops:
  0.0 2.0 collective-permute-start.7
  5.3 2.5 %collective-permute-start.17 = (bf16[2,250,128]{2,1,0:T(8,128)(2,1)S(1)}, bf16[2,250,128]{2,1,0:T(8,128)(2,1)S(1)}, u32[]{:S(2)}, u32[]{:S(2)}) collective-permute-start(bf16[2,250,128]{2,1,0:T(8,128)(2,1)S(1)} %get-tuple-element.39), channel_id=1, source_target_pairs={{0,16},{1,17},{2,18},{3,19},{4,20},{5,21},{6,22},{7,23},{8,24},{9,... | collective-permute-start | bytes 384008 | tf_op jit(solution)/shard_map/ppermute | solution.py:30
  10.5 2.6 %collective-permute-done.17 = bf16[2,250,128]{2,1,0:T(8,128)(2,1)S(1)} collective-permute-done((bf16[2,250,128]{2,1,0:T(8,128)(2,1)S(1)}, bf16[2,250,128]{2,1,0:T(8,128)(2,1)S(1)}, u32[]{:S(2)}, u32[]{:S(2)}) %collective-permute-start.17) | collective-permute-done | bytes 128032 | tf_op jit(solution)/shard_map/ppermute | solution.py:30
  15.9 43.0 %collective-permute-start.23 = (bf16[2,250,128]{2,1,0:T(8,128)(2,1)}, bf16[2,250,128]{2,1,0:T(8,128)(2,1)S(1)}, u32[]{:S(2)}, u32[]{:S(2)}) collective-permute-start(bf16[2,250,128]{2,1,0:T(8,128)(2,1)} %get-tuple-element.35), channel_id=1, source_target_pairs={{0,4},{1,5},{2,6},{3,7},{4,0},{5,1},{6,2},{7,3},{8,12},{9,13},{10,... | collective-permute-start | bytes 384008 | tf_op jit(solution)/shard_map/ppermute | solution.py:30
  62.1 5.4 %invert_block.1 = f32[512,512]{1,0:T(8,128)S(1)} custom-call(s32[2]{0:T(128)S(1)} %pad_add_fusion.where_ref, f32[512,1024]{1,0:T(8,128)S(1)} %copy-done.6), custom_call_target="tpu_custom_call" | custom-call | tf_op jit(solution)/shard_map/invert_block/pallas_call | solution.py:202
  67.6 4.8 %collective-permute-start.3 = (bf16[500,512]{1,0:T(8,128)(2,1)}, bf16[500,512]{1,0:T(8,128)(2,1)}, u32[]{:S(2)}, u32[]{:S(2)}) collective-permute-start(bf16[500,512]{1,0:T(8,128)(2,1)} %cp_ref), channel_id=1, source_target_pairs={{2,0},{3,1},{4,2},{5,3},{6,4},{7,5},{10,8},{11,9},{12,10},{13,11},... | collective-permute-start | bytes 1536008 | tf_op jit(solution)/shard_map/ppermute | solution.py:30
  74.6 2.2 collective-permute-start.26
  78.4 2.7 %collective-permute-done.3 = bf16[500,512]{1,0:T(8,128)(2,1)} collective-permute-done((bf16[500,512]{1,0:T(8,128)(2,1)}, bf16[500,512]{1,0:T(8,128)(2,1)}, u32[]{:S(2)}, u32[]{:S(2)}) %collective-permute-start.3) | collective-permute-done | bytes 512032 | tf_op jit(solution)/shard_map/ppermute | solution.py:30
  81.1 4.4 %collective-permute-done.25 = bf16[3,2,250,128]{3,2,1,0:T(8,128)(2,1)} collective-permute-done((bf16[3,2,250,128]{3,2,1,0:T(8,128)(2,1)}, bf16[3,2,250,128]{3,2,1,0:T(8,128)(2,1)}, u32[]{:S(2)}, u32[]{:S(2)}) %collective-permute-start.25) | collective-permute-done | bytes 384032 | tf_op jit(solution)/shard_map/ppermute | solution.py:30
  85.5 3.3 %fusion.2 = (bf16[2,512,512]{2,1,0:T(8,128)(2,1)}, bf16[2,512,512]{2,1,0:T(8,128)(2,1)}) fusion(f32[1,512,512]{2,1,0:T(8,128)} %get-tuple-element.24, f32[1,512,512]{2,1,0:T(8,128)} %get-tuple-element.23), kind=kLoop, calls=%fused_computation.8 | loop fusion | flops 2621440 | bytes 4194304 | tf_op jit(solution)/shard_map/convert_element_type | solution.py:37
  88.9 3.0 %collective-permute-done.26 = bf16[3,2,250,128]{3,2,1,0:T(8,128)(2,1)} collective-permute-done((bf16[3,2,250,128]{3,2,1,0:T(8,128)(2,1)}, bf16[3,2,250,128]{3,2,1,0:T(8,128)(2,1)}, u32[]{:S(2)}, u32[]{:S(2)}) %collective-permute-start.26) | collective-permute-done | bytes 384032 | tf_op jit(solution)/shard_map/ppermute | solution.py:30
  93.2 4.6 %collective-permute-start.4 = (bf16[500,512]{1,0:T(8,128)(2,1)}, bf16[500,512]{1,0:T(8,128)(2,1)S(1)}, u32[]{:S(2)}, u32[]{:S(2)}) collective-permute-start(bf16[500,512]{1,0:T(8,128)(2,1)} %collective-permute-done.3), channel_id=1, source_target_pairs={{2,0},{3,1},{4,2},{5,3},{6,4},{7,5},{10,8},{11,9},{12,10},{13,11},... | collective-permute-start | bytes 1536008 | tf_op jit(solution)/shard_map/ppermute | solution.py:30
  103.2 2.1 collective-permute-done.1
  105.3 2.2 collective-permute-start.19
  109.6 4.7 %collective-permute-start.5 = (bf16[500,512]{1,0:T(8,128)(2,1)S(1)}, bf16[500,512]{1,0:T(8,128)(2,1)S(1)}, u32[]{:S(2)}, u32[]{:S(2)}) collective-permute-start(bf16[500,512]{1,0:T(8,128)(2,1)S(1)} %collective-permute-done.4), channel_id=1, source_target_pairs={{2,0},{3,1},{4,2},{5,3},{6,4},{7,5},{10,8},{11,9},{12,10},{13,11},... | collective-permute-start | bytes 1536008 | tf_op jit(solution)/shard_map/ppermute | solution.py:30
  114.4 4.7 %fusion.14 = f32[512,512]{1,0:T(8,128)S(1)} fusion(f32[512,512]{1,0:T(8,128)} %collective-permute-done.6, f32[512,1024]{1,0:T(8,128)S(1)} %copy-done.7), kind=kOutput, calls=%fused_computation.27 | convolution fusion | flops 1610612736 | bytes 3145728 | tf_op jit(solution)/shard_map/dot_general | solution.py:310
  119.1 2.9 %fusion.10 = f32[512,512]{1,0:T(8,128)} fusion(f32[512,512]{1,0:T(8,128)S(1)} %invert_block.1, f32[512,512]{1,0:T(8,128)S(1)} %fusion.14, pred[]{:T(512)S(6)} %eq.46), kind=kOutput, calls=%fused_computation.18 | convolution fusion | flops 1611137024 | bytes 3145729 | tf_op jit(solution)/shard_map/dot_general | solution.py:311
  122.0 2.5 %collective-permute-start.20 = (bf16[2,250,128]{2,1,0:T(8,128)(2,1)}, bf16[2,250,128]{2,1,0:T(8,128)(2,1)}, u32[]{:S(2)}, u32[]{:S(2)}) collective-permute-start(bf16[2,250,128]{2,1,0:T(8,128)(2,1)} %get-tuple-element.33.rest_0_), channel_id=1, source_target_pairs={{0,16},{1,17},{2,18},{3,19},{4,20},{5,21},{6,22},{7,23},{8,24},{9,... | collective-permute-start | bytes 384008 | tf_op jit(solution)/shard_map/ppermute | solution.py:30
  125.8 2.3 fusion.16
  129.4 2.8 %pivot_entries.1 = f32[8,8]{1,0:T(8,128)} custom-call(s32[8]{0:T(128)} %get-tuple-element.54.row_ref, bf16[500,8,250]{2,1,0:T(8,128)(2,1)} %bitcast.8.own_ref, bf16[500,8,250]{2,1,0:T(8,128)(2,1)} %bitcast.62, s32[8]{0:T(128)} %get-tuple-element.55.own_col_ref, s32[8]{0:T(128)} %get-tuple-element.53.sib_col_ref), custom_call_target="tpu_custom_call" | custom-call | tf_op jit(solution)/shard_map/pivot_entries/pallas_call | solution.py:63
  132.2 3.8 %collective-permute-start.12 = (f32[8,8]{1,0:T(8,128)}, f32[8,8]{1,0:T(8,128)S(1)}, u32[]{:S(2)}, u32[]{:S(2)}) collective-permute-start(f32[8,8]{1,0:T(8,128)} %pivot_entries.1), channel_id=1, source_target_pairs={{0,6},{1,7},{2,4},{3,5},{4,2},{5,3},{6,0},{7,1},{8,14},{9,15},{10,... | collective-permute-start | bytes 776 | tf_op jit(solution)/shard_map/ppermute | solution.py:30
  141.3 7.6 %project.6 = f32[8,512]{1,0:T(8,128)S(1)} custom-call(s32[5]{0:T(128)S(1)} %stack.96.where_ref, bf16[4000,250]{1,0:T(8,128)(2,1)} %bitcast.14.own_ref, bf16[4000,250]{1,0:T(8,128)(2,1)S(1)} %bitcast.63, bf16[500,512]{1,0:T(8,128)(2,1)S(1)} %copy-done.12, bf16[2,250,128]{2,1,0:T(8,128)(2,1)S(1)} %collective-permute-done.23.rest_0_, ...), custom_call_target="tpu_custom_call" | custom-call | tf_op jit(solution)/shard_map/project/pallas_call | solution.py:141
  149.7 2.8 %collective-permute-start.29 = (f32[8,512]{1,0:T(8,128)S(1)}, f32[8,512]{1,0:T(8,128)S(1)}, u32[]{:S(2)}, u32[]{:S(2)}) collective-permute-start(f32[8,512]{1,0:T(8,128)S(1)} %project.6), channel_id=1, source_target_pairs={{0,4},{1,5},{2,6},{3,7},{4,0},{5,1},{6,2},{7,3},{8,12},{9,13},{10,... | collective-permute-start | bytes 49160 | tf_op jit(solution)/shard_map/ppermute | solution.py:30
  152.5 7.8 %project.4 = f32[8,512]{1,0:T(8,128)S(1)} custom-call(s32[5]{0:T(128)S(1)} %stack.96.where_ref, bf16[4000,250]{1,0:T(8,128)(2,1)} %bitcast.14.own_ref, bf16[4000,250]{1,0:T(8,128)(2,1)S(1)} %bitcast.64, bf16[500,512]{1,0:T(8,128)(2,1)} %cp_ref, bf16[2,250,128]{2,1,0:T(8,128)(2,1)} %get-tuple-element.33.rest_0_, ...), custom_call_target="tpu_custom_call" | custom-call | tf_op jit(solution)/shard_map/project/pallas_call | solution.py:141
  160.3 7.4 %project.5 = f32[8,512]{1,0:T(8,128)S(1)} custom-call(s32[5]{0:T(128)S(1)} %stack.96.where_ref, bf16[4000,250]{1,0:T(8,128)(2,1)} %bitcast.14.own_ref, bf16[4000,250]{1,0:T(8,128)(2,1)S(1)} %bitcast.65, bf16[500,512]{1,0:T(8,128)(2,1)S(1)} %copy-done.11, bf16[2,250,128]{2,1,0:T(8,128)(2,1)S(1)} %collective-permute-done.22.rest_0_, ...), custom_call_target="tpu_custom_call" | custom-call | tf_op jit(solution)/shard_map/project/pallas_call | solution.py:141
  169.3 5.4 %fusion.3 = f32[512,1024]{1,0:T(8,128)S(1)} fusion(f32[512,1024]{1,0:T(8,128)} %collective-permute-done.8, f32[512,1024]{1,0:T(8,128)} %collective-permute-done.7, pred[]{:T(512)S(6)} %eq.46, f32[512,512]{1,0:T(8,128)S(1)} %invert_block.1), kind=kOutput, calls=%fused_computation.12 | convolution fusion | flops 3222011904 | bytes 7340033 | tf_op jit(solution)/shard_map/dot_general | solution.py:320
  174.8 5.5 %fusion.7 = f32[512,1024]{1,0:T(8,128)S(1)} fusion(f32[512,1024]{1,0:T(8,128)S(1)} %fusion.3, f32[512,512]{1,0:T(8,128)S(1)} %copy-done.22, f32[512,1024]{1,0:T(8,128)} %collective-permute-done.7, f32[512,1024]{1,0:T(8,128)} %collective-permute-done.8, pred[]{:T(512)S(6)} %eq.46), kind=kOutput, calls=%fused_computation.16 | convolution fusion | flops 3222274048 | bytes 9437185 | tf_op jit(solution)/shard_map/dot_general | solution.py:320
  183.2 7.4 %project.7 = f32[8,512]{1,0:T(8,128)S(1)} custom-call(s32[5]{0:T(128)S(1)} %stack.96.where_ref, bf16[4000,250]{1,0:T(8,128)(2,1)} %bitcast.14.own_ref, bf16[4000,250]{1,0:T(8,128)(2,1)S(1)} %bitcast.66, bf16[500,512]{1,0:T(8,128)(2,1)S(1)} %copy-done.10, bf16[2,250,128]{2,1,0:T(8,128)(2,1)S(1)} %collective-permute-done.24.rest_0_, ...), custom_call_target="tpu_custom_call" | custom-call | tf_op jit(solution)/shard_map/project/pallas_call | solution.py:141
  196.4 3.4 %collective-permute-start.31 = (f32[8,512]{1,0:T(8,128)S(1)}, f32[8,512]{1,0:T(8,128)S(1)}, u32[]{:S(2)}, u32[]{:S(2)}) collective-permute-start(f32[8,512]{1,0:T(8,128)S(1)} %add_add_fusion), channel_id=1, source_target_pairs={{0,8},{1,9},{2,10},{3,11},{4,12},{5,13},{6,14},{7,15},{8,0},{9,1},... | collective-permute-start | bytes 49160 | tf_op jit(solution)/shard_map/ppermute | solution.py:30
  214.2 2.1 collective-permute-done.40
  216.3 2.0 collective-permute-done.42
  234.5 7.1 %collective-permute-done.53 = f32[2,512]{1,0:T(2,128)S(1)} collective-permute-done((f32[2,512]{1,0:T(2,128)S(1)}, f32[2,512]{1,0:T(2,128)S(1)}, u32[]{:S(2)}, u32[]{:S(2)}) %collective-permute-start.53) | collective-permute-done | bytes 4128 | tf_op jit(solution)/shard_map/ppermute | solution.py:30
  (178 shorter events, 74.5 us)
Async XLA Ops:
  0.0 77.8 %collective-permute-start.7 = (f32[512,1024]{1,0:T(8,128)}, f32[512,1024]{1,0:T(8,128)}, u32[]{:S(2)}, u32[]{:S(2)}) collective-permute-start(f32[512,1024]{1,0:T(8,128)} %block_ref.1), channel_id=1, source_target_pairs={{2,10},{3,11},{12,20},{13,21},{22,30},{23,31}} | collective-permute-start | bytes 6291464 | tf_op jit(solution)/shard_map/ppermute | solution.py:30
  5.3 7.8 %collective-permute-start.17 = (bf16[2,250,128]{2,1,0:T(8,128)(2,1)S(1)}, bf16[2,250,128]{2,1,0:T(8,128)(2,1)S(1)}, u32[]{:S(2)}, u32[]{:S(2)}) collective-permute-start(bf16[2,250,128]{2,1,0:T(8,128)(2,1)S(1)} %get-tuple-element.39), channel_id=1, source_target_pairs={{0,16},{1,17},{2,18},{3,19},{4,20},{5,21},{6,22},{7,23},{8,24},{9,... | collective-permute-start | bytes 384008 | tf_op jit(solution)/shard_map/ppermute | solution.py:30
  9.2 67.6 %collective-permute-start = (bf16[500,512]{1,0:T(8,128)(2,1)}, bf16[500,512]{1,0:T(8,128)(2,1)}, u32[]{:S(2)}, u32[]{:S(2)}) collective-permute-start(bf16[500,512]{1,0:T(8,128)(2,1)} %cp_ref), channel_id=1, source_target_pairs={{0,2},{1,3},{2,4},{3,5},{4,6},{5,7},{8,10},{9,11},{10,12},{11,13},... | collective-permute-start | bytes 1536008 | tf_op jit(solution)/shard_map/ppermute | solution.py:30
  15.9 51.7 %collective-permute-start.24 = (bf16[2,250,128]{2,1,0:T(8,128)(2,1)}, bf16[2,250,128]{2,1,0:T(8,128)(2,1)S(1)}, u32[]{:S(2)}, u32[]{:S(2)}) collective-permute-start(bf16[2,250,128]{2,1,0:T(8,128)(2,1)} %get-tuple-element.34), channel_id=1, source_target_pairs={{0,6},{1,7},{2,4},{3,5},{4,2},{5,3},{6,0},{7,1},{8,14},{9,15},{10,... | collective-permute-start | bytes 384008 | tf_op jit(solution)/shard_map/ppermute | solution.py:30
  15.9 56.5 %collective-permute-start.23 = (bf16[2,250,128]{2,1,0:T(8,128)(2,1)}, bf16[2,250,128]{2,1,0:T(8,128)(2,1)S(1)}, u32[]{:S(2)}, u32[]{:S(2)}) collective-permute-start(bf16[2,250,128]{2,1,0:T(8,128)(2,1)} %get-tuple-element.35), channel_id=1, source_target_pairs={{0,4},{1,5},{2,6},{3,7},{4,0},{5,1},{6,2},{7,3},{8,12},{9,13},{10,... | collective-permute-start | bytes 384008 | tf_op jit(solution)/shard_map/ppermute | solution.py:30
  58.9 13.5 %collective-permute-start.22 = (bf16[2,250,128]{2,1,0:T(8,128)(2,1)}, bf16[2,250,128]{2,1,0:T(8,128)(2,1)S(1)}, u32[]{:S(2)}, u32[]{:S(2)}) collective-permute-start(bf16[2,250,128]{2,1,0:T(8,128)(2,1)} %get-tuple-element.36), channel_id=1, source_target_pairs={{0,2},{1,3},{2,0},{3,1},{4,6},{5,7},{6,4},{7,5},{8,10},{9,11},{10,... | collective-permute-start | bytes 384008 | tf_op jit(solution)/shard_map/ppermute | solution.py:30
  67.6 13.5 %collective-permute-start.3 = (bf16[500,512]{1,0:T(8,128)(2,1)}, bf16[500,512]{1,0:T(8,128)(2,1)}, u32[]{:S(2)}, u32[]{:S(2)}) collective-permute-start(bf16[500,512]{1,0:T(8,128)(2,1)} %cp_ref), channel_id=1, source_target_pairs={{2,0},{3,1},{4,2},{5,3},{6,4},{7,5},{10,8},{11,9},{12,10},{13,11},... | collective-permute-start | bytes 1536008 | tf_op jit(solution)/shard_map/ppermute | solution.py:30
  73.2 12.4 %collective-permute-start.25 = (bf16[3,2,250,128]{3,2,1,0:T(8,128)(2,1)}, bf16[3,2,250,128]{3,2,1,0:T(8,128)(2,1)}, u32[]{:S(2)}, u32[]{:S(2)}) collective-permute-start(bf16[3,2,250,128]{3,2,1,0:T(8,128)(2,1)} %pad_maximum_fusion.4), channel_id=1, source_target_pairs={{0,8},{1,9},{2,10},{3,11},{4,12},{5,13},{6,14},{7,15},{8,0},{9,1},... | collective-permute-start | bytes 1152008 | tf_op jit(solution)/shard_map/ppermute | solution.py:30
  74.6 17.4 %collective-permute-start.26 = (bf16[3,2,250,128]{3,2,1,0:T(8,128)(2,1)}, bf16[3,2,250,128]{3,2,1,0:T(8,128)(2,1)}, u32[]{:S(2)}, u32[]{:S(2)}) collective-permute-start(bf16[3,2,250,128]{3,2,1,0:T(8,128)(2,1)} %pad_maximum_fusion.4), channel_id=1, source_target_pairs={{0,16},{1,17},{2,18},{3,19},{4,20},{5,21},{6,22},{7,23},{8,24},{9,... | collective-permute-start | bytes 1152008 | tf_op jit(solution)/shard_map/ppermute | solution.py:30
  76.8 16.4 %collective-permute-start.27 = (bf16[3,2,250,128]{3,2,1,0:T(8,128)(2,1)}, bf16[3,2,250,128]{3,2,1,0:T(8,128)(2,1)}, u32[]{:S(2)}, u32[]{:S(2)}) collective-permute-start(bf16[3,2,250,128]{3,2,1,0:T(8,128)(2,1)} %pad_maximum_fusion.4), channel_id=1, source_target_pairs={{0,24},{1,25},{2,26},{3,27},{4,28},{5,29},{6,30},{7,31},{8,16},{9,... | collective-permute-start | bytes 1152008 | tf_op jit(solution)/shard_map/ppermute | solution.py:30
  77.8 89.9 %collective-permute-start.8 = (f32[512,1024]{1,0:T(8,128)}, f32[512,1024]{1,0:T(8,128)}, u32[]{:S(2)}, u32[]{:S(2)}) collective-permute-start(f32[512,1024]{1,0:T(8,128)} %collective-permute-done.7), channel_id=1, source_target_pairs={{0,1},{1,0},{2,3},{3,2},{4,5},{5,4},{6,7},{7,6},{8,9},{9,8},{10,11... | collective-permute-start | bytes 6291464 | tf_op jit(solution)/shard_map/ppermute | solution.py:30
  81.1 28.5 %collective-permute-start.6 = (f32[512,512]{1,0:T(8,128)S(1)}, f32[512,512]{1,0:T(8,128)}, u32[]{:S(2)}, u32[]{:S(2)}) collective-permute-start(f32[512,512]{1,0:T(8,128)S(1)} %invert_block.1), channel_id=1, source_target_pairs={{0,1},{1,0},{2,3},{3,2},{4,5},{5,4},{6,7},{7,6},{8,9},{9,8},{10,11... | collective-permute-start | bytes 3145736 | tf_op jit(solution)/shard_map/ppermute | solution.py:30
  85.5 42.5 %collective-permute-start.9 = (bf16[8,500,250]{2,0,1:T(8,128)(2,1)}, bf16[8,500,250]{2,0,1:T(8,128)(2,1)S(1)}, u32[]{:S(2)}, u32[]{:S(2)}) collective-permute-start(bf16[8,500,250]{2,0,1:T(8,128)(2,1)} %param.4), channel_id=1, source_target_pairs={{0,1},{1,0},{2,3},{3,2},{4,5},{5,4},{6,7},{7,6},{8,9},{9,8},{10,11... | collective-permute-start | bytes 6000008 | tf_op jit(solution)/shard_map/ppermute | solution.py:30
  91.9 13.4 %collective-permute-start.1 = (bf16[500,512]{1,0:T(8,128)(2,1)}, bf16[500,512]{1,0:T(8,128)(2,1)S(1)}, u32[]{:S(2)}, u32[]{:S(2)}) collective-permute-start(bf16[500,512]{1,0:T(8,128)(2,1)} %collective-permute-done), channel_id=1, source_target_pairs={{0,2},{1,3},{2,4},{3,5},{4,6},{5,7},{8,10},{9,11},{10,12},{11,13},... | collective-permute-start | bytes 1536008 | tf_op jit(solution)/shard_map/ppermute | solution.py:30
  93.2 14.3 %collective-permute-start.4 = (bf16[500,512]{1,0:T(8,128)(2,1)}, bf16[500,512]{1,0:T(8,128)(2,1)S(1)}, u32[]{:S(2)}, u32[]{:S(2)}) collective-permute-start(bf16[500,512]{1,0:T(8,128)(2,1)} %collective-permute-done.3), channel_id=1, source_target_pairs={{2,0},{3,1},{4,2},{5,3},{6,4},{7,5},{10,8},{11,9},{12,10},{13,11},... | collective-permute-start | bytes 1536008 | tf_op jit(solution)/shard_map/ppermute | solution.py:30
  105.3 43.6 %collective-permute-start.19 = (bf16[2,250,128]{2,1,0:T(8,128)(2,1)}, bf16[2,250,128]{2,1,0:T(8,128)(2,1)}, u32[]{:S(2)}, u32[]{:S(2)}) collective-permute-start(bf16[2,250,128]{2,1,0:T(8,128)(2,1)} %get-tuple-element.33.rest_0_), channel_id=1, source_target_pairs={{0,8},{1,9},{2,10},{3,11},{4,12},{5,13},{6,14},{7,15},{8,0},{9,1},... | collective-permute-start | bytes 384008 | tf_op jit(solution)/shard_map/ppermute | solution.py:30
  107.5 14.5 %collective-permute-start.2 = (bf16[500,512]{1,0:T(8,128)(2,1)S(1)}, bf16[500,512]{1,0:T(8,128)(2,1)S(1)}, u32[]{:S(2)}, u32[]{:S(2)}) collective-permute-start(bf16[500,512]{1,0:T(8,128)(2,1)S(1)} %collective-permute-done.1), channel_id=1, source_target_pairs={{0,2},{1,3},{2,4},{3,5},{4,6},{5,7},{8,10},{9,11},{10,12},{11,13},... | collective-permute-start | bytes 1536008 | tf_op jit(solution)/shard_map/ppermute | solution.py:30
  109.6 14.8 %collective-permute-start.5 = (bf16[500,512]{1,0:T(8,128)(2,1)S(1)}, bf16[500,512]{1,0:T(8,128)(2,1)S(1)}, u32[]{:S(2)}, u32[]{:S(2)}) collective-permute-start(bf16[500,512]{1,0:T(8,128)(2,1)S(1)} %collective-permute-done.4), channel_id=1, source_target_pairs={{2,0},{3,1},{4,2},{5,3},{6,4},{7,5},{10,8},{11,9},{12,10},{13,11},... | collective-permute-start | bytes 1536008 | tf_op jit(solution)/shard_map/ppermute | solution.py:30
  122.0 27.3 %collective-permute-start.20 = (bf16[2,250,128]{2,1,0:T(8,128)(2,1)}, bf16[2,250,128]{2,1,0:T(8,128)(2,1)}, u32[]{:S(2)}, u32[]{:S(2)}) collective-permute-start(bf16[2,250,128]{2,1,0:T(8,128)(2,1)} %get-tuple-element.33.rest_0_), channel_id=1, source_target_pairs={{0,16},{1,17},{2,18},{3,19},{4,20},{5,21},{6,22},{7,23},{8,24},{9,... | collective-permute-start | bytes 384008 | tf_op jit(solution)/shard_map/ppermute | solution.py:30
  124.4 25.3 %collective-permute-start.21 = (bf16[2,250,128]{2,1,0:T(8,128)(2,1)}, bf16[2,250,128]{2,1,0:T(8,128)(2,1)}, u32[]{:S(2)}, u32[]{:S(2)}) collective-permute-start(bf16[2,250,128]{2,1,0:T(8,128)(2,1)} %get-tuple-element.33.rest_0_), channel_id=1, source_target_pairs={{0,24},{1,25},{2,26},{3,27},{4,28},{5,29},{6,30},{7,31},{8,16},{9,... | collective-permute-start | bytes 384008 | tf_op jit(solution)/shard_map/ppermute | solution.py:30
  132.2 58.4 %collective-permute-start.12 = (f32[8,8]{1,0:T(8,128)}, f32[8,8]{1,0:T(8,128)S(1)}, u32[]{:S(2)}, u32[]{:S(2)}) collective-permute-start(f32[8,8]{1,0:T(8,128)} %pivot_entries.1), channel_id=1, source_target_pairs={{0,6},{1,7},{2,4},{3,5},{4,2},{5,3},{6,0},{7,1},{8,14},{9,15},{10,... | collective-permute-start | bytes 776 | tf_op jit(solution)/shard_map/ppermute | solution.py:30
  149.0 41.9 %collective-permute-start.11 = (f32[8,8]{1,0:T(8,128)S(1)}, f32[8,8]{1,0:T(8,128)S(1)}, u32[]{:S(2)}, u32[]{:S(2)}) collective-permute-start(f32[8,8]{1,0:T(8,128)S(1)} %copy-done.24), channel_id=1, source_target_pairs={{0,4},{1,5},{2,6},{3,7},{4,0},{5,1},{6,2},{7,3},{8,12},{9,13},{10,... | collective-permute-start | bytes 776 | tf_op jit(solution)/shard_map/ppermute | solution.py:30
  149.3 41.5 %collective-permute-start.10 = (f32[8,8]{1,0:T(8,128)S(1)}, f32[8,8]{1,0:T(8,128)S(1)}, u32[]{:S(2)}, u32[]{:S(2)}) collective-permute-start(f32[8,8]{1,0:T(8,128)S(1)} %copy-done.24), channel_id=1, source_target_pairs={{0,2},{1,3},{2,0},{3,1},{4,6},{5,7},{6,4},{7,5},{8,10},{9,11},{10,... | collective-permute-start | bytes 776 | tf_op jit(solution)/shard_map/ppermute | solution.py:30
  149.7 43.0 %collective-permute-start.29 = (f32[8,512]{1,0:T(8,128)S(1)}, f32[8,512]{1,0:T(8,128)S(1)}, u32[]{:S(2)}, u32[]{:S(2)}) collective-permute-start(f32[8,512]{1,0:T(8,128)S(1)} %project.6), channel_id=1, source_target_pairs={{0,4},{1,5},{2,6},{3,7},{4,0},{5,1},{6,2},{7,3},{8,12},{9,13},{10,... | collective-permute-start | bytes 49160 | tf_op jit(solution)/shard_map/ppermute | solution.py:30
  167.8 26.6 %collective-permute-start.28 = (f32[8,512]{1,0:T(8,128)S(1)}, f32[8,512]{1,0:T(8,128)S(1)}, u32[]{:S(2)}, u32[]{:S(2)}) collective-permute-start(f32[8,512]{1,0:T(8,128)S(1)} %project.5), channel_id=1, source_target_pairs={{0,2},{1,3},{2,0},{3,1},{4,6},{5,7},{6,4},{7,5},{8,10},{9,11},{10,... | collective-permute-start | bytes 49160 | tf_op jit(solution)/shard_map/ppermute | solution.py:30
  192.5 7.2 %collective-permute-start.14 = (f32[8,8]{1,0:T(8,128)S(1)}, f32[8,8]{1,0:T(8,128)S(1)}, u32[]{:S(2)}, u32[]{:S(2)}) collective-permute-start(f32[8,8]{1,0:T(8,128)S(1)} %add_add_fusion.3), channel_id=1, source_target_pairs={{0,16},{1,17},{2,18},{3,19},{4,20},{5,21},{6,22},{7,23},{8,24},{9,... | collective-permute-start | bytes 776 | tf_op jit(solution)/shard_map/ppermute | solution.py:30
  208.6 7.7 %collective-permute-start.40 = (f32[8,512]{1,0:T(8,128)S(1)}, f32[8,512]{1,0:T(8,128)S(1)}, u32[]{:S(2)}, u32[]{:S(2)}) collective-permute-start(f32[8,512]{1,0:T(8,128)S(1)} %apply_weights.8.bias_ref), channel_id=1, source_target_pairs={{0,6},{1,7}} | collective-permute-start | bytes 49160 | tf_op jit(solution)/shard_map/ppermute | solution.py:30
  210.6 7.7 %collective-permute-start.42 = (f32[8,512]{1,0:T(8,128)S(1)}, f32[8,512]{1,0:T(8,128)S(1)}, u32[]{:S(2)}, u32[]{:S(2)}) collective-permute-start(f32[8,512]{1,0:T(8,128)S(1)} %apply_weights.8.bias_ref), channel_id=1, source_target_pairs={{0,7},{1,6}} | collective-permute-start | bytes 49160 | tf_op jit(solution)/shard_map/ppermute | solution.py:30
  212.8 7.8 %collective-permute-start.47 = (f32[8,512]{1,0:T(8,128)S(1)}, f32[8,512]{1,0:T(8,128)S(1)}, u32[]{:S(2)}, u32[]{:S(2)}) collective-permute-start(f32[8,512]{1,0:T(8,128)S(1)} %broadcast_select_fusion), channel_id=1, source_target_pairs={{10,14},{11,15}} | collective-permute-start | bytes 49160 | tf_op jit(solution)/shard_map/ppermute | solution.py:30
  231.8 9.7 %collective-permute-start.53 = (f32[2,512]{1,0:T(2,128)S(1)}, f32[2,512]{1,0:T(2,128)S(1)}, u32[]{:S(2)}, u32[]{:S(2)}) collective-permute-start(f32[2,512]{1,0:T(2,128)S(1)} %get-tuple-element.51), channel_id=1, source_target_pairs={{0,24},{1,25},{10,18},{11,19},{20,12},{21,13},{30,6},{31,7}} | collective-permute-start | bytes 12296 | tf_op jit(solution)/shard_map/ppermute | solution.py:30
  233.1 8.4 %collective-permute-start.52 = (f32[2,512]{1,0:T(2,128)S(1)}, f32[2,512]{1,0:T(2,128)S(1)}, u32[]{:S(2)}, u32[]{:S(2)}) collective-permute-start(f32[2,512]{1,0:T(2,128)S(1)} %get-tuple-element.52), channel_id=1, source_target_pairs={{0,16},{1,17},{10,26},{11,27},{20,4},{21,5},{30,14},{31,15}} | collective-permute-start | bytes 12296 | tf_op jit(solution)/shard_map/ppermute | solution.py:30
  233.8 7.8 %collective-permute-start.51 = (f32[2,512]{1,0:T(2,128)S(1)}, f32[2,512]{1,0:T(2,128)S(1)}, u32[]{:S(2)}, u32[]{:S(2)}) collective-permute-start(f32[2,512]{1,0:T(2,128)S(1)} %get-tuple-element.50), channel_id=1, source_target_pairs={{0,8},{1,9},{10,2},{11,3},{20,28},{21,29},{30,22},{31,23}} | collective-permute-start | bytes 12296 | tf_op jit(solution)/shard_map/ppermute | solution.py:30
  (48 other events, 296.8 us)

commit v3 on v2

v3 whole, which is shorter than its diff:
```python
import functools

import jax
import jax.numpy as jnp
from jax import lax
from jax.experimental import pallas as pl
from jax.experimental.pallas import tpu as pltpu
from jax.sharding import PartitionSpec as P

NORB = 2000
F32 = jnp.float32
BF16 = jnp.bfloat16
BOTH = ("gen", "fit")
HIGHEST = lax.Precision.HIGHEST


def mover(gen_count):
    fit_count = 2 * gen_count

    def move(value, target):
        pairs = []
        for g in range(gen_count):
            for j in range(gen_count):
                for c in range(2):
                    to = target(g, j, c)
                    if to is not None:
                        pairs.append(
                            (g * fit_count + 2 * j + c, to[0] * fit_count + 2 * to[1] + to[2])
                        )
        return lax.ppermute(value, BOTH, pairs)

    return move


def split_hi_lo(x):
    hi = lax.reduce_precision(x, 8, 7)
    return hi.astype(BF16), (x - hi).astype(BF16)


def pivot_kernel(row_ref, own_ref, sib_ref, own_col_ref, sib_col_ref, out_ref, buffer, sems):
    count, orb = out_ref.shape[1], own_ref.shape[0]
    copies = []
    for i in range(count):
        row = jnp.clip(row_ref[i], 0, orb - 1)
        for n, ref in enumerate((own_ref, sib_ref)):
            copies.append(
                pltpu.make_async_copy(ref.at[row], buffer.at[2 * i + n], sems.at[2 * i + n])
            )
            copies[-1].start()
    lane = lax.broadcasted_iota(jnp.int32, buffer.shape[1:], 1)
    for i in range(count):
        copies[2 * i].wait()
        copies[2 * i + 1].wait()
        local = jnp.logical_and(row_ref[i] >= 0, row_ref[i] < orb)
        kept = jnp.where(lane == own_col_ref[i], buffer[2 * i].astype(F32), 0.0)
        kept += jnp.where(lane == sib_col_ref[i], buffer[2 * i + 1].astype(F32), 0.0)
        kept = jnp.where(local, kept, 0.0)
        out_ref[:, i : i + 1] = jnp.sum(kept, axis=1, keepdims=True)


def pivot_entries(own, sib, rows, own_cols, sib_cols):
    vec_total, pair = own.shape[1:]
    return pl.pallas_call(
        pivot_kernel,
        in_specs=[
            pl.BlockSpec(memory_space=pltpu.SMEM),
            pl.BlockSpec(memory_space=pl.ANY),
            pl.BlockSpec(memory_space=pl.ANY),
            pl.BlockSpec(memory_space=pltpu.SMEM),
            pl.BlockSpec(memory_space=pltpu.SMEM),
        ],
        out_specs=pl.BlockSpec(memory_space=pltpu.VMEM),
        out_shape=jax.ShapeDtypeStruct((vec_total, vec_total), F32),
        scratch_shapes=[
            pltpu.VMEM((2 * vec_total, vec_total, pair), BF16),
            pltpu.SemaphoreType.DMA((2 * vec_total,)),
        ],
        name="pivot_entries",
    )(rows, own, sib, own_cols, sib_cols)


def factor_inverse_kernel(block_ref, out_ref):
    a = block_ref[...]
    n = a.shape[0]
    row = lax.broadcasted_iota(jnp.int32, (n, n), 0)
    col = lax.broadcasted_iota(jnp.int32, (n, n), 1)
    w = (row == col).astype(F32)
    for i in range(n):
        pivot = a[i : i + 1, i : i + 1]
        scale = jnp.where(row[:, :1] > i, a[:, i : i + 1] / pivot, 0.0)
        w = w - scale * w[i : i + 1, :]
        a = a - scale * a[i : i + 1, :]
    diag = jnp.sum(jnp.where(row == col, a, 0.0), axis=1, keepdims=True)
    out_ref[...] = w / jnp.sqrt(diag)


def factor_inverse(block):
    return pl.pallas_call(
        factor_inverse_kernel,
        out_shape=jax.ShapeDtypeStruct(block.shape, F32),
        name="factor_inverse",
    )(block)


def project_kernel(vec_total, chunk, where_ref, own_ref, sib_ref, cp_ref, entries_ref, *rest):
    part_refs, (out_ref, cq, cp, acc) = rest[:-4], rest[-4:]
    part = part_refs[0].shape[-1]
    points = cp.shape[1]
    step = pl.program_id(0)
    core = where_ref[0]

    @pl.when(step == 0)
    def _():
        for n, ref in enumerate(part_refs):
            start = 0
            if len(part_refs) > 1:
                start = pl.multiple_of(where_ref[1 + n] * part, part)
            cq[:, :, pl.ds(start, part)] = ref[0]
        cp[...] = cp_ref[...].astype(F32)
        acc[...] = jnp.zeros_like(acc)
        out_ref[:, points:] = jnp.zeros((vec_total, out_ref.shape[1] - points), F32)
        out_ref[:, points : points + vec_total] = entries_ref[...]

    mixed = jnp.dot(own_ref[...], cq[core], preferred_element_type=F32)
    mixed += jnp.dot(sib_ref[...], cq[1 - core], preferred_element_type=F32)
    total = acc[...]
    for p in range(chunk):
        total += mixed[p * vec_total : (p + 1) * vec_total] * cp[pl.ds(step * chunk + p, 1), :]
    acc[...] = total

    @pl.when(step == pl.num_programs(0) - 1)
    def _():
        out_ref[:, :points] = acc[...]


def project(where, own, sib, cp, entries, parts, slot):
    orb, points = cp.shape
    pair = own.shape[1]
    vec_total = own.shape[0] // orb
    chunk = 125
    part_shape = (1,) + parts[0].shape[1:]
    return pl.pallas_call(
        functools.partial(project_kernel, vec_total, chunk),
        grid_spec=pltpu.PrefetchScalarGridSpec(
            num_scalar_prefetch=1,
            grid=(orb // chunk,),
            in_specs=[
                pl.BlockSpec((chunk * vec_total, pair), lambda i, s: (i, 0)),
                pl.BlockSpec((chunk * vec_total, pair), lambda i, s: (i, 0)),
                pl.BlockSpec((orb, points), lambda i, s: (0, 0)),
                pl.BlockSpec((vec_total, vec_total), lambda i, s: (0, 0)),
            ]
            + [pl.BlockSpec(part_shape, lambda i, s: (slot, 0, 0, 0))] * len(parts),
            out_specs=pl.BlockSpec((vec_total, points + 128), lambda i, s: (0, 0)),
            scratch_shapes=[
                pltpu.VMEM((2, pair, points), BF16),
                pltpu.VMEM((orb, points), F32),
                pltpu.VMEM((vec_total, points), F32),
            ],
        ),
        out_shape=jax.ShapeDtypeStruct((vec_total, points + 128), F32),
        compiler_params=pltpu.CompilerParams(vmem_limit_bytes=20 << 20),
        cost_estimate=pl.CostEstimate(
            flops=4 * orb * vec_total * pair * points, transcendentals=0, bytes_accessed=1 << 20
        ),
        name="project",
    )(where, own, sib, cp, entries, *parts)


def invert_kernel(own_ref, sib_ref, own_out, sib_out):
    n = own_ref.shape[0]
    tile = 128
    row = lax.broadcasted_iota(jnp.int32, (tile, tile), 0)
    col = lax.broadcasted_iota(jnp.int32, (tile, tile), 1)
    eye = (row == col).astype(F32)
    dot = functools.partial(jnp.dot, precision=HIGHEST, preferred_element_type=F32)
    pairs = ((own_ref, own_out), (sib_ref, sib_out))
    places = [(ref, out, b) for ref, out in pairs for b in range(0, n, tile)]
    parts = [ref[b : b + tile, b : b + tile] for ref, _, b in places]
    xs = [eye / jnp.sum(part * eye, axis=1, keepdims=True) for part in parts]
    size = 1
    while size < tile:
        pick = (row // (2 * size) == col // (2 * size)) & (row // size > col // size)
        inner = [dot(jnp.where(pick, part, 0.0), x) for part, x in zip(parts, xs)]
        xs = [x - dot(x, y) for x, y in zip(xs, inner)]
        size *= 2
    own_out[...] = jnp.zeros_like(own_out)
    sib_out[...] = jnp.zeros_like(sib_out)
    for (_, out, b), x in zip(places, xs):
        out[b : b + tile, b : b + tile] = x
    size = tile
    while size < n:
        for ref, out in pairs:
            for b in range(0, n, 2 * size):
                mid, end = b + size, b + 2 * size
                inner = dot(ref[mid:end, b:mid], out[b:mid, b:mid])
                out[mid:end, b:mid] = -dot(out[mid:end, mid:end], inner)
        size *= 2


def invert_blocks(own, sib):
    shape = jax.ShapeDtypeStruct(own.shape, F32)
    return pl.pallas_call(
        invert_kernel,
        out_shape=(shape, shape),
        compiler_params=pltpu.CompilerParams(vmem_limit_bytes=16 << 20),
        cost_estimate=pl.CostEstimate(flops=8 << 30, transcendentals=0, bytes_accessed=1 << 22),
        name="invert_blocks",
    )(own, sib)


def weigh(hi_ref, lo_ref, halves):
    dims = (((1,), (1,)), ((), ()))
    total = None
    for half, x in halves:
        hi = x.astype(BF16)
        lo = (x - hi.astype(F32)).astype(BF16)
        n = x.shape[0]
        both = lax.dot_general(
            jnp.concatenate([hi, lo]), hi_ref[half], dims, preferred_element_type=F32
        )
        part = both[:n] + both[n:]
        part += lax.dot_general(hi, lo_ref[half], dims, preferred_element_type=F32)
        total = part if total is None else total + part
    return total


def apply_kernel(where_ref, hi_ref, lo_ref, xa_ref, xb_ref, out_ref):
    core = where_ref[0]
    out_ref[...] = weigh(hi_ref, lo_ref, [(core, xa_ref[...]), (1 - core, xb_ref[...])])


def apply_weights(where, weights, xa, xb):
    return pl.pallas_call(
        apply_kernel,
        in_specs=[pl.BlockSpec(memory_space=pltpu.SMEM)] + [pl.BlockSpec(memory_space=pltpu.VMEM)] * 4,
        out_specs=pl.BlockSpec(memory_space=pltpu.VMEM),
        out_shape=jax.ShapeDtypeStruct(xa.shape, F32),
        compiler_params=pltpu.CompilerParams(vmem_limit_bytes=12 << 20),
        cost_estimate=pl.CostEstimate(flops=1 << 30, transcendentals=0, bytes_accessed=1 << 21),
        name="apply_weights",
    )(where, *weights, xa, xb)


def turn_kernel(where_ref, *refs):
    own_hi, own_lo, sib_hi, sib_lo, inv_hi, inv_lo, xa, xb, own_rest, sib_rest, out_ref = refs
    core = where_ref[0]
    halves = [(core, xa[...]), (1 - core, xb[...])]
    own = own_rest[...] - weigh(own_hi, own_lo, halves)
    sib = sib_rest[...] - weigh(sib_hi, sib_lo, halves)
    out_ref[...] = weigh(inv_hi, inv_lo, [(core, own), (1 - core, sib)])


def turn(where, left_own, left_sib, inverse, xa, xb, own_rest, sib_rest):
    return pl.pallas_call(
        turn_kernel,
        in_specs=[pl.BlockSpec(memory_space=pltpu.SMEM)] + [pl.BlockSpec(memory_space=pltpu.VMEM)] * 10,
        out_specs=pl.BlockSpec(memory_space=pltpu.VMEM),
        out_shape=jax.ShapeDtypeStruct(xa.shape, F32),
        compiler_params=pltpu.CompilerParams(vmem_limit_bytes=20 << 20),
        cost_estimate=pl.CostEstimate(flops=2 << 30, transcendentals=0, bytes_accessed=1 << 22),
        name="turn",
    )(where, *left_own, *left_sib, *inverse, xa, xb, own_rest, sib_rest)


def combine_kernel(inverse_ref, x_ref, out_ref):
    x = x_ref[...]
    inverse = inverse_ref[...]
    total = inverse[:, :1] * x[:1]
    for i in range(1, x.shape[0]):
        total += inverse[:, i : i + 1] * x[i : i + 1]
    out_ref[...] = total


def combine(inverse, x):
    return pl.pallas_call(
        combine_kernel, out_shape=jax.ShapeDtypeStruct(x.shape, F32), name="combine"
    )(inverse, x)


def on_device(raw_columns, pivot_pairs, collocation, metric_factor):
    vec_total, orb_block, pair_block = raw_columns.shape
    gen_count = lax.axis_size("gen")
    gen_index = lax.axis_index("gen")
    fit_index = lax.axis_index("fit")
    chip = fit_index // 2
    core = fit_index % 2
    points = metric_factor.shape[0]
    vec_dev = vec_total // gen_count
    move = mover(gen_count)
    others = range(1, gen_count)
    diagonal = gen_index == chip
    swap = lambda g, j, c: (g, j, 1 - c)

    part = points // gen_count
    halves = collocation.reshape(2, orb_block // 2, points)
    spread = []
    for k in range(gen_count):
        piece = lax.dynamic_slice_in_dim(halves, (gen_index ^ k) * part, part, 2)
        spread.append(move(piece, lambda g, j, c, k=k: (g ^ k, j, c)) if k else piece)
    spread = jnp.stack(spread)
    own_block = jnp.where(core == 0, metric_factor[:, :points], metric_factor[:, points:])
    own_block = jnp.where(diagonal, own_block, jnp.eye(points, dtype=F32))
    sibling = move(raw_columns, swap)
    sib_block = move(own_block, swap)
    spread, first, sibling, sib_block = lax.optimization_barrier(
        (spread, collocation, sibling, sib_block)
    )
    first_side = [first] + [move(first, lambda g, j, c, k=k: (g, j ^ k, c)) for k in (1, 2)]
    own_parts = []
    for k in range(gen_count):
        piece = lax.dynamic_index_in_dim(spread, gen_index ^ chip ^ k, 0, keepdims=False)
        own_parts.append(move(piece, lambda g, j, c, k=k: (g, j ^ k, c)) if k else piece)
    own_parts, first, first_side[1] = lax.optimization_barrier((own_parts, first, first_side[1]))
    for k in range(3, gen_count):
        first_side.append(move(first, lambda g, j, c, k=k: (g, j ^ k, c)))
    all_parts = [jnp.stack(own_parts)]
    for k in others:
        all_parts.append(move(all_parts[0], lambda g, j, c, k=k: (g ^ k, j, c)))

    def second_side(k):
        if part % 128 == 0:
            return all_parts
        whole = jnp.zeros(halves.shape, BF16)
        for n, x in enumerate(all_parts):
            whole = lax.dynamic_update_slice_in_dim(whole, x[k], (gen_index ^ n) * part, 2)
        return [whole[None]]

    own_raw = raw_columns.transpose(1, 0, 2)
    sib_raw = sibling.transpose(1, 0, 2)
    pivot_rows = pivot_pairs // NORB - gen_index * orb_block
    own_cols = pivot_pairs % NORB - fit_index * pair_block
    sib_cols = pivot_pairs % NORB - (fit_index ^ 1) * pair_block
    entries = pivot_entries(own_raw, sib_raw, pivot_rows, own_cols, sib_cols)

    own_inverse, upper = invert_blocks(own_block, sib_block)
    corner = jnp.dot(metric_factor[:, :points], upper, precision=HIGHEST)
    corner = -jnp.dot(own_inverse, corner, precision=HIGHEST)
    zeros = jnp.zeros_like(own_inverse)
    inverse_rows = split_hi_lo(
        jnp.stack(
            [jnp.where(core == 0, own_inverse, corner), jnp.where(core == 0, zeros, own_inverse)]
        )
    )

    own_hi, own_lo = split_hi_lo(jnp.stack([metric_factor[:, :points], metric_factor[:, points:]]))
    all_parts, first_side[2], entries, inverse_rows, left_hi, left_lo = lax.optimization_barrier(
        (all_parts, first_side[2], entries, inverse_rows, own_hi, own_lo)
    )
    to_diagonal = lambda g, j, c: (g + 1, j, c) if j == g + 1 else None
    left_own = (move(left_hi, to_diagonal), move(left_lo, to_diagonal))
    left_sib = (move(left_own[0], swap), move(left_own[1], swap))

    own_raw = own_raw.reshape(orb_block * vec_total, pair_block)
    sib_raw = sib_raw.reshape(orb_block * vec_total, pair_block)
    where = jnp.stack([core] + [gen_index ^ k for k in range(gen_count)])
    total = None
    for k in range(gen_count):
        block = first_side[k]
        if k == gen_count - 1:
            block, inverse_rows = lax.optimization_barrier((block, inverse_rows))
        share = project(where, own_raw, sib_raw, block, entries, second_side(k), k if part % 128 == 0 else 0)
        if k:
            share = move(share, lambda g, j, c, k=k: (g, j ^ k, c))
        total = share if total is None else total + share
    total = sum([move(total, lambda g, j, c, k=k: (g ^ k, j, c)) for k in others], total)
    rest = total[:, :points]
    pivot_block = total[:, points : points + vec_total]

    at_core = core[None]
    nothing = jnp.zeros_like(rest)
    sib_rest = move(rest, swap)
    solved = apply_weights(at_core, inverse_rows, rest, sib_rest)
    kept = solved
    for t in range(gen_count - 1):
        near = move(solved, lambda g, j, c: (t + 1, t + 1, c) if g == j == t else None)
        near_sib = move(solved, lambda g, j, c: (t + 1, t + 1, 1 - c) if g == j == t else None)
        if t + 2 < gen_count:
            far, far_sib = nothing, nothing
            for z in range(t + 2, gen_count):
                far += move(solved, lambda g, j, c: (t, z, c) if g == j == t else None)
                far_sib += move(solved, lambda g, j, c: (t, z, 1 - c) if g == j == t else None)
            brought = apply_weights(at_core, (own_hi, own_lo), far, far_sib)
            brought = move(brought, lambda g, j, c: (j, j, c) if g == t and j >= t + 2 else None)
        solved = turn(
            at_core, left_own, left_sib, inverse_rows, near, near_sib, rest, sib_rest
        )
        kept = jnp.where(jnp.logical_and(diagonal, gen_index == t + 1), solved, kept)
        if t + 2 < gen_count:
            rest = rest - brought
            sib_rest = move(rest, swap)
    kept = combine(factor_inverse(pivot_block), kept)

    def rows_of(index):
        return lax.dynamic_slice_in_dim(kept, index * vec_dev, vec_dev, 0)

    result = jnp.where(diagonal, rows_of(gen_index), 0.0)
    for k in others:
        result += move(
            rows_of(gen_index ^ k), lambda g, j, c, k=k: (g ^ k, j, c) if g == j else None
        )
    return result


def solution(mesh):
    in_specs = (P(None, "gen", "fit"), P(), P("gen", "fit"), P("fit", "gen"))
    out_specs = P("gen", "fit")
    return jax.shard_map(
        on_device, mesh=mesh, in_specs=in_specs, out_specs=out_specs, check_vma=False
    )
```

time: 245 us -> 214 us (0.87)
  starting transfers between devices: 109 us -> 76.3 us
  waiting for transfers between devices: 31.1 us -> 53.5 us
  matrix products: 19.3 us -> 6.59 us
  local copies, waits for them, and re-layouts: 22.5 us -> 12.8 us
    ppermute x54 -> x44, starting transfers between devices: 109 us -> 76.3 us  [move(): return lax.ppermute(value, BOTH, pairs)]
    ppermute x54 -> x44, waiting for transfers between devices: 31.1 us -> 53.5 us  [move(): return lax.ppermute(value, BOTH, pairs)]
    dot_general x3 -> x0, matrix products: 11.7 us -> none  [the longest x1 5.49 us: on_device(): jnp.dot(inverse_rows[0], top, precision=HIGHEST)]
    unnamed x52 -> x40, local copies, waits for them, and re-layouts: 13 us -> 7.46 us
    squeeze x3 -> x0, local copies, waits for them, and re-layouts: 5.38 us -> none  [second_side(): parts = near_parts if k == 0 else [x[k - 1] for x in far_parts]]
    another operation x2, other arithmetic: 0.87 us -> 4.38 us  [the longest x1 3.41 us: on_device(): jnp.stack([metric_factor[:, :points], metric_factor[:, points:]])]
    select_n x5 -> x1, other arithmetic: 3.18 us -> 0.62 us  [on_device(): jnp.where(jnp.logical_and(diagonal, gen_index == t + 1), solved, kept)]
    pallas_call x13 -> x12, Pallas kernels: 43 us -> 45.4 us  [the longest x4 19.3 us: project(): pl.pallas_call(functools.partial(project_kernel, vec_total, chunk), grid_...]
  transfers between devices with their start and end apart: 54 -> 44, of which waited for: 11 -> 14; matrix products, arithmetic and copies ran while one was open for 16% -> 10% of each run, Pallas kernels for 19% -> 19%
where the time goes in v3:
time: 214 us; the launch traced here: 213 us
  starting transfers between devices  76.3 us (36%)
  waiting for transfers between devices  53.5 us (25%)
  Pallas kernels  50.1 us (23%)
  other arithmetic  13 us (6%)
  local copies, waits for them, and re-layouts  12.8 us (6%)
  matrix products  6.59 us (3%)
    ppermute x44, starting transfers between devices, move(): return lax.ppermute(value, BOTH, pairs)  76.3 us
    ppermute x44, waiting for transfers between devices, move(): return lax.ppermute(value, BOTH, pairs)  53.5 us
    pallas_call x4, Pallas kernels, project(): pl.pallas_call(functools.partial(project_kernel, vec_total, chunk), grid_...  19.3 us
    pallas_call x3, Pallas kernels, turn(): pl.pallas_call(turn_kernel, in_specs=[pl.BlockSpec(memory_space=pltpu.SME...  10.6 us
    pallas_call x1, Pallas kernels, invert_blocks(): pl.pallas_call(invert_kernel, out_shape=(shape, shape), compiler_params=p...  9.69 us
    unnamed x40, local copies, waits for them, and re-layouts  7.46 us
    convert_element_type x2, other arithmetic, split_hi_lo(): return (hi.astype(BF16), (x - hi).astype(BF16))  4.91 us
    pallas_call x3, Pallas kernels, apply_weights(): pl.pallas_call(apply_kernel, in_specs=[pl.BlockSpec(memory_space=pltpu.SM...  4.38 us
  transfers between devices with their start and end apart: 44, of which 14 were waited for; matrix products, arithmetic and copies ran while one was open for 10% of the time, Pallas kernels for 19%

profile of v3, /device:TPU:24, one launch (start us, length us, event | category | flops | bytes accessed | tf_op | source)
XLA Modules:
  0.0 212.9 jit_solution(14557261680996562320)
XLA Ops:
  0.0 3.4 %slice_bitcast_fusion.1 = (f32[1,512,512]{2,1,0:T(8,128)}, f32[1,512,512]{2,1,0:T(8,128)}, f32[512,512]{1,0:T(8,128)S(1)}) fusion(f32[512,1024]{1,0:T(8,128)} %param.7, pred[]{:T(512)S(6)} %eq.26, pred[]{:T(512)S(6)} %eq.25), kind=kLoop, calls=%fused_computation.15 | loop fusion | flops 1048576 | bytes 5242882 | tf_op jit(solution)/shard_map/stack | solution.py:346
  3.9 2.0 reshape.10
  5.9 1.8 dynamic-slice_bitcast_fusion.4
  7.7 2.5 %collective-permute-start.2 = (bf16[2,250,128]{2,1,0:T(8,128)(2,1)}, bf16[2,250,128]{2,1,0:T(8,128)(2,1)}, u32[]{:S(2)}, u32[]{:S(2)}) collective-permute-start(bf16[2,250,128]{2,1,0:T(8,128)(2,1)} %get-tuple-element.69), channel_id=1, source_target_pairs={{0,24},{1,25},{2,26},{3,27},{4,28},{5,29},{6,30},{7,31},{8,16},{9,... | collective-permute-start | bytes 384008 | tf_op jit(solution)/shard_map/ppermute | solution.py:30
  11.8 3.2 %fusion.1 = (bf16[2,512,512]{2,1,0:T(8,128)(2,1)}, bf16[2,512,512]{2,1,0:T(8,128)(2,1)}) fusion(f32[1,512,512]{2,1,0:T(8,128)} %get-tuple-element.60, f32[1,512,512]{2,1,0:T(8,128)} %get-tuple-element.59), kind=kLoop, calls=%fused_computation.5 | loop fusion | flops 2621440 | bytes 4194304 | tf_op jit(solution)/shard_map/convert_element_type | solution.py:37
  15.2 2.4 %collective-permute-done = bf16[2,250,128]{2,1,0:T(8,128)(2,1)} collective-permute-done((bf16[2,250,128]{2,1,0:T(8,128)(2,1)S(1)}, bf16[2,250,128]{2,1,0:T(8,128)(2,1)}, u32[]{:S(2)}, u32[]{:S(2)}) %collective-permute-start) | collective-permute-done | bytes 128032 | tf_op jit(solution)/shard_map/ppermute | solution.py:30
  20.8 9.7 %invert_blocks.1 = (f32[512,512]{1,0:T(8,128)S(1)}, f32[512,512]{1,0:T(8,128)S(1)}) custom-call(f32[512,512]{1,0:T(8,128)S(1)} %copy-done.9, f32[512,512]{1,0:T(8,128)} %collective-permute-done.4.sib_ref), custom_call_target="tpu_custom_call" | custom-call | flops 8589934592 | bytes 4194304 | tf_op jit(solution)/shard_map/invert_blocks/pallas_call | solution.py:203
  32.2 2.6 %collective-permute-start.6 = (bf16[2,250,128]{2,1,0:T(8,128)(2,1)S(1)}, bf16[2,250,128]{2,1,0:T(8,128)(2,1)S(1)}, u32[]{:S(2)}, u32[]{:S(2)}) collective-permute-start(bf16[2,250,128]{2,1,0:T(8,128)(2,1)S(1)} %get-tuple-element.65), channel_id=1, source_target_pairs={{0,4},{1,5},{2,6},{3,7},{4,0},{5,1},{6,2},{7,3},{8,12},{9,13},{10,... | collective-permute-start | bytes 384008 | tf_op jit(solution)/shard_map/ppermute | solution.py:30
  35.0 3.7 %fusion.4 = f32[512,512]{1,0:T(8,128)S(1)} fusion(f32[512,512]{1,0:T(8,128)S(1)} %get-tuple-element.39, f32[512,1024]{1,0:T(8,128)S(1)} %copy-done.17), kind=kOutput, calls=%fused_computation.16 | convolution fusion | flops 1610612736 | bytes 3145728 | tf_op jit(solution)/shard_map/dot_general | solution.py:337
  38.8 9.3 %collective-permute-done.5 = bf16[2,250,128]{2,1,0:T(8,128)(2,1)S(1)} collective-permute-done((bf16[2,250,128]{2,1,0:T(8,128)(2,1)S(1)}, bf16[2,250,128]{2,1,0:T(8,128)(2,1)S(1)}, u32[]{:S(2)}, u32[]{:S(2)}) %collective-permute-start.5) | collective-permute-done | bytes 128032 | tf_op jit(solution)/shard_map/ppermute | solution.py:30
  48.0 6.3 %collective-permute-done.6 = bf16[2,250,128]{2,1,0:T(8,128)(2,1)S(1)} collective-permute-done((bf16[2,250,128]{2,1,0:T(8,128)(2,1)S(1)}, bf16[2,250,128]{2,1,0:T(8,128)(2,1)S(1)}, u32[]{:S(2)}, u32[]{:S(2)}) %collective-permute-start.6) | collective-permute-done | bytes 128032 | tf_op jit(solution)/shard_map/ppermute | solution.py:30
  58.8 2.9 %fusion.3 = f32[1,512,512]{2,1,0:T(8,128)} fusion(f32[512,512]{1,0:T(8,128)S(1)} %get-tuple-element.38, f32[512,512]{1,0:T(8,128)S(1)} %fusion.4, pred[]{:T(512)S(6)} %eq.26), kind=kOutput, calls=%fused_computation.10 | convolution fusion | flops 1611137024 | bytes 3145729 | tf_op jit(solution)/shard_map/dot_general | solution.py:338
  61.7 2.8 %pivot_entries.1.entries_ref = f32[8,8]{1,0:T(8,128)} custom-call(s32[8]{0:T(128)} %get-tuple-element.76.row_ref, bf16[500,8,250]{2,1,0:T(8,128)(2,1)} %bitcast.39, bf16[500,8,250]{2,1,0:T(8,128)(2,1)} %bitcast.44, s32[8]{0:T(128)} %get-tuple-element.77.own_col_ref, s32[8]{0:T(128)} %get-tuple-element.75.sib_col_ref), custom_call_target="tpu_custom_call" | custom-call | tf_op jit(solution)/shard_map/pivot_entries/pallas_call | solution.py:63
  65.7 1.7 fusion
  67.4 11.0 %collective-permute-done.10.rest_2_ = bf16[4,2,250,128]{3,2,1,0:T(8,128)(2,1)} collective-permute-done((bf16[4,2,250,128]{3,2,1,0:T(8,128)(2,1)}, bf16[4,2,250,128]{3,2,1,0:T(8,128)(2,1)}, u32[]{:S(2)}, u32[]{:S(2)}) %collective-permute-start.10) | collective-permute-done | bytes 512032 | tf_op jit(solution)/shard_map/ppermute | solution.py:30
  83.0 2.5 %collective-permute-start.15 = (bf16[500,512]{1,0:T(8,128)(2,1)}, bf16[500,512]{1,0:T(8,128)(2,1)}, u32[]{:S(2)}, u32[]{:S(2)}) collective-permute-start(bf16[500,512]{1,0:T(8,128)(2,1)} %cp_ref), channel_id=1, source_target_pairs={{0,6},{1,7},{2,4},{3,5},{4,2},{5,3},{6,0},{7,1},{8,14},{9,15},{10,... | collective-permute-start | bytes 1536008 | tf_op jit(solution)/shard_map/ppermute | solution.py:30
  88.2 4.7 %project.5 = f32[8,640]{1,0:T(8,128)S(1)} custom-call(s32[5]{0:T(128)S(1)} %stack.71.where_ref, bf16[4000,250]{1,0:T(8,128)(2,1)S(1)} %bitcast.40, bf16[4000,250]{1,0:T(8,128)(2,1)S(1)} %bitcast.45, bf16[500,512]{1,0:T(8,128)(2,1)S(1)} %copy-done.16, f32[8,8]{1,0:T(8,128)S(1)} %copy-done.10, bf16[4,2,250,128]{3,2,1,0:T(8,128)(2,1)} %pad_maximum_fusion.3.rest_0_, ...), custom_call_target="tpu_custom_call" | custom-call | flops 2048000000 | bytes 1048576 | tf_op jit(solution)/shard_map/project/pallas_call | solution.py:142
  92.9 5.9 %collective-permute-start.13 = (f32[8,640]{1,0:T(8,128)S(1)}, f32[8,640]{1,0:T(8,128)S(1)}, u32[]{:S(2)}, u32[]{:S(2)}) collective-permute-start(f32[8,640]{1,0:T(8,128)S(1)} %project.5), channel_id=1, source_target_pairs={{0,2},{1,3},{2,0},{3,1},{4,6},{5,7},{6,4},{7,5},{8,10},{9,11},{10,... | collective-permute-start | bytes 61448 | tf_op jit(solution)/shard_map/ppermute | solution.py:30
  99.3 4.9 %project.6 = f32[8,640]{1,0:T(8,128)S(1)} custom-call(s32[5]{0:T(128)S(1)} %stack.71.where_ref, bf16[4000,250]{1,0:T(8,128)(2,1)S(1)} %bitcast.41, bf16[4000,250]{1,0:T(8,128)(2,1)S(1)} %bitcast.46, bf16[500,512]{1,0:T(8,128)(2,1)} %collective-permute-done.12.cp_ref, f32[8,8]{1,0:T(8,128)S(1)} %copy-done.10, ...), custom_call_target="tpu_custom_call" | custom-call | flops 2048000000 | bytes 1048576 | tf_op jit(solution)/shard_map/project/pallas_call | solution.py:142
  104.2 32.4 %collective-permute-start.14 = (f32[8,640]{1,0:T(8,128)S(1)}, f32[8,640]{1,0:T(8,128)S(1)}, u32[]{:S(2)}, u32[]{:S(2)}) collective-permute-start(f32[8,640]{1,0:T(8,128)S(1)} %project.6), channel_id=1, source_target_pairs={{0,4},{1,5},{2,6},{3,7},{4,0},{5,1},{6,2},{7,3},{8,12},{9,13},{10,... | collective-permute-start | bytes 61448 | tf_op jit(solution)/shard_map/ppermute | solution.py:30
  136.6 4.9 %project.7 = f32[8,640]{1,0:T(8,128)S(1)} custom-call(s32[5]{0:T(128)S(1)} %stack.71.where_ref, bf16[4000,250]{1,0:T(8,128)(2,1)S(1)} %bitcast.42, bf16[4000,250]{1,0:T(8,128)(2,1)S(1)} %bitcast.47, bf16[500,512]{1,0:T(8,128)(2,1)} %collective-permute-done.15.cp_ref, f32[8,8]{1,0:T(8,128)S(1)} %copy-done.10, ...), custom_call_target="tpu_custom_call" | custom-call | flops 2048000000 | bytes 1048576 | tf_op jit(solution)/shard_map/project/pallas_call | solution.py:142
  141.6 4.9 %project.4 = f32[8,640]{1,0:T(8,128)S(1)} custom-call(s32[5]{0:T(128)S(1)} %stack.71.where_ref, bf16[4000,250]{1,0:T(8,128)(2,1)S(1)} %bitcast.43, bf16[4000,250]{1,0:T(8,128)(2,1)S(1)} %bitcast.48, bf16[500,512]{1,0:T(8,128)(2,1)} %cp_ref, f32[8,8]{1,0:T(8,128)S(1)} %copy-done.10, bf16[4,2,250,128]{3,2,1,0:T(8,128)(2,1)} %pad_maximum_fusion.3.rest_0_, ...), custom_call_target="tpu_custom_call" | custom-call | flops 2048000000 | bytes 1048576 | tf_op jit(solution)/shard_map/project/pallas_call | solution.py:142
  147.1 2.6 %collective-permute-start.17 = (f32[8,640]{1,0:T(8,128)S(1)}, f32[8,640]{1,0:T(8,128)S(1)}, u32[]{:S(2)}, u32[]{:S(2)}) collective-permute-start(f32[8,640]{1,0:T(8,128)S(1)} %add_add_fusion.1), channel_id=1, source_target_pairs={{0,8},{1,9},{2,10},{3,11},{4,12},{5,13},{6,14},{7,15},{8,0},{9,1},... | collective-permute-start | bytes 61448 | tf_op jit(solution)/shard_map/ppermute | solution.py:30
  151.6 2.2 %collective-permute-done.18 = f32[8,640]{1,0:T(8,128)S(1)} collective-permute-done((f32[8,640]{1,0:T(8,128)S(1)}, f32[8,640]{1,0:T(8,128)S(1)}, u32[]{:S(2)}, u32[]{:S(2)}) %collective-permute-start.18) | collective-permute-done | bytes 20512 | tf_op jit(solution)/shard_map/ppermute | solution.py:30
  160.8 3.6 %collective-permute-done.32 = f32[8,512]{1,0:T(8,128)S(1)} collective-permute-done((f32[8,512]{1,0:T(8,128)S(1)}, f32[8,512]{1,0:T(8,128)S(1)}, u32[]{:S(2)}, u32[]{:S(2)}) %collective-permute-start.32) | collective-permute-done | bytes 16416 | tf_op jit(solution)/shard_map/ppermute | solution.py:30
  167.4 4.0 %turn.3 = f32[8,512]{1,0:T(8,128)S(1)} custom-call(s32[1]{0:T(128)} %bitcast.where_ref, bf16[2,512,512]{2,1,0:T(8,128)(2,1)} %collective-permute-done.20.refs_0_, bf16[2,512,512]{2,1,0:T(8,128)(2,1)} %collective-permute-done.21.refs_1_, bf16[2,512,512]{2,1,0:T(8,128)(2,1)S(1)} %collective-permute-done.22.refs_2_, ...), custom_call_target="tpu_custom_call" | custom-call | flops 2147483648 | bytes 4194304 | tf_op jit(solution)/shard_map/turn/pallas_call | solution.py:255
  172.8 1.9 apply_weights.4
  175.9 1.9 apply_weights.5
  181.1 3.3 %turn.4 = f32[8,512]{1,0:T(8,128)S(1)} custom-call(s32[1]{0:T(128)} %bitcast.where_ref, bf16[2,512,512]{2,1,0:T(8,128)(2,1)} %collective-permute-done.20.refs_0_, bf16[2,512,512]{2,1,0:T(8,128)(2,1)} %collective-permute-done.21.refs_1_, bf16[2,512,512]{2,1,0:T(8,128)(2,1)S(1)} %collective-permute-done.22.refs_2_, ...), custom_call_target="tpu_custom_call" | custom-call | flops 2147483648 | bytes 4194304 | tf_op jit(solution)/shard_map/turn/pallas_call | solution.py:255
  186.4 1.9 factor_inverse.1.inverse_ref
  190.8 3.3 %turn.5 = f32[8,512]{1,0:T(8,128)S(1)} custom-call(s32[1]{0:T(128)} %bitcast.where_ref, bf16[2,512,512]{2,1,0:T(8,128)(2,1)} %collective-permute-done.20.refs_0_, bf16[2,512,512]{2,1,0:T(8,128)(2,1)} %collective-permute-done.21.refs_1_, bf16[2,512,512]{2,1,0:T(8,128)(2,1)S(1)} %copy-done.12, bf16[2,512,512]{2,1,0:T(8,128)(2,1)S(1)} %copy-done.14, ...), custom_call_target="tpu_custom_call" | custom-call | flops 2147483648 | bytes 4194304 | tf_op jit(solution)/shard_map/turn/pallas_call | solution.py:255
  199.6 12.0 %collective-permute-done.43 = f32[2,512]{1,0:T(2,128)S(1)} collective-permute-done((f32[2,512]{1,0:T(2,128)S(1)}, f32[2,512]{1,0:T(2,128)S(1)}, u32[]{:S(2)}, u32[]{:S(2)}) %collective-permute-start.43) | collective-permute-done | bytes 4128 | tf_op jit(solution)/shard_map/ppermute | solution.py:30
  (133 shorter events, 50.4 us)
Async XLA Ops:
  0.0 18.7 %collective-permute-start.3 = (bf16[8,500,250]{2,0,1:T(8,128)(2,1)}, bf16[8,500,250]{2,0,1:T(8,128)(2,1)S(1)}, u32[]{:S(2)}, u32[]{:S(2)}) collective-permute-start(bf16[8,500,250]{2,0,1:T(8,128)(2,1)} %param.4), channel_id=1, source_target_pairs={{0,1},{1,0},{2,3},{3,2},{4,5},{5,4},{6,7},{7,6},{8,9},{9,8},{10,11... | collective-permute-start | bytes 6000008 | tf_op jit(solution)/shard_map/ppermute | solution.py:30
  3.4 15.3 %collective-permute-start.4 = (f32[512,512]{1,0:T(8,128)S(1)}, f32[512,512]{1,0:T(8,128)}, u32[]{:S(2)}, u32[]{:S(2)}) collective-permute-start(f32[512,512]{1,0:T(8,128)S(1)} %get-tuple-element.61.own_ref), channel_id=1, source_target_pairs={{0,1},{1,0},{2,3},{3,2},{4,5},{5,4},{6,7},{7,6},{8,9},{9,8},{10,11... | collective-permute-start | bytes 3145736 | tf_op jit(solution)/shard_map/ppermute | solution.py:30
  7.7 7.6 %collective-permute-start.2 = (bf16[2,250,128]{2,1,0:T(8,128)(2,1)}, bf16[2,250,128]{2,1,0:T(8,128)(2,1)}, u32[]{:S(2)}, u32[]{:S(2)}) collective-permute-start(bf16[2,250,128]{2,1,0:T(8,128)(2,1)} %get-tuple-element.69), channel_id=1, source_target_pairs={{0,24},{1,25},{2,26},{3,27},{4,28},{5,29},{6,30},{7,31},{8,16},{9,... | collective-permute-start | bytes 384008 | tf_op jit(solution)/shard_map/ppermute | solution.py:30
  10.2 7.4 %collective-permute-start = (bf16[2,250,128]{2,1,0:T(8,128)(2,1)S(1)}, bf16[2,250,128]{2,1,0:T(8,128)(2,1)}, u32[]{:S(2)}, u32[]{:S(2)}) collective-permute-start(bf16[2,250,128]{2,1,0:T(8,128)(2,1)S(1)} %get-tuple-element.71), channel_id=1, source_target_pairs={{0,8},{1,9},{2,10},{3,11},{4,12},{5,13},{6,14},{7,15},{8,0},{9,1},... | collective-permute-start | bytes 384008 | tf_op jit(solution)/shard_map/ppermute | solution.py:30
  10.7 6.9 %collective-permute-start.1 = (bf16[2,250,128]{2,1,0:T(8,128)(2,1)S(1)}, bf16[2,250,128]{2,1,0:T(8,128)(2,1)}, u32[]{:S(2)}, u32[]{:S(2)}) collective-permute-start(bf16[2,250,128]{2,1,0:T(8,128)(2,1)S(1)} %get-tuple-element.70), channel_id=1, source_target_pairs={{0,16},{1,17},{2,18},{3,19},{4,20},{5,21},{6,22},{7,23},{8,24},{9,... | collective-permute-start | bytes 384008 | tf_op jit(solution)/shard_map/ppermute | solution.py:30
  18.7 35.6 %collective-permute-start.8 = (bf16[500,512]{1,0:T(8,128)(2,1)}, bf16[500,512]{1,0:T(8,128)(2,1)S(1)}, u32[]{:S(2)}, u32[]{:S(2)}) collective-permute-start(bf16[500,512]{1,0:T(8,128)(2,1)} %cp_ref), channel_id=1, source_target_pairs={{0,2},{1,3},{2,0},{3,1},{4,6},{5,7},{6,4},{7,5},{8,10},{9,11},{10,... | collective-permute-start | bytes 1536008 | tf_op jit(solution)/shard_map/ppermute | solution.py:30
  19.2 48.2 %collective-permute-start.12 = (bf16[500,512]{1,0:T(8,128)(2,1)}, bf16[500,512]{1,0:T(8,128)(2,1)}, u32[]{:S(2)}, u32[]{:S(2)}) collective-permute-start(bf16[500,512]{1,0:T(8,128)(2,1)} %cp_ref), channel_id=1, source_target_pairs={{0,4},{1,5},{2,6},{3,7},{4,0},{5,1},{6,2},{7,3},{8,12},{9,13},{10,... | collective-permute-start | bytes 1536008 | tf_op jit(solution)/shard_map/ppermute | solution.py:30
  30.6 17.5 %collective-permute-start.5 = (bf16[2,250,128]{2,1,0:T(8,128)(2,1)S(1)}, bf16[2,250,128]{2,1,0:T(8,128)(2,1)S(1)}, u32[]{:S(2)}, u32[]{:S(2)}) collective-permute-start(bf16[2,250,128]{2,1,0:T(8,128)(2,1)S(1)} %get-tuple-element.66), channel_id=1, source_target_pairs={{0,2},{1,3},{2,0},{3,1},{4,6},{5,7},{6,4},{7,5},{8,10},{9,11},{10,... | collective-permute-start | bytes 384008 | tf_op jit(solution)/shard_map/ppermute | solution.py:30
  32.2 22.1 %collective-permute-start.6 = (bf16[2,250,128]{2,1,0:T(8,128)(2,1)S(1)}, bf16[2,250,128]{2,1,0:T(8,128)(2,1)S(1)}, u32[]{:S(2)}, u32[]{:S(2)}) collective-permute-start(bf16[2,250,128]{2,1,0:T(8,128)(2,1)S(1)} %get-tuple-element.65), channel_id=1, source_target_pairs={{0,4},{1,5},{2,6},{3,7},{4,0},{5,1},{6,2},{7,3},{8,12},{9,13},{10,... | collective-permute-start | bytes 384008 | tf_op jit(solution)/shard_map/ppermute | solution.py:30
  34.8 19.5 %collective-permute-start.7 = (bf16[2,250,128]{2,1,0:T(8,128)(2,1)S(1)}, bf16[2,250,128]{2,1,0:T(8,128)(2,1)S(1)}, u32[]{:S(2)}, u32[]{:S(2)}) collective-permute-start(bf16[2,250,128]{2,1,0:T(8,128)(2,1)S(1)} %get-tuple-element.64), channel_id=1, source_target_pairs={{0,6},{1,7},{2,4},{3,5},{4,2},{5,3},{6,0},{7,1},{8,14},{9,15},{10,... | collective-permute-start | bytes 384008 | tf_op jit(solution)/shard_map/ppermute | solution.py:30
  55.3 23.1 %collective-permute-start.10 = (bf16[4,2,250,128]{3,2,1,0:T(8,128)(2,1)}, bf16[4,2,250,128]{3,2,1,0:T(8,128)(2,1)}, u32[]{:S(2)}, u32[]{:S(2)}) collective-permute-start(bf16[4,2,250,128]{3,2,1,0:T(8,128)(2,1)} %pad_maximum_fusion.3.rest_0_), channel_id=1, source_target_pairs={{0,16},{1,17},{2,18},{3,19},{4,20},{5,21},{6,22},{7,23},{8,24},{9,... | collective-permute-start | bytes 1536008 | tf_op jit(solution)/shard_map/ppermute | solution.py:30
  56.9 21.6 %collective-permute-start.11 = (bf16[4,2,250,128]{3,2,1,0:T(8,128)(2,1)}, bf16[4,2,250,128]{3,2,1,0:T(8,128)(2,1)}, u32[]{:S(2)}, u32[]{:S(2)}) collective-permute-start(bf16[4,2,250,128]{3,2,1,0:T(8,128)(2,1)} %pad_maximum_fusion.3.rest_0_), channel_id=1, source_target_pairs={{0,24},{1,25},{2,26},{3,27},{4,28},{5,29},{6,30},{7,31},{8,16},{9,... | collective-permute-start | bytes 1536008 | tf_op jit(solution)/shard_map/ppermute | solution.py:30
  58.3 21.4 %collective-permute-start.9 = (bf16[4,2,250,128]{3,2,1,0:T(8,128)(2,1)}, bf16[4,2,250,128]{3,2,1,0:T(8,128)(2,1)}, u32[]{:S(2)}, u32[]{:S(2)}) collective-permute-start(bf16[4,2,250,128]{3,2,1,0:T(8,128)(2,1)} %pad_maximum_fusion.3.rest_0_), channel_id=1, source_target_pairs={{0,8},{1,9},{2,10},{3,11},{4,12},{5,13},{6,14},{7,15},{8,0},{9,1},... | collective-permute-start | bytes 1536008 | tf_op jit(solution)/shard_map/ppermute | solution.py:30
  79.7 19.1 %collective-permute-start.20 = (bf16[2,512,512]{2,1,0:T(8,128)(2,1)}, bf16[2,512,512]{2,1,0:T(8,128)(2,1)}, u32[]{:S(2)}, u32[]{:S(2)}) collective-permute-start(bf16[2,512,512]{2,1,0:T(8,128)(2,1)} %get-tuple-element.51.hi_ref), channel_id=1, source_target_pairs={{2,10},{3,11},{12,20},{13,21},{22,30},{23,31}} | collective-permute-start | bytes 3145736 | tf_op jit(solution)/shard_map/ppermute | solution.py:30
  81.3 17.4 %collective-permute-start.21 = (bf16[2,512,512]{2,1,0:T(8,128)(2,1)S(1)}, bf16[2,512,512]{2,1,0:T(8,128)(2,1)}, u32[]{:S(2)}, u32[]{:S(2)}) collective-permute-start(bf16[2,512,512]{2,1,0:T(8,128)(2,1)S(1)} %copy-done.3), channel_id=1, source_target_pairs={{2,10},{3,11},{12,20},{13,21},{22,30},{23,31}} | collective-permute-start | bytes 3145736 | tf_op jit(solution)/shard_map/ppermute | solution.py:30
  83.0 53.6 %collective-permute-start.15 = (bf16[500,512]{1,0:T(8,128)(2,1)}, bf16[500,512]{1,0:T(8,128)(2,1)}, u32[]{:S(2)}, u32[]{:S(2)}) collective-permute-start(bf16[500,512]{1,0:T(8,128)(2,1)} %cp_ref), channel_id=1, source_target_pairs={{0,6},{1,7},{2,4},{3,5},{4,2},{5,3},{6,0},{7,1},{8,14},{9,15},{10,... | collective-permute-start | bytes 1536008 | tf_op jit(solution)/shard_map/ppermute | solution.py:30
  92.9 53.5 %collective-permute-start.13 = (f32[8,640]{1,0:T(8,128)S(1)}, f32[8,640]{1,0:T(8,128)S(1)}, u32[]{:S(2)}, u32[]{:S(2)}) collective-permute-start(f32[8,640]{1,0:T(8,128)S(1)} %project.5), channel_id=1, source_target_pairs={{0,2},{1,3},{2,0},{3,1},{4,6},{5,7},{6,4},{7,5},{8,10},{9,11},{10,... | collective-permute-start | bytes 61448 | tf_op jit(solution)/shard_map/ppermute | solution.py:30
  98.8 68.6 %collective-permute-start.22 = (bf16[2,512,512]{2,1,0:T(8,128)(2,1)}, bf16[2,512,512]{2,1,0:T(8,128)(2,1)S(1)}, u32[]{:S(2)}, u32[]{:S(2)}) collective-permute-start(bf16[2,512,512]{2,1,0:T(8,128)(2,1)} %collective-permute-done.20.refs_0_), channel_id=1, source_target_pairs={{0,1},{1,0},{2,3},{3,2},{4,5},{5,4},{6,7},{7,6},{8,9},{9,8},{10,11... | collective-permute-start | bytes 3145736 | tf_op jit(solution)/shard_map/ppermute | solution.py:30
  98.8 68.6 %collective-permute-start.23 = (bf16[2,512,512]{2,1,0:T(8,128)(2,1)}, bf16[2,512,512]{2,1,0:T(8,128)(2,1)S(1)}, u32[]{:S(2)}, u32[]{:S(2)}) collective-permute-start(bf16[2,512,512]{2,1,0:T(8,128)(2,1)} %collective-permute-done.21.refs_1_), channel_id=1, source_target_pairs={{0,1},{1,0},{2,3},{3,2},{4,5},{5,4},{6,7},{7,6},{8,9},{9,8},{10,11... | collective-permute-start | bytes 3145736 | tf_op jit(solution)/shard_map/ppermute | solution.py:30
  104.2 42.3 %collective-permute-start.14 = (f32[8,640]{1,0:T(8,128)S(1)}, f32[8,640]{1,0:T(8,128)S(1)}, u32[]{:S(2)}, u32[]{:S(2)}) collective-permute-start(f32[8,640]{1,0:T(8,128)S(1)} %project.6), channel_id=1, source_target_pairs={{0,4},{1,5},{2,6},{3,7},{4,0},{5,1},{6,2},{7,3},{8,12},{9,13},{10,... | collective-permute-start | bytes 61448 | tf_op jit(solution)/shard_map/ppermute | solution.py:30
  141.5 5.6 %collective-permute-start.16 = (f32[8,640]{1,0:T(8,128)S(1)}, f32[8,640]{1,0:T(8,128)S(1)}, u32[]{:S(2)}, u32[]{:S(2)}) collective-permute-start(f32[8,640]{1,0:T(8,128)S(1)} %project.7), channel_id=1, source_target_pairs={{0,6},{1,7},{2,4},{3,5},{4,2},{5,3},{6,0},{7,1},{8,14},{9,15},{10,... | collective-permute-start | bytes 61448 | tf_op jit(solution)/shard_map/ppermute | solution.py:30
  147.1 4.5 %collective-permute-start.17 = (f32[8,640]{1,0:T(8,128)S(1)}, f32[8,640]{1,0:T(8,128)S(1)}, u32[]{:S(2)}, u32[]{:S(2)}) collective-permute-start(f32[8,640]{1,0:T(8,128)S(1)} %add_add_fusion.1), channel_id=1, source_target_pairs={{0,8},{1,9},{2,10},{3,11},{4,12},{5,13},{6,14},{7,15},{8,0},{9,1},... | collective-permute-start | bytes 61448 | tf_op jit(solution)/shard_map/ppermute | solution.py:30
  149.8 4.0 %collective-permute-start.18 = (f32[8,640]{1,0:T(8,128)S(1)}, f32[8,640]{1,0:T(8,128)S(1)}, u32[]{:S(2)}, u32[]{:S(2)}) collective-permute-start(f32[8,640]{1,0:T(8,128)S(1)} %add_add_fusion.1), channel_id=1, source_target_pairs={{0,16},{1,17},{2,18},{3,19},{4,20},{5,21},{6,22},{7,23},{8,24},{9,... | collective-permute-start | bytes 61448 | tf_op jit(solution)/shard_map/ppermute | solution.py:30
  150.2 4.7 %collective-permute-start.19 = (f32[8,640]{1,0:T(8,128)S(1)}, f32[8,640]{1,0:T(8,128)S(1)}, u32[]{:S(2)}, u32[]{:S(2)}) collective-permute-start(f32[8,640]{1,0:T(8,128)S(1)} %add_add_fusion.1), channel_id=1, source_target_pairs={{0,24},{1,25},{2,26},{3,27},{4,28},{5,29},{6,30},{7,31},{8,16},{9,... | collective-permute-start | bytes 61448 | tf_op jit(solution)/shard_map/ppermute | solution.py:30
  157.5 6.9 %collective-permute-start.32 = (f32[8,512]{1,0:T(8,128)S(1)}, f32[8,512]{1,0:T(8,128)S(1)}, u32[]{:S(2)}, u32[]{:S(2)}) collective-permute-start(f32[8,512]{1,0:T(8,128)S(1)} %apply_weights.3), channel_id=1, source_target_pairs={{0,7},{1,6}} | collective-permute-start | bytes 49160 | tf_op jit(solution)/shard_map/ppermute | solution.py:30
  158.8 6.2 %collective-permute-start.29 = (f32[8,512]{1,0:T(8,128)S(1)}, f32[8,512]{1,0:T(8,128)S(1)}, u32[]{:S(2)}, u32[]{:S(2)}) collective-permute-start(f32[8,512]{1,0:T(8,128)S(1)} %apply_weights.3), channel_id=1, source_target_pairs={{0,4},{1,5}} | collective-permute-start | bytes 49160 | tf_op jit(solution)/shard_map/ppermute | solution.py:30
  159.5 7.8 %collective-permute-start.30 = (f32[8,512]{1,0:T(8,128)S(1)}, f32[8,512]{1,0:T(8,128)S(1)}, u32[]{:S(2)}, u32[]{:S(2)}) collective-permute-start(f32[8,512]{1,0:T(8,128)S(1)} %apply_weights.3), channel_id=1, source_target_pairs={{0,6},{1,7}} | collective-permute-start | bytes 49160 | tf_op jit(solution)/shard_map/ppermute | solution.py:30
  171.4 4.5 %collective-permute-start.37 = (f32[8,512]{1,0:T(8,128)S(1)}, f32[8,512]{1,0:T(8,128)S(1)}, u32[]{:S(2)}, u32[]{:S(2)}) collective-permute-start(f32[8,512]{1,0:T(8,128)S(1)} %turn.3), channel_id=1, source_target_pairs={{10,14},{11,15}} | collective-permute-start | bytes 49160 | tf_op jit(solution)/shard_map/ppermute | solution.py:30
  174.6 5.2 %collective-permute-start.33 = (f32[8,512]{1,0:T(8,128)S(1)}, f32[8,512]{1,0:T(8,128)S(1)}, u32[]{:S(2)}, u32[]{:S(2)}) collective-permute-start(f32[8,512]{1,0:T(8,128)S(1)} %apply_weights.4), channel_id=1, source_target_pairs={{4,20},{5,21},{6,30},{7,31}} | collective-permute-start | bytes 49160 | tf_op jit(solution)/shard_map/ppermute | solution.py:30
  180.0 8.3 %collective-permute-start.40 = (f32[8,512]{1,0:T(8,128)S(1)}, f32[8,512]{1,0:T(8,128)S(1)}, u32[]{:S(2)}, u32[]{:S(2)}) collective-permute-start(f32[8,512]{1,0:T(8,128)S(1)} %get-tuple-element.55.refs_8_), channel_id=1, source_target_pairs={{0,1},{1,0},{2,3},{3,2},{4,5},{5,4},{6,7},{7,6},{8,9},{9,8},{10,11... | collective-permute-start | bytes 49160 | tf_op jit(solution)/shard_map/ppermute | solution.py:30
  184.4 3.9 %collective-permute-start.35 = (f32[8,512]{1,0:T(8,128)S(1)}, f32[8,512]{1,0:T(8,128)S(1)}, u32[]{:S(2)}, u32[]{:S(2)}) collective-permute-start(f32[8,512]{1,0:T(8,128)S(1)} %turn.4), channel_id=1, source_target_pairs={{20,30},{21,31}} | collective-permute-start | bytes 49160 | tf_op jit(solution)/shard_map/ppermute | solution.py:30
  198.2 13.3 %collective-permute-start.43 = (f32[2,512]{1,0:T(2,128)S(1)}, f32[2,512]{1,0:T(2,128)S(1)}, u32[]{:S(2)}, u32[]{:S(2)}) collective-permute-start(f32[2,512]{1,0:T(2,128)S(1)} %get-tuple-element.73), channel_id=1, source_target_pairs={{0,24},{1,25},{10,18},{11,19},{20,12},{21,13},{30,6},{31,7}} | collective-permute-start | bytes 12296 | tf_op jit(solution)/shard_map/ppermute | solution.py:30
  (32 other events, 216.6 us)

commit v4 on v3

--- a/solution.py
+++ b/solution.py
@@ -220,7 +220,8 @@
             jnp.concatenate([hi, lo]), hi_ref[half], dims, preferred_element_type=F32
         )
         part = both[:n] + both[n:]
-        part += lax.dot_general(hi, lo_ref[half], dims, preferred_element_type=F32)
+        if lo_ref is not None:
+            part += lax.dot_general(hi, lo_ref[half], dims, preferred_element_type=F32)
         total = part if total is None else total + part
     return total
 
@@ -243,39 +244,50 @@
 
 
 def turn_kernel(where_ref, *refs):
-    own_hi, own_lo, sib_hi, sib_lo, inv_hi, inv_lo, xa, xb, own_rest, sib_rest, out_ref = refs
+    own_left, sib_left, inv_hi, inv_lo, xa, xb, own_rest, sib_rest, out_ref = refs
     core = where_ref[0]
     halves = [(core, xa[...]), (1 - core, xb[...])]
-    own = own_rest[...] - weigh(own_hi, own_lo, halves)
-    sib = sib_rest[...] - weigh(sib_hi, sib_lo, halves)
+    own = own_rest[...] - weigh(own_left, None, halves)
+    sib = sib_rest[...] - weigh(sib_left, None, halves)
     out_ref[...] = weigh(inv_hi, inv_lo, [(core, own), (1 - core, sib)])
 
 
 def turn(where, left_own, left_sib, inverse, xa, xb, own_rest, sib_rest):
     return pl.pallas_call(
         turn_kernel,
-        in_specs=[pl.BlockSpec(memory_space=pltpu.SMEM)] + [pl.BlockSpec(memory_space=pltpu.VMEM)] * 10,
+        in_specs=[pl.BlockSpec(memory_space=pltpu.SMEM)] + [pl.BlockSpec(memory_space=pltpu.VMEM)] * 8,
         out_specs=pl.BlockSpec(memory_space=pltpu.VMEM),
         out_shape=jax.ShapeDtypeStruct(xa.shape, F32),
-        compiler_params=pltpu.CompilerParams(vmem_limit_bytes=20 << 20),
+        compiler_params=pltpu.CompilerParams(vmem_limit_bytes=16 << 20),
         cost_estimate=pl.CostEstimate(flops=2 << 30, transcendentals=0, bytes_accessed=1 << 22),
         name="turn",
-    )(where, *left_own, *left_sib, *inverse, xa, xb, own_rest, sib_rest)
-
-
-def combine_kernel(inverse_ref, x_ref, out_ref):
-    x = x_ref[...]
+    )(where, left_own, left_sib, *inverse, xa, xb, own_rest, sib_rest)
+
+
+def combine_kernel(count, turn_ref, inverse_ref, *refs):
+    x_refs, out_refs = refs[:count], refs[count:]
+    x = jnp.zeros(x_refs[0].shape, F32)
+    for t, ref in enumerate(x_refs):
+        x = jnp.where(turn_ref[0] == t, ref[...], x)
     inverse = inverse_ref[...]
     total = inverse[:, :1] * x[:1]
     for i in range(1, x.shape[0]):
         total += inverse[:, i : i + 1] * x[i : i + 1]
-    out_ref[...] = total
-
-
-def combine(inverse, x):
-    return pl.pallas_call(
-        combine_kernel, out_shape=jax.ShapeDtypeStruct(x.shape, F32), name="combine"
-    )(inverse, x)
+    rows = out_refs[0].shape[0]
+    for n, ref in enumerate(out_refs):
+        ref[...] = total[n * rows : (n + 1) * rows]
+
+
+def combine(which, inverse, turns, rows):
+    count = len(turns)
+    share = jax.ShapeDtypeStruct((rows, turns[0].shape[1]), F32)
+    return pl.pallas_call(
+        functools.partial(combine_kernel, count),
+        in_specs=[pl.BlockSpec(memory_space=pltpu.SMEM)]
+        + [pl.BlockSpec(memory_space=pltpu.VMEM)] * (count + 1),
+        out_shape=[share] * count,
+        name="combine",
+    )(which, inverse, *turns)
 
 
 def on_device(raw_columns, pivot_pairs, collocation, metric_factor):
@@ -299,21 +311,20 @@
         piece = lax.dynamic_slice_in_dim(halves, (gen_index ^ k) * part, part, 2)
         spread.append(move(piece, lambda g, j, c, k=k: (g ^ k, j, c)) if k else piece)
     spread = jnp.stack(spread)
-    own_block = jnp.where(core == 0, metric_factor[:, :points], metric_factor[:, points:])
+    across = lambda k: lambda g, j, c: (g, j ^ k, c)
+    sibling = move(raw_columns, swap)
+    spread, sibling, metric_late = lax.optimization_barrier((spread, sibling, metric_factor))
+    own_block = jnp.where(core == 0, metric_late[:, :points], metric_late[:, points:])
     own_block = jnp.where(diagonal, own_block, jnp.eye(points, dtype=F32))
-    sibling = move(raw_columns, swap)
     sib_block = move(own_block, swap)
-    spread, first, sibling, sib_block = lax.optimization_barrier(
-        (spread, collocation, sibling, sib_block)
-    )
-    first_side = [first] + [move(first, lambda g, j, c, k=k: (g, j ^ k, c)) for k in (1, 2)]
     own_parts = []
     for k in range(gen_count):
         piece = lax.dynamic_index_in_dim(spread, gen_index ^ chip ^ k, 0, keepdims=False)
-        own_parts.append(move(piece, lambda g, j, c, k=k: (g, j ^ k, c)) if k else piece)
-    own_parts, first, first_side[1] = lax.optimization_barrier((own_parts, first, first_side[1]))
-    for k in range(3, gen_count):
-        first_side.append(move(first, lambda g, j, c, k=k: (g, j ^ k, c)))
+        own_parts.append(move(piece, across(k)) if k else piece)
+    own_parts, first, own_block, sib_block = lax.optimization_barrier(
+        (own_parts, collocation, own_block, sib_block)
+    )
+    first_side = [collocation] + [move(first, across(k)) for k in others]
     all_parts = [jnp.stack(own_parts)]
     for k in others:
         all_parts.append(move(all_parts[0], lambda g, j, c, k=k: (g ^ k, j, c)))
@@ -344,12 +355,10 @@
     )
 
     own_hi, own_lo = split_hi_lo(jnp.stack([metric_factor[:, :points], metric_factor[:, points:]]))
-    all_parts, first_side[2], entries, inverse_rows, left_hi, left_lo = lax.optimization_barrier(
-        (all_parts, first_side[2], entries, inverse_rows, own_hi, own_lo)
+    all_parts, first_side[2], entries, inverse_rows, left_hi = lax.optimization_barrier(
+        (all_parts, first_side[2], entries, inverse_rows, own_hi)
     )
-    to_diagonal = lambda g, j, c: (g + 1, j, c) if j == g + 1 else None
-    left_own = (move(left_hi, to_diagonal), move(left_lo, to_diagonal))
-    left_sib = (move(left_own[0], swap), move(left_own[1], swap))
+    left_own = move(left_hi, lambda g, j, c: (g + 1, j, c) if j == g + 1 else None)
 
     own_raw = own_raw.reshape(orb_block * vec_total, pair_block)
     sib_raw = sib_raw.reshape(orb_block * vec_total, pair_block)
@@ -357,48 +366,56 @@
     total = None
     for k in range(gen_count):
         block = first_side[k]
-        if k == gen_count - 1:
-            block, inverse_rows = lax.optimization_barrier((block, inverse_rows))
         share = project(where, own_raw, sib_raw, block, entries, second_side(k), k if part % 128 == 0 else 0)
         if k:
             share = move(share, lambda g, j, c, k=k: (g, j ^ k, c))
         total = share if total is None else total + share
+    total, left_own = lax.optimization_barrier((total, left_own))
+    left_sib = move(left_own, swap)
     total = sum([move(total, lambda g, j, c, k=k: (g ^ k, j, c)) for k in others], total)
     rest = total[:, :points]
     pivot_block = total[:, points : points + vec_total]
 
     at_core = core[None]
-    nothing = jnp.zeros_like(rest)
     sib_rest = move(rest, swap)
     solved = apply_weights(at_core, inverse_rows, rest, sib_rest)
-    kept = solved
-    for t in range(gen_count - 1):
-        near = move(solved, lambda g, j, c: (t + 1, t + 1, c) if g == j == t else None)
-        near_sib = move(solved, lambda g, j, c: (t + 1, t + 1, 1 - c) if g == j == t else None)
+    turns = [solved]
+    waiting = None
+    for t in range(gen_count):
+        if t + 1 < gen_count:
+            near = move(solved, lambda g, j, c: (t + 1, t + 1, c) if g == j == t else None)
+            near_sib = move(solved, lambda g, j, c: (t + 1, t + 1, 1 - c) if g == j == t else None)
+            near, near_sib, late = lax.optimization_barrier((near, near_sib, solved))
+        if waiting is not None:
+            if t + 1 < gen_count:
+                waiting, near, near_sib = lax.optimization_barrier((waiting, near, near_sib))
+            brought = apply_weights(at_core, (own_hi, own_lo), *waiting)
+            brought = move(
+                brought, lambda g, j, c: (j, j, c) if g == t - 1 and j >= t + 1 else None
+            )
+        far = None
         if t + 2 < gen_count:
-            far, far_sib = nothing, nothing
+            far = far_sib = None
             for z in range(t + 2, gen_count):
-                far += move(solved, lambda g, j, c: (t, z, c) if g == j == t else None)
-                far_sib += move(solved, lambda g, j, c: (t, z, 1 - c) if g == j == t else None)
-            brought = apply_weights(at_core, (own_hi, own_lo), far, far_sib)
-            brought = move(brought, lambda g, j, c: (j, j, c) if g == t and j >= t + 2 else None)
-        solved = turn(
-            at_core, left_own, left_sib, inverse_rows, near, near_sib, rest, sib_rest
-        )
-        kept = jnp.where(jnp.logical_and(diagonal, gen_index == t + 1), solved, kept)
-        if t + 2 < gen_count:
+                one = move(late, lambda g, j, c: (t, z, c) if g == j == t else None)
+                two = move(late, lambda g, j, c: (t, z, 1 - c) if g == j == t else None)
+                far = one if far is None else far + one
+                far_sib = two if far_sib is None else far_sib + two
+        if waiting is not None:
             rest = rest - brought
             sib_rest = move(rest, swap)
-    kept = combine(factor_inverse(pivot_block), kept)
-
-    def rows_of(index):
-        return lax.dynamic_slice_in_dim(kept, index * vec_dev, vec_dev, 0)
-
-    result = jnp.where(diagonal, rows_of(gen_index), 0.0)
+        waiting = None if far is None else (far, far_sib)
+        if t + 1 < gen_count:
+            solved = turn(at_core, left_own, left_sib, inverse_rows, near, near_sib, rest, sib_rest)
+            turns.append(solved)
+
+    inverse_factor = factor_inverse(pivot_block).reshape(gen_count, vec_dev, vec_total)
+    order = jnp.stack([gen_index ^ k for k in range(gen_count)])
+    inverse_factor = inverse_factor[order].reshape(vec_total, vec_total)
+    shares = combine(jnp.where(diagonal, gen_index, -1)[None], inverse_factor, turns, vec_dev)
+    result = shares[0]
     for k in others:
-        result += move(
-            rows_of(gen_index ^ k), lambda g, j, c, k=k: (g ^ k, j, c) if g == j else None
-        )
+        result += move(shares[k], lambda g, j, c, k=k: (g ^ k, j, c) if g == j else None)
     return result
 
 

time: 214 us -> 176 us (0.82)
  starting transfers between devices: 76.3 us -> 42.9 us
  local copies, waits for them, and re-layouts: 12.8 us -> 18.5 us
  other arithmetic: 13 us -> 7.89 us
  Pallas kernels: 50.1 us -> 45.2 us
    ppermute x44 -> x42, starting transfers between devices: 76.3 us -> 42.9 us  [move(): return lax.ppermute(value, BOTH, pairs)]
    unnamed x40 -> x60, local copies, waits for them, and re-layouts: 7.46 us -> 10.9 us
    another operation x1 -> x0, other arithmetic: 3.41 us -> none  [on_device(): jnp.stack([metric_factor[:, :points], metric_factor[:, points:]])]
    another operation x0 -> x1, local copies, waits for them, and re-layouts: none -> 3.12 us  [on_device(): jnp.stack([metric_factor[:, :points], metric_factor[:, points:]])]
    pallas_call x3, Pallas kernels: 10.6 us -> 7.62 us  [turn(): pl.pallas_call(turn_kernel, in_specs=[pl.BlockSpec(memory_space=pltpu.SME...]
    convert_element_type x2 -> x1, other arithmetic: 4.91 us -> 2.38 us  [split_hi_lo(): return (hi.astype(BF16), (x - hi).astype(BF16))]
    ppermute x44 -> x42, waiting for transfers between devices: 53.5 us -> 54 us  [move(): return lax.ppermute(value, BOTH, pairs)]
  transfers between devices with their start and end apart: 44 -> 42, of which waited for: 14 -> 14; matrix products, arithmetic and copies ran while one was open for 10% -> 10% of each run, Pallas kernels for 19% -> 20%
where the time goes in v4:
time: 176 us; the launch traced here: 175 us
  waiting for transfers between devices  54 us (31%)
  Pallas kernels  45.2 us (26%)
  starting transfers between devices  42.9 us (24%)
  local copies, waits for them, and re-layouts  18.5 us (11%)
  other arithmetic  7.89 us (4%)
  matrix products  5.54 us (3%)
    ppermute x42, waiting for transfers between devices, move(): return lax.ppermute(value, BOTH, pairs)  54 us
    ppermute x42, starting transfers between devices, move(): return lax.ppermute(value, BOTH, pairs)  42.9 us
    pallas_call x4, Pallas kernels, project(): pl.pallas_call(functools.partial(project_kernel, vec_total, chunk), grid_...  17.5 us
    unnamed x60, local copies, waits for them, and re-layouts  10.9 us
    pallas_call x1, Pallas kernels, invert_blocks(): pl.pallas_call(invert_kernel, out_shape=(shape, shape), compiler_params=p...  9.51 us
    pallas_call x3, Pallas kernels, turn(): pl.pallas_call(turn_kernel, in_specs=[pl.BlockSpec(memory_space=pltpu.SME...  7.62 us
    pallas_call x3, Pallas kernels, apply_weights(): pl.pallas_call(apply_kernel, in_specs=[pl.BlockSpec(memory_space=pltpu.SM...  4.38 us
    dot_general x1, matrix products, on_device(): corner = jnp.dot(metric_factor[:, :points], upper, precision=HIGHEST)  3.65 us
  transfers between devices with their start and end apart: 42, of which 14 were waited for; matrix products, arithmetic and copies ran while one was open for 10% of the time, Pallas kernels for 20%

profile of v4, /device:TPU:24, one launch (start us, length us, event | category | flops | bytes accessed | tf_op | source)
XLA Modules:
  0.0 174.7 jit_solution(1054684059406976806)
XLA Ops:
  4.8 5.1 %collective-permute-done.1 = bf16[2,250,128]{2,1,0:T(8,128)(2,1)S(1)} collective-permute-done((bf16[2,250,128]{2,1,0:T(8,128)(2,1)S(1)}, bf16[2,250,128]{2,1,0:T(8,128)(2,1)S(1)}, u32[]{:S(2)}, u32[]{:S(2)}) %collective-permute-start.1) | collective-permute-done | bytes 128032 | tf_op jit(solution)/shard_map/ppermute | solution.py:30
  12.2 2.5 %convert_select_fusion.own_ref = f32[512,512]{1,0:T(8,128)S(1)} fusion(f32[512,1024]{1,0:T(8,128)} %param.7, pred[]{:T(512)S(6)} %eq.17, pred[]{:T(512)S(6)} %eq.16), kind=kLoop, calls=%fused_computation.14 | loop fusion | flops 1048576 | bytes 3145730 | tf_op jit(solution)/shard_map/jit(_where)/select_n | solution.py:318
  14.8 3.1 %slice_bitcast_fusion.1 = (f32[1,512,512]{2,1,0:T(8,128)}, f32[1,512,512]{2,1,0:T(8,128)}) fusion(f32[512,1024]{1,0:T(8,128)} %param.7), kind=kLoop, calls=%fused_computation.16 | loop fusion | bytes 4194304 | tf_op jit(solution)/shard_map/stack | solution.py:357
  19.3 3.8 %collective-permute-start.6 = (bf16[2,250,128]{2,1,0:T(8,128)(2,1)S(1)}, bf16[2,250,128]{2,1,0:T(8,128)(2,1)S(1)}, u32[]{:S(2)}, u32[]{:S(2)}) collective-permute-start(bf16[2,250,128]{2,1,0:T(8,128)(2,1)S(1)} %get-tuple-element.97), channel_id=1, source_target_pairs={{0,6},{1,7},{2,4},{3,5},{4,2},{5,3},{6,0},{7,1},{8,14},{9,15},{10,... | collective-permute-start | bytes 384008 | tf_op jit(solution)/shard_map/ppermute | solution.py:30
  23.6 2.8 %pivot_entries.1.entries_ref = f32[8,8]{1,0:T(8,128)} custom-call(s32[8]{0:T(128)} %get-tuple-element.106.row_ref, bf16[500,8,250]{2,1,0:T(8,128)(2,1)} %bitcast.48, bf16[500,8,250]{2,1,0:T(8,128)(2,1)} %bitcast.53, s32[8]{0:T(128)} %get-tuple-element.107.own_col_ref, s32[8]{0:T(128)} %get-tuple-element.105.sib_col_ref), custom_call_target="tpu_custom_call" | custom-call | tf_op jit(solution)/shard_map/pivot_entries/pallas_call | solution.py:63
  26.5 5.5 %collective-permute-done.5 = bf16[2,250,128]{2,1,0:T(8,128)(2,1)S(1)} collective-permute-done((bf16[2,250,128]{2,1,0:T(8,128)(2,1)S(1)}, bf16[2,250,128]{2,1,0:T(8,128)(2,1)S(1)}, u32[]{:S(2)}, u32[]{:S(2)}) %collective-permute-start.5) | collective-permute-done | bytes 128032 | tf_op jit(solution)/shard_map/ppermute | solution.py:30
  32.1 2.5 %collective-permute-start.10 = (bf16[4,2,250,128]{3,2,1,0:T(8,128)(2,1)S(1)}, bf16[4,2,250,128]{3,2,1,0:T(8,128)(2,1)S(1)}, u32[]{:S(2)}, u32[]{:S(2)}) collective-permute-start(bf16[4,2,250,128]{3,2,1,0:T(8,128)(2,1)S(1)} %pad_maximum_fusion.3.rest_0_), channel_id=1, source_target_pairs={{0,24},{1,25},{2,26},{3,27},{4,28},{5,29},{6,30},{7,31},{8,16},{9,... | collective-permute-start | bytes 1536008 | tf_op jit(solution)/shard_map/ppermute | solution.py:30
  35.6 2.5 %collective-permute-start.11 = (bf16[500,512]{1,0:T(8,128)(2,1)}, bf16[500,512]{1,0:T(8,128)(2,1)S(1)}, u32[]{:S(2)}, u32[]{:S(2)}) collective-permute-start(bf16[500,512]{1,0:T(8,128)(2,1)} %cp_ref.1), channel_id=1, source_target_pairs={{0,4},{1,5},{2,6},{3,7},{4,0},{5,1},{6,2},{7,3},{8,12},{9,13},{10,... | collective-permute-start | bytes 1536008 | tf_op jit(solution)/shard_map/ppermute | solution.py:30
  38.3 9.5 %invert_blocks.1 = (f32[512,512]{1,0:T(8,128)S(1)}, f32[512,512]{1,0:T(8,128)S(1)}) custom-call(f32[512,512]{1,0:T(8,128)S(1)} %convert_select_fusion.own_ref, f32[512,512]{1,0:T(8,128)} %collective-permute-done.7.sib_ref), custom_call_target="tpu_custom_call" | custom-call | flops 8589934592 | bytes 4194304 | tf_op jit(solution)/shard_map/invert_blocks/pallas_call | solution.py:203
  47.8 3.6 %fusion.4 = f32[512,512]{1,0:T(8,128)S(1)} fusion(f32[512,512]{1,0:T(8,128)S(1)} %get-tuple-element.59, f32[512,1024]{1,0:T(8,128)S(1)} %copy-done.25), kind=kOutput, calls=%fused_computation.17 | convolution fusion | flops 1610612736 | bytes 3145728 | tf_op jit(solution)/shard_map/dot_general | solution.py:348
  51.6 1.9 %fusion.3 = f32[1,512,512]{2,1,0:T(8,128)S(1)} fusion(f32[512,512]{1,0:T(8,128)S(1)} %get-tuple-element.58, f32[512,512]{1,0:T(8,128)S(1)} %fusion.4, pred[]{:T(512)S(6)} %eq.17), kind=kOutput, calls=%fused_computation.11 | convolution fusion | flops 1611137024 | bytes 3145729 | tf_op jit(solution)/shard_map/dot_general | solution.py:349
  54.3 2.4 %collective-permute-start.15 = (bf16[500,512]{1,0:T(8,128)(2,1)}, bf16[500,512]{1,0:T(8,128)(2,1)}, u32[]{:S(2)}, u32[]{:S(2)}) collective-permute-start(bf16[500,512]{1,0:T(8,128)(2,1)} %cp_ref.1), channel_id=1, source_target_pairs={{0,6},{1,7},{2,4},{3,5},{4,2},{5,3},{6,0},{7,1},{8,14},{9,15},{10,... | collective-permute-start | bytes 1536008 | tf_op jit(solution)/shard_map/ppermute | solution.py:30
  56.7 2.4 %fusion = (bf16[2,512,512]{2,1,0:T(8,128)(2,1)S(1)}, bf16[2,512,512]{2,1,0:T(8,128)(2,1)}, bf16[2,512,512]{2,1,0:T(8,128)(2,1)}, bf16[2,512,512]{2,1,0:T(8,128)(2,1)}) fusion(f32[1,512,512]{2,1,0:T(8,128)S(1)} %select_bitcast_fusion, f32[1,512,512]{2,1,0:T(8,128)S(1)} %fusion.3, f32[1,512,512]{2,1,0:T(8,128)S(1)} %copy-done.27, f32[1,512,512]{2,1,0:T(8,128)S(1)} %copy-done.26), kind=kLoop, calls=%fused_computation.5 | loop fusion | flops 5242880 | bytes 8388608 | tf_op jit(solution)/shard_map/convert_element_type | solution.py:37
  60.7 12.5 %collective-permute-done.11.cp_ref = bf16[500,512]{1,0:T(8,128)(2,1)S(1)} collective-permute-done((bf16[500,512]{1,0:T(8,128)(2,1)}, bf16[500,512]{1,0:T(8,128)(2,1)S(1)}, u32[]{:S(2)}, u32[]{:S(2)}) %collective-permute-start.11) | collective-permute-done | bytes 512032 | tf_op jit(solution)/shard_map/ppermute | solution.py:30
  74.0 1.6 collective-permute-start.17
  81.5 4.6 %project.5 = f32[8,640]{1,0:T(8,128)S(1)} custom-call(s32[5]{0:T(128)S(1)} %stack.86.where_ref, bf16[4000,250]{1,0:T(8,128)(2,1)S(1)} %bitcast.49, bf16[4000,250]{1,0:T(8,128)(2,1)S(1)} %bitcast.54, bf16[500,512]{1,0:T(8,128)(2,1)} %collective-permute-done.12.cp_ref, f32[8,8]{1,0:T(8,128)S(1)} %copy-done.13, bf16[4,2,250,128]{3,2,1,0:T(8,128)(2,1)S(1)} %copy-done.7, ...), custom_call_target="tpu_custom_call" | custom-call | flops 2048000000 | bytes 1048576 | tf_op jit(solution)/shard_map/project/pallas_call | solution.py:142
  86.2 3.6 %project.6 = f32[8,640]{1,0:T(8,128)S(1)} custom-call(s32[5]{0:T(128)S(1)} %stack.86.where_ref, bf16[4000,250]{1,0:T(8,128)(2,1)S(1)} %bitcast.50, bf16[4000,250]{1,0:T(8,128)(2,1)S(1)} %bitcast.55, bf16[500,512]{1,0:T(8,128)(2,1)S(1)} %copy-done.24, f32[8,8]{1,0:T(8,128)S(1)} %copy-done.13, bf16[4,2,250,128]{3,2,1,0:T(8,128)(2,1)S(1)} %copy-done.7, ...), custom_call_target="tpu_custom_call" | custom-call | flops 2048000000 | bytes 1048576 | tf_op jit(solution)/shard_map/project/pallas_call | solution.py:142
  89.8 2.0 %collective-permute-start.14 = (f32[8,640]{1,0:T(8,128)S(1)}, f32[8,640]{1,0:T(8,128)S(1)}, u32[]{:S(2)}, u32[]{:S(2)}) collective-permute-start(f32[8,640]{1,0:T(8,128)S(1)} %project.6), channel_id=1, source_target_pairs={{0,4},{1,5},{2,6},{3,7},{4,0},{5,1},{6,2},{7,3},{8,12},{9,13},{10,... | collective-permute-start | bytes 61448 | tf_op jit(solution)/shard_map/ppermute | solution.py:30
  91.9 4.6 %project.7 = f32[8,640]{1,0:T(8,128)S(1)} custom-call(s32[5]{0:T(128)S(1)} %stack.86.where_ref, bf16[4000,250]{1,0:T(8,128)(2,1)S(1)} %bitcast.51, bf16[4000,250]{1,0:T(8,128)(2,1)S(1)} %bitcast.56, bf16[500,512]{1,0:T(8,128)(2,1)} %collective-permute-done.15.cp_ref, f32[8,8]{1,0:T(8,128)S(1)} %copy-done.13, bf16[4,2,250,128]{3,2,1,0:T(8,128)(2,1)S(1)} %copy-done.8, ...), custom_call_target="tpu_custom_call" | custom-call | flops 2048000000 | bytes 1048576 | tf_op jit(solution)/shard_map/project/pallas_call | solution.py:142
  96.5 2.5 %collective-permute-start.16 = (f32[8,640]{1,0:T(8,128)S(1)}, f32[8,640]{1,0:T(8,128)S(1)}, u32[]{:S(2)}, u32[]{:S(2)}) collective-permute-start(f32[8,640]{1,0:T(8,128)S(1)} %project.7), channel_id=1, source_target_pairs={{0,6},{1,7},{2,4},{3,5},{4,2},{5,3},{6,0},{7,1},{8,14},{9,15},{10,... | collective-permute-start | bytes 61448 | tf_op jit(solution)/shard_map/ppermute | solution.py:30
  99.0 4.6 %project.4 = f32[8,640]{1,0:T(8,128)S(1)} custom-call(s32[5]{0:T(128)S(1)} %stack.86.where_ref, bf16[4000,250]{1,0:T(8,128)(2,1)S(1)} %bitcast.52, bf16[4000,250]{1,0:T(8,128)(2,1)S(1)} %bitcast.57, bf16[500,512]{1,0:T(8,128)(2,1)} %cp_ref.1, f32[8,8]{1,0:T(8,128)S(1)} %copy-done.13, bf16[4,2,250,128]{3,2,1,0:T(8,128)(2,1)S(1)} %copy-done.8, ...), custom_call_target="tpu_custom_call" | custom-call | flops 2048000000 | bytes 1048576 | tf_op jit(solution)/shard_map/project/pallas_call | solution.py:142
  105.3 2.9 %collective-permute-start.19 = (f32[8,640]{1,0:T(8,128)S(1)}, f32[8,640]{1,0:T(8,128)S(1)}, u32[]{:S(2)}, u32[]{:S(2)}) collective-permute-start(f32[8,640]{1,0:T(8,128)S(1)} %add_add_fusion.1), channel_id=1, source_target_pairs={{0,16},{1,17},{2,18},{3,19},{4,20},{5,21},{6,22},{7,23},{8,24},{9,... | collective-permute-start | bytes 61448 | tf_op jit(solution)/shard_map/ppermute | solution.py:30
  109.9 2.9 %collective-permute-done.20 = f32[8,640]{1,0:T(8,128)S(1)} collective-permute-done((f32[8,640]{1,0:T(8,128)S(1)}, f32[8,640]{1,0:T(8,128)S(1)}, u32[]{:S(2)}, u32[]{:S(2)}) %collective-permute-start.20) | collective-permute-done | bytes 20512 | tf_op jit(solution)/shard_map/ppermute | solution.py:30
  120.2 2.8 %turn.3.refs_1_ = f32[8,512]{1,0:T(8,128)S(1)} custom-call(s32[1]{0:T(128)} %bitcast.1.where_ref, bf16[2,512,512]{2,1,0:T(8,128)(2,1)} %collective-permute-done.17.refs_0_, bf16[2,512,512]{2,1,0:T(8,128)(2,1)S(1)} %collective-permute-done.22.refs_1_, bf16[2,512,512]{2,1,0:T(8,128)(2,1)S(1)} %copy-done.3, ...), custom_call_target="tpu_custom_call" | custom-call | flops 2147483648 | bytes 4194304 | tf_op jit(solution)/shard_map/turn/pallas_call | solution.py:256
  124.7 3.7 %collective-permute-done.26 = f32[8,512]{1,0:T(8,128)S(1)} collective-permute-done((f32[8,512]{1,0:T(8,128)S(1)}, f32[8,512]{1,0:T(8,128)S(1)}, u32[]{:S(2)}, u32[]{:S(2)}) %collective-permute-start.26) | collective-permute-done | bytes 16416 | tf_op jit(solution)/shard_map/ppermute | solution.py:30
  128.4 1.9 %apply_weights.4 = f32[8,512]{1,0:T(8,128)S(1)} custom-call(s32[1]{0:T(128)} %bitcast.1.where_ref, bf16[2,512,512]{2,1,0:T(8,128)(2,1)} %get-tuple-element.66.hi_ref, bf16[2,512,512]{2,1,0:T(8,128)(2,1)S(1)} %copy-done.5, f32[8,512]{1,0:T(8,128)S(1)} %add.99.xa_ref, f32[8,512]{1,0:T(8,128)S(1)} %add.100.xb_ref), custom_call_target="tpu_custom_call" | custom-call | flops 1073741824 | bytes 2097152 | tf_op jit(solution)/shard_map/apply_weights/pallas_call | solution.py:235
  134.2 2.4 %turn.4.refs_2_ = f32[8,512]{1,0:T(8,128)S(1)} custom-call(s32[1]{0:T(128)} %bitcast.1.where_ref, bf16[2,512,512]{2,1,0:T(8,128)(2,1)} %collective-permute-done.17.refs_0_, bf16[2,512,512]{2,1,0:T(8,128)(2,1)S(1)} %collective-permute-done.22.refs_1_, bf16[2,512,512]{2,1,0:T(8,128)(2,1)S(1)} %copy-done.3, ...), custom_call_target="tpu_custom_call" | custom-call | flops 2147483648 | bytes 4194304 | tf_op jit(solution)/shard_map/turn/pallas_call | solution.py:256
  139.5 1.9 %apply_weights.5 = f32[8,512]{1,0:T(8,128)S(1)} custom-call(s32[1]{0:T(128)} %bitcast.1.where_ref, bf16[2,512,512]{2,1,0:T(8,128)(2,1)} %get-tuple-element.66.hi_ref, bf16[2,512,512]{2,1,0:T(8,128)(2,1)S(1)} %copy-done.5, f32[8,512]{1,0:T(8,128)S(1)} %collective-permute-done.33.xa_ref, f32[8,512]{1,0:T(8,128)S(1)} %collective-permute-done.34.xb_ref), custom_call_target="tpu_custom_call" | custom-call | flops 1073741824 | bytes 2097152 | tf_op jit(solution)/shard_map/apply_weights/pallas_call | solution.py:235
  143.0 1.9 %factor_inverse.1 = f32[8,8]{1,0:T(8,128)} custom-call(f32[8,8]{1,0:T(8,128)} %slice.27.block_ref), custom_call_target="tpu_custom_call" | custom-call | tf_op jit(solution)/shard_map/factor_inverse/pallas_call | solution.py:98
  144.9 1.8 %gather_fusion = f32[4,2,8]{2,1,0:T(2,128)} fusion(f32[4,2,8]{2,1,0:T(2,128)} %bitcast.66, s32[1024]{0:T(1024)S(1)} %pad_clamp_fusion), kind=kCustom, calls=%fused_computation | custom fusion | bytes 528 | tf_op jit(solution)/shard_map/gather | solution.py:414
  148.0 2.4 %turn.5.refs_3_ = f32[8,512]{1,0:T(8,128)S(1)} custom-call(s32[1]{0:T(128)} %bitcast.1.where_ref, bf16[2,512,512]{2,1,0:T(8,128)(2,1)} %collective-permute-done.17.refs_0_, bf16[2,512,512]{2,1,0:T(8,128)(2,1)S(1)} %copy-done.15, bf16[2,512,512]{2,1,0:T(8,128)(2,1)S(1)} %copy-done.4, bf16[2,512,512]{2,1,0:T(8,128)(2,1)S(1)} %get-tuple-element.69.lo_ref.refs_3_, ...), custom_call_target="tpu_custom_call" | custom-call | flops 2147483648 | bytes 4194304 | tf_op jit(solution)/shard_map/turn/pallas_call | solution.py:256
  155.1 18.3 %collective-permute-done.41 = f32[2,512]{1,0:T(2,128)S(1)} collective-permute-done((f32[2,512]{1,0:T(2,128)}, f32[2,512]{1,0:T(2,128)S(1)}, u32[]{:S(2)}, u32[]{:S(2)}) %collective-permute-start.41) | collective-permute-done | bytes 4128 | tf_op jit(solution)/shard_map/ppermute | solution.py:30
  (151 shorter events, 47.4 us)
Async XLA Ops:
  0.0 12.2 %collective-permute-start.3 = (bf16[8,500,250]{2,0,1:T(8,128)(2,1)}, bf16[8,500,250]{2,0,1:T(8,128)(2,1)S(1)}, u32[]{:S(2)}, u32[]{:S(2)}) collective-permute-start(bf16[8,500,250]{2,0,1:T(8,128)(2,1)} %param.4), channel_id=1, source_target_pairs={{0,1},{1,0},{2,3},{3,2},{4,5},{5,4},{6,7},{7,6},{8,9},{9,8},{10,11... | collective-permute-start | bytes 6000008 | tf_op jit(solution)/shard_map/ppermute | solution.py:30
  1.3 8.7 %collective-permute-start.1 = (bf16[2,250,128]{2,1,0:T(8,128)(2,1)S(1)}, bf16[2,250,128]{2,1,0:T(8,128)(2,1)S(1)}, u32[]{:S(2)}, u32[]{:S(2)}) collective-permute-start(bf16[2,250,128]{2,1,0:T(8,128)(2,1)S(1)} %get-tuple-element.103), channel_id=1, source_target_pairs={{0,16},{1,17},{2,18},{3,19},{4,20},{5,21},{6,22},{7,23},{8,24},{9,... | collective-permute-start | bytes 384008 | tf_op jit(solution)/shard_map/ppermute | solution.py:30
  2.9 7.3 %collective-permute-start.2 = (bf16[2,250,128]{2,1,0:T(8,128)(2,1)S(1)}, bf16[2,250,128]{2,1,0:T(8,128)(2,1)S(1)}, u32[]{:S(2)}, u32[]{:S(2)}) collective-permute-start(bf16[2,250,128]{2,1,0:T(8,128)(2,1)S(1)} %get-tuple-element.102), channel_id=1, source_target_pairs={{0,24},{1,25},{2,26},{3,27},{4,28},{5,29},{6,30},{7,31},{8,16},{9,... | collective-permute-start | bytes 384008 | tf_op jit(solution)/shard_map/ppermute | solution.py:30
  4.3 7.0 %collective-permute-start = (bf16[2,250,128]{2,1,0:T(8,128)(2,1)S(1)}, bf16[2,250,128]{2,1,0:T(8,128)(2,1)S(1)}, u32[]{:S(2)}, u32[]{:S(2)}) collective-permute-start(bf16[2,250,128]{2,1,0:T(8,128)(2,1)S(1)} %get-tuple-element.104), channel_id=1, source_target_pairs={{0,8},{1,9},{2,10},{3,11},{4,12},{5,13},{6,14},{7,15},{8,0},{9,1},... | collective-permute-start | bytes 384008 | tf_op jit(solution)/shard_map/ppermute | solution.py:30
  14.7 17.3 %collective-permute-start.7 = (f32[512,512]{1,0:T(8,128)S(1)}, f32[512,512]{1,0:T(8,128)}, u32[]{:S(2)}, u32[]{:S(2)}) collective-permute-start(f32[512,512]{1,0:T(8,128)S(1)} %convert_select_fusion.own_ref), channel_id=1, source_target_pairs={{0,1},{1,0},{2,3},{3,2},{4,5},{5,4},{6,7},{7,6},{8,9},{9,8},{10,11... | collective-permute-start | bytes 3145736 | tf_op jit(solution)/shard_map/ppermute | solution.py:30
  18.6 7.8 %collective-permute-start.4 = (bf16[2,250,128]{2,1,0:T(8,128)(2,1)}, bf16[2,250,128]{2,1,0:T(8,128)(2,1)S(1)}, u32[]{:S(2)}, u32[]{:S(2)}) collective-permute-start(bf16[2,250,128]{2,1,0:T(8,128)(2,1)} %get-tuple-element.99), channel_id=1, source_target_pairs={{0,2},{1,3},{2,0},{3,1},{4,6},{5,7},{6,4},{7,5},{8,10},{9,11},{10,... | collective-permute-start | bytes 384008 | tf_op jit(solution)/shard_map/ppermute | solution.py:30
  19.1 12.9 %collective-permute-start.5 = (bf16[2,250,128]{2,1,0:T(8,128)(2,1)S(1)}, bf16[2,250,128]{2,1,0:T(8,128)(2,1)S(1)}, u32[]{:S(2)}, u32[]{:S(2)}) collective-permute-start(bf16[2,250,128]{2,1,0:T(8,128)(2,1)S(1)} %get-tuple-element.98), channel_id=1, source_target_pairs={{0,4},{1,5},{2,6},{3,7},{4,0},{5,1},{6,2},{7,3},{8,12},{9,13},{10,... | collective-permute-start | bytes 384008 | tf_op jit(solution)/shard_map/ppermute | solution.py:30
  19.3 12.7 %collective-permute-start.6 = (bf16[2,250,128]{2,1,0:T(8,128)(2,1)S(1)}, bf16[2,250,128]{2,1,0:T(8,128)(2,1)S(1)}, u32[]{:S(2)}, u32[]{:S(2)}) collective-permute-start(bf16[2,250,128]{2,1,0:T(8,128)(2,1)S(1)} %get-tuple-element.97), channel_id=1, source_target_pairs={{0,6},{1,7},{2,4},{3,5},{4,2},{5,3},{6,0},{7,1},{8,14},{9,15},{10,... | collective-permute-start | bytes 384008 | tf_op jit(solution)/shard_map/ppermute | solution.py:30
  32.1 21.4 %collective-permute-start.10 = (bf16[4,2,250,128]{3,2,1,0:T(8,128)(2,1)S(1)}, bf16[4,2,250,128]{3,2,1,0:T(8,128)(2,1)S(1)}, u32[]{:S(2)}, u32[]{:S(2)}) collective-permute-start(bf16[4,2,250,128]{3,2,1,0:T(8,128)(2,1)S(1)} %pad_maximum_fusion.3.rest_0_), channel_id=1, source_target_pairs={{0,24},{1,25},{2,26},{3,27},{4,28},{5,29},{6,30},{7,31},{8,16},{9,... | collective-permute-start | bytes 1536008 | tf_op jit(solution)/shard_map/ppermute | solution.py:30
  34.6 24.5 %collective-permute-start.8 = (bf16[4,2,250,128]{3,2,1,0:T(8,128)(2,1)S(1)}, bf16[4,2,250,128]{3,2,1,0:T(8,128)(2,1)S(1)}, u32[]{:S(2)}, u32[]{:S(2)}) collective-permute-start(bf16[4,2,250,128]{3,2,1,0:T(8,128)(2,1)S(1)} %pad_maximum_fusion.3.rest_0_), channel_id=1, source_target_pairs={{0,8},{1,9},{2,10},{3,11},{4,12},{5,13},{6,14},{7,15},{8,0},{9,1},... | collective-permute-start | bytes 1536008 | tf_op jit(solution)/shard_map/ppermute | solution.py:30
  35.1 24.8 %collective-permute-start.9 = (bf16[4,2,250,128]{3,2,1,0:T(8,128)(2,1)S(1)}, bf16[4,2,250,128]{3,2,1,0:T(8,128)(2,1)S(1)}, u32[]{:S(2)}, u32[]{:S(2)}) collective-permute-start(bf16[4,2,250,128]{3,2,1,0:T(8,128)(2,1)S(1)} %pad_maximum_fusion.3.rest_0_), channel_id=1, source_target_pairs={{0,16},{1,17},{2,18},{3,19},{4,20},{5,21},{6,22},{7,23},{8,24},{9,... | collective-permute-start | bytes 1536008 | tf_op jit(solution)/shard_map/ppermute | solution.py:30
  35.6 37.6 %collective-permute-start.11 = (bf16[500,512]{1,0:T(8,128)(2,1)}, bf16[500,512]{1,0:T(8,128)(2,1)S(1)}, u32[]{:S(2)}, u32[]{:S(2)}) collective-permute-start(bf16[500,512]{1,0:T(8,128)(2,1)} %cp_ref.1), channel_id=1, source_target_pairs={{0,4},{1,5},{2,6},{3,7},{4,0},{5,1},{6,2},{7,3},{8,12},{9,13},{10,... | collective-permute-start | bytes 1536008 | tf_op jit(solution)/shard_map/ppermute | solution.py:30
  38.1 37.6 %collective-permute-start.12 = (bf16[500,512]{1,0:T(8,128)(2,1)}, bf16[500,512]{1,0:T(8,128)(2,1)}, u32[]{:S(2)}, u32[]{:S(2)}) collective-permute-start(bf16[500,512]{1,0:T(8,128)(2,1)} %cp_ref.1), channel_id=1, source_target_pairs={{0,2},{1,3},{2,0},{3,1},{4,6},{5,7},{6,4},{7,5},{8,10},{9,11},{10,... | collective-permute-start | bytes 1536008 | tf_op jit(solution)/shard_map/ppermute | solution.py:30
  54.3 37.5 %collective-permute-start.15 = (bf16[500,512]{1,0:T(8,128)(2,1)}, bf16[500,512]{1,0:T(8,128)(2,1)}, u32[]{:S(2)}, u32[]{:S(2)}) collective-permute-start(bf16[500,512]{1,0:T(8,128)(2,1)} %cp_ref.1), channel_id=1, source_target_pairs={{0,6},{1,7},{2,4},{3,5},{4,2},{5,3},{6,0},{7,1},{8,14},{9,15},{10,... | collective-permute-start | bytes 1536008 | tf_op jit(solution)/shard_map/ppermute | solution.py:30
  74.0 29.7 %collective-permute-start.17 = (bf16[2,512,512]{2,1,0:T(8,128)(2,1)}, bf16[2,512,512]{2,1,0:T(8,128)(2,1)}, u32[]{:S(2)}, u32[]{:S(2)}) collective-permute-start(bf16[2,512,512]{2,1,0:T(8,128)(2,1)} %get-tuple-element.66.hi_ref), channel_id=1, source_target_pairs={{2,10},{3,11},{12,20},{13,21},{22,30},{23,31}} | collective-permute-start | bytes 3145736 | tf_op jit(solution)/shard_map/ppermute | solution.py:30
  86.2 17.5 %collective-permute-start.13 = (f32[8,640]{1,0:T(8,128)S(1)}, f32[8,640]{1,0:T(8,128)S(1)}, u32[]{:S(2)}, u32[]{:S(2)}) collective-permute-start(f32[8,640]{1,0:T(8,128)S(1)} %project.5), channel_id=1, source_target_pairs={{0,2},{1,3},{2,0},{3,1},{4,6},{5,7},{6,4},{7,5},{8,10},{9,11},{10,... | collective-permute-start | bytes 61448 | tf_op jit(solution)/shard_map/ppermute | solution.py:30
  89.8 13.8 %collective-permute-start.14 = (f32[8,640]{1,0:T(8,128)S(1)}, f32[8,640]{1,0:T(8,128)S(1)}, u32[]{:S(2)}, u32[]{:S(2)}) collective-permute-start(f32[8,640]{1,0:T(8,128)S(1)} %project.6), channel_id=1, source_target_pairs={{0,4},{1,5},{2,6},{3,7},{4,0},{5,1},{6,2},{7,3},{8,12},{9,13},{10,... | collective-permute-start | bytes 61448 | tf_op jit(solution)/shard_map/ppermute | solution.py:30
  96.5 7.1 %collective-permute-start.16 = (f32[8,640]{1,0:T(8,128)S(1)}, f32[8,640]{1,0:T(8,128)S(1)}, u32[]{:S(2)}, u32[]{:S(2)}) collective-permute-start(f32[8,640]{1,0:T(8,128)S(1)} %project.7), channel_id=1, source_target_pairs={{0,6},{1,7},{2,4},{3,5},{4,2},{5,3},{6,0},{7,1},{8,14},{9,15},{10,... | collective-permute-start | bytes 61448 | tf_op jit(solution)/shard_map/ppermute | solution.py:30
  103.7 16.5 %collective-permute-start.22 = (bf16[2,512,512]{2,1,0:T(8,128)(2,1)}, bf16[2,512,512]{2,1,0:T(8,128)(2,1)S(1)}, u32[]{:S(2)}, u32[]{:S(2)}) collective-permute-start(bf16[2,512,512]{2,1,0:T(8,128)(2,1)} %collective-permute-done.17.refs_0_), channel_id=1, source_target_pairs={{0,1},{1,0},{2,3},{3,2},{4,5},{5,4},{6,7},{7,6},{8,9},{9,8},{10,11... | collective-permute-start | bytes 3145736 | tf_op jit(solution)/shard_map/ppermute | solution.py:30
  103.8 5.8 %collective-permute-start.18 = (f32[8,640]{1,0:T(8,128)S(1)}, f32[8,640]{1,0:T(8,128)S(1)}, u32[]{:S(2)}, u32[]{:S(2)}) collective-permute-start(f32[8,640]{1,0:T(8,128)S(1)} %add_add_fusion.1), channel_id=1, source_target_pairs={{0,8},{1,9},{2,10},{3,11},{4,12},{5,13},{6,14},{7,15},{8,0},{9,1},... | collective-permute-start | bytes 61448 | tf_op jit(solution)/shard_map/ppermute | solution.py:30
  105.3 4.6 %collective-permute-start.19 = (f32[8,640]{1,0:T(8,128)S(1)}, f32[8,640]{1,0:T(8,128)S(1)}, u32[]{:S(2)}, u32[]{:S(2)}) collective-permute-start(f32[8,640]{1,0:T(8,128)S(1)} %add_add_fusion.1), channel_id=1, source_target_pairs={{0,16},{1,17},{2,18},{3,19},{4,20},{5,21},{6,22},{7,23},{8,24},{9,... | collective-permute-start | bytes 61448 | tf_op jit(solution)/shard_map/ppermute | solution.py:30
  108.2 4.7 %collective-permute-start.20 = (f32[8,640]{1,0:T(8,128)S(1)}, f32[8,640]{1,0:T(8,128)S(1)}, u32[]{:S(2)}, u32[]{:S(2)}) collective-permute-start(f32[8,640]{1,0:T(8,128)S(1)} %add_add_fusion.1), channel_id=1, source_target_pairs={{0,24},{1,25},{2,26},{3,27},{4,28},{5,29},{6,30},{7,31},{8,16},{9,... | collective-permute-start | bytes 61448 | tf_op jit(solution)/shard_map/ppermute | solution.py:30
  116.3 7.4 %collective-permute-start.27 = (f32[8,512]{1,0:T(8,128)S(1)}, f32[8,512]{1,0:T(8,128)S(1)}, u32[]{:S(2)}, u32[]{:S(2)}) collective-permute-start(f32[8,512]{1,0:T(8,128)S(1)} %apply_weights.3.refs_0_), channel_id=1, source_target_pairs={{0,5},{1,4}} | collective-permute-start | bytes 49160 | tf_op jit(solution)/shard_map/ppermute | solution.py:30
  117.0 7.7 %collective-permute-start.28 = (f32[8,512]{1,0:T(8,128)S(1)}, f32[8,512]{1,0:T(8,128)S(1)}, u32[]{:S(2)}, u32[]{:S(2)}) collective-permute-start(f32[8,512]{1,0:T(8,128)S(1)} %apply_weights.3.refs_0_), channel_id=1, source_target_pairs={{0,7},{1,6}} | collective-permute-start | bytes 49160 | tf_op jit(solution)/shard_map/ppermute | solution.py:30
  118.3 6.4 %collective-permute-start.25 = (f32[8,512]{1,0:T(8,128)S(1)}, f32[8,512]{1,0:T(8,128)S(1)}, u32[]{:S(2)}, u32[]{:S(2)}) collective-permute-start(f32[8,512]{1,0:T(8,128)S(1)} %apply_weights.3.refs_0_), channel_id=1, source_target_pairs={{0,4},{1,5}} | collective-permute-start | bytes 49160 | tf_op jit(solution)/shard_map/ppermute | solution.py:30
  118.9 9.5 %collective-permute-start.26 = (f32[8,512]{1,0:T(8,128)S(1)}, f32[8,512]{1,0:T(8,128)S(1)}, u32[]{:S(2)}, u32[]{:S(2)}) collective-permute-start(f32[8,512]{1,0:T(8,128)S(1)} %apply_weights.3.refs_0_), channel_id=1, source_target_pairs={{0,6},{1,7}} | collective-permute-start | bytes 49160 | tf_op jit(solution)/shard_map/ppermute | solution.py:30
  123.0 5.4 %collective-permute-start.29 = (f32[8,512]{1,0:T(8,128)S(1)}, f32[8,512]{1,0:T(8,128)S(1)}, u32[]{:S(2)}, u32[]{:S(2)}) collective-permute-start(f32[8,512]{1,0:T(8,128)S(1)} %turn.3.refs_1_), channel_id=1, source_target_pairs={{10,20},{11,21}} | collective-permute-start | bytes 49160 | tf_op jit(solution)/shard_map/ppermute | solution.py:30
  123.7 4.7 %collective-permute-start.30 = (f32[8,512]{1,0:T(8,128)S(1)}, f32[8,512]{1,0:T(8,128)S(1)}, u32[]{:S(2)}, u32[]{:S(2)}) collective-permute-start(f32[8,512]{1,0:T(8,128)S(1)} %turn.3.refs_1_), channel_id=1, source_target_pairs={{10,21},{11,20}} | collective-permute-start | bytes 49160 | tf_op jit(solution)/shard_map/ppermute | solution.py:30
  130.3 2.7 %collective-permute-start.31 = (f32[8,512]{1,0:T(8,128)S(1)}, f32[8,512]{1,0:T(8,128)S(1)}, u32[]{:S(2)}, u32[]{:S(2)}) collective-permute-start(f32[8,512]{1,0:T(8,128)S(1)} %apply_weights.4), channel_id=1, source_target_pairs={{4,20},{5,21},{6,30},{7,31}} | collective-permute-start | bytes 49160 | tf_op jit(solution)/shard_map/ppermute | solution.py:30
  136.6 2.8 %collective-permute-start.35 = (f32[8,512]{1,0:T(8,128)S(1)}, f32[8,512]{1,0:T(8,128)S(1)}, u32[]{:S(2)}, u32[]{:S(2)}) collective-permute-start(f32[8,512]{1,0:T(8,128)S(1)} %turn.4.refs_2_), channel_id=1, source_target_pairs={{20,30},{21,31}} | collective-permute-start | bytes 49160 | tf_op jit(solution)/shard_map/ppermute | solution.py:30
  142.1 4.6 %collective-permute-start.38 = (f32[8,512]{1,0:T(8,128)S(1)}, f32[8,512]{1,0:T(8,128)S(1)}, u32[]{:S(2)}, u32[]{:S(2)}) collective-permute-start(f32[8,512]{1,0:T(8,128)S(1)} %sub.49.refs_6_), channel_id=1, source_target_pairs={{0,1},{1,0},{2,3},{3,2},{4,5},{5,4},{6,7},{7,6},{8,9},{9,8},{10,11... | collective-permute-start | bytes 49160 | tf_op jit(solution)/shard_map/ppermute | solution.py:30
  153.8 19.6 %collective-permute-start.41 = (f32[2,512]{1,0:T(2,128)}, f32[2,512]{1,0:T(2,128)S(1)}, u32[]{:S(2)}, u32[]{:S(2)}) collective-permute-start(f32[2,512]{1,0:T(2,128)} %get-tuple-element.90), channel_id=1, source_target_pairs={{0,24},{1,25},{10,18},{11,19},{20,12},{21,13},{30,6},{31,7}} | collective-permute-start | bytes 12296 | tf_op jit(solution)/shard_map/ppermute | solution.py:30
  (40 other events, 231.2 us)

commit v5 on v4

--- a/solution.py
+++ b/solution.py
@@ -102,72 +102,101 @@
     )(block)
 
 
-def project_kernel(vec_total, chunk, where_ref, own_ref, sib_ref, cp_ref, entries_ref, *rest):
-    part_refs, (out_ref, cq, cp, acc) = rest[:-4], rest[-4:]
-    part = part_refs[0].shape[-1]
-    points = cp.shape[1]
+def project_kernel(vec_total, chunk, cp_counts, cq_count, where_ref, own_ref, sib_ref, entries_ref, *rest):
+    blocks = len(cp_counts)
+    cp_refs, rest = rest[: sum(cp_counts)], rest[sum(cp_counts) :]
+    cq_refs, rest = rest[: blocks * cq_count], rest[blocks * cq_count :]
+    out_refs, (cq, cp, acc) = rest[:blocks], rest[blocks:]
+    points = cp.shape[2]
     step = pl.program_id(0)
     core = where_ref[0]
 
     @pl.when(step == 0)
     def _():
-        for n, ref in enumerate(part_refs):
+        for b in range(blocks):
+            for n in range(cq_count):
+                ref = cq_refs[b * cq_count + n]
+                part = ref.shape[-1]
+                start = 0
+                if cq_count > 1:
+                    start = pl.multiple_of(where_ref[1 + n] * part, part)
+                cq[b, :, :, pl.ds(start, part)] = ref[0]
             start = 0
-            if len(part_refs) > 1:
-                start = pl.multiple_of(where_ref[1 + n] * part, part)
-            cq[:, :, pl.ds(start, part)] = ref[0]
-        cp[...] = cp_ref[...].astype(F32)
+            for ref in cp_refs[sum(cp_counts[:b]) : sum(cp_counts[: b + 1])]:
+                cp[b, :, start : start + ref.shape[1]] = ref[...].astype(F32)
+                start += ref.shape[1]
+            out_ref = out_refs[b]
+            out_ref[:, points:] = jnp.zeros((vec_total, out_ref.shape[1] - points), F32)
+            out_ref[:, points : points + vec_total] = entries_ref[...]
         acc[...] = jnp.zeros_like(acc)
-        out_ref[:, points:] = jnp.zeros((vec_total, out_ref.shape[1] - points), F32)
-        out_ref[:, points : points + vec_total] = entries_ref[...]
-
-    mixed = jnp.dot(own_ref[...], cq[core], preferred_element_type=F32)
-    mixed += jnp.dot(sib_ref[...], cq[1 - core], preferred_element_type=F32)
-    total = acc[...]
-    for p in range(chunk):
-        total += mixed[p * vec_total : (p + 1) * vec_total] * cp[pl.ds(step * chunk + p, 1), :]
-    acc[...] = total
+
+    for b in range(blocks):
+        mixed = jnp.dot(own_ref[...], cq[b, core], preferred_element_type=F32)
+        mixed += jnp.dot(sib_ref[...], cq[b, 1 - core], preferred_element_type=F32)
+        total = acc[b]
+        for p in range(chunk):
+            row = cp[b, pl.ds(step * chunk + p, 1), :]
+            total += mixed[p * vec_total : (p + 1) * vec_total] * row
+        acc[b] = total
 
     @pl.when(step == pl.num_programs(0) - 1)
     def _():
-        out_ref[:, :points] = acc[...]
-
-
-def project(where, own, sib, cp, entries, parts, slot):
-    orb, points = cp.shape
+        for b in range(blocks):
+            out_refs[b][:, :points] = acc[b]
+
+
+def project(where, own, sib, entries, first, second, slots):
+    orb = first[0][0].shape[0]
+    points = sum(x.shape[1] for x in first[0])
     pair = own.shape[1]
     vec_total = own.shape[0] // orb
     chunk = 125
-    part_shape = (1,) + parts[0].shape[1:]
-    return pl.pallas_call(
-        functools.partial(project_kernel, vec_total, chunk),
+    blocks = len(first)
+    whole = lambda i, s: (0, 0)
+    specs, arrays = [], []
+    for parts in first:
+        for x in parts:
+            specs.append(pl.BlockSpec(x.shape, whole))
+            arrays.append(x)
+    for parts, slot in zip(second, slots):
+        for x in parts:
+            specs.append(
+                pl.BlockSpec((1,) + x.shape[1:], lambda i, s, slot=slot: (slot, 0, 0, 0))
+            )
+            arrays.append(x)
+    kernel = functools.partial(
+        project_kernel, vec_total, chunk, tuple(len(x) for x in first), len(second[0])
+    )
+    return pl.pallas_call(
+        kernel,
         grid_spec=pltpu.PrefetchScalarGridSpec(
             num_scalar_prefetch=1,
             grid=(orb // chunk,),
             in_specs=[
                 pl.BlockSpec((chunk * vec_total, pair), lambda i, s: (i, 0)),
                 pl.BlockSpec((chunk * vec_total, pair), lambda i, s: (i, 0)),
-                pl.BlockSpec((orb, points), lambda i, s: (0, 0)),
-                pl.BlockSpec((vec_total, vec_total), lambda i, s: (0, 0)),
+                pl.BlockSpec((vec_total, vec_total), whole),
             ]
-            + [pl.BlockSpec(part_shape, lambda i, s: (slot, 0, 0, 0))] * len(parts),
-            out_specs=pl.BlockSpec((vec_total, points + 128), lambda i, s: (0, 0)),
+            + specs,
+            out_specs=[pl.BlockSpec((vec_total, points + 128), whole)] * blocks,
             scratch_shapes=[
-                pltpu.VMEM((2, pair, points), BF16),
-                pltpu.VMEM((orb, points), F32),
-                pltpu.VMEM((vec_total, points), F32),
+                pltpu.VMEM((blocks, 2, pair, points), BF16),
+                pltpu.VMEM((blocks, orb, points), F32),
+                pltpu.VMEM((blocks, vec_total, points), F32),
             ],
         ),
-        out_shape=jax.ShapeDtypeStruct((vec_total, points + 128), F32),
-        compiler_params=pltpu.CompilerParams(vmem_limit_bytes=20 << 20),
+        out_shape=[jax.ShapeDtypeStruct((vec_total, points + 128), F32)] * blocks,
+        compiler_params=pltpu.CompilerParams(vmem_limit_bytes=32 << 20),
         cost_estimate=pl.CostEstimate(
-            flops=4 * orb * vec_total * pair * points, transcendentals=0, bytes_accessed=1 << 20
+            flops=4 * orb * vec_total * pair * points * blocks,
+            transcendentals=0,
+            bytes_accessed=1 << 20,
         ),
         name="project",
-    )(where, own, sib, cp, entries, *parts)
-
-
-def invert_kernel(own_ref, sib_ref, own_out, sib_out):
+    )(where, own, sib, entries, *arrays)
+
+
+def invert_kernel(where_ref, own_ref, sib_ref, own_out, sib_out):
     n = own_ref.shape[0]
     tile = 128
     row = lax.broadcasted_iota(jnp.int32, (tile, tile), 0)
@@ -176,7 +205,8 @@
     dot = functools.partial(jnp.dot, precision=HIGHEST, preferred_element_type=F32)
     pairs = ((own_ref, own_out), (sib_ref, sib_out))
     places = [(ref, out, b) for ref, out in pairs for b in range(0, n, tile)]
-    parts = [ref[b : b + tile, b : b + tile] for ref, _, b in places]
+    holds = where_ref[1] == 1
+    parts = [jnp.where(holds, ref[b : b + tile, b : b + tile], eye) for ref, _, b in places]
     xs = [eye / jnp.sum(part * eye, axis=1, keepdims=True) for part in parts]
     size = 1
     while size < tile:
@@ -198,15 +228,18 @@
         size *= 2
 
 
-def invert_blocks(own, sib):
+def invert_blocks(where, own, sib):
     shape = jax.ShapeDtypeStruct(own.shape, F32)
+    vmem = pl.BlockSpec(memory_space=pltpu.VMEM)
     return pl.pallas_call(
         invert_kernel,
+        in_specs=[pl.BlockSpec(memory_space=pltpu.SMEM), vmem, vmem],
+        out_specs=(vmem, vmem),
         out_shape=(shape, shape),
         compiler_params=pltpu.CompilerParams(vmem_limit_bytes=16 << 20),
         cost_estimate=pl.CostEstimate(flops=8 << 30, transcendentals=0, bytes_accessed=1 << 22),
         name="invert_blocks",
-    )(own, sib)
+    )(where, own, sib)
 
 
 def weigh(hi_ref, lo_ref, halves):
@@ -216,12 +249,14 @@
         hi = x.astype(BF16)
         lo = (x - hi.astype(F32)).astype(BF16)
         n = x.shape[0]
+        width = x.shape[1]
+        columns = pl.ds(pl.multiple_of(half * width, width), width)
         both = lax.dot_general(
-            jnp.concatenate([hi, lo]), hi_ref[half], dims, preferred_element_type=F32
+            jnp.concatenate([hi, lo]), hi_ref[:, columns], dims, preferred_element_type=F32
         )
         part = both[:n] + both[n:]
         if lo_ref is not None:
-            part += lax.dot_general(hi, lo_ref[half], dims, preferred_element_type=F32)
+            part += lax.dot_general(hi, lo_ref[:, columns], dims, preferred_element_type=F32)
         total = part if total is None else total + part
     return total
 
@@ -243,32 +278,57 @@
     )(where, *weights, xa, xb)
 
 
-def turn_kernel(where_ref, *refs):
-    own_left, sib_left, inv_hi, inv_lo, xa, xb, own_rest, sib_rest, out_ref = refs
+def turn_kernel(count, where_ref, *refs):
+    lefts, refs = refs[: 2 * count], refs[2 * count :]
+    inv_hi, inv_lo, xa, xb, own_rest, sib_rest, out_ref, buffer, sems = refs
     core = where_ref[0]
-    halves = [(core, xa[...]), (1 - core, xb[...])]
-    own = own_rest[...] - weigh(own_left, None, halves)
-    sib = sib_rest[...] - weigh(sib_left, None, halves)
-    out_ref[...] = weigh(inv_hi, inv_lo, [(core, own), (1 - core, sib)])
+    n = own_rest.shape[0]
+    copies = [
+        pltpu.make_async_copy(ref, buffer.at[i], sems.at[i]) for i, ref in enumerate(lefts)
+    ]
+    for copy in copies:
+        copy.start()
+    own, sib = own_rest[...], sib_rest[...]
+    for i in range(count):
+        d = count - i
+        halves = [(core, xa[i * n : (i + 1) * n]), (1 - core, xb[i * n : (i + 1) * n])]
+        copies[2 * d - 2].wait()
+        own -= weigh(buffer.at[2 * d - 2], None, halves)
+        copies[2 * d - 1].wait()
+        sib -= weigh(buffer.at[2 * d - 1], None, halves)
+    out_ref[: count * n] = xa[...]
+    out_ref[count * n :] = weigh(inv_hi, inv_lo, [(core, own), (1 - core, sib)])
 
 
 def turn(where, left_own, left_sib, inverse, xa, xb, own_rest, sib_rest):
-    return pl.pallas_call(
-        turn_kernel,
-        in_specs=[pl.BlockSpec(memory_space=pltpu.SMEM)] + [pl.BlockSpec(memory_space=pltpu.VMEM)] * 8,
+    n, points = own_rest.shape
+    count = xa.shape[0] // n
+    lefts = []
+    for d in range(1, count + 1):
+        lefts += [left_own[d], left_sib[d]]
+    return pl.pallas_call(
+        functools.partial(turn_kernel, count),
+        in_specs=[pl.BlockSpec(memory_space=pltpu.SMEM)]
+        + [pl.BlockSpec(memory_space=pl.ANY)] * len(lefts)
+        + [pl.BlockSpec(memory_space=pltpu.VMEM)] * 6,
         out_specs=pl.BlockSpec(memory_space=pltpu.VMEM),
-        out_shape=jax.ShapeDtypeStruct(xa.shape, F32),
-        compiler_params=pltpu.CompilerParams(vmem_limit_bytes=16 << 20),
+        out_shape=jax.ShapeDtypeStruct(((count + 1) * n, points), F32),
+        scratch_shapes=[
+            pltpu.VMEM((len(lefts),) + lefts[0].shape, BF16),
+            pltpu.SemaphoreType.DMA((len(lefts),)),
+        ],
+        compiler_params=pltpu.CompilerParams(vmem_limit_bytes=32 << 20),
         cost_estimate=pl.CostEstimate(flops=2 << 30, transcendentals=0, bytes_accessed=1 << 22),
         name="turn",
-    )(where, left_own, left_sib, *inverse, xa, xb, own_rest, sib_rest)
+    )(where, *lefts, *inverse, xa, xb, own_rest, sib_rest)
 
 
 def combine_kernel(count, turn_ref, inverse_ref, *refs):
     x_refs, out_refs = refs[:count], refs[count:]
     x = jnp.zeros(x_refs[0].shape, F32)
+    n = x.shape[0]
     for t, ref in enumerate(x_refs):
-        x = jnp.where(turn_ref[0] == t, ref[...], x)
+        x = jnp.where(turn_ref[0] == t, ref[t * n :], x)
     inverse = inverse_ref[...]
     total = inverse[:, :1] * x[:1]
     for i in range(1, x.shape[0]):
@@ -305,26 +365,40 @@
     swap = lambda g, j, c: (g, j, 1 - c)
 
     part = points // gen_count
+    across = lambda k: lambda g, j, c: (g, j ^ k, c)
+    leftwards = lambda d: lambda g, j, c: (g + d, j, c) if j == g + d else None
     halves = collocation.reshape(2, orb_block // 2, points)
     spread = []
     for k in range(gen_count):
         piece = lax.dynamic_slice_in_dim(halves, (gen_index ^ k) * part, part, 2)
         spread.append(move(piece, lambda g, j, c, k=k: (g ^ k, j, c)) if k else piece)
     spread = jnp.stack(spread)
-    across = lambda k: lambda g, j, c: (g, j ^ k, c)
+    early = 2
+    half = points // 2
+    early_parts = [move(collocation[:, :half], across(early))]
     sibling = move(raw_columns, swap)
-    spread, sibling, metric_late = lax.optimization_barrier((spread, sibling, metric_factor))
-    own_block = jnp.where(core == 0, metric_late[:, :points], metric_late[:, points:])
-    own_block = jnp.where(diagonal, own_block, jnp.eye(points, dtype=F32))
+    spread, sibling, early_parts, metric_late, first = lax.optimization_barrier(
+        (spread, sibling, early_parts, metric_factor, collocation)
+    )
+    early_parts.append(move(first[:, half:], across(early)))
+    own_block = lax.dynamic_slice_in_dim(metric_late, core * points, points, 1)
     sib_block = move(own_block, swap)
+    own_rows = metric_late.astype(BF16)
+    left_own = {d: move(own_rows, leftwards(d)) for d in (1, 2)}
+    spread, early_parts, first, sib_block = lax.optimization_barrier(
+        (spread, early_parts, first, sib_block)
+    )
     own_parts = []
     for k in range(gen_count):
         piece = lax.dynamic_index_in_dim(spread, gen_index ^ chip ^ k, 0, keepdims=False)
         own_parts.append(move(piece, across(k)) if k else piece)
-    own_parts, first, own_block, sib_block = lax.optimization_barrier(
-        (own_parts, collocation, own_block, sib_block)
-    )
-    first_side = [collocation] + [move(first, across(k)) for k in others]
+    own_parts, first, own_block, sib_block, left_own = lax.optimization_barrier(
+        (own_parts, first, own_block, sib_block, left_own)
+    )
+    first_side = {0: [collocation], early: early_parts}
+    for k in others:
+        if k != early:
+            first_side[k] = [move(first, across(k))]
     all_parts = [jnp.stack(own_parts)]
     for k in others:
         all_parts.append(move(all_parts[0], lambda g, j, c, k=k: (g ^ k, j, c)))
@@ -344,35 +418,51 @@
     sib_cols = pivot_pairs % NORB - (fit_index ^ 1) * pair_block
     entries = pivot_entries(own_raw, sib_raw, pivot_rows, own_cols, sib_cols)
 
-    own_inverse, upper = invert_blocks(own_block, sib_block)
+    own_inverse, upper = invert_blocks(
+        jnp.stack([core, diagonal.astype(jnp.int32)]), own_block, sib_block
+    )
     corner = jnp.dot(metric_factor[:, :points], upper, precision=HIGHEST)
     corner = -jnp.dot(own_inverse, corner, precision=HIGHEST)
-    zeros = jnp.zeros_like(own_inverse)
     inverse_rows = split_hi_lo(
-        jnp.stack(
-            [jnp.where(core == 0, own_inverse, corner), jnp.where(core == 0, zeros, own_inverse)]
+        jnp.concatenate(
+            [
+                jnp.where(core == 0, own_inverse, corner),
+                jnp.where(core == 0, jnp.zeros_like(own_inverse), own_inverse),
+            ],
+            axis=1,
         )
     )
 
-    own_hi, own_lo = split_hi_lo(jnp.stack([metric_factor[:, :points], metric_factor[:, points:]]))
-    all_parts, first_side[2], entries, inverse_rows, left_hi = lax.optimization_barrier(
-        (all_parts, first_side[2], entries, inverse_rows, own_hi)
-    )
-    left_own = move(left_hi, lambda g, j, c: (g + 1, j, c) if j == g + 1 else None)
+    _, inverse_rows, left_hi, left_own = lax.optimization_barrier(
+        (all_parts, inverse_rows, own_rows, left_own)
+    )
+    for d in range(3, gen_count):
+        left_own[d] = move(left_hi, leftwards(d))
+    left_sib = {d: move(left_own[d], swap) for d in (1, 2)}
 
     own_raw = own_raw.reshape(orb_block * vec_total, pair_block)
     sib_raw = sib_raw.reshape(orb_block * vec_total, pair_block)
     where = jnp.stack([core] + [gen_index ^ k for k in range(gen_count)])
     total = None
-    for k in range(gen_count):
-        block = first_side[k]
-        share = project(where, own_raw, sib_raw, block, entries, second_side(k), k if part % 128 == 0 else 0)
-        if k:
-            share = move(share, lambda g, j, c, k=k: (g, j ^ k, c))
-        total = share if total is None else total + share
-    total, left_own = lax.optimization_barrier((total, left_own))
-    left_sib = move(left_own, swap)
+    late = [k for k in others if k != early]
+    for group in [[0, early]] + [late[i : i + 2] for i in range(0, len(late), 2)]:
+        shares = project(
+            where,
+            own_raw,
+            sib_raw,
+            entries,
+            [first_side[k] for k in group],
+            [second_side(k) for k in group],
+            [k if part % 128 == 0 else 0 for k in group],
+        )
+        for k, share in zip(group, shares):
+            if k:
+                share = move(share, across(k))
+            total = share if total is None else total + share
     total = sum([move(total, lambda g, j, c, k=k: (g ^ k, j, c)) for k in others], total)
+    for d in range(3, gen_count):
+        total, left_own[d] = lax.optimization_barrier((total, left_own[d]))
+        left_sib[d] = move(left_own[d], swap)
     rest = total[:, :points]
     pivot_block = total[:, points : points + vec_total]
 
@@ -380,34 +470,11 @@
     sib_rest = move(rest, swap)
     solved = apply_weights(at_core, inverse_rows, rest, sib_rest)
     turns = [solved]
-    waiting = None
-    for t in range(gen_count):
-        if t + 1 < gen_count:
-            near = move(solved, lambda g, j, c: (t + 1, t + 1, c) if g == j == t else None)
-            near_sib = move(solved, lambda g, j, c: (t + 1, t + 1, 1 - c) if g == j == t else None)
-            near, near_sib, late = lax.optimization_barrier((near, near_sib, solved))
-        if waiting is not None:
-            if t + 1 < gen_count:
-                waiting, near, near_sib = lax.optimization_barrier((waiting, near, near_sib))
-            brought = apply_weights(at_core, (own_hi, own_lo), *waiting)
-            brought = move(
-                brought, lambda g, j, c: (j, j, c) if g == t - 1 and j >= t + 1 else None
-            )
-        far = None
-        if t + 2 < gen_count:
-            far = far_sib = None
-            for z in range(t + 2, gen_count):
-                one = move(late, lambda g, j, c: (t, z, c) if g == j == t else None)
-                two = move(late, lambda g, j, c: (t, z, 1 - c) if g == j == t else None)
-                far = one if far is None else far + one
-                far_sib = two if far_sib is None else far_sib + two
-        if waiting is not None:
-            rest = rest - brought
-            sib_rest = move(rest, swap)
-        waiting = None if far is None else (far, far_sib)
-        if t + 1 < gen_count:
-            solved = turn(at_core, left_own, left_sib, inverse_rows, near, near_sib, rest, sib_rest)
-            turns.append(solved)
+    for t in range(1, gen_count):
+        near = move(solved, lambda g, j, c: (t, t, c) if g == j == t - 1 else None)
+        near_sib = move(solved, lambda g, j, c: (t, t, 1 - c) if g == j == t - 1 else None)
+        solved = turn(at_core, left_own, left_sib, inverse_rows, near, near_sib, rest, sib_rest)
+        turns.append(solved)
 
     inverse_factor = factor_inverse(pivot_block).reshape(gen_count, vec_dev, vec_total)
     order = jnp.stack([gen_index ^ k for k in range(gen_count)])

time: 176 us -> 170 us (0.966)
  starting transfers between devices: 42.9 us -> 57.4 us
  waiting for transfers between devices: 54 us -> 47.7 us
  Pallas kernels: 45.2 us -> 39.1 us
  local copies, waits for them, and re-layouts: 18.5 us -> 12.7 us
  other arithmetic: 7.89 us -> 4.65 us
    ppermute x42 -> x37, starting transfers between devices: 42.9 us -> 57.4 us  [move(): return lax.ppermute(value, BOTH, pairs)]
    unnamed x60 -> x38, local copies, waits for them, and re-layouts: 10.9 us -> 3.12 us
    ppermute x42 -> x37, waiting for transfers between devices: 54 us -> 47.7 us  [move(): return lax.ppermute(value, BOTH, pairs)]
    pallas_call x3 -> x1, Pallas kernels: 4.38 us -> 0.65 us  [apply_weights(): pl.pallas_call(apply_kernel, in_specs=[pl.BlockSpec(memory_space=pltpu.SM...]
    another operation x1 -> x0, local copies, waits for them, and re-layouts: 3.12 us -> none  [on_device(): jnp.stack([metric_factor[:, :points], metric_factor[:, points:]])]
    dynamic_slice x0 -> x1, local copies, waits for them, and re-layouts: none -> 3.01 us  [on_device(): own_block = lax.dynamic_slice_in_dim(metric_late, core * points, points, 1)]
    pallas_call x8 -> x6, Pallas kernels: 34.6 us -> 32.1 us  [the longest x2 11.8 us: project(): pl.pallas_call(kernel, grid_spec=pltpu.PrefetchScalarGridSpec(num_scalar_...]
    select_n x1, other arithmetic: 2.51 us -> 0.09 us  [on_device(): jnp.where(core == 0, jnp.zeros_like(own_inverse), own_inverse)]
  transfers between devices with their start and end apart: 42 -> 37, of which waited for: 14 -> 11; matrix products, arithmetic and copies ran while one was open for 10% -> 9% of each run, Pallas kernels for 20% -> 20%
where the time goes in v5:
time: 170 us; the launch traced here: 168 us
  starting transfers between devices  57.4 us (34%)
  waiting for transfers between devices  47.7 us (28%)
  Pallas kernels  39.1 us (23%)
  local copies, waits for them, and re-layouts  12.7 us (7%)
  matrix products  5.57 us (3%)
  other arithmetic  4.65 us (3%)
    ppermute x37, starting transfers between devices, move(): return lax.ppermute(value, BOTH, pairs)  57.4 us
    ppermute x37, waiting for transfers between devices, move(): return lax.ppermute(value, BOTH, pairs)  47.7 us
    pallas_call x2, Pallas kernels, project(): pl.pallas_call(kernel, grid_spec=pltpu.PrefetchScalarGridSpec(num_scalar_...  11.8 us
    pallas_call x3, Pallas kernels, turn(): pl.pallas_call(functools.partial(turn_kernel, count), in_specs=[pl.BlockS...  10.5 us
    pallas_call x1, Pallas kernels, invert_blocks(): pl.pallas_call(invert_kernel, in_specs=[pl.BlockSpec(memory_space=pltpu.S...  9.87 us
    dot_general x1, matrix products, on_device(): corner = jnp.dot(metric_factor[:, :points], upper, precision=HIGHEST)  3.67 us
  transfers between devices with their start and end apart: 37, of which 11 were waited for; matrix products, arithmetic and copies ran while one was open for 9% of the time, Pallas kernels for 20%

profile of v5, /device:TPU:24, one launch (start us, length us, event | category | flops | bytes accessed | tf_op | source)
XLA Modules:
  0.0 167.7 jit_solution(10966158222915018276)
XLA Ops:
  6.8 5.0 %collective-permute-done.1 = bf16[2,250,128]{2,1,0:T(8,128)(2,1)S(1)} collective-permute-done((bf16[2,250,128]{2,1,0:T(8,128)(2,1)}, bf16[2,250,128]{2,1,0:T(8,128)(2,1)S(1)}, u32[]{:S(2)}, u32[]{:S(2)}) %collective-permute-start.1) | collective-permute-done | bytes 128032 | tf_op jit(solution)/shard_map/ppermute | solution.py:30
  13.8 2.2 %collective-permute-done.4.rest_1_ = bf16[500,256]{1,0:T(8,128)(2,1)S(1)} collective-permute-done((bf16[500,256]{1,0:T(8,128)(2,1)S(1)}, bf16[500,256]{1,0:T(8,128)(2,1)S(1)}, u32[]{:S(2)}, u32[]{:S(2)}) %collective-permute-start.4) | collective-permute-done | bytes 256032 | tf_op jit(solution)/shard_map/ppermute | solution.py:30
  16.0 3.0 %constant_dynamic-slice_fusion.own_ref = f32[512,512]{1,0:T(8,128)} fusion(f32[512,1024]{1,0:T(8,128)} %param.7, s32[]{:T(128)S(6)} %select_n.87), kind=kLoop, calls=%fused_computation.22 | loop fusion | bytes 2097156 | tf_op jit(solution)/shard_map/dynamic_slice | solution.py:384
  20.2 1.6 collective-permute-start.10
  22.6 3.2 %collective-permute-start.5 = (bf16[500,256]{1,0:T(8,128)(2,1)S(1)}, bf16[500,256]{1,0:T(8,128)(2,1)S(1)}, u32[]{:S(2)}, u32[]{:S(2)}) collective-permute-start(bf16[500,256]{1,0:T(8,128)(2,1)S(1)} %slice.16), channel_id=1, source_target_pairs={{0,4},{1,5},{2,6},{3,7},{4,0},{5,1},{6,2},{7,3},{8,12},{9,13},{10,... | collective-permute-start | bytes 768008 | tf_op jit(solution)/shard_map/ppermute | solution.py:30
  25.8 11.8 %collective-permute-done.5.rest_2_ = bf16[500,256]{1,0:T(8,128)(2,1)S(1)} collective-permute-done((bf16[500,256]{1,0:T(8,128)(2,1)S(1)}, bf16[500,256]{1,0:T(8,128)(2,1)S(1)}, u32[]{:S(2)}, u32[]{:S(2)}) %collective-permute-start.5) | collective-permute-done | bytes 256032 | tf_op jit(solution)/shard_map/ppermute | solution.py:30
  39.8 3.4 %collective-permute-start.9 = (bf16[2,250,128]{2,1,0:T(8,128)(2,1)S(1)}, bf16[2,250,128]{2,1,0:T(8,128)(2,1)S(1)}, u32[]{:S(2)}, u32[]{:S(2)}) collective-permute-start(bf16[2,250,128]{2,1,0:T(8,128)(2,1)S(1)} %get-tuple-element.79), channel_id=1, source_target_pairs={{0,6},{1,7},{2,4},{3,5},{4,2},{5,3},{6,0},{7,1},{8,14},{9,15},{10,... | collective-permute-start | bytes 384008 | tf_op jit(solution)/shard_map/ppermute | solution.py:30
  43.9 2.8 %pivot_entries.1.entries_ref = f32[8,8]{1,0:T(8,128)} custom-call(s32[8]{0:T(128)} %get-tuple-element.88.row_ref, bf16[500,8,250]{2,1,0:T(8,128)(2,1)} %bitcast.41, bf16[500,8,250]{2,1,0:T(8,128)(2,1)} %bitcast.44, s32[8]{0:T(128)} %get-tuple-element.89.own_col_ref, s32[8]{0:T(128)} %get-tuple-element.87.sib_col_ref), custom_call_target="tpu_custom_call" | custom-call | tf_op jit(solution)/shard_map/pivot_entries/pallas_call | solution.py:63
  46.8 5.0 %collective-permute-done.8 = bf16[2,250,128]{2,1,0:T(8,128)(2,1)S(1)} collective-permute-done((bf16[2,250,128]{2,1,0:T(8,128)(2,1)S(1)}, bf16[2,250,128]{2,1,0:T(8,128)(2,1)S(1)}, u32[]{:S(2)}, u32[]{:S(2)}) %collective-permute-start.8) | collective-permute-done | bytes 128032 | tf_op jit(solution)/shard_map/ppermute | solution.py:30
  51.9 1.9 %collective-permute-start.12 = (bf16[4,2,250,128]{3,2,1,0:T(8,128)(2,1)S(1)}, bf16[4,2,250,128]{3,2,1,0:T(8,128)(2,1)S(1)}, u32[]{:S(2)}, u32[]{:S(2)}) collective-permute-start(bf16[4,2,250,128]{3,2,1,0:T(8,128)(2,1)S(1)} %pad_maximum_fusion.2.rest_3_.rest_7_.rest_2_.rest_6_), channel_id=1, source_target_pairs={{0,8},{1,9},{2,10},{3,11},{4,12},{5,13},{6,14},{7,15},{8,0},{9,1},... | collective-permute-start | bytes 1536008 | tf_op jit(solution)/shard_map/ppermute | solution.py:30
  53.7 1.7 %collective-permute-start.14 = (bf16[4,2,250,128]{3,2,1,0:T(8,128)(2,1)S(1)}, bf16[4,2,250,128]{3,2,1,0:T(8,128)(2,1)S(1)}, u32[]{:S(2)}, u32[]{:S(2)}) collective-permute-start(bf16[4,2,250,128]{3,2,1,0:T(8,128)(2,1)S(1)} %pad_maximum_fusion.2.rest_3_.rest_7_.rest_2_.rest_6_), channel_id=1, source_target_pairs={{0,24},{1,25},{2,26},{3,27},{4,28},{5,29},{6,30},{7,31},{8,16},{9,... | collective-permute-start | bytes 1536008 | tf_op jit(solution)/shard_map/ppermute | solution.py:30
  55.4 17.3 %collective-permute-start.16 = (bf16[500,512]{1,0:T(8,128)(2,1)S(1)}, bf16[500,512]{1,0:T(8,128)(2,1)S(1)}, u32[]{:S(2)}, u32[]{:S(2)}) collective-permute-start(bf16[500,512]{1,0:T(8,128)(2,1)S(1)} %copy-done), channel_id=1, source_target_pairs={{0,2},{1,3},{2,0},{3,1},{4,6},{5,7},{6,4},{7,5},{8,10},{9,11},{10,... | collective-permute-start | bytes 1536008 | tf_op jit(solution)/shard_map/ppermute | solution.py:30
  72.7 9.9 %invert_blocks.1 = (f32[512,512]{1,0:T(8,128)S(1)}, f32[512,512]{1,0:T(8,128)S(1)}) custom-call(s32[2]{0:T(128)S(1)} %pad_add_fusion.where_ref, f32[512,512]{1,0:T(8,128)} %constant_dynamic-slice_fusion.own_ref, f32[512,512]{1,0:T(8,128)} %collective-permute-done.6.sib_ref), custom_call_target="tpu_custom_call" | custom-call | flops 8589934592 | bytes 4194304 | tf_op jit(solution)/shard_map/invert_blocks/pallas_call | solution.py:234
  82.6 3.7 %fusion.2 = f32[512,512]{1,0:T(8,128)S(1)} fusion(f32[512,512]{1,0:T(8,128)S(1)} %get-tuple-element.63, f32[512,1024]{1,0:T(8,128)S(1)} %copy-done.17), kind=kOutput, calls=%fused_computation.7 | convolution fusion | flops 1610612736 | bytes 3145728 | tf_op jit(solution)/shard_map/dot_general | solution.py:424
  86.3 1.9 %fusion.1 = f32[512,512]{1,0:T(8,128)S(1)} fusion(f32[512,512]{1,0:T(8,128)S(1)} %get-tuple-element.62, f32[512,512]{1,0:T(8,128)S(1)} %fusion.2, pred[]{:T(512)S(6)} %eq.13), kind=kOutput, calls=%fused_computation.6 | convolution fusion | flops 1611137024 | bytes 3145729 | tf_op jit(solution)/shard_map/dot_general | solution.py:425
  88.7 4.6 %collective-permute-start.23 = (bf16[512,1024]{1,0:T(8,128)(2,1)}, bf16[512,1024]{1,0:T(8,128)(2,1)}, u32[]{:S(2)}, u32[]{:S(2)}) collective-permute-start(bf16[512,1024]{1,0:T(8,128)(2,1)} %convert_element_type.10), channel_id=1, source_target_pairs={{6,30},{7,31}} | collective-permute-start | bytes 3145736 | tf_op jit(solution)/shard_map/ppermute | solution.py:30
  93.3 5.9 %project.2 = (f32[8,640]{1,0:T(8,128)S(1)}, f32[8,640]{1,0:T(8,128)S(1)}) custom-call(s32[5]{0:T(128)S(1)} %stack.78.where_ref, bf16[4000,250]{1,0:T(8,128)(2,1)S(1)} %bitcast.42, bf16[4000,250]{1,0:T(8,128)(2,1)S(1)} %bitcast.45, f32[8,8]{1,0:T(8,128)S(1)} %copy-done.15, bf16[500,512]{1,0:T(8,128)(2,1)S(1)} %copy-done, ...), custom_call_target="tpu_custom_call" | custom-call | flops 4096000000 | bytes 1048576 | tf_op jit(solution)/shard_map/project/pallas_call | solution.py:170
  99.4 5.9 %project.3 = (f32[8,640]{1,0:T(8,128)S(1)}, f32[8,640]{1,0:T(8,128)S(1)}) custom-call(s32[5]{0:T(128)S(1)} %stack.78.where_ref, bf16[4000,250]{1,0:T(8,128)(2,1)S(1)} %bitcast.43, bf16[4000,250]{1,0:T(8,128)(2,1)S(1)} %bitcast.46, f32[8,8]{1,0:T(8,128)S(1)} %copy-done.15, bf16[500,512]{1,0:T(8,128)(2,1)S(1)} %collective-permute-done.16.rest_0_, ...), custom_call_target="tpu_custom_call" | custom-call | flops 4096000000 | bytes 1048576 | tf_op jit(solution)/shard_map/project/pallas_call | solution.py:170
  105.3 4.2 %collective-permute-start.18 = (f32[8,640]{1,0:T(8,128)S(1)}, f32[8,640]{1,0:T(8,128)S(1)}, u32[]{:S(2)}, u32[]{:S(2)}) collective-permute-start(f32[8,640]{1,0:T(8,128)S(1)} %get-tuple-element.58), channel_id=1, source_target_pairs={{0,2},{1,3},{2,0},{3,1},{4,6},{5,7},{6,4},{7,5},{8,10},{9,11},{10,... | collective-permute-start | bytes 61448 | tf_op jit(solution)/shard_map/ppermute | solution.py:30
  109.5 2.3 %collective-permute-start.19 = (f32[8,640]{1,0:T(8,128)S(1)}, f32[8,640]{1,0:T(8,128)S(1)}, u32[]{:S(2)}, u32[]{:S(2)}) collective-permute-start(f32[8,640]{1,0:T(8,128)S(1)} %get-tuple-element.59), channel_id=1, source_target_pairs={{0,6},{1,7},{2,4},{3,5},{4,2},{5,3},{6,0},{7,1},{8,14},{9,15},{10,... | collective-permute-start | bytes 61448 | tf_op jit(solution)/shard_map/ppermute | solution.py:30
  112.0 3.0 %collective-permute-done.19 = f32[8,640]{1,0:T(8,128)S(1)} collective-permute-done((f32[8,640]{1,0:T(8,128)S(1)}, f32[8,640]{1,0:T(8,128)S(1)}, u32[]{:S(2)}, u32[]{:S(2)}) %collective-permute-start.19) | collective-permute-done | bytes 20512 | tf_op jit(solution)/shard_map/ppermute | solution.py:30
  115.7 1.7 %collective-permute-start.21 = (f32[8,640]{1,0:T(8,128)S(1)}, f32[8,640]{1,0:T(8,128)S(1)}, u32[]{:S(2)}, u32[]{:S(2)}) collective-permute-start(f32[8,640]{1,0:T(8,128)S(1)} %add_add_fusion.1), channel_id=1, source_target_pairs={{0,16},{1,17},{2,18},{3,19},{4,20},{5,21},{6,22},{7,23},{8,24},{9,... | collective-permute-start | bytes 61448 | tf_op jit(solution)/shard_map/ppermute | solution.py:30
  118.9 1.8 %collective-permute-start.22 = (f32[8,640]{1,0:T(8,128)S(1)}, f32[8,640]{1,0:T(8,128)S(1)}, u32[]{:S(2)}, u32[]{:S(2)}) collective-permute-start(f32[8,640]{1,0:T(8,128)S(1)} %add_add_fusion.1), channel_id=1, source_target_pairs={{0,24},{1,25},{2,26},{3,27},{4,28},{5,29},{6,30},{7,31},{8,16},{9,... | collective-permute-start | bytes 61448 | tf_op jit(solution)/shard_map/ppermute | solution.py:30
  120.7 2.9 %collective-permute-done.22 = f32[8,640]{1,0:T(8,128)S(1)} collective-permute-done((f32[8,640]{1,0:T(8,128)S(1)}, f32[8,640]{1,0:T(8,128)S(1)}, u32[]{:S(2)}, u32[]{:S(2)}) %collective-permute-start.22) | collective-permute-done | bytes 20512 | tf_op jit(solution)/shard_map/ppermute | solution.py:30
  124.2 1.8 %collective-permute-done.24.xb_ref.refs_7_.refs_9_.refs_11_ = f32[8,512]{1,0:T(8,128)S(1)} collective-permute-done((f32[8,512]{1,0:T(8,128)S(1)}, f32[8,512]{1,0:T(8,128)S(1)}, u32[]{:S(2)}, u32[]{:S(2)}) %collective-permute-start.24) | collective-permute-done | bytes 16416 | tf_op jit(solution)/shard_map/ppermute | solution.py:30
  128.0 2.9 %turn.3.refs_1_ = f32[16,512]{1,0:T(8,128)S(1)} custom-call(s32[1]{0:T(128)} %bitcast.1.where_ref, bf16[512,1024]{1,0:T(8,128)(2,1)} %collective-permute-done.10.refs_0_, bf16[512,1024]{1,0:T(8,128)(2,1)S(1)} %collective-permute-done.25.refs_1_, bf16[512,1024]{1,0:T(8,128)(2,1)S(1)} %get-tuple-element.68.hi_ref.refs_2_.refs_4_.refs_6_, ...), custom_call_target="tpu_custom_call" | custom-call | flops 2147483648 | bytes 4194304 | tf_op jit(solution)/shard_map/turn/pallas_call | solution.py:309
  132.5 3.0 %turn.4.refs_2_ = f32[24,512]{1,0:T(8,128)S(1)} custom-call(s32[1]{0:T(128)} %bitcast.1.where_ref, bf16[512,1024]{1,0:T(8,128)(2,1)} %collective-permute-done.10.refs_0_, bf16[512,1024]{1,0:T(8,128)(2,1)S(1)} %collective-permute-done.25.refs_1_, bf16[512,1024]{1,0:T(8,128)(2,1)S(1)} %copy-done.5, bf16[512,1024]{1,0:T(8,128)(2,1)S(1)} %collective-permute-done.28.refs_3_, ...), custom_call_target="tpu_custom_call" | custom-call | flops 2147483648 | bytes 4194304 | tf_op jit(solution)/shard_map/turn/pallas_call | solution.py:309
  137.5 1.9 %factor_inverse.1 = f32[8,8]{1,0:T(8,128)} custom-call(f32[8,8]{1,0:T(8,128)} %slice.18.block_ref), custom_call_target="tpu_custom_call" | custom-call | tf_op jit(solution)/shard_map/factor_inverse/pallas_call | solution.py:98
  139.4 1.8 %gather_fusion = f32[4,2,8]{2,1,0:T(2,128)} fusion(f32[4,2,8]{2,1,0:T(2,128)} %bitcast.54, s32[1024]{0:T(1024)S(1)} %pad_clamp_fusion), kind=kCustom, calls=%fused_computation | custom fusion | bytes 528 | tf_op jit(solution)/shard_map/gather | solution.py:481
  143.7 4.5 %turn.5.refs_3_ = f32[32,512]{1,0:T(8,128)S(1)} custom-call(s32[1]{0:T(128)} %bitcast.1.where_ref, bf16[512,1024]{1,0:T(8,128)(2,1)} %collective-permute-done.10.refs_0_, bf16[512,1024]{1,0:T(8,128)(2,1)S(1)} %copy-done.8, bf16[512,1024]{1,0:T(8,128)(2,1)S(1)} %copy-done.6, bf16[512,1024]{1,0:T(8,128)(2,1)S(1)} %copy-done.10, ...), custom_call_target="tpu_custom_call" | custom-call | flops 2147483648 | bytes 4194304 | tf_op jit(solution)/shard_map/turn/pallas_call | solution.py:309
  148.9 1.6 combine.1
  153.1 13.3 %collective-permute-done.36 = f32[2,512]{1,0:T(2,128)S(1)} collective-permute-done((f32[2,512]{1,0:T(2,128)}, f32[2,512]{1,0:T(2,128)S(1)}, u32[]{:S(2)}, u32[]{:S(2)}) %collective-permute-start.36) | collective-permute-done | bytes 4128 | tf_op jit(solution)/shard_map/ppermute | solution.py:30
  (114 shorter events, 29.7 us)
Async XLA Ops:
  0.0 16.0 %collective-permute-start.3 = (bf16[8,500,250]{2,0,1:T(8,128)(2,1)}, bf16[8,500,250]{2,0,1:T(8,128)(2,1)S(1)}, u32[]{:S(2)}, u32[]{:S(2)}) collective-permute-start(bf16[8,500,250]{2,0,1:T(8,128)(2,1)} %param.4), channel_id=1, source_target_pairs={{0,1},{1,0},{2,3},{3,2},{4,5},{5,4},{6,7},{7,6},{8,9},{9,8},{10,11... | collective-permute-start | bytes 6000008 | tf_op jit(solution)/shard_map/ppermute | solution.py:30
  1.0 15.0 %collective-permute-start.4 = (bf16[500,256]{1,0:T(8,128)(2,1)S(1)}, bf16[500,256]{1,0:T(8,128)(2,1)S(1)}, u32[]{:S(2)}, u32[]{:S(2)}) collective-permute-start(bf16[500,256]{1,0:T(8,128)(2,1)S(1)} %slice.15), channel_id=1, source_target_pairs={{0,4},{1,5},{2,6},{3,7},{4,0},{5,1},{6,2},{7,3},{8,12},{9,13},{10,... | collective-permute-start | bytes 768008 | tf_op jit(solution)/shard_map/ppermute | solution.py:30
  3.3 8.5 %collective-permute-start.1 = (bf16[2,250,128]{2,1,0:T(8,128)(2,1)}, bf16[2,250,128]{2,1,0:T(8,128)(2,1)S(1)}, u32[]{:S(2)}, u32[]{:S(2)}) collective-permute-start(bf16[2,250,128]{2,1,0:T(8,128)(2,1)} %get-tuple-element.85), channel_id=1, source_target_pairs={{0,16},{1,17},{2,18},{3,19},{4,20},{5,21},{6,22},{7,23},{8,24},{9,... | collective-permute-start | bytes 384008 | tf_op jit(solution)/shard_map/ppermute | solution.py:30
  4.8 7.3 %collective-permute-start.2 = (bf16[2,250,128]{2,1,0:T(8,128)(2,1)S(1)}, bf16[2,250,128]{2,1,0:T(8,128)(2,1)S(1)}, u32[]{:S(2)}, u32[]{:S(2)}) collective-permute-start(bf16[2,250,128]{2,1,0:T(8,128)(2,1)S(1)} %get-tuple-element.84), channel_id=1, source_target_pairs={{0,24},{1,25},{2,26},{3,27},{4,28},{5,29},{6,30},{7,31},{8,16},{9,... | collective-permute-start | bytes 384008 | tf_op jit(solution)/shard_map/ppermute | solution.py:30
  6.2 6.7 %collective-permute-start = (bf16[2,250,128]{2,1,0:T(8,128)(2,1)S(1)}, bf16[2,250,128]{2,1,0:T(8,128)(2,1)S(1)}, u32[]{:S(2)}, u32[]{:S(2)}) collective-permute-start(bf16[2,250,128]{2,1,0:T(8,128)(2,1)S(1)} %get-tuple-element.86), channel_id=1, source_target_pairs={{0,8},{1,9},{2,10},{3,11},{4,12},{5,13},{6,14},{7,15},{8,0},{9,1},... | collective-permute-start | bytes 384008 | tf_op jit(solution)/shard_map/ppermute | solution.py:30
  19.0 18.6 %collective-permute-start.6 = (f32[512,512]{1,0:T(8,128)}, f32[512,512]{1,0:T(8,128)}, u32[]{:S(2)}, u32[]{:S(2)}) collective-permute-start(f32[512,512]{1,0:T(8,128)} %constant_dynamic-slice_fusion.own_ref), channel_id=1, source_target_pairs={{0,1},{1,0},{2,3},{3,2},{4,5},{5,4},{6,7},{7,6},{8,9},{9,8},{10,11... | collective-permute-start | bytes 3145736 | tf_op jit(solution)/shard_map/ppermute | solution.py:30
  20.2 26.5 %collective-permute-start.10 = (bf16[512,1024]{1,0:T(8,128)(2,1)}, bf16[512,1024]{1,0:T(8,128)(2,1)}, u32[]{:S(2)}, u32[]{:S(2)}) collective-permute-start(bf16[512,1024]{1,0:T(8,128)(2,1)} %convert_element_type.10), channel_id=1, source_target_pairs={{2,10},{3,11},{12,20},{13,21},{22,30},{23,31}} | collective-permute-start | bytes 3145736 | tf_op jit(solution)/shard_map/ppermute | solution.py:30
  21.9 24.9 %collective-permute-start.11 = (bf16[512,1024]{1,0:T(8,128)(2,1)}, bf16[512,1024]{1,0:T(8,128)(2,1)S(1)}, u32[]{:S(2)}, u32[]{:S(2)}) collective-permute-start(bf16[512,1024]{1,0:T(8,128)(2,1)} %convert_element_type.10), channel_id=1, source_target_pairs={{4,20},{5,21},{14,30},{15,31}} | collective-permute-start | bytes 3145736 | tf_op jit(solution)/shard_map/ppermute | solution.py:30
  22.6 14.9 %collective-permute-start.5 = (bf16[500,256]{1,0:T(8,128)(2,1)S(1)}, bf16[500,256]{1,0:T(8,128)(2,1)S(1)}, u32[]{:S(2)}, u32[]{:S(2)}) collective-permute-start(bf16[500,256]{1,0:T(8,128)(2,1)S(1)} %slice.16), channel_id=1, source_target_pairs={{0,4},{1,5},{2,6},{3,7},{4,0},{5,1},{6,2},{7,3},{8,12},{9,13},{10,... | collective-permute-start | bytes 768008 | tf_op jit(solution)/shard_map/ppermute | solution.py:30
  38.7 8.0 %collective-permute-start.7 = (bf16[2,250,128]{2,1,0:T(8,128)(2,1)S(1)}, bf16[2,250,128]{2,1,0:T(8,128)(2,1)S(1)}, u32[]{:S(2)}, u32[]{:S(2)}) collective-permute-start(bf16[2,250,128]{2,1,0:T(8,128)(2,1)S(1)} %get-tuple-element.81), channel_id=1, source_target_pairs={{0,2},{1,3},{2,0},{3,1},{4,6},{5,7},{6,4},{7,5},{8,10},{9,11},{10,... | collective-permute-start | bytes 384008 | tf_op jit(solution)/shard_map/ppermute | solution.py:30
  38.8 13.0 %collective-permute-start.8 = (bf16[2,250,128]{2,1,0:T(8,128)(2,1)S(1)}, bf16[2,250,128]{2,1,0:T(8,128)(2,1)S(1)}, u32[]{:S(2)}, u32[]{:S(2)}) collective-permute-start(bf16[2,250,128]{2,1,0:T(8,128)(2,1)S(1)} %get-tuple-element.80), channel_id=1, source_target_pairs={{0,4},{1,5},{2,6},{3,7},{4,0},{5,1},{6,2},{7,3},{8,12},{9,13},{10,... | collective-permute-start | bytes 384008 | tf_op jit(solution)/shard_map/ppermute | solution.py:30
  39.8 12.0 %collective-permute-start.9 = (bf16[2,250,128]{2,1,0:T(8,128)(2,1)S(1)}, bf16[2,250,128]{2,1,0:T(8,128)(2,1)S(1)}, u32[]{:S(2)}, u32[]{:S(2)}) collective-permute-start(bf16[2,250,128]{2,1,0:T(8,128)(2,1)S(1)} %get-tuple-element.79), channel_id=1, source_target_pairs={{0,6},{1,7},{2,4},{3,5},{4,2},{5,3},{6,0},{7,1},{8,14},{9,15},{10,... | collective-permute-start | bytes 384008 | tf_op jit(solution)/shard_map/ppermute | solution.py:30
  51.9 36.9 %collective-permute-start.12 = (bf16[4,2,250,128]{3,2,1,0:T(8,128)(2,1)S(1)}, bf16[4,2,250,128]{3,2,1,0:T(8,128)(2,1)S(1)}, u32[]{:S(2)}, u32[]{:S(2)}) collective-permute-start(bf16[4,2,250,128]{3,2,1,0:T(8,128)(2,1)S(1)} %pad_maximum_fusion.2.rest_3_.rest_7_.rest_2_.rest_6_), channel_id=1, source_target_pairs={{0,8},{1,9},{2,10},{3,11},{4,12},{5,13},{6,14},{7,15},{8,0},{9,1},... | collective-permute-start | bytes 1536008 | tf_op jit(solution)/shard_map/ppermute | solution.py:30
  53.7 35.0 %collective-permute-start.13 = (bf16[4,2,250,128]{3,2,1,0:T(8,128)(2,1)S(1)}, bf16[4,2,250,128]{3,2,1,0:T(8,128)(2,1)S(1)}, u32[]{:S(2)}, u32[]{:S(2)}) collective-permute-start(bf16[4,2,250,128]{3,2,1,0:T(8,128)(2,1)S(1)} %pad_maximum_fusion.2.rest_3_.rest_7_.rest_2_.rest_6_), channel_id=1, source_target_pairs={{0,16},{1,17},{2,18},{3,19},{4,20},{5,21},{6,22},{7,23},{8,24},{9,... | collective-permute-start | bytes 1536008 | tf_op jit(solution)/shard_map/ppermute | solution.py:30
  53.7 35.0 %collective-permute-start.14 = (bf16[4,2,250,128]{3,2,1,0:T(8,128)(2,1)S(1)}, bf16[4,2,250,128]{3,2,1,0:T(8,128)(2,1)S(1)}, u32[]{:S(2)}, u32[]{:S(2)}) collective-permute-start(bf16[4,2,250,128]{3,2,1,0:T(8,128)(2,1)S(1)} %pad_maximum_fusion.2.rest_3_.rest_7_.rest_2_.rest_6_), channel_id=1, source_target_pairs={{0,24},{1,25},{2,26},{3,27},{4,28},{5,29},{6,30},{7,31},{8,16},{9,... | collective-permute-start | bytes 1536008 | tf_op jit(solution)/shard_map/ppermute | solution.py:30
  55.4 44.0 %collective-permute-start.16 = (bf16[500,512]{1,0:T(8,128)(2,1)S(1)}, bf16[500,512]{1,0:T(8,128)(2,1)S(1)}, u32[]{:S(2)}, u32[]{:S(2)}) collective-permute-start(bf16[500,512]{1,0:T(8,128)(2,1)S(1)} %copy-done), channel_id=1, source_target_pairs={{0,2},{1,3},{2,0},{3,1},{4,6},{5,7},{6,4},{7,5},{8,10},{9,11},{10,... | collective-permute-start | bytes 1536008 | tf_op jit(solution)/shard_map/ppermute | solution.py:30
  72.7 26.7 %collective-permute-start.17 = (bf16[500,512]{1,0:T(8,128)(2,1)S(1)}, bf16[500,512]{1,0:T(8,128)(2,1)S(1)}, u32[]{:S(2)}, u32[]{:S(2)}) collective-permute-start(bf16[500,512]{1,0:T(8,128)(2,1)S(1)} %copy-done), channel_id=1, source_target_pairs={{0,6},{1,7},{2,4},{3,5},{4,2},{5,3},{6,0},{7,1},{8,14},{9,15},{10,... | collective-permute-start | bytes 1536008 | tf_op jit(solution)/shard_map/ppermute | solution.py:30
  88.7 34.9 %collective-permute-start.23 = (bf16[512,1024]{1,0:T(8,128)(2,1)}, bf16[512,1024]{1,0:T(8,128)(2,1)}, u32[]{:S(2)}, u32[]{:S(2)}) collective-permute-start(bf16[512,1024]{1,0:T(8,128)(2,1)} %convert_element_type.10), channel_id=1, source_target_pairs={{6,30},{7,31}} | collective-permute-start | bytes 3145736 | tf_op jit(solution)/shard_map/ppermute | solution.py:30
  99.2 12.6 %collective-permute-start.15 = (f32[8,640]{1,0:T(8,128)S(1)}, f32[8,640]{1,0:T(8,128)S(1)}, u32[]{:S(2)}, u32[]{:S(2)}) collective-permute-start(f32[8,640]{1,0:T(8,128)S(1)} %get-tuple-element.56), channel_id=1, source_target_pairs={{0,4},{1,5},{2,6},{3,7},{4,0},{5,1},{6,2},{7,3},{8,12},{9,13},{10,... | collective-permute-start | bytes 61448 | tf_op jit(solution)/shard_map/ppermute | solution.py:30
  99.3 28.7 %collective-permute-start.25 = (bf16[512,1024]{1,0:T(8,128)(2,1)}, bf16[512,1024]{1,0:T(8,128)(2,1)S(1)}, u32[]{:S(2)}, u32[]{:S(2)}) collective-permute-start(bf16[512,1024]{1,0:T(8,128)(2,1)} %collective-permute-done.10.refs_0_), channel_id=1, source_target_pairs={{0,1},{1,0},{2,3},{3,2},{4,5},{5,4},{6,7},{7,6},{8,9},{9,8},{10,11... | collective-permute-start | bytes 3145736 | tf_op jit(solution)/shard_map/ppermute | solution.py:30
  105.3 6.7 %collective-permute-start.18 = (f32[8,640]{1,0:T(8,128)S(1)}, f32[8,640]{1,0:T(8,128)S(1)}, u32[]{:S(2)}, u32[]{:S(2)}) collective-permute-start(f32[8,640]{1,0:T(8,128)S(1)} %get-tuple-element.58), channel_id=1, source_target_pairs={{0,2},{1,3},{2,0},{3,1},{4,6},{5,7},{6,4},{7,5},{8,10},{9,11},{10,... | collective-permute-start | bytes 61448 | tf_op jit(solution)/shard_map/ppermute | solution.py:30
  109.5 5.6 %collective-permute-start.19 = (f32[8,640]{1,0:T(8,128)S(1)}, f32[8,640]{1,0:T(8,128)S(1)}, u32[]{:S(2)}, u32[]{:S(2)}) collective-permute-start(f32[8,640]{1,0:T(8,128)S(1)} %get-tuple-element.59), channel_id=1, source_target_pairs={{0,6},{1,7},{2,4},{3,5},{4,2},{5,3},{6,0},{7,1},{8,14},{9,15},{10,... | collective-permute-start | bytes 61448 | tf_op jit(solution)/shard_map/ppermute | solution.py:30
  111.8 20.6 %collective-permute-start.28 = (bf16[512,1024]{1,0:T(8,128)(2,1)S(1)}, bf16[512,1024]{1,0:T(8,128)(2,1)S(1)}, u32[]{:S(2)}, u32[]{:S(2)}) collective-permute-start(bf16[512,1024]{1,0:T(8,128)(2,1)S(1)} %copy-done.5), channel_id=1, source_target_pairs={{0,1},{1,0},{2,3},{3,2},{4,5},{5,4},{6,7},{7,6},{8,9},{9,8},{10,11... | collective-permute-start | bytes 3145736 | tf_op jit(solution)/shard_map/ppermute | solution.py:30
  115.1 3.8 %collective-permute-start.20 = (f32[8,640]{1,0:T(8,128)S(1)}, f32[8,640]{1,0:T(8,128)S(1)}, u32[]{:S(2)}, u32[]{:S(2)}) collective-permute-start(f32[8,640]{1,0:T(8,128)S(1)} %add_add_fusion.1), channel_id=1, source_target_pairs={{0,8},{1,9},{2,10},{3,11},{4,12},{5,13},{6,14},{7,15},{8,0},{9,1},... | collective-permute-start | bytes 61448 | tf_op jit(solution)/shard_map/ppermute | solution.py:30
  115.7 5.0 %collective-permute-start.21 = (f32[8,640]{1,0:T(8,128)S(1)}, f32[8,640]{1,0:T(8,128)S(1)}, u32[]{:S(2)}, u32[]{:S(2)}) collective-permute-start(f32[8,640]{1,0:T(8,128)S(1)} %add_add_fusion.1), channel_id=1, source_target_pairs={{0,16},{1,17},{2,18},{3,19},{4,20},{5,21},{6,22},{7,23},{8,24},{9,... | collective-permute-start | bytes 61448 | tf_op jit(solution)/shard_map/ppermute | solution.py:30
  118.9 4.7 %collective-permute-start.22 = (f32[8,640]{1,0:T(8,128)S(1)}, f32[8,640]{1,0:T(8,128)S(1)}, u32[]{:S(2)}, u32[]{:S(2)}) collective-permute-start(f32[8,640]{1,0:T(8,128)S(1)} %add_add_fusion.1), channel_id=1, source_target_pairs={{0,24},{1,25},{2,26},{3,27},{4,28},{5,29},{6,30},{7,31},{8,16},{9,... | collective-permute-start | bytes 61448 | tf_op jit(solution)/shard_map/ppermute | solution.py:30
  123.6 17.6 %collective-permute-start.31 = (bf16[512,1024]{1,0:T(8,128)(2,1)}, bf16[512,1024]{1,0:T(8,128)(2,1)}, u32[]{:S(2)}, u32[]{:S(2)}) collective-permute-start(bf16[512,1024]{1,0:T(8,128)(2,1)} %collective-permute-done.23.refs_4_), channel_id=1, source_target_pairs={{0,1},{1,0},{2,3},{3,2},{4,5},{5,4},{6,7},{7,6},{8,9},{9,8},{10,11... | collective-permute-start | bytes 3145736 | tf_op jit(solution)/shard_map/ppermute | solution.py:30
  123.7 2.3 %collective-permute-start.24 = (f32[8,512]{1,0:T(8,128)S(1)}, f32[8,512]{1,0:T(8,128)S(1)}, u32[]{:S(2)}, u32[]{:S(2)}) collective-permute-start(f32[8,512]{1,0:T(8,128)S(1)} %slice.19.xa_ref.refs_6_.refs_8_.refs_10_), channel_id=1, source_target_pairs={{0,1},{1,0},{2,3},{3,2},{4,5},{5,4},{6,7},{7,6},{8,9},{9,8},{10,11... | collective-permute-start | bytes 49160 | tf_op jit(solution)/shard_map/ppermute | solution.py:30
  135.5 5.7 %collective-permute-start.32 = (f32[24,512]{1,0:T(8,128)S(1)}, f32[24,512]{1,0:T(8,128)S(1)}, u32[]{:S(2)}, u32[]{:S(2)}) collective-permute-start(f32[24,512]{1,0:T(8,128)S(1)} %turn.4.refs_2_), channel_id=1, source_target_pairs={{20,30},{21,31}} | collective-permute-start | bytes 147464 | tf_op jit(solution)/shard_map/ppermute | solution.py:30
  136.2 5.1 %collective-permute-start.33 = (f32[24,512]{1,0:T(8,128)S(1)}, f32[24,512]{1,0:T(8,128)S(1)}, u32[]{:S(2)}, u32[]{:S(2)}) collective-permute-start(f32[24,512]{1,0:T(8,128)S(1)} %turn.4.refs_2_), channel_id=1, source_target_pairs={{20,31},{21,30}} | collective-permute-start | bytes 147464 | tf_op jit(solution)/shard_map/ppermute | solution.py:30
  150.5 2.6 %collective-permute-start.34 = (f32[2,512]{1,0:T(2,128)}, f32[2,512]{1,0:T(2,128)S(1)}, u32[]{:S(2)}, u32[]{:S(2)}) collective-permute-start(f32[2,512]{1,0:T(2,128)} %get-tuple-element.74), channel_id=1, source_target_pairs={{0,8},{1,9},{10,2},{11,3},{20,28},{21,29},{30,22},{31,23}} | collective-permute-start | bytes 12296 | tf_op jit(solution)/shard_map/ppermute | solution.py:30
  151.8 14.7 %collective-permute-start.36 = (f32[2,512]{1,0:T(2,128)}, f32[2,512]{1,0:T(2,128)S(1)}, u32[]{:S(2)}, u32[]{:S(2)}) collective-permute-start(f32[2,512]{1,0:T(2,128)} %get-tuple-element.76), channel_id=1, source_target_pairs={{0,24},{1,25},{10,18},{11,19},{20,12},{21,13},{30,6},{31,7}} | collective-permute-start | bytes 12296 | tf_op jit(solution)/shard_map/ppermute | solution.py:30
  (24 other events, 185.8 us)

commit v6 on v5

--- a/solution.py
+++ b/solution.py
@@ -80,8 +80,8 @@
 
 
 def factor_inverse_kernel(block_ref, out_ref):
-    a = block_ref[...]
-    n = a.shape[0]
+    n = block_ref.shape[0]
+    a = block_ref[:, block_ref.shape[1] - 128 :][:, :n]
     row = lax.broadcasted_iota(jnp.int32, (n, n), 0)
     col = lax.broadcasted_iota(jnp.int32, (n, n), 1)
     w = (row == col).astype(F32)
@@ -97,7 +97,7 @@
 def factor_inverse(block):
     return pl.pallas_call(
         factor_inverse_kernel,
-        out_shape=jax.ShapeDtypeStruct(block.shape, F32),
+        out_shape=jax.ShapeDtypeStruct((block.shape[0], block.shape[0]), F32),
         name="factor_inverse",
     )(block)
 
@@ -263,7 +263,9 @@
 
 def apply_kernel(where_ref, hi_ref, lo_ref, xa_ref, xb_ref, out_ref):
     core = where_ref[0]
-    out_ref[...] = weigh(hi_ref, lo_ref, [(core, xa_ref[...]), (1 - core, xb_ref[...])])
+    points = out_ref.shape[1]
+    halves = [(core, xa_ref[:, :points]), (1 - core, xb_ref[:, :points])]
+    out_ref[...] = weigh(hi_ref, lo_ref, halves)
 
 
 def apply_weights(where, weights, xa, xb):
@@ -271,7 +273,7 @@
         apply_kernel,
         in_specs=[pl.BlockSpec(memory_space=pltpu.SMEM)] + [pl.BlockSpec(memory_space=pltpu.VMEM)] * 4,
         out_specs=pl.BlockSpec(memory_space=pltpu.VMEM),
-        out_shape=jax.ShapeDtypeStruct(xa.shape, F32),
+        out_shape=jax.ShapeDtypeStruct((xa.shape[0], weights[0].shape[0]), F32),
         compiler_params=pltpu.CompilerParams(vmem_limit_bytes=12 << 20),
         cost_estimate=pl.CostEstimate(flops=1 << 30, transcendentals=0, bytes_accessed=1 << 21),
         name="apply_weights",
@@ -288,7 +290,8 @@
     ]
     for copy in copies:
         copy.start()
-    own, sib = own_rest[...], sib_rest[...]
+    points = xa.shape[1]
+    own, sib = own_rest[:, :points], sib_rest[:, :points]
     for i in range(count):
         d = count - i
         halves = [(core, xa[i * n : (i + 1) * n]), (1 - core, xb[i * n : (i + 1) * n])]
@@ -300,12 +303,9 @@
     out_ref[count * n :] = weigh(inv_hi, inv_lo, [(core, own), (1 - core, sib)])
 
 
-def turn(where, left_own, left_sib, inverse, xa, xb, own_rest, sib_rest):
-    n, points = own_rest.shape
+def turn(where, lefts, inverse, xa, xb, own_rest, sib_rest):
+    n, points = own_rest.shape[0], xa.shape[1]
     count = xa.shape[0] // n
-    lefts = []
-    for d in range(1, count + 1):
-        lefts += [left_own[d], left_sib[d]]
     return pl.pallas_call(
         functools.partial(turn_kernel, count),
         in_specs=[pl.BlockSpec(memory_space=pltpu.SMEM)]
@@ -329,13 +329,13 @@
     n = x.shape[0]
     for t, ref in enumerate(x_refs):
         x = jnp.where(turn_ref[0] == t, ref[t * n :], x)
-    inverse = inverse_ref[...]
-    total = inverse[:, :1] * x[:1]
-    for i in range(1, x.shape[0]):
-        total += inverse[:, i : i + 1] * x[i : i + 1]
     rows = out_refs[0].shape[0]
-    for n, ref in enumerate(out_refs):
-        ref[...] = total[n * rows : (n + 1) * rows]
+    for k, ref in enumerate(out_refs):
+        inverse = inverse_ref[pl.ds(turn_ref[1 + k] * rows, rows), :]
+        total = inverse[:, :1] * x[:1]
+        for i in range(1, x.shape[0]):
+            total += inverse[:, i : i + 1] * x[i : i + 1]
+        ref[...] = total
 
 
 def combine(which, inverse, turns, rows):
@@ -366,7 +366,6 @@
 
     part = points // gen_count
     across = lambda k: lambda g, j, c: (g, j ^ k, c)
-    leftwards = lambda d: lambda g, j, c: (g + d, j, c) if j == g + d else None
     halves = collocation.reshape(2, orb_block // 2, points)
     spread = []
     for k in range(gen_count):
@@ -377,16 +376,31 @@
     half = points // 2
     early_parts = [move(collocation[:, :half], across(early))]
     sibling = move(raw_columns, swap)
-    spread, sibling, early_parts, metric_late, first = lax.optimization_barrier(
-        (spread, sibling, early_parts, metric_factor, collocation)
-    )
-    early_parts.append(move(first[:, half:], across(early)))
+    sibling, metric_late = lax.optimization_barrier((sibling, metric_factor))
     own_block = lax.dynamic_slice_in_dim(metric_late, core * points, points, 1)
+    own_rows = metric_late.astype(BF16)
+    second_half = collocation[:, half:]
+    spread, sibling, early_parts, own_block, own_rows, second_half, first = lax.optimization_barrier(
+        (spread, sibling, early_parts, own_block, own_rows, second_half, collocation)
+    )
+    early_parts.append(move(second_half, across(early)))
     sib_block = move(own_block, swap)
-    own_rows = metric_late.astype(BF16)
-    left_own = {d: move(own_rows, leftwards(d)) for d in (1, 2)}
-    spread, early_parts, first, sib_block = lax.optimization_barrier(
-        (spread, early_parts, first, sib_block)
+
+    if gen_count == 4:
+        bunches = [[(1, 1), (2, 1), (3, 1)], [(3, 2)], [(2, 2), (3, 3)]]
+        soon = 2
+    else:
+        bunches = [[(j, d) for j in range(d, gen_count)] for d in others]
+        soon = 1
+    bunch_of = {place: n for n, bunch in enumerate(bunches) for place in bunch}
+
+    def leftwards(n):
+        away = dict(bunches[n])
+        return lambda g, j, c: (j, j, c) if j in away and g == j - away[j] else None
+
+    left_own = [move(own_rows, leftwards(n)) for n in range(soon)]
+    spread, early_parts, first, sib_block, left_own[0] = lax.optimization_barrier(
+        (spread, early_parts, first, sib_block, left_own[0])
     )
     own_parts = []
     for k in range(gen_count):
@@ -433,12 +447,12 @@
         )
     )
 
-    _, inverse_rows, left_hi, left_own = lax.optimization_barrier(
-        (all_parts, inverse_rows, own_rows, left_own)
-    )
-    for d in range(3, gen_count):
-        left_own[d] = move(left_hi, leftwards(d))
-    left_sib = {d: move(left_own[d], swap) for d in (1, 2)}
+    _, _, inverse_rows, left_rows, left_own = lax.optimization_barrier(
+        (all_parts, first_side, inverse_rows, own_rows, left_own)
+    )
+    for n in range(soon, len(bunches)):
+        left_own.append(move(left_rows, leftwards(n)))
+    left_sib = [move(left_own[n], swap) for n in range(soon)]
 
     own_raw = own_raw.reshape(orb_block * vec_total, pair_block)
     sib_raw = sib_raw.reshape(orb_block * vec_total, pair_block)
@@ -455,31 +469,35 @@
             [second_side(k) for k in group],
             [k if part % 128 == 0 else 0 for k in group],
         )
+        if 0 in group:
+            entries, left_sib = lax.optimization_barrier((entries, left_sib))
         for k, share in zip(group, shares):
             if k:
                 share = move(share, across(k))
             total = share if total is None else total + share
     total = sum([move(total, lambda g, j, c, k=k: (g ^ k, j, c)) for k in others], total)
-    for d in range(3, gen_count):
-        total, left_own[d] = lax.optimization_barrier((total, left_own[d]))
-        left_sib[d] = move(left_own[d], swap)
-    rest = total[:, :points]
-    pivot_block = total[:, points : points + vec_total]
-
     at_core = core[None]
-    sib_rest = move(rest, swap)
-    solved = apply_weights(at_core, inverse_rows, rest, sib_rest)
+    sib_total = move(total, swap)
+    solved = apply_weights(at_core, inverse_rows, total, sib_total)
+    inverse_factor = factor_inverse(total)
     turns = [solved]
     for t in range(1, gen_count):
         near = move(solved, lambda g, j, c: (t, t, c) if g == j == t - 1 else None)
         near_sib = move(solved, lambda g, j, c: (t, t, 1 - c) if g == j == t - 1 else None)
-        solved = turn(at_core, left_own, left_sib, inverse_rows, near, near_sib, rest, sib_rest)
+        if t == 1:
+            near, inverse_factor = lax.optimization_barrier((near, inverse_factor))
+        lefts = []
+        for d in range(1, t + 1):
+            lefts += [left_own[bunch_of[t, d]], left_sib[bunch_of[t, d]]]
+        solved = turn(at_core, lefts, inverse_rows, near, near_sib, total, sib_total)
         turns.append(solved)
-
-    inverse_factor = factor_inverse(pivot_block).reshape(gen_count, vec_dev, vec_total)
-    order = jnp.stack([gen_index ^ k for k in range(gen_count)])
-    inverse_factor = inverse_factor[order].reshape(vec_total, vec_total)
-    shares = combine(jnp.where(diagonal, gen_index, -1)[None], inverse_factor, turns, vec_dev)
+        if t == 1:
+            for n in range(soon, len(bunches)):
+                _, left_own[n] = lax.optimization_barrier((solved, left_own[n]))
+                left_sib.append(move(left_own[n], swap))
+
+    which = jnp.stack([jnp.where(diagonal, gen_index, -1)] + [gen_index ^ k for k in range(gen_count)])
+    shares = combine(which, inverse_factor, turns, vec_dev)
     result = shares[0]
     for k in others:
         result += move(shares[k], lambda g, j, c, k=k: (g ^ k, j, c) if g == j else None)

time: 170 us -> 181 us (1.065)
  waiting for transfers between devices: 47.7 us -> 60.8 us
  starting transfers between devices: 57.4 us -> 46 us
  local copies, waits for them, and re-layouts: 12.7 us -> 20.7 us
  other arithmetic: 4.65 us -> 8.13 us
    ppermute x37, waiting for transfers between devices: 47.7 us -> 60.8 us  [move(): return lax.ppermute(value, BOTH, pairs)]
    unnamed x38 -> x68, local copies, waits for them, and re-layouts: 3.12 us -> 15.6 us
    ppermute x37, starting transfers between devices: 57.4 us -> 46 us  [move(): return lax.ppermute(value, BOTH, pairs)]
    convert_element_type x1, other arithmetic: 1.16 us -> 3.51 us  [on_device(): own_rows = metric_late.astype(BF16)]
    dynamic_slice x1, local copies, waits for them, and re-layouts: 3.01 us -> 1.09 us  [on_device(): own_block = lax.dynamic_slice_in_dim(metric_late, core * points, points, 1)]
    gather x1 -> x0, local copies, waits for them, and re-layouts: 1.84 us -> none  [on_device(): inverse_factor = inverse_factor[order].reshape(vec_total, vec_total)]
  transfers between devices with their start and end apart: 37 -> 37, of which waited for: 11 -> 15; matrix products, arithmetic and copies ran while one was open for 9% -> 10% of each run, Pallas kernels for 20% -> 16%
where the time goes in v6:
time: 181 us; the launch traced here: 180 us
  waiting for transfers between devices  60.8 us (34%)
  starting transfers between devices  46 us (25%)
  Pallas kernels  37.9 us (21%)
  local copies, waits for them, and re-layouts  20.7 us (11%)
  other arithmetic  8.13 us (4%)
  matrix products  5.65 us (3%)
    ppermute x37, waiting for transfers between devices, move(): return lax.ppermute(value, BOTH, pairs)  60.8 us
    ppermute x37, starting transfers between devices, move(): return lax.ppermute(value, BOTH, pairs)  46 us
    unnamed x68, local copies, waits for them, and re-layouts  15.6 us
    pallas_call x2, Pallas kernels, project(): pl.pallas_call(kernel, grid_spec=pltpu.PrefetchScalarGridSpec(num_scalar_...  11.8 us
    pallas_call x3, Pallas kernels, turn(): pl.pallas_call(functools.partial(turn_kernel, count), in_specs=[pl.BlockS...  9.56 us
    pallas_call x1, Pallas kernels, invert_blocks(): pl.pallas_call(invert_kernel, in_specs=[pl.BlockSpec(memory_space=pltpu.S...  9.56 us
    dot_general x1, matrix products, on_device(): corner = jnp.dot(metric_factor[:, :points], upper, precision=HIGHEST)  3.75 us
  transfers between devices with their start and end apart: 37, of which 15 were waited for; matrix products, arithmetic and copies ran while one was open for 10% of the time, Pallas kernels for 16%

profile of v6, /device:TPU:24, one launch (start us, length us, event | category | flops | bytes accessed | tf_op | source)
XLA Modules:
  0.0 179.7 jit_solution(8203912968308915795)
XLA Ops:
  6.0 2.6 %collective-permute-done = bf16[2,250,128]{2,1,0:T(8,128)(2,1)} collective-permute-done((bf16[2,250,128]{2,1,0:T(8,128)(2,1)}, bf16[2,250,128]{2,1,0:T(8,128)(2,1)}, u32[]{:S(2)}, u32[]{:S(2)}) %collective-permute-start) | collective-permute-done | bytes 128032 | tf_op jit(solution)/shard_map/ppermute | solution.py:30
  8.6 3.7 %collective-permute-done.1 = bf16[2,250,128]{2,1,0:T(8,128)(2,1)} collective-permute-done((bf16[2,250,128]{2,1,0:T(8,128)(2,1)}, bf16[2,250,128]{2,1,0:T(8,128)(2,1)}, u32[]{:S(2)}, u32[]{:S(2)}) %collective-permute-start.1) | collective-permute-done | bytes 128032 | tf_op jit(solution)/shard_map/ppermute | solution.py:30
  12.2 2.1 %pad_maximum_fusion.1 = bf16[4,2,250,128]{3,2,1,0:T(8,128)(2,1)} fusion(bf16[1,2,250,128]{3,2,1,0:T(8,128)(2,1)} %bitcast.9, bf16[1,2,250,128]{3,2,1,0:T(8,128)(2,1)} %bitcast.8, bf16[1,2,250,128]{3,2,1,0:T(8,128)(2,1)} %bitcast.7, bf16[1,2,250,128]{3,2,1,0:T(8,128)(2,1)S(1)} %get-tuple-element.101), kind=kLoop, calls=%fused_computation.8 | loop fusion | flops 768000 | bytes 1024000 | tf_op jit(solution)/shard_map/stack | solution.py:374
  14.3 3.5 %convert_element_type.10 = bf16[512,1024]{1,0:T(8,128)(2,1)} convert(f32[512,1024]{1,0:T(8,128)} %param.7) | non-fusion elementwise | flops 524288 | bytes 3145728 | tf_op jit(solution)/shard_map/convert_element_type | solution.py:381
  19.7 1.7 collective-permute-start.7
  21.4 1.6 collective-permute-start.11
  23.0 2.3 %collective-permute-start.5 = (bf16[500,256]{1,0:T(8,128)(2,1)S(1)}, bf16[500,256]{1,0:T(8,128)(2,1)S(1)}, u32[]{:S(2)}, u32[]{:S(2)}) collective-permute-start(bf16[500,256]{1,0:T(8,128)(2,1)S(1)} %get-tuple-element.54), channel_id=1, source_target_pairs={{0,4},{1,5},{2,6},{3,7},{4,0},{5,1},{6,2},{7,3},{8,12},{9,13},{10,... | collective-permute-start | bytes 768008 | tf_op jit(solution)/shard_map/ppermute | solution.py:30
  25.3 11.9 %collective-permute-done.5.rest_2_ = bf16[500,256]{1,0:T(8,128)(2,1)S(1)} collective-permute-done((bf16[500,256]{1,0:T(8,128)(2,1)S(1)}, bf16[500,256]{1,0:T(8,128)(2,1)S(1)}, u32[]{:S(2)}, u32[]{:S(2)}) %collective-permute-start.5) | collective-permute-done | bytes 256032 | tf_op jit(solution)/shard_map/ppermute | solution.py:30
  39.6 8.2 %collective-permute-start.8 = (bf16[2,250,128]{2,1,0:T(8,128)(2,1)S(1)}, bf16[2,250,128]{2,1,0:T(8,128)(2,1)S(1)}, u32[]{:S(2)}, u32[]{:S(2)}) collective-permute-start(bf16[2,250,128]{2,1,0:T(8,128)(2,1)S(1)} %get-tuple-element.99), channel_id=1, source_target_pairs={{0,2},{1,3},{2,0},{3,1},{4,6},{5,7},{6,4},{7,5},{8,10},{9,11},{10,... | collective-permute-start | bytes 384008 | tf_op jit(solution)/shard_map/ppermute | solution.py:30
  47.9 3.7 %collective-permute-done.8 = bf16[2,250,128]{2,1,0:T(8,128)(2,1)S(1)} collective-permute-done((bf16[2,250,128]{2,1,0:T(8,128)(2,1)S(1)}, bf16[2,250,128]{2,1,0:T(8,128)(2,1)S(1)}, u32[]{:S(2)}, u32[]{:S(2)}) %collective-permute-start.8) | collective-permute-done | bytes 128032 | tf_op jit(solution)/shard_map/ppermute | solution.py:30
  51.5 4.7 %collective-permute-done.9 = bf16[2,250,128]{2,1,0:T(8,128)(2,1)S(1)} collective-permute-done((bf16[2,250,128]{2,1,0:T(8,128)(2,1)S(1)}, bf16[2,250,128]{2,1,0:T(8,128)(2,1)S(1)}, u32[]{:S(2)}, u32[]{:S(2)}) %collective-permute-start.9) | collective-permute-done | bytes 128032 | tf_op jit(solution)/shard_map/ppermute | solution.py:30
  56.3 2.9 %collective-permute-start.12 = (bf16[4,2,250,128]{3,2,1,0:T(8,128)(2,1)S(1)}, bf16[4,2,250,128]{3,2,1,0:T(8,128)(2,1)S(1)}, u32[]{:S(2)}, u32[]{:S(2)}) collective-permute-start(bf16[4,2,250,128]{3,2,1,0:T(8,128)(2,1)S(1)} %pad_maximum_fusion.2.rest_3_.rest_7_.rest_2_.rest_6_), channel_id=1, source_target_pairs={{0,8},{1,9},{2,10},{3,11},{4,12},{5,13},{6,14},{7,15},{8,0},{9,1},... | collective-permute-start | bytes 1536008 | tf_op jit(solution)/shard_map/ppermute | solution.py:30
  59.2 5.3 %collective-permute-start.13 = (bf16[4,2,250,128]{3,2,1,0:T(8,128)(2,1)S(1)}, bf16[4,2,250,128]{3,2,1,0:T(8,128)(2,1)S(1)}, u32[]{:S(2)}, u32[]{:S(2)}) collective-permute-start(bf16[4,2,250,128]{3,2,1,0:T(8,128)(2,1)S(1)} %pad_maximum_fusion.2.rest_3_.rest_7_.rest_2_.rest_6_), channel_id=1, source_target_pairs={{0,16},{1,17},{2,18},{3,19},{4,20},{5,21},{6,22},{7,23},{8,24},{9,... | collective-permute-start | bytes 1536008 | tf_op jit(solution)/shard_map/ppermute | solution.py:30
  66.5 9.6 %invert_blocks.1 = (f32[512,512]{1,0:T(8,128)S(1)}, f32[512,512]{1,0:T(8,128)S(1)}) custom-call(s32[2]{0:T(128)S(1)} %pad_add_fusion.where_ref, f32[512,512]{1,0:T(8,128)} %constant_dynamic-slice_fusion.own_ref, f32[512,512]{1,0:T(8,128)S(1)} %collective-permute-done.6.sib_ref), custom_call_target="tpu_custom_call" | custom-call | flops 8589934592 | bytes 4194304 | tf_op jit(solution)/shard_map/invert_blocks/pallas_call | solution.py:234
  76.0 3.7 %fusion.2 = f32[512,512]{1,0:T(8,128)S(1)} fusion(f32[512,512]{1,0:T(8,128)S(1)} %get-tuple-element.72, f32[512,1024]{1,0:T(8,128)S(1)} %copy-done.32), kind=kOutput, calls=%fused_computation.6 | convolution fusion | flops 1610612736 | bytes 3145728 | tf_op jit(solution)/shard_map/dot_general | solution.py:438
  79.9 1.9 %fusion.1 = f32[512,512]{1,0:T(8,128)S(1)} fusion(f32[512,512]{1,0:T(8,128)S(1)} %get-tuple-element.71, f32[512,512]{1,0:T(8,128)S(1)} %fusion.2, pred[]{:T(512)S(6)} %eq.13), kind=kOutput, calls=%fused_computation.5 | convolution fusion | flops 1611137024 | bytes 3145729 | tf_op jit(solution)/shard_map/dot_general | solution.py:439
  83.1 2.6 %collective-permute-done.13.rest_5_.rest_9_.rest_4_.rest_8_ = bf16[4,2,250,128]{3,2,1,0:T(8,128)(2,1)S(1)} collective-permute-done((bf16[4,2,250,128]{3,2,1,0:T(8,128)(2,1)S(1)}, bf16[4,2,250,128]{3,2,1,0:T(8,128)(2,1)S(1)}, u32[]{:S(2)}, u32[]{:S(2)}) %collective-permute-start.13) | collective-permute-done | bytes 512032 | tf_op jit(solution)/shard_map/ppermute | solution.py:30
  91.2 2.8 %pivot_entries.1.entries_ref = f32[8,8]{1,0:T(8,128)} custom-call(s32[8]{0:T(128)} %get-tuple-element.108.row_ref, bf16[500,8,250]{2,1,0:T(8,128)(2,1)} %bitcast.33, bf16[500,8,250]{2,1,0:T(8,128)(2,1)} %bitcast.36, s32[8]{0:T(128)} %get-tuple-element.109.own_col_ref, s32[8]{0:T(128)} %get-tuple-element.107.sib_col_ref), custom_call_target="tpu_custom_call" | custom-call | tf_op jit(solution)/shard_map/pivot_entries/pallas_call | solution.py:63
  101.9 5.9 %project.2 = (f32[8,640]{1,0:T(8,128)S(1)}, f32[8,640]{1,0:T(8,128)S(1)}) custom-call(s32[5]{0:T(128)S(1)} %stack.85.where_ref, bf16[4000,250]{1,0:T(8,128)(2,1)S(1)} %bitcast.34, bf16[4000,250]{1,0:T(8,128)(2,1)S(1)} %bitcast.37, f32[8,8]{1,0:T(8,128)S(1)} %copy-done.15, bf16[500,512]{1,0:T(8,128)(2,1)S(1)} %copy-done, ...), custom_call_target="tpu_custom_call" | custom-call | flops 4096000000 | bytes 1048576 | tf_op jit(solution)/shard_map/project/pallas_call | solution.py:170
  107.8 1.8 %collective-permute-start.17 = (f32[8,640]{1,0:T(8,128)S(1)}, f32[8,640]{1,0:T(8,128)S(1)}, u32[]{:S(2)}, u32[]{:S(2)}) collective-permute-start(f32[8,640]{1,0:T(8,128)S(1)} %get-tuple-element.79), channel_id=1, source_target_pairs={{0,4},{1,5},{2,6},{3,7},{4,0},{5,1},{6,2},{7,3},{8,12},{9,13},{10,... | collective-permute-start | bytes 61448 | tf_op jit(solution)/shard_map/ppermute | solution.py:30
  109.6 3.5 %collective-permute-start.28 = (bf16[512,1024]{1,0:T(8,128)(2,1)}, bf16[512,1024]{1,0:T(8,128)(2,1)S(1)}, u32[]{:S(2)}, u32[]{:S(2)}) collective-permute-start(bf16[512,1024]{1,0:T(8,128)(2,1)} %convert_element_type.10), channel_id=1, source_target_pairs={{4,20},{5,21},{6,30},{7,31}} | collective-permute-start | bytes 3145736 | tf_op jit(solution)/shard_map/ppermute | solution.py:30
  114.2 5.9 %project.3 = (f32[8,640]{1,0:T(8,128)S(1)}, f32[8,640]{1,0:T(8,128)S(1)}) custom-call(s32[5]{0:T(128)S(1)} %stack.85.where_ref, bf16[4000,250]{1,0:T(8,128)(2,1)S(1)} %bitcast.35, bf16[4000,250]{1,0:T(8,128)(2,1)S(1)} %bitcast.38, f32[8,8]{1,0:T(8,128)S(1)} %copy-done.15, bf16[500,512]{1,0:T(8,128)(2,1)S(1)} %copy-done.26, bf16[500,512]{1,0:T(8,128)(2,1)S(1)} %copy-done.28, ...), custom_call_target="tpu_custom_call" | custom-call | flops 4096000000 | bytes 1048576 | tf_op jit(solution)/shard_map/project/pallas_call | solution.py:170
  120.9 3.0 %collective-permute-done.20 = f32[8,640]{1,0:T(8,128)S(1)} collective-permute-done((f32[8,640]{1,0:T(8,128)S(1)}, f32[8,640]{1,0:T(8,128)S(1)}, u32[]{:S(2)}, u32[]{:S(2)}) %collective-permute-start.20) | collective-permute-done | bytes 20512 | tf_op jit(solution)/shard_map/ppermute | solution.py:30
  124.0 2.5 %collective-permute-done.21 = f32[8,640]{1,0:T(8,128)S(1)} collective-permute-done((f32[8,640]{1,0:T(8,128)S(1)}, f32[8,640]{1,0:T(8,128)S(1)}, u32[]{:S(2)}, u32[]{:S(2)}) %collective-permute-start.21) | collective-permute-done | bytes 20512 | tf_op jit(solution)/shard_map/ppermute | solution.py:30
  126.9 3.1 %collective-permute-start.24 = (f32[8,640]{1,0:T(8,128)S(1)}, f32[8,640]{1,0:T(8,128)S(1)}, u32[]{:S(2)}, u32[]{:S(2)}) collective-permute-start(f32[8,640]{1,0:T(8,128)S(1)} %add_add_fusion.1), channel_id=1, source_target_pairs={{0,24},{1,25},{2,26},{3,27},{4,28},{5,29},{6,30},{7,31},{8,16},{9,... | collective-permute-start | bytes 61448 | tf_op jit(solution)/shard_map/ppermute | solution.py:30
  130.1 6.2 %collective-permute-done.22 = f32[8,640]{1,0:T(8,128)S(1)} collective-permute-done((f32[8,640]{1,0:T(8,128)S(1)}, f32[8,640]{1,0:T(8,128)S(1)}, u32[]{:S(2)}, u32[]{:S(2)}) %collective-permute-start.22) | collective-permute-done | bytes 20512 | tf_op jit(solution)/shard_map/ppermute | solution.py:30
  139.7 2.0 %factor_inverse.1.inverse_ref = f32[8,8]{1,0:T(8,128)} custom-call(f32[8,640]{1,0:T(8,128)} %copy-done.9), custom_call_target="tpu_custom_call" | custom-call | tf_op jit(solution)/shard_map/factor_inverse/pallas_call | solution.py:98
  142.4 2.6 %turn.3.refs_1_ = f32[16,512]{1,0:T(8,128)S(1)} custom-call(s32[1]{0:T(128)} %bitcast.5.where_ref, bf16[512,1024]{1,0:T(8,128)(2,1)} %collective-permute-done.7.refs_0_, bf16[512,1024]{1,0:T(8,128)(2,1)} %collective-permute-done.18.refs_1_, bf16[512,1024]{1,0:T(8,128)(2,1)S(1)} %get-tuple-element.75.hi_ref.refs_2_.refs_4_.refs_6_, ...), custom_call_target="tpu_custom_call" | custom-call | flops 2147483648 | bytes 4194304 | tf_op jit(solution)/shard_map/turn/pallas_call | solution.py:309
  147.8 3.0 %turn.4.refs_2_ = f32[24,512]{1,0:T(8,128)S(1)} custom-call(s32[1]{0:T(128)} %bitcast.5.where_ref, bf16[512,1024]{1,0:T(8,128)(2,1)} %collective-permute-done.7.refs_0_, bf16[512,1024]{1,0:T(8,128)(2,1)} %collective-permute-done.18.refs_1_, bf16[512,1024]{1,0:T(8,128)(2,1)S(1)} %collective-permute-done.28.refs_2_.refs_4_, ...), custom_call_target="tpu_custom_call" | custom-call | flops 2147483648 | bytes 4194304 | tf_op jit(solution)/shard_map/turn/pallas_call | solution.py:309
  154.0 4.0 %turn.5.refs_3_ = f32[32,512]{1,0:T(8,128)S(1)} custom-call(s32[1]{0:T(128)} %bitcast.5.where_ref, bf16[512,1024]{1,0:T(8,128)(2,1)} %collective-permute-done.7.refs_0_, bf16[512,1024]{1,0:T(8,128)(2,1)} %collective-permute-done.18.refs_1_, bf16[512,1024]{1,0:T(8,128)(2,1)} %collective-permute-done.11.refs_2_, ...), custom_call_target="tpu_custom_call" | custom-call | flops 2147483648 | bytes 4194304 | tf_op jit(solution)/shard_map/turn/pallas_call | solution.py:309
  158.7 1.7 combine.1
  163.0 15.5 %collective-permute-done.36 = f32[2,512]{1,0:T(2,128)S(1)} collective-permute-done((f32[2,512]{1,0:T(2,128)}, f32[2,512]{1,0:T(2,128)S(1)}, u32[]{:S(2)}, u32[]{:S(2)}) %collective-permute-start.36) | collective-permute-done | bytes 4128 | tf_op jit(solution)/shard_map/ppermute | solution.py:30
  (139 shorter events, 44.1 us)
Async XLA Ops:
  0.0 14.3 %collective-permute-start.3 = (bf16[8,500,250]{2,0,1:T(8,128)(2,1)}, bf16[8,500,250]{2,0,1:T(8,128)(2,1)S(1)}, u32[]{:S(2)}, u32[]{:S(2)}) collective-permute-start(bf16[8,500,250]{2,0,1:T(8,128)(2,1)} %param.4), channel_id=1, source_target_pairs={{0,1},{1,0},{2,3},{3,2},{4,5},{5,4},{6,7},{7,6},{8,9},{9,8},{10,11... | collective-permute-start | bytes 6000008 | tf_op jit(solution)/shard_map/ppermute | solution.py:30
  2.1 6.5 %collective-permute-start = (bf16[2,250,128]{2,1,0:T(8,128)(2,1)}, bf16[2,250,128]{2,1,0:T(8,128)(2,1)}, u32[]{:S(2)}, u32[]{:S(2)}) collective-permute-start(bf16[2,250,128]{2,1,0:T(8,128)(2,1)} %get-tuple-element.104), channel_id=1, source_target_pairs={{0,8},{1,9},{2,10},{3,11},{4,12},{5,13},{6,14},{7,15},{8,0},{9,1},... | collective-permute-start | bytes 384008 | tf_op jit(solution)/shard_map/ppermute | solution.py:30
  3.5 8.7 %collective-permute-start.1 = (bf16[2,250,128]{2,1,0:T(8,128)(2,1)}, bf16[2,250,128]{2,1,0:T(8,128)(2,1)}, u32[]{:S(2)}, u32[]{:S(2)}) collective-permute-start(bf16[2,250,128]{2,1,0:T(8,128)(2,1)} %get-tuple-element.103), channel_id=1, source_target_pairs={{0,16},{1,17},{2,18},{3,19},{4,20},{5,21},{6,22},{7,23},{8,24},{9,... | collective-permute-start | bytes 384008 | tf_op jit(solution)/shard_map/ppermute | solution.py:30
  5.1 7.2 %collective-permute-start.2 = (bf16[2,250,128]{2,1,0:T(8,128)(2,1)}, bf16[2,250,128]{2,1,0:T(8,128)(2,1)}, u32[]{:S(2)}, u32[]{:S(2)}) collective-permute-start(bf16[2,250,128]{2,1,0:T(8,128)(2,1)} %get-tuple-element.102), channel_id=1, source_target_pairs={{0,24},{1,25},{2,26},{3,27},{4,28},{5,29},{6,30},{7,31},{8,16},{9,... | collective-permute-start | bytes 384008 | tf_op jit(solution)/shard_map/ppermute | solution.py:30
  5.6 14.1 %collective-permute-start.4 = (bf16[500,256]{1,0:T(8,128)(2,1)S(1)}, bf16[500,256]{1,0:T(8,128)(2,1)S(1)}, u32[]{:S(2)}, u32[]{:S(2)}) collective-permute-start(bf16[500,256]{1,0:T(8,128)(2,1)S(1)} %get-tuple-element.106), channel_id=1, source_target_pairs={{0,4},{1,5},{2,6},{3,7},{4,0},{5,1},{6,2},{7,3},{8,12},{9,13},{10,... | collective-permute-start | bytes 768008 | tf_op jit(solution)/shard_map/ppermute | solution.py:30
  19.7 17.4 %collective-permute-start.6 = (f32[512,512]{1,0:T(8,128)}, f32[512,512]{1,0:T(8,128)S(1)}, u32[]{:S(2)}, u32[]{:S(2)}) collective-permute-start(f32[512,512]{1,0:T(8,128)} %constant_dynamic-slice_fusion.own_ref), channel_id=1, source_target_pairs={{0,1},{1,0},{2,3},{3,2},{4,5},{5,4},{6,7},{7,6},{8,9},{9,8},{10,11... | collective-permute-start | bytes 3145736 | tf_op jit(solution)/shard_map/ppermute | solution.py:30
  19.7 17.4 %collective-permute-start.7 = (bf16[512,1024]{1,0:T(8,128)(2,1)}, bf16[512,1024]{1,0:T(8,128)(2,1)}, u32[]{:S(2)}, u32[]{:S(2)}) collective-permute-start(bf16[512,1024]{1,0:T(8,128)(2,1)} %convert_element_type.10), channel_id=1, source_target_pairs={{2,10},{3,11},{12,20},{13,21},{22,30},{23,31}} | collective-permute-start | bytes 3145736 | tf_op jit(solution)/shard_map/ppermute | solution.py:30
  21.4 26.5 %collective-permute-start.11 = (bf16[512,1024]{1,0:T(8,128)(2,1)}, bf16[512,1024]{1,0:T(8,128)(2,1)}, u32[]{:S(2)}, u32[]{:S(2)}) collective-permute-start(bf16[512,1024]{1,0:T(8,128)(2,1)} %convert_element_type.10), channel_id=1, source_target_pairs={{14,30},{15,31}} | collective-permute-start | bytes 3145736 | tf_op jit(solution)/shard_map/ppermute | solution.py:30
  23.0 14.1 %collective-permute-start.5 = (bf16[500,256]{1,0:T(8,128)(2,1)S(1)}, bf16[500,256]{1,0:T(8,128)(2,1)S(1)}, u32[]{:S(2)}, u32[]{:S(2)}) collective-permute-start(bf16[500,256]{1,0:T(8,128)(2,1)S(1)} %get-tuple-element.54), channel_id=1, source_target_pairs={{0,4},{1,5},{2,6},{3,7},{4,0},{5,1},{6,2},{7,3},{8,12},{9,13},{10,... | collective-permute-start | bytes 768008 | tf_op jit(solution)/shard_map/ppermute | solution.py:30
  38.4 9.5 %collective-permute-start.10 = (bf16[2,250,128]{2,1,0:T(8,128)(2,1)S(1)}, bf16[2,250,128]{2,1,0:T(8,128)(2,1)S(1)}, u32[]{:S(2)}, u32[]{:S(2)}) collective-permute-start(bf16[2,250,128]{2,1,0:T(8,128)(2,1)S(1)} %get-tuple-element.97), channel_id=1, source_target_pairs={{0,6},{1,7},{2,4},{3,5},{4,2},{5,3},{6,0},{7,1},{8,14},{9,15},{10,... | collective-permute-start | bytes 384008 | tf_op jit(solution)/shard_map/ppermute | solution.py:30
  39.6 11.9 %collective-permute-start.8 = (bf16[2,250,128]{2,1,0:T(8,128)(2,1)S(1)}, bf16[2,250,128]{2,1,0:T(8,128)(2,1)S(1)}, u32[]{:S(2)}, u32[]{:S(2)}) collective-permute-start(bf16[2,250,128]{2,1,0:T(8,128)(2,1)S(1)} %get-tuple-element.99), channel_id=1, source_target_pairs={{0,2},{1,3},{2,0},{3,1},{4,6},{5,7},{6,4},{7,5},{8,10},{9,11},{10,... | collective-permute-start | bytes 384008 | tf_op jit(solution)/shard_map/ppermute | solution.py:30
  47.8 8.4 %collective-permute-start.9 = (bf16[2,250,128]{2,1,0:T(8,128)(2,1)S(1)}, bf16[2,250,128]{2,1,0:T(8,128)(2,1)S(1)}, u32[]{:S(2)}, u32[]{:S(2)}) collective-permute-start(bf16[2,250,128]{2,1,0:T(8,128)(2,1)S(1)} %get-tuple-element.98), channel_id=1, source_target_pairs={{0,4},{1,5},{2,6},{3,7},{4,0},{5,1},{6,2},{7,3},{8,12},{9,13},{10,... | collective-permute-start | bytes 384008 | tf_op jit(solution)/shard_map/ppermute | solution.py:30
  56.3 25.9 %collective-permute-start.12 = (bf16[4,2,250,128]{3,2,1,0:T(8,128)(2,1)S(1)}, bf16[4,2,250,128]{3,2,1,0:T(8,128)(2,1)S(1)}, u32[]{:S(2)}, u32[]{:S(2)}) collective-permute-start(bf16[4,2,250,128]{3,2,1,0:T(8,128)(2,1)S(1)} %pad_maximum_fusion.2.rest_3_.rest_7_.rest_2_.rest_6_), channel_id=1, source_target_pairs={{0,8},{1,9},{2,10},{3,11},{4,12},{5,13},{6,14},{7,15},{8,0},{9,1},... | collective-permute-start | bytes 1536008 | tf_op jit(solution)/shard_map/ppermute | solution.py:30
  59.2 26.6 %collective-permute-start.13 = (bf16[4,2,250,128]{3,2,1,0:T(8,128)(2,1)S(1)}, bf16[4,2,250,128]{3,2,1,0:T(8,128)(2,1)S(1)}, u32[]{:S(2)}, u32[]{:S(2)}) collective-permute-start(bf16[4,2,250,128]{3,2,1,0:T(8,128)(2,1)S(1)} %pad_maximum_fusion.2.rest_3_.rest_7_.rest_2_.rest_6_), channel_id=1, source_target_pairs={{0,16},{1,17},{2,18},{3,19},{4,20},{5,21},{6,22},{7,23},{8,24},{9,... | collective-permute-start | bytes 1536008 | tf_op jit(solution)/shard_map/ppermute | solution.py:30
  64.4 23.1 %collective-permute-start.14 = (bf16[4,2,250,128]{3,2,1,0:T(8,128)(2,1)S(1)}, bf16[4,2,250,128]{3,2,1,0:T(8,128)(2,1)S(1)}, u32[]{:S(2)}, u32[]{:S(2)}) collective-permute-start(bf16[4,2,250,128]{3,2,1,0:T(8,128)(2,1)S(1)} %pad_maximum_fusion.2.rest_3_.rest_7_.rest_2_.rest_6_), channel_id=1, source_target_pairs={{0,24},{1,25},{2,26},{3,27},{4,28},{5,29},{6,30},{7,31},{8,16},{9,... | collective-permute-start | bytes 1536008 | tf_op jit(solution)/shard_map/ppermute | solution.py:30
  65.4 23.0 %collective-permute-start.15 = (bf16[500,512]{1,0:T(8,128)(2,1)S(1)}, bf16[500,512]{1,0:T(8,128)(2,1)S(1)}, u32[]{:S(2)}, u32[]{:S(2)}) collective-permute-start(bf16[500,512]{1,0:T(8,128)(2,1)S(1)} %copy-done), channel_id=1, source_target_pairs={{0,2},{1,3},{2,0},{3,1},{4,6},{5,7},{6,4},{7,5},{8,10},{9,11},{10,... | collective-permute-start | bytes 1536008 | tf_op jit(solution)/shard_map/ppermute | solution.py:30
  65.4 23.8 %collective-permute-start.16 = (bf16[500,512]{1,0:T(8,128)(2,1)S(1)}, bf16[500,512]{1,0:T(8,128)(2,1)S(1)}, u32[]{:S(2)}, u32[]{:S(2)}) collective-permute-start(bf16[500,512]{1,0:T(8,128)(2,1)S(1)} %copy-done), channel_id=1, source_target_pairs={{0,6},{1,7},{2,4},{3,5},{4,2},{5,3},{6,0},{7,1},{8,14},{9,15},{10,... | collective-permute-start | bytes 1536008 | tf_op jit(solution)/shard_map/ppermute | solution.py:30
  89.9 23.2 %collective-permute-start.18 = (bf16[512,1024]{1,0:T(8,128)(2,1)}, bf16[512,1024]{1,0:T(8,128)(2,1)}, u32[]{:S(2)}, u32[]{:S(2)}) collective-permute-start(bf16[512,1024]{1,0:T(8,128)(2,1)} %collective-permute-done.7.refs_0_), channel_id=1, source_target_pairs={{0,1},{1,0},{2,3},{3,2},{4,5},{5,4},{6,7},{7,6},{8,9},{9,8},{10,11... | collective-permute-start | bytes 3145736 | tf_op jit(solution)/shard_map/ppermute | solution.py:30
  89.9 23.2 %collective-permute-start.19 = (bf16[512,1024]{1,0:T(8,128)(2,1)}, bf16[512,1024]{1,0:T(8,128)(2,1)}, u32[]{:S(2)}, u32[]{:S(2)}) collective-permute-start(bf16[512,1024]{1,0:T(8,128)(2,1)} %collective-permute-done.11.refs_2_), channel_id=1, source_target_pairs={{0,1},{1,0},{2,3},{3,2},{4,5},{5,4},{6,7},{7,6},{8,9},{9,8},{10,11... | collective-permute-start | bytes 3145736 | tf_op jit(solution)/shard_map/ppermute | solution.py:30
  107.8 13.1 %collective-permute-start.17 = (f32[8,640]{1,0:T(8,128)S(1)}, f32[8,640]{1,0:T(8,128)S(1)}, u32[]{:S(2)}, u32[]{:S(2)}) collective-permute-start(f32[8,640]{1,0:T(8,128)S(1)} %get-tuple-element.79), channel_id=1, source_target_pairs={{0,4},{1,5},{2,6},{3,7},{4,0},{5,1},{6,2},{7,3},{8,12},{9,13},{10,... | collective-permute-start | bytes 61448 | tf_op jit(solution)/shard_map/ppermute | solution.py:30
  109.6 35.4 %collective-permute-start.28 = (bf16[512,1024]{1,0:T(8,128)(2,1)}, bf16[512,1024]{1,0:T(8,128)(2,1)S(1)}, u32[]{:S(2)}, u32[]{:S(2)}) collective-permute-start(bf16[512,1024]{1,0:T(8,128)(2,1)} %convert_element_type.10), channel_id=1, source_target_pairs={{4,20},{5,21},{6,30},{7,31}} | collective-permute-start | bytes 3145736 | tf_op jit(solution)/shard_map/ppermute | solution.py:30
  120.1 3.8 %collective-permute-start.20 = (f32[8,640]{1,0:T(8,128)S(1)}, f32[8,640]{1,0:T(8,128)S(1)}, u32[]{:S(2)}, u32[]{:S(2)}) collective-permute-start(f32[8,640]{1,0:T(8,128)S(1)} %get-tuple-element.83), channel_id=1, source_target_pairs={{0,2},{1,3},{2,0},{3,1},{4,6},{5,7},{6,4},{7,5},{8,10},{9,11},{10,... | collective-permute-start | bytes 61448 | tf_op jit(solution)/shard_map/ppermute | solution.py:30
  120.9 5.6 %collective-permute-start.21 = (f32[8,640]{1,0:T(8,128)S(1)}, f32[8,640]{1,0:T(8,128)S(1)}, u32[]{:S(2)}, u32[]{:S(2)}) collective-permute-start(f32[8,640]{1,0:T(8,128)S(1)} %get-tuple-element.84), channel_id=1, source_target_pairs={{0,6},{1,7},{2,4},{3,5},{4,2},{5,3},{6,0},{7,1},{8,14},{9,15},{10,... | collective-permute-start | bytes 61448 | tf_op jit(solution)/shard_map/ppermute | solution.py:30
  126.5 9.8 %collective-permute-start.22 = (f32[8,640]{1,0:T(8,128)S(1)}, f32[8,640]{1,0:T(8,128)S(1)}, u32[]{:S(2)}, u32[]{:S(2)}) collective-permute-start(f32[8,640]{1,0:T(8,128)S(1)} %add_add_fusion.1), channel_id=1, source_target_pairs={{0,8},{1,9},{2,10},{3,11},{4,12},{5,13},{6,14},{7,15},{8,0},{9,1},... | collective-permute-start | bytes 61448 | tf_op jit(solution)/shard_map/ppermute | solution.py:30
  126.6 9.7 %collective-permute-start.23 = (f32[8,640]{1,0:T(8,128)S(1)}, f32[8,640]{1,0:T(8,128)S(1)}, u32[]{:S(2)}, u32[]{:S(2)}) collective-permute-start(f32[8,640]{1,0:T(8,128)S(1)} %add_add_fusion.1), channel_id=1, source_target_pairs={{0,16},{1,17},{2,18},{3,19},{4,20},{5,21},{6,22},{7,23},{8,24},{9,... | collective-permute-start | bytes 61448 | tf_op jit(solution)/shard_map/ppermute | solution.py:30
  126.9 9.5 %collective-permute-start.24 = (f32[8,640]{1,0:T(8,128)S(1)}, f32[8,640]{1,0:T(8,128)S(1)}, u32[]{:S(2)}, u32[]{:S(2)}) collective-permute-start(f32[8,640]{1,0:T(8,128)S(1)} %add_add_fusion.1), channel_id=1, source_target_pairs={{0,24},{1,25},{2,26},{3,27},{4,28},{5,29},{6,30},{7,31},{8,16},{9,... | collective-permute-start | bytes 61448 | tf_op jit(solution)/shard_map/ppermute | solution.py:30
  138.4 3.3 %collective-permute-start.26 = (f32[8,512]{1,0:T(8,128)S(1)}, f32[8,512]{1,0:T(8,128)S(1)}, u32[]{:S(2)}, u32[]{:S(2)}) collective-permute-start(f32[8,512]{1,0:T(8,128)S(1)} %apply_weights.1.refs_0_), channel_id=1, source_target_pairs={{0,10},{1,11}} | collective-permute-start | bytes 49160 | tf_op jit(solution)/shard_map/ppermute | solution.py:30
  139.1 2.6 %collective-permute-start.27 = (f32[8,512]{1,0:T(8,128)S(1)}, f32[8,512]{1,0:T(8,128)S(1)}, u32[]{:S(2)}, u32[]{:S(2)}) collective-permute-start(f32[8,512]{1,0:T(8,128)S(1)} %apply_weights.1.refs_0_), channel_id=1, source_target_pairs={{0,11},{1,10}} | collective-permute-start | bytes 49160 | tf_op jit(solution)/shard_map/ppermute | solution.py:30
  145.1 2.7 %collective-permute-start.29 = (bf16[512,1024]{1,0:T(8,128)(2,1)S(1)}, bf16[512,1024]{1,0:T(8,128)(2,1)S(1)}, u32[]{:S(2)}, u32[]{:S(2)}) collective-permute-start(bf16[512,1024]{1,0:T(8,128)(2,1)S(1)} %collective-permute-done.28.refs_2_.refs_4_), channel_id=1, source_target_pairs={{0,1},{1,0},{2,3},{3,2},{4,5},{5,4},{6,7},{7,6},{8,9},{9,8},{10,11... | collective-permute-start | bytes 3145736 | tf_op jit(solution)/shard_map/ppermute | solution.py:30
  150.8 2.0 %collective-permute-start.32 = (f32[24,512]{1,0:T(8,128)S(1)}, f32[24,512]{1,0:T(8,128)S(1)}, u32[]{:S(2)}, u32[]{:S(2)}) collective-permute-start(f32[24,512]{1,0:T(8,128)S(1)} %turn.4.refs_2_), channel_id=1, source_target_pairs={{20,30},{21,31}} | collective-permute-start | bytes 147464 | tf_op jit(solution)/shard_map/ppermute | solution.py:30
  160.3 2.6 %collective-permute-start.34 = (f32[2,512]{1,0:T(2,128)}, f32[2,512]{1,0:T(2,128)S(1)}, u32[]{:S(2)}, u32[]{:S(2)}) collective-permute-start(f32[2,512]{1,0:T(2,128)} %get-tuple-element.92), channel_id=1, source_target_pairs={{0,8},{1,9},{10,2},{11,3},{20,28},{21,29},{30,22},{31,23}} | collective-permute-start | bytes 12296 | tf_op jit(solution)/shard_map/ppermute | solution.py:30
  161.7 16.8 %collective-permute-start.36 = (f32[2,512]{1,0:T(2,128)}, f32[2,512]{1,0:T(2,128)S(1)}, u32[]{:S(2)}, u32[]{:S(2)}) collective-permute-start(f32[2,512]{1,0:T(2,128)} %get-tuple-element.94), channel_id=1, source_target_pairs={{0,24},{1,25},{10,18},{11,19},{20,12},{21,13},{30,6},{31,7}} | collective-permute-start | bytes 12296 | tf_op jit(solution)/shard_map/ppermute | solution.py:30
  (39 other events, 213.1 us)

commit v7 on v6

--- a/solution.py
+++ b/solution.py
@@ -64,8 +64,8 @@
         pivot_kernel,
         in_specs=[
             pl.BlockSpec(memory_space=pltpu.SMEM),
-            pl.BlockSpec(memory_space=pl.ANY),
-            pl.BlockSpec(memory_space=pl.ANY),
+            pl.BlockSpec(memory_space=pltpu.HBM),
+            pl.BlockSpec(memory_space=pltpu.HBM),
             pl.BlockSpec(memory_space=pltpu.SMEM),
             pl.BlockSpec(memory_space=pltpu.SMEM),
         ],
@@ -196,17 +196,16 @@
     )(where, own, sib, entries, *arrays)
 
 
-def invert_kernel(where_ref, own_ref, sib_ref, own_out, sib_out):
-    n = own_ref.shape[0]
+def invert_kernel(where_ref, block_ref, out_ref):
+    n = block_ref.shape[0]
     tile = 128
     row = lax.broadcasted_iota(jnp.int32, (tile, tile), 0)
     col = lax.broadcasted_iota(jnp.int32, (tile, tile), 1)
     eye = (row == col).astype(F32)
     dot = functools.partial(jnp.dot, precision=HIGHEST, preferred_element_type=F32)
-    pairs = ((own_ref, own_out), (sib_ref, sib_out))
-    places = [(ref, out, b) for ref, out in pairs for b in range(0, n, tile)]
     holds = where_ref[1] == 1
-    parts = [jnp.where(holds, ref[b : b + tile, b : b + tile], eye) for ref, _, b in places]
+    places = range(0, n, tile)
+    parts = [jnp.where(holds, block_ref[b : b + tile, b : b + tile], eye) for b in places]
     xs = [eye / jnp.sum(part * eye, axis=1, keepdims=True) for part in parts]
     size = 1
     while size < tile:
@@ -214,32 +213,33 @@
         inner = [dot(jnp.where(pick, part, 0.0), x) for part, x in zip(parts, xs)]
         xs = [x - dot(x, y) for x, y in zip(xs, inner)]
         size *= 2
-    own_out[...] = jnp.zeros_like(own_out)
-    sib_out[...] = jnp.zeros_like(sib_out)
-    for (_, out, b), x in zip(places, xs):
-        out[b : b + tile, b : b + tile] = x
+    out_ref[...] = jnp.zeros_like(out_ref)
+    for b, x in zip(places, xs):
+        out_ref[b : b + tile, b : b + tile] = x
     size = tile
     while size < n:
-        for ref, out in pairs:
-            for b in range(0, n, 2 * size):
-                mid, end = b + size, b + 2 * size
-                inner = dot(ref[mid:end, b:mid], out[b:mid, b:mid])
-                out[mid:end, b:mid] = -dot(out[mid:end, mid:end], inner)
+        for b in range(0, n, 2 * size):
+            mid, end = b + size, b + 2 * size
+            inner = dot(block_ref[mid:end, b:mid], out_ref[b:mid, b:mid])
+            out_ref[mid:end, b:mid] = -dot(out_ref[mid:end, mid:end], inner)
         size *= 2
 
 
-def invert_blocks(where, own, sib):
-    shape = jax.ShapeDtypeStruct(own.shape, F32)
-    vmem = pl.BlockSpec(memory_space=pltpu.VMEM)
+def invert_block(where, metric):
+    n = metric.shape[0]
     return pl.pallas_call(
         invert_kernel,
-        in_specs=[pl.BlockSpec(memory_space=pltpu.SMEM), vmem, vmem],
-        out_specs=(vmem, vmem),
-        out_shape=(shape, shape),
+        grid_spec=pltpu.PrefetchScalarGridSpec(
+            num_scalar_prefetch=1,
+            grid=(1,),
+            in_specs=[pl.BlockSpec((n, n), lambda i, s: (0, s[0]))],
+            out_specs=pl.BlockSpec((n, n), lambda i, s: (0, 0)),
+        ),
+        out_shape=jax.ShapeDtypeStruct((n, n), F32),
         compiler_params=pltpu.CompilerParams(vmem_limit_bytes=16 << 20),
-        cost_estimate=pl.CostEstimate(flops=8 << 30, transcendentals=0, bytes_accessed=1 << 22),
-        name="invert_blocks",
-    )(where, own, sib)
+        cost_estimate=pl.CostEstimate(flops=4 << 30, transcendentals=0, bytes_accessed=1 << 22),
+        name="invert_block",
+    )(where, metric)
 
 
 def weigh(hi_ref, lo_ref, halves):
@@ -261,8 +261,10 @@
     return total
 
 
-def apply_kernel(where_ref, hi_ref, lo_ref, xa_ref, xb_ref, out_ref):
+def apply_kernel(where_ref, *refs):
+    weights, (xa_ref, xb_ref, out_ref) = refs[:-3], refs[-3:]
     core = where_ref[0]
+    hi_ref, lo_ref = weights if len(weights) == 2 else (weights[0], None)
     points = out_ref.shape[1]
     halves = [(core, xa_ref[:, :points]), (1 - core, xb_ref[:, :points])]
     out_ref[...] = weigh(hi_ref, lo_ref, halves)
@@ -271,7 +273,8 @@
 def apply_weights(where, weights, xa, xb):
     return pl.pallas_call(
         apply_kernel,
-        in_specs=[pl.BlockSpec(memory_space=pltpu.SMEM)] + [pl.BlockSpec(memory_space=pltpu.VMEM)] * 4,
+        in_specs=[pl.BlockSpec(memory_space=pltpu.SMEM)]
+        + [pl.BlockSpec(memory_space=pltpu.VMEM)] * (len(weights) + 2),
         out_specs=pl.BlockSpec(memory_space=pltpu.VMEM),
         out_shape=jax.ShapeDtypeStruct((xa.shape[0], weights[0].shape[0]), F32),
         compiler_params=pltpu.CompilerParams(vmem_limit_bytes=12 << 20),
@@ -280,44 +283,38 @@
     )(where, *weights, xa, xb)
 
 
-def turn_kernel(count, where_ref, *refs):
-    lefts, refs = refs[: 2 * count], refs[2 * count :]
-    inv_hi, inv_lo, xa, xb, own_rest, sib_rest, out_ref, buffer, sems = refs
+def turn_kernel(where_ref, *refs):
+    left_own, left_sib, inv_hi, inv_lo, xa, xb, own_rest, sib_rest, out_ref, buffer, sems = refs
     core = where_ref[0]
-    n = own_rest.shape[0]
     copies = [
-        pltpu.make_async_copy(ref, buffer.at[i], sems.at[i]) for i, ref in enumerate(lefts)
+        pltpu.make_async_copy(ref, buffer.at[i], sems.at[i])
+        for i, ref in enumerate((left_own, left_sib))
     ]
     for copy in copies:
         copy.start()
     points = xa.shape[1]
-    own, sib = own_rest[:, :points], sib_rest[:, :points]
-    for i in range(count):
-        d = count - i
-        halves = [(core, xa[i * n : (i + 1) * n]), (1 - core, xb[i * n : (i + 1) * n])]
-        copies[2 * d - 2].wait()
-        own -= weigh(buffer.at[2 * d - 2], None, halves)
-        copies[2 * d - 1].wait()
-        sib -= weigh(buffer.at[2 * d - 1], None, halves)
-    out_ref[: count * n] = xa[...]
-    out_ref[count * n :] = weigh(inv_hi, inv_lo, [(core, own), (1 - core, sib)])
+    halves = [(core, xa[...]), (1 - core, xb[...])]
+    copies[0].wait()
+    own = own_rest[:, :points] - weigh(buffer.at[0], None, halves)
+    copies[1].wait()
+    sib = sib_rest[:, :points] - weigh(buffer.at[1], None, halves)
+    out_ref[...] = weigh(inv_hi, inv_lo, [(core, own), (1 - core, sib)])
 
 
 def turn(where, lefts, inverse, xa, xb, own_rest, sib_rest):
-    n, points = own_rest.shape[0], xa.shape[1]
-    count = xa.shape[0] // n
-    return pl.pallas_call(
-        functools.partial(turn_kernel, count),
+    vmem = pl.BlockSpec(memory_space=pltpu.VMEM)
+    return pl.pallas_call(
+        turn_kernel,
         in_specs=[pl.BlockSpec(memory_space=pltpu.SMEM)]
-        + [pl.BlockSpec(memory_space=pl.ANY)] * len(lefts)
-        + [pl.BlockSpec(memory_space=pltpu.VMEM)] * 6,
-        out_specs=pl.BlockSpec(memory_space=pltpu.VMEM),
-        out_shape=jax.ShapeDtypeStruct(((count + 1) * n, points), F32),
+        + [pl.BlockSpec(memory_space=pl.ANY)] * 2
+        + [vmem] * 6,
+        out_specs=vmem,
+        out_shape=jax.ShapeDtypeStruct(xa.shape, F32),
         scratch_shapes=[
-            pltpu.VMEM((len(lefts),) + lefts[0].shape, BF16),
-            pltpu.SemaphoreType.DMA((len(lefts),)),
+            pltpu.VMEM((2,) + lefts[0].shape, BF16),
+            pltpu.SemaphoreType.DMA((2,)),
         ],
-        compiler_params=pltpu.CompilerParams(vmem_limit_bytes=32 << 20),
+        compiler_params=pltpu.CompilerParams(vmem_limit_bytes=16 << 20),
         cost_estimate=pl.CostEstimate(flops=2 << 30, transcendentals=0, bytes_accessed=1 << 22),
         name="turn",
     )(where, *lefts, *inverse, xa, xb, own_rest, sib_rest)
@@ -326,9 +323,8 @@
 def combine_kernel(count, turn_ref, inverse_ref, *refs):
     x_refs, out_refs = refs[:count], refs[count:]
     x = jnp.zeros(x_refs[0].shape, F32)
-    n = x.shape[0]
     for t, ref in enumerate(x_refs):
-        x = jnp.where(turn_ref[0] == t, ref[t * n :], x)
+        x = jnp.where(turn_ref[0] == t, ref[...], x)
     rows = out_refs[0].shape[0]
     for k, ref in enumerate(out_refs):
         inverse = inverse_ref[pl.ds(turn_ref[1 + k] * rows, rows), :]
@@ -372,43 +368,34 @@
         piece = lax.dynamic_slice_in_dim(halves, (gen_index ^ k) * part, part, 2)
         spread.append(move(piece, lambda g, j, c, k=k: (g ^ k, j, c)) if k else piece)
     spread = jnp.stack(spread)
-    early = 2
-    half = points // 2
+    early, half = 2, points // 2
+    sibling = move(raw_columns, swap)
     early_parts = [move(collocation[:, :half], across(early))]
-    sibling = move(raw_columns, swap)
-    sibling, metric_late = lax.optimization_barrier((sibling, metric_factor))
-    own_block = lax.dynamic_slice_in_dim(metric_late, core * points, points, 1)
+    second_half = collocation[:, half:]
+    spread, sibling, early_parts, second_half, metric_late = lax.optimization_barrier(
+        (spread, sibling, early_parts, second_half, metric_factor)
+    )
+    early_parts.append(move(second_half, across(early)))
     own_rows = metric_late.astype(BF16)
-    second_half = collocation[:, half:]
-    spread, sibling, early_parts, own_block, own_rows, second_half, first = lax.optimization_barrier(
-        (spread, sibling, early_parts, own_block, own_rows, second_half, collocation)
-    )
-    early_parts.append(move(second_half, across(early)))
-    sib_block = move(own_block, swap)
-
-    if gen_count == 4:
-        bunches = [[(1, 1), (2, 1), (3, 1)], [(3, 2)], [(2, 2), (3, 3)]]
-        soon = 2
-    else:
-        bunches = [[(j, d) for j in range(d, gen_count)] for d in others]
-        soon = 1
-    bunch_of = {place: n for n, bunch in enumerate(bunches) for place in bunch}
-
-    def leftwards(n):
-        away = dict(bunches[n])
-        return lambda g, j, c: (j, j, c) if j in away and g == j - away[j] else None
-
-    left_own = [move(own_rows, leftwards(n)) for n in range(soon)]
-    spread, early_parts, first, sib_block, left_own[0] = lax.optimization_barrier(
-        (spread, early_parts, first, sib_block, left_own[0])
-    )
+    left_own = move(own_rows, lambda g, j, c: (g + 1, j, c) if j == g + 1 else None)
     own_parts = []
     for k in range(gen_count):
         piece = lax.dynamic_index_in_dim(spread, gen_index ^ chip ^ k, 0, keepdims=False)
         own_parts.append(move(piece, across(k)) if k else piece)
-    own_parts, first, own_block, sib_block, left_own = lax.optimization_barrier(
-        (own_parts, first, own_block, sib_block, left_own)
-    )
+    own_parts, sibling, metric_late = lax.optimization_barrier((own_parts, sibling, metric_late))
+
+    own_raw = raw_columns.transpose(1, 0, 2)
+    sib_raw = sibling.transpose(1, 0, 2)
+    pivot_rows = pivot_pairs // NORB - gen_index * orb_block
+    own_cols = pivot_pairs % NORB - fit_index * pair_block
+    sib_cols = pivot_pairs % NORB - (fit_index ^ 1) * pair_block
+    entries = pivot_entries(own_raw, sib_raw, pivot_rows, own_cols, sib_cols)
+
+    own_inverse = invert_block(jnp.stack([core, diagonal.astype(jnp.int32)]), metric_late)
+    own_parts, first, early_parts, left_own, own_inverse, entries = lax.optimization_barrier(
+        (own_parts, collocation, early_parts, left_own, own_inverse, entries)
+    )
+    upper = move(own_inverse, swap)
     first_side = {0: [collocation], early: early_parts}
     for k in others:
         if k != early:
@@ -425,16 +412,6 @@
             whole = lax.dynamic_update_slice_in_dim(whole, x[k], (gen_index ^ n) * part, 2)
         return [whole[None]]
 
-    own_raw = raw_columns.transpose(1, 0, 2)
-    sib_raw = sibling.transpose(1, 0, 2)
-    pivot_rows = pivot_pairs // NORB - gen_index * orb_block
-    own_cols = pivot_pairs % NORB - fit_index * pair_block
-    sib_cols = pivot_pairs % NORB - (fit_index ^ 1) * pair_block
-    entries = pivot_entries(own_raw, sib_raw, pivot_rows, own_cols, sib_cols)
-
-    own_inverse, upper = invert_blocks(
-        jnp.stack([core, diagonal.astype(jnp.int32)]), own_block, sib_block
-    )
     corner = jnp.dot(metric_factor[:, :points], upper, precision=HIGHEST)
     corner = -jnp.dot(own_inverse, corner, precision=HIGHEST)
     inverse_rows = split_hi_lo(
@@ -447,19 +424,16 @@
         )
     )
 
-    _, _, inverse_rows, left_rows, left_own = lax.optimization_barrier(
-        (all_parts, first_side, inverse_rows, own_rows, left_own)
-    )
-    for n in range(soon, len(bunches)):
-        left_own.append(move(left_rows, leftwards(n)))
-    left_sib = [move(left_own[n], swap) for n in range(soon)]
+    all_parts, first_side, entries, inverse_rows = lax.optimization_barrier(
+        (all_parts, first_side, entries, inverse_rows)
+    )
+    left_sib = move(left_own, swap)
 
     own_raw = own_raw.reshape(orb_block * vec_total, pair_block)
     sib_raw = sib_raw.reshape(orb_block * vec_total, pair_block)
     where = jnp.stack([core] + [gen_index ^ k for k in range(gen_count)])
     total = None
-    late = [k for k in others if k != early]
-    for group in [[0, early]] + [late[i : i + 2] for i in range(0, len(late), 2)]:
+    for group in [list(range(i, min(i + 4, gen_count))) for i in range(0, gen_count, 4)]:
         shares = project(
             where,
             own_raw,
@@ -469,32 +443,38 @@
             [second_side(k) for k in group],
             [k if part % 128 == 0 else 0 for k in group],
         )
-        if 0 in group:
-            entries, left_sib = lax.optimization_barrier((entries, left_sib))
+        if group[0] == 0:
+            shares, left_sib = lax.optimization_barrier((shares, left_sib))
         for k, share in zip(group, shares):
             if k:
                 share = move(share, across(k))
             total = share if total is None else total + share
     total = sum([move(total, lambda g, j, c, k=k: (g ^ k, j, c)) for k in others], total)
+
     at_core = core[None]
-    sib_total = move(total, swap)
-    solved = apply_weights(at_core, inverse_rows, total, sib_total)
     inverse_factor = factor_inverse(total)
+    rest, sib_rest = total, move(total, swap)
+    solved = apply_weights(at_core, inverse_rows, rest, sib_rest)
     turns = [solved]
-    for t in range(1, gen_count):
-        near = move(solved, lambda g, j, c: (t, t, c) if g == j == t - 1 else None)
-        near_sib = move(solved, lambda g, j, c: (t, t, 1 - c) if g == j == t - 1 else None)
-        if t == 1:
+    far = {}
+    for t in range(gen_count - 1):
+        near = move(solved, lambda g, j, c: (t + 1, t + 1, c) if g == j == t else None)
+        near_sib = move(solved, lambda g, j, c: (t + 1, t + 1, 1 - c) if g == j == t else None)
+        for z in range(t + 2, gen_count):
+            one = move(solved, lambda g, j, c: (t, z, c) if g == j == t else None)
+            far[t] = far[t] + one if t in far else one
+        if t == 0:
             near, inverse_factor = lax.optimization_barrier((near, inverse_factor))
-        lefts = []
-        for d in range(1, t + 1):
-            lefts += [left_own[bunch_of[t, d]], left_sib[bunch_of[t, d]]]
-        solved = turn(at_core, lefts, inverse_rows, near, near_sib, total, sib_total)
+        if t - 1 in far:
+            gone, _ = lax.optimization_barrier((far[t - 1], solved))
+            brought = apply_weights(at_core, [own_rows], gone, move(gone, swap))
+            brought = move(
+                brought, lambda g, j, c: (j, j, c) if g == t - 1 and j >= t + 1 else None
+            )
+            rest = rest[:, :points] - brought
+            sib_rest = move(rest, swap)
+        solved = turn(at_core, (left_own, left_sib), inverse_rows, near, near_sib, rest, sib_rest)
         turns.append(solved)
-        if t == 1:
-            for n in range(soon, len(bunches)):
-                _, left_own[n] = lax.optimization_barrier((solved, left_own[n]))
-                left_sib.append(move(left_own[n], swap))
 
     which = jnp.stack([jnp.where(diagonal, gen_index, -1)] + [gen_index ^ k for k in range(gen_count)])
     shares = combine(which, inverse_factor, turns, vec_dev)

time: 181 us -> 164 us (0.906)
  local copies, waits for them, and re-layouts: 20.7 us -> 10.2 us
  starting transfers between devices: 46 us -> 42 us
  other arithmetic: 8.13 us -> 4.84 us
  waiting for transfers between devices: 60.8 us -> 63.9 us
  Pallas kernels: 37.9 us -> 35 us
    unnamed x68 -> x36, local copies, waits for them, and re-layouts: 15.6 us -> 6.26 us
    pallas_call x4, Pallas kernels: 19.1 us -> 13.1 us  [the longest x3 7.71 us: turn(): pl.pallas_call(turn_kernel, in_specs=[pl.BlockSpec(memory_space=pltpu.SME...]
    ppermute x37 -> x42, starting transfers between devices: 46 us -> 42 us  [move(): return lax.ppermute(value, BOTH, pairs)]
    pallas_call x1 -> x3, Pallas kernels: 0.65 us -> 3.85 us  [apply_weights(): pl.pallas_call(apply_kernel, in_specs=[pl.BlockSpec(memory_space=pltpu.SM...]
    ppermute x37 -> x42, waiting for transfers between devices: 60.8 us -> 63.9 us  [move(): return lax.ppermute(value, BOTH, pairs)]
    convert_element_type x1, other arithmetic: 3.51 us -> 1.14 us  [on_device(): own_rows = metric_late.astype(BF16)]
    another operation x1, other arithmetic: 2.05 us -> 0.07 us  [on_device(): spread = jnp.stack(spread)]
    slice x1, local copies, waits for them, and re-layouts: 0.03 us -> 1.96 us  [on_device(): second_half = collocation[:, half:]]
  transfers between devices with their start and end apart: 37 -> 42, of which waited for: 15 -> 21; matrix products, arithmetic and copies ran while one was open for 10% -> 8% of each run, Pallas kernels for 16% -> 15%
where the time goes in v7:
time: 164 us; the launch traced here: 163 us
  waiting for transfers between devices  63.9 us (39%)
  starting transfers between devices  42 us (26%)
  Pallas kernels  35 us (21%)
  local copies, waits for them, and re-layouts  10.2 us (6%)
  matrix products  6.59 us (4%)
  other arithmetic  4.84 us (3%)
    ppermute x42, waiting for transfers between devices, move(): return lax.ppermute(value, BOTH, pairs)  63.9 us
    ppermute x42, starting transfers between devices, move(): return lax.ppermute(value, BOTH, pairs)  42 us
    pallas_call x1, Pallas kernels, project(): pl.pallas_call(kernel, grid_spec=pltpu.PrefetchScalarGridSpec(num_scalar_...  11.8 us
    pallas_call x3, Pallas kernels, turn(): pl.pallas_call(turn_kernel, in_specs=[pl.BlockSpec(memory_space=pltpu.SME...  7.71 us
    unnamed x36, local copies, waits for them, and re-layouts  6.26 us
    pallas_call x1, Pallas kernels, invert_block(): pl.pallas_call(invert_kernel, grid_spec=pltpu.PrefetchScalarGridSpec(num_...  5.35 us
    dot_general x1, matrix products, on_device(): corner = jnp.dot(metric_factor[:, :points], upper, precision=HIGHEST)  4.69 us
    pallas_call x3, Pallas kernels, apply_weights(): pl.pallas_call(apply_kernel, in_specs=[pl.BlockSpec(memory_space=pltpu.SM...  3.85 us
  transfers between devices with their start and end apart: 42, of which 21 were waited for; matrix products, arithmetic and copies ran while one was open for 8% of the time, Pallas kernels for 15%

profile of v7, /device:TPU:24, one launch (start us, length us, event | category | flops | bytes accessed | tf_op | source)
XLA Modules:
  0.0 163.1 jit_solution(15838415892075063760)
XLA Ops:
  0.0 2.0 %fusion.5 = (bf16[500,256]{1,0:T(8,128)(2,1)}, bf16[500,256]{1,0:T(8,128)(2,1)S(1)}) fusion(bf16[500,512]{1,0:T(8,128)(2,1)} %rest_0_), kind=kLoop, calls=%fused_computation.29 | loop fusion | bytes 1024000 | tf_op jit(solution)/shard_map/slice | solution.py:374
  3.6 1.6 collective-permute-start
  7.1 2.3 %collective-permute-done = bf16[2,250,128]{2,1,0:T(8,128)(2,1)S(1)} collective-permute-done((bf16[2,250,128]{2,1,0:T(8,128)(2,1)S(1)}, bf16[2,250,128]{2,1,0:T(8,128)(2,1)S(1)}, u32[]{:S(2)}, u32[]{:S(2)}) %collective-permute-start) | collective-permute-done | bytes 128032 | tf_op jit(solution)/shard_map/ppermute | solution.py:30
  9.5 3.7 %collective-permute-done.1 = bf16[2,250,128]{2,1,0:T(8,128)(2,1)S(1)} collective-permute-done((bf16[2,250,128]{2,1,0:T(8,128)(2,1)S(1)}, bf16[2,250,128]{2,1,0:T(8,128)(2,1)S(1)}, u32[]{:S(2)}, u32[]{:S(2)}) %collective-permute-start.1) | collective-permute-done | bytes 128032 | tf_op jit(solution)/shard_map/ppermute | solution.py:30
  13.2 3.5 %collective-permute-done.4.rest_2_ = bf16[500,256]{1,0:T(8,128)(2,1)S(1)} collective-permute-done((bf16[500,256]{1,0:T(8,128)(2,1)S(1)}, bf16[500,256]{1,0:T(8,128)(2,1)S(1)}, u32[]{:S(2)}, u32[]{:S(2)}) %collective-permute-start.4) | collective-permute-done | bytes 256032 | tf_op jit(solution)/shard_map/ppermute | solution.py:30
  17.9 1.6 %collective-permute-start.9 = (bf16[512,1024]{1,0:T(8,128)(2,1)}, bf16[512,1024]{1,0:T(8,128)(2,1)}, u32[]{:S(2)}, u32[]{:S(2)}) collective-permute-start(bf16[512,1024]{1,0:T(8,128)(2,1)} %convert_element_type.10.refs_0_), channel_id=1, source_target_pairs={{2,10},{3,11},{12,20},{13,21},{22,30},{23,31}} | collective-permute-start | bytes 3145736 | tf_op jit(solution)/shard_map/ppermute | solution.py:30
  19.7 2.4 %collective-permute-start.6 = (bf16[2,250,128]{2,1,0:T(8,128)(2,1)S(1)}, bf16[2,250,128]{2,1,0:T(8,128)(2,1)}, u32[]{:S(2)}, u32[]{:S(2)}) collective-permute-start(bf16[2,250,128]{2,1,0:T(8,128)(2,1)S(1)} %get-tuple-element.108), channel_id=1, source_target_pairs={{0,4},{1,5},{2,6},{3,7},{4,0},{5,1},{6,2},{7,3},{8,12},{9,13},{10,... | collective-permute-start | bytes 384008 | tf_op jit(solution)/shard_map/ppermute | solution.py:30
  22.0 2.0 %collective-permute-start.7 = (bf16[2,250,128]{2,1,0:T(8,128)(2,1)S(1)}, bf16[2,250,128]{2,1,0:T(8,128)(2,1)}, u32[]{:S(2)}, u32[]{:S(2)}) collective-permute-start(bf16[2,250,128]{2,1,0:T(8,128)(2,1)S(1)} %get-tuple-element.107), channel_id=1, source_target_pairs={{0,6},{1,7},{2,4},{3,5},{4,2},{5,3},{6,0},{7,1},{8,14},{9,15},{10,... | collective-permute-start | bytes 384008 | tf_op jit(solution)/shard_map/ppermute | solution.py:30
  26.1 1.6 %collective-permute-done.5 = bf16[2,250,128]{2,1,0:T(8,128)(2,1)} collective-permute-done((bf16[2,250,128]{2,1,0:T(8,128)(2,1)S(1)}, bf16[2,250,128]{2,1,0:T(8,128)(2,1)}, u32[]{:S(2)}, u32[]{:S(2)}) %collective-permute-start.5) | collective-permute-done | bytes 128032 | tf_op jit(solution)/shard_map/ppermute | solution.py:30
  27.8 10.5 %collective-permute-done.6 = bf16[2,250,128]{2,1,0:T(8,128)(2,1)} collective-permute-done((bf16[2,250,128]{2,1,0:T(8,128)(2,1)S(1)}, bf16[2,250,128]{2,1,0:T(8,128)(2,1)}, u32[]{:S(2)}, u32[]{:S(2)}) %collective-permute-start.6) | collective-permute-done | bytes 128032 | tf_op jit(solution)/shard_map/ppermute | solution.py:30
  38.3 2.8 %pivot_entries.1.entries_ref = f32[8,8]{1,0:T(8,128)} custom-call(s32[8]{0:T(128)} %get-tuple-element.118.row_ref, bf16[500,8,250]{2,1,0:T(8,128)(2,1)} %bitcast.33, bf16[500,8,250]{2,1,0:T(8,128)(2,1)} %bitcast.16.sib_ref, s32[8]{0:T(128)} %get-tuple-element.119.own_col_ref, s32[8]{0:T(128)} %get-tuple-element.117.sib_col_ref), custom_call_target="tpu_custom_call" | custom-call | tf_op jit(solution)/shard_map/pivot_entries/pallas_call | solution.py:63
  41.1 5.3 %invert_block.1 = f32[512,512]{1,0:T(8,128)S(1)} custom-call(s32[2]{0:T(128)S(1)} %pad_add_fusion.where_ref, f32[512,1024]{1,0:T(8,128)S(1)} %copy-done), custom_call_target="tpu_custom_call" | custom-call | flops 4294967296 | bytes 4194304 | tf_op jit(solution)/shard_map/invert_block/pallas_call | solution.py:230
  47.8 1.7 %collective-permute-start.10 = (bf16[4,2,250,128]{3,2,1,0:T(8,128)(2,1)S(1)}, bf16[4,2,250,128]{3,2,1,0:T(8,128)(2,1)S(1)}, u32[]{:S(2)}, u32[]{:S(2)}) collective-permute-start(bf16[4,2,250,128]{3,2,1,0:T(8,128)(2,1)S(1)} %pad_maximum_fusion.2.rest_5_.rest_9_.rest_13_.rest_17_), channel_id=1, source_target_pairs={{0,8},{1,9},{2,10},{3,11},{4,12},{5,13},{6,14},{7,15},{8,0},{9,1},... | collective-permute-start | bytes 1536008 | tf_op jit(solution)/shard_map/ppermute | solution.py:30
  49.5 2.7 %collective-permute-start.11 = (bf16[4,2,250,128]{3,2,1,0:T(8,128)(2,1)S(1)}, bf16[4,2,250,128]{3,2,1,0:T(8,128)(2,1)S(1)}, u32[]{:S(2)}, u32[]{:S(2)}) collective-permute-start(bf16[4,2,250,128]{3,2,1,0:T(8,128)(2,1)S(1)} %pad_maximum_fusion.2.rest_5_.rest_9_.rest_13_.rest_17_), channel_id=1, source_target_pairs={{0,16},{1,17},{2,18},{3,19},{4,20},{5,21},{6,22},{7,23},{8,24},{9,... | collective-permute-start | bytes 1536008 | tf_op jit(solution)/shard_map/ppermute | solution.py:30
  53.6 3.4 %collective-permute-start.13 = (bf16[500,512]{1,0:T(8,128)(2,1)}, bf16[500,512]{1,0:T(8,128)(2,1)S(1)}, u32[]{:S(2)}, u32[]{:S(2)}) collective-permute-start(bf16[500,512]{1,0:T(8,128)(2,1)} %rest_0_), channel_id=1, source_target_pairs={{0,2},{1,3},{2,0},{3,1},{4,6},{5,7},{6,4},{7,5},{8,10},{9,11},{10,... | collective-permute-start | bytes 1536008 | tf_op jit(solution)/shard_map/ppermute | solution.py:30
  58.5 4.7 %fusion.2 = f32[512,512]{1,0:T(8,128)S(1)} fusion(f32[512,512]{1,0:T(8,128)} %collective-permute-done.15, f32[512,1024]{1,0:T(8,128)S(1)} %copy-done), kind=kOutput, calls=%fused_computation.6 | convolution fusion | flops 1610612736 | bytes 3145728 | tf_op jit(solution)/shard_map/dot_general | solution.py:415
  63.3 1.9 %fusion.1 = f32[512,512]{1,0:T(8,128)S(1)} fusion(f32[512,512]{1,0:T(8,128)S(1)} %invert_block.1, f32[512,512]{1,0:T(8,128)S(1)} %fusion.2, pred[]{:T(512)S(6)} %eq.13), kind=kOutput, calls=%fused_computation.5 | convolution fusion | flops 1611137024 | bytes 3145729 | tf_op jit(solution)/shard_map/dot_general | solution.py:416
  65.7 9.6 %collective-permute-done.11.rest_7_.rest_11_.rest_15_.rest_19_ = bf16[4,2,250,128]{3,2,1,0:T(8,128)(2,1)S(1)} collective-permute-done((bf16[4,2,250,128]{3,2,1,0:T(8,128)(2,1)S(1)}, bf16[4,2,250,128]{3,2,1,0:T(8,128)(2,1)S(1)}, u32[]{:S(2)}, u32[]{:S(2)}) %collective-permute-start.11) | collective-permute-done | bytes 512032 | tf_op jit(solution)/shard_map/ppermute | solution.py:30
  75.3 1.8 %collective-permute-done.12.rest_8_.rest_12_.rest_16_.rest_20_ = bf16[4,2,250,128]{3,2,1,0:T(8,128)(2,1)S(1)} collective-permute-done((bf16[4,2,250,128]{3,2,1,0:T(8,128)(2,1)S(1)}, bf16[4,2,250,128]{3,2,1,0:T(8,128)(2,1)S(1)}, u32[]{:S(2)}, u32[]{:S(2)}) %collective-permute-start.12) | collective-permute-done | bytes 512032 | tf_op jit(solution)/shard_map/ppermute | solution.py:30
  77.1 4.1 %collective-permute-done.14.rest_4_ = bf16[500,512]{1,0:T(8,128)(2,1)S(1)} collective-permute-done((bf16[500,512]{1,0:T(8,128)(2,1)S(1)}, bf16[500,512]{1,0:T(8,128)(2,1)S(1)}, u32[]{:S(2)}, u32[]{:S(2)}) %collective-permute-start.14) | collective-permute-done | bytes 512032 | tf_op jit(solution)/shard_map/ppermute | solution.py:30
  81.2 11.8 %project.1 = (f32[8,640]{1,0:T(8,128)S(1)}, f32[8,640]{1,0:T(8,128)S(1)}, f32[8,640]{1,0:T(8,128)S(1)}, f32[8,640]{1,0:T(8,128)S(1)}) custom-call(s32[5]{0:T(128)S(1)} %stack.85.where_ref, bf16[4000,250]{1,0:T(8,128)(2,1)S(1)} %bitcast.34, bf16[4000,250]{1,0:T(8,128)(2,1)} %bitcast.22.sib_ref, f32[8,8]{1,0:T(8,128)S(1)} %copy-done.13, ...), custom_call_target="tpu_custom_call" | custom-call | flops 8192000000 | bytes 1048576 | tf_op jit(solution)/shard_map/project/pallas_call | solution.py:170
  93.1 2.9 %collective-permute-start.18 = (f32[8,640]{1,0:T(8,128)S(1)}, f32[8,640]{1,0:T(8,128)S(1)}, u32[]{:S(2)}, u32[]{:S(2)}) collective-permute-start(f32[8,640]{1,0:T(8,128)S(1)} %get-tuple-element.94), channel_id=1, source_target_pairs={{0,4},{1,5},{2,6},{3,7},{4,0},{5,1},{6,2},{7,3},{8,12},{9,13},{10,... | collective-permute-start | bytes 61448 | tf_op jit(solution)/shard_map/ppermute | solution.py:30
  97.9 3.8 %collective-permute-done.19 = f32[8,640]{1,0:T(8,128)S(1)} collective-permute-done((f32[8,640]{1,0:T(8,128)S(1)}, f32[8,640]{1,0:T(8,128)S(1)}, u32[]{:S(2)}, u32[]{:S(2)}) %collective-permute-start.19) | collective-permute-done | bytes 20512 | tf_op jit(solution)/shard_map/ppermute | solution.py:30
  106.1 2.4 %collective-permute-done.22 = f32[8,640]{1,0:T(8,128)S(1)} collective-permute-done((f32[8,640]{1,0:T(8,128)S(1)}, f32[8,640]{1,0:T(8,128)S(1)}, u32[]{:S(2)}, u32[]{:S(2)}) %collective-permute-start.22) | collective-permute-done | bytes 20512 | tf_op jit(solution)/shard_map/ppermute | solution.py:30
  113.8 2.0 %factor_inverse.1.inverse_ref = f32[8,8]{1,0:T(8,128)} custom-call(f32[8,640]{1,0:T(8,128)} %copy-done.7), custom_call_target="tpu_custom_call" | custom-call | tf_op jit(solution)/shard_map/factor_inverse/pallas_call | solution.py:98
  115.7 3.5 %collective-permute-done.29 = f32[8,512]{1,0:T(8,128)S(1)} collective-permute-done((f32[8,512]{1,0:T(8,128)S(1)}, f32[8,512]{1,0:T(8,128)S(1)}, u32[]{:S(2)}, u32[]{:S(2)}) %collective-permute-start.29) | collective-permute-done | bytes 16416 | tf_op jit(solution)/shard_map/ppermute | solution.py:30
  122.4 2.6 %turn.3.refs_1_ = f32[8,512]{1,0:T(8,128)S(1)} custom-call(s32[1]{0:T(128)} %bitcast.5.where_ref, bf16[512,1024]{1,0:T(8,128)(2,1)} %collective-permute-done.9.refs_0_, bf16[512,1024]{1,0:T(8,128)(2,1)S(1)} %copy-done.15, bf16[512,1024]{1,0:T(8,128)(2,1)S(1)} %copy-done.4, bf16[512,1024]{1,0:T(8,128)(2,1)S(1)} %get-tuple-element.76.refs_1_.refs_3_, ...), custom_call_target="tpu_custom_call" | custom-call | flops 2147483648 | bytes 4194304 | tf_op jit(solution)/shard_map/turn/pallas_call | solution.py:306
  126.3 1.6 apply_weights.4
  131.8 2.6 %turn.4.refs_2_ = f32[8,512]{1,0:T(8,128)S(1)} custom-call(s32[1]{0:T(128)} %bitcast.5.where_ref, bf16[512,1024]{1,0:T(8,128)(2,1)} %collective-permute-done.9.refs_0_, bf16[512,1024]{1,0:T(8,128)(2,1)S(1)} %copy-done.15, bf16[512,1024]{1,0:T(8,128)(2,1)S(1)} %copy-done.5, bf16[512,1024]{1,0:T(8,128)(2,1)S(1)} %get-tuple-element.76.refs_1_.refs_3_, ...), custom_call_target="tpu_custom_call" | custom-call | flops 2147483648 | bytes 4194304 | tf_op jit(solution)/shard_map/turn/pallas_call | solution.py:306
  135.7 1.6 apply_weights.5
  143.0 2.6 %turn.5.refs_3_ = f32[8,512]{1,0:T(8,128)S(1)} custom-call(s32[1]{0:T(128)} %bitcast.5.where_ref, bf16[512,1024]{1,0:T(8,128)(2,1)} %collective-permute-done.9.refs_0_, bf16[512,1024]{1,0:T(8,128)(2,1)S(1)} %copy-done.16, bf16[512,1024]{1,0:T(8,128)(2,1)S(1)} %copy-done.6, bf16[512,1024]{1,0:T(8,128)(2,1)S(1)} %get-tuple-element.76.refs_1_.refs_3_, ...), custom_call_target="tpu_custom_call" | custom-call | flops 2147483648 | bytes 4194304 | tf_op jit(solution)/shard_map/turn/pallas_call | solution.py:306
  150.4 11.5 %collective-permute-done.41 = f32[2,512]{1,0:T(2,128)S(1)} collective-permute-done((f32[2,512]{1,0:T(2,128)}, f32[2,512]{1,0:T(2,128)S(1)}, u32[]{:S(2)}, u32[]{:S(2)}) %collective-permute-start.41) | collective-permute-done | bytes 4128 | tf_op jit(solution)/shard_map/ppermute | solution.py:30
  (120 shorter events, 44.5 us)
Async XLA Ops:
  0.0 16.8 %collective-permute-start.3 = (bf16[8,500,250]{2,0,1:T(8,128)(2,1)}, bf16[8,500,250]{2,0,1:T(8,128)(2,1)}, u32[]{:S(2)}, u32[]{:S(2)}) collective-permute-start(bf16[8,500,250]{2,0,1:T(8,128)(2,1)} %param.4), channel_id=1, source_target_pairs={{0,1},{1,0},{2,3},{3,2},{4,5},{5,4},{6,7},{7,6},{8,9},{9,8},{10,11... | collective-permute-start | bytes 6000008 | tf_op jit(solution)/shard_map/ppermute | solution.py:30
  2.0 14.8 %collective-permute-start.4 = (bf16[500,256]{1,0:T(8,128)(2,1)S(1)}, bf16[500,256]{1,0:T(8,128)(2,1)S(1)}, u32[]{:S(2)}, u32[]{:S(2)}) collective-permute-start(bf16[500,256]{1,0:T(8,128)(2,1)S(1)} %get-tuple-element.116), channel_id=1, source_target_pairs={{0,4},{1,5},{2,6},{3,7},{4,0},{5,1},{6,2},{7,3},{8,12},{9,13},{10,... | collective-permute-start | bytes 768008 | tf_op jit(solution)/shard_map/ppermute | solution.py:30
  3.6 5.9 %collective-permute-start = (bf16[2,250,128]{2,1,0:T(8,128)(2,1)S(1)}, bf16[2,250,128]{2,1,0:T(8,128)(2,1)S(1)}, u32[]{:S(2)}, u32[]{:S(2)}) collective-permute-start(bf16[2,250,128]{2,1,0:T(8,128)(2,1)S(1)} %get-tuple-element.114), channel_id=1, source_target_pairs={{0,8},{1,9},{2,10},{3,11},{4,12},{5,13},{6,14},{7,15},{8,0},{9,1},... | collective-permute-start | bytes 384008 | tf_op jit(solution)/shard_map/ppermute | solution.py:30
  5.2 8.0 %collective-permute-start.1 = (bf16[2,250,128]{2,1,0:T(8,128)(2,1)S(1)}, bf16[2,250,128]{2,1,0:T(8,128)(2,1)S(1)}, u32[]{:S(2)}, u32[]{:S(2)}) collective-permute-start(bf16[2,250,128]{2,1,0:T(8,128)(2,1)S(1)} %get-tuple-element.113), channel_id=1, source_target_pairs={{0,16},{1,17},{2,18},{3,19},{4,20},{5,21},{6,22},{7,23},{8,24},{9,... | collective-permute-start | bytes 384008 | tf_op jit(solution)/shard_map/ppermute | solution.py:30
  6.7 6.5 %collective-permute-start.2 = (bf16[2,250,128]{2,1,0:T(8,128)(2,1)S(1)}, bf16[2,250,128]{2,1,0:T(8,128)(2,1)S(1)}, u32[]{:S(2)}, u32[]{:S(2)}) collective-permute-start(bf16[2,250,128]{2,1,0:T(8,128)(2,1)S(1)} %get-tuple-element.112), channel_id=1, source_target_pairs={{0,24},{1,25},{2,26},{3,27},{4,28},{5,29},{6,30},{7,31},{8,16},{9,... | collective-permute-start | bytes 384008 | tf_op jit(solution)/shard_map/ppermute | solution.py:30
  17.9 28.6 %collective-permute-start.9 = (bf16[512,1024]{1,0:T(8,128)(2,1)}, bf16[512,1024]{1,0:T(8,128)(2,1)}, u32[]{:S(2)}, u32[]{:S(2)}) collective-permute-start(bf16[512,1024]{1,0:T(8,128)(2,1)} %convert_element_type.10.refs_0_), channel_id=1, source_target_pairs={{2,10},{3,11},{12,20},{13,21},{22,30},{23,31}} | collective-permute-start | bytes 3145736 | tf_op jit(solution)/shard_map/ppermute | solution.py:30
  19.6 8.2 %collective-permute-start.5 = (bf16[2,250,128]{2,1,0:T(8,128)(2,1)S(1)}, bf16[2,250,128]{2,1,0:T(8,128)(2,1)}, u32[]{:S(2)}, u32[]{:S(2)}) collective-permute-start(bf16[2,250,128]{2,1,0:T(8,128)(2,1)S(1)} %get-tuple-element.109), channel_id=1, source_target_pairs={{0,2},{1,3},{2,0},{3,1},{4,6},{5,7},{6,4},{7,5},{8,10},{9,11},{10,... | collective-permute-start | bytes 384008 | tf_op jit(solution)/shard_map/ppermute | solution.py:30
  19.7 18.6 %collective-permute-start.6 = (bf16[2,250,128]{2,1,0:T(8,128)(2,1)S(1)}, bf16[2,250,128]{2,1,0:T(8,128)(2,1)}, u32[]{:S(2)}, u32[]{:S(2)}) collective-permute-start(bf16[2,250,128]{2,1,0:T(8,128)(2,1)S(1)} %get-tuple-element.108), channel_id=1, source_target_pairs={{0,4},{1,5},{2,6},{3,7},{4,0},{5,1},{6,2},{7,3},{8,12},{9,13},{10,... | collective-permute-start | bytes 384008 | tf_op jit(solution)/shard_map/ppermute | solution.py:30
  22.0 16.3 %collective-permute-start.7 = (bf16[2,250,128]{2,1,0:T(8,128)(2,1)S(1)}, bf16[2,250,128]{2,1,0:T(8,128)(2,1)}, u32[]{:S(2)}, u32[]{:S(2)}) collective-permute-start(bf16[2,250,128]{2,1,0:T(8,128)(2,1)S(1)} %get-tuple-element.107), channel_id=1, source_target_pairs={{0,6},{1,7},{2,4},{3,5},{4,2},{5,3},{6,0},{7,1},{8,14},{9,15},{10,... | collective-permute-start | bytes 384008 | tf_op jit(solution)/shard_map/ppermute | solution.py:30
  24.7 21.7 %collective-permute-start.8 = (bf16[500,256]{1,0:T(8,128)(2,1)}, bf16[500,256]{1,0:T(8,128)(2,1)}, u32[]{:S(2)}, u32[]{:S(2)}) collective-permute-start(bf16[500,256]{1,0:T(8,128)(2,1)} %get-tuple-element.63), channel_id=1, source_target_pairs={{0,4},{1,5},{2,6},{3,7},{4,0},{5,1},{6,2},{7,3},{8,12},{9,13},{10,... | collective-permute-start | bytes 768008 | tf_op jit(solution)/shard_map/ppermute | solution.py:30
  46.5 10.5 %collective-permute-start.15 = (f32[512,512]{1,0:T(8,128)S(1)}, f32[512,512]{1,0:T(8,128)}, u32[]{:S(2)}, u32[]{:S(2)}) collective-permute-start(f32[512,512]{1,0:T(8,128)S(1)} %invert_block.1), channel_id=1, source_target_pairs={{0,1},{1,0},{2,3},{3,2},{4,5},{5,4},{6,7},{7,6},{8,9},{9,8},{10,11... | collective-permute-start | bytes 3145736 | tf_op jit(solution)/shard_map/ppermute | solution.py:30
  47.8 15.4 %collective-permute-start.10 = (bf16[4,2,250,128]{3,2,1,0:T(8,128)(2,1)S(1)}, bf16[4,2,250,128]{3,2,1,0:T(8,128)(2,1)S(1)}, u32[]{:S(2)}, u32[]{:S(2)}) collective-permute-start(bf16[4,2,250,128]{3,2,1,0:T(8,128)(2,1)S(1)} %pad_maximum_fusion.2.rest_5_.rest_9_.rest_13_.rest_17_), channel_id=1, source_target_pairs={{0,8},{1,9},{2,10},{3,11},{4,12},{5,13},{6,14},{7,15},{8,0},{9,1},... | collective-permute-start | bytes 1536008 | tf_op jit(solution)/shard_map/ppermute | solution.py:30
  49.5 25.7 %collective-permute-start.11 = (bf16[4,2,250,128]{3,2,1,0:T(8,128)(2,1)S(1)}, bf16[4,2,250,128]{3,2,1,0:T(8,128)(2,1)S(1)}, u32[]{:S(2)}, u32[]{:S(2)}) collective-permute-start(bf16[4,2,250,128]{3,2,1,0:T(8,128)(2,1)S(1)} %pad_maximum_fusion.2.rest_5_.rest_9_.rest_13_.rest_17_), channel_id=1, source_target_pairs={{0,16},{1,17},{2,18},{3,19},{4,20},{5,21},{6,22},{7,23},{8,24},{9,... | collective-permute-start | bytes 1536008 | tf_op jit(solution)/shard_map/ppermute | solution.py:30
  52.2 24.9 %collective-permute-start.12 = (bf16[4,2,250,128]{3,2,1,0:T(8,128)(2,1)S(1)}, bf16[4,2,250,128]{3,2,1,0:T(8,128)(2,1)S(1)}, u32[]{:S(2)}, u32[]{:S(2)}) collective-permute-start(bf16[4,2,250,128]{3,2,1,0:T(8,128)(2,1)S(1)} %pad_maximum_fusion.2.rest_5_.rest_9_.rest_13_.rest_17_), channel_id=1, source_target_pairs={{0,24},{1,25},{2,26},{3,27},{4,28},{5,29},{6,30},{7,31},{8,16},{9,... | collective-permute-start | bytes 1536008 | tf_op jit(solution)/shard_map/ppermute | solution.py:30
  53.6 23.5 %collective-permute-start.13 = (bf16[500,512]{1,0:T(8,128)(2,1)}, bf16[500,512]{1,0:T(8,128)(2,1)S(1)}, u32[]{:S(2)}, u32[]{:S(2)}) collective-permute-start(bf16[500,512]{1,0:T(8,128)(2,1)} %rest_0_), channel_id=1, source_target_pairs={{0,2},{1,3},{2,0},{3,1},{4,6},{5,7},{6,4},{7,5},{8,10},{9,11},{10,... | collective-permute-start | bytes 1536008 | tf_op jit(solution)/shard_map/ppermute | solution.py:30
  57.1 24.1 %collective-permute-start.14 = (bf16[500,512]{1,0:T(8,128)(2,1)S(1)}, bf16[500,512]{1,0:T(8,128)(2,1)S(1)}, u32[]{:S(2)}, u32[]{:S(2)}) collective-permute-start(bf16[500,512]{1,0:T(8,128)(2,1)S(1)} %copy-done.1), channel_id=1, source_target_pairs={{0,6},{1,7},{2,4},{3,5},{4,2},{5,3},{6,0},{7,1},{8,14},{9,15},{10,... | collective-permute-start | bytes 1536008 | tf_op jit(solution)/shard_map/ppermute | solution.py:30
  63.2 29.8 %collective-permute-start.16 = (bf16[512,1024]{1,0:T(8,128)(2,1)}, bf16[512,1024]{1,0:T(8,128)(2,1)S(1)}, u32[]{:S(2)}, u32[]{:S(2)}) collective-permute-start(bf16[512,1024]{1,0:T(8,128)(2,1)} %collective-permute-done.9.refs_0_), channel_id=1, source_target_pairs={{0,1},{1,0},{2,3},{3,2},{4,5},{5,4},{6,7},{7,6},{8,9},{9,8},{10,11... | collective-permute-start | bytes 3145736 | tf_op jit(solution)/shard_map/ppermute | solution.py:30
  93.1 4.5 %collective-permute-start.17 = (f32[8,640]{1,0:T(8,128)S(1)}, f32[8,640]{1,0:T(8,128)S(1)}, u32[]{:S(2)}, u32[]{:S(2)}) collective-permute-start(f32[8,640]{1,0:T(8,128)S(1)} %get-tuple-element.93), channel_id=1, source_target_pairs={{0,2},{1,3},{2,0},{3,1},{4,6},{5,7},{6,4},{7,5},{8,10},{9,11},{10,... | collective-permute-start | bytes 61448 | tf_op jit(solution)/shard_map/ppermute | solution.py:30
  93.1 4.7 %collective-permute-start.18 = (f32[8,640]{1,0:T(8,128)S(1)}, f32[8,640]{1,0:T(8,128)S(1)}, u32[]{:S(2)}, u32[]{:S(2)}) collective-permute-start(f32[8,640]{1,0:T(8,128)S(1)} %get-tuple-element.94), channel_id=1, source_target_pairs={{0,4},{1,5},{2,6},{3,7},{4,0},{5,1},{6,2},{7,3},{8,12},{9,13},{10,... | collective-permute-start | bytes 61448 | tf_op jit(solution)/shard_map/ppermute | solution.py:30
  96.1 5.6 %collective-permute-start.19 = (f32[8,640]{1,0:T(8,128)S(1)}, f32[8,640]{1,0:T(8,128)S(1)}, u32[]{:S(2)}, u32[]{:S(2)}) collective-permute-start(f32[8,640]{1,0:T(8,128)S(1)} %get-tuple-element.95), channel_id=1, source_target_pairs={{0,6},{1,7},{2,4},{3,5},{4,2},{5,3},{6,0},{7,1},{8,14},{9,15},{10,... | collective-permute-start | bytes 61448 | tf_op jit(solution)/shard_map/ppermute | solution.py:30
  101.7 3.8 %collective-permute-start.20 = (f32[8,640]{1,0:T(8,128)S(1)}, f32[8,640]{1,0:T(8,128)S(1)}, u32[]{:S(2)}, u32[]{:S(2)}) collective-permute-start(f32[8,640]{1,0:T(8,128)S(1)} %add_add_fusion.1), channel_id=1, source_target_pairs={{0,8},{1,9},{2,10},{3,11},{4,12},{5,13},{6,14},{7,15},{8,0},{9,1},... | collective-permute-start | bytes 61448 | tf_op jit(solution)/shard_map/ppermute | solution.py:30
  102.3 3.8 %collective-permute-start.21 = (f32[8,640]{1,0:T(8,128)S(1)}, f32[8,640]{1,0:T(8,128)S(1)}, u32[]{:S(2)}, u32[]{:S(2)}) collective-permute-start(f32[8,640]{1,0:T(8,128)S(1)} %add_add_fusion.1), channel_id=1, source_target_pairs={{0,16},{1,17},{2,18},{3,19},{4,20},{5,21},{6,22},{7,23},{8,24},{9,... | collective-permute-start | bytes 61448 | tf_op jit(solution)/shard_map/ppermute | solution.py:30
  103.8 4.7 %collective-permute-start.22 = (f32[8,640]{1,0:T(8,128)S(1)}, f32[8,640]{1,0:T(8,128)S(1)}, u32[]{:S(2)}, u32[]{:S(2)}) collective-permute-start(f32[8,640]{1,0:T(8,128)S(1)} %add_add_fusion.1), channel_id=1, source_target_pairs={{0,24},{1,25},{2,26},{3,27},{4,28},{5,29},{6,30},{7,31},{8,16},{9,... | collective-permute-start | bytes 61448 | tf_op jit(solution)/shard_map/ppermute | solution.py:30
  110.4 5.3 %collective-permute-start.24 = (f32[8,512]{1,0:T(8,128)S(1)}, f32[8,512]{1,0:T(8,128)S(1)}, u32[]{:S(2)}, u32[]{:S(2)}) collective-permute-start(f32[8,512]{1,0:T(8,128)S(1)} %apply_weights.3.refs_0_), channel_id=1, source_target_pairs={{0,10},{1,11}} | collective-permute-start | bytes 49160 | tf_op jit(solution)/shard_map/ppermute | solution.py:30
  111.1 4.6 %collective-permute-start.28 = (f32[8,512]{1,0:T(8,128)S(1)}, f32[8,512]{1,0:T(8,128)S(1)}, u32[]{:S(2)}, u32[]{:S(2)}) collective-permute-start(f32[8,512]{1,0:T(8,128)S(1)} %apply_weights.3.refs_0_), channel_id=1, source_target_pairs={{0,4},{1,5}} | collective-permute-start | bytes 49160 | tf_op jit(solution)/shard_map/ppermute | solution.py:30
  111.8 7.4 %collective-permute-start.29 = (f32[8,512]{1,0:T(8,128)S(1)}, f32[8,512]{1,0:T(8,128)S(1)}, u32[]{:S(2)}, u32[]{:S(2)}) collective-permute-start(f32[8,512]{1,0:T(8,128)S(1)} %apply_weights.3.refs_0_), channel_id=1, source_target_pairs={{0,6},{1,7}} | collective-permute-start | bytes 49160 | tf_op jit(solution)/shard_map/ppermute | solution.py:30
  113.1 6.1 %collective-permute-start.25 = (f32[8,512]{1,0:T(8,128)S(1)}, f32[8,512]{1,0:T(8,128)S(1)}, u32[]{:S(2)}, u32[]{:S(2)}) collective-permute-start(f32[8,512]{1,0:T(8,128)S(1)} %apply_weights.3.refs_0_), channel_id=1, source_target_pairs={{0,11},{1,10}} | collective-permute-start | bytes 49160 | tf_op jit(solution)/shard_map/ppermute | solution.py:30
  127.9 2.7 %collective-permute-start.31 = (f32[8,512]{1,0:T(8,128)S(1)}, f32[8,512]{1,0:T(8,128)S(1)}, u32[]{:S(2)}, u32[]{:S(2)}) collective-permute-start(f32[8,512]{1,0:T(8,128)S(1)} %apply_weights.4), channel_id=1, source_target_pairs={{4,20},{5,21},{6,30},{7,31}} | collective-permute-start | bytes 49160 | tf_op jit(solution)/shard_map/ppermute | solution.py:30
  129.2 2.3 %collective-permute-start.26 = (f32[8,512]{1,0:T(8,128)S(1)}, f32[8,512]{1,0:T(8,128)S(1)}, u32[]{:S(2)}, u32[]{:S(2)}) collective-permute-start(f32[8,512]{1,0:T(8,128)S(1)} %turn.3.refs_1_), channel_id=1, source_target_pairs={{10,20},{11,21}} | collective-permute-start | bytes 49160 | tf_op jit(solution)/shard_map/ppermute | solution.py:30
  130.8 3.6 %collective-permute-start.35 = (f32[8,512]{1,0:T(8,128)S(1)}, f32[8,512]{1,0:T(8,128)S(1)}, u32[]{:S(2)}, u32[]{:S(2)}) collective-permute-start(f32[8,512]{1,0:T(8,128)S(1)} %turn.3.refs_1_), channel_id=1, source_target_pairs={{10,14},{11,15}} | collective-permute-start | bytes 49160 | tf_op jit(solution)/shard_map/ppermute | solution.py:30
  147.7 2.6 %collective-permute-start.39 = (f32[2,512]{1,0:T(2,128)}, f32[2,512]{1,0:T(2,128)S(1)}, u32[]{:S(2)}, u32[]{:S(2)}) collective-permute-start(f32[2,512]{1,0:T(2,128)} %get-tuple-element.102), channel_id=1, source_target_pairs={{0,8},{1,9},{10,2},{11,3},{20,28},{21,29},{30,22},{31,23}} | collective-permute-start | bytes 12296 | tf_op jit(solution)/shard_map/ppermute | solution.py:30
  149.0 12.8 %collective-permute-start.41 = (f32[2,512]{1,0:T(2,128)}, f32[2,512]{1,0:T(2,128)S(1)}, u32[]{:S(2)}, u32[]{:S(2)}) collective-permute-start(f32[2,512]{1,0:T(2,128)} %get-tuple-element.104), channel_id=1, source_target_pairs={{0,24},{1,25},{10,18},{11,19},{20,12},{21,13},{30,6},{31,7}} | collective-permute-start | bytes 12296 | tf_op jit(solution)/shard_map/ppermute | solution.py:30
  (28 other events, 198.2 us)

commit v8 on v7

--- a/solution.py
+++ b/solution.py
@@ -283,48 +283,61 @@
     )(where, *weights, xa, xb)
 
 
-def turn_kernel(where_ref, *refs):
-    left_own, left_sib, inv_hi, inv_lo, xa, xb, own_rest, sib_rest, out_ref, buffer, sems = refs
+def turn_kernel(count, where_ref, *refs):
+    weights, refs = refs[: 2 * count + 2], refs[2 * count + 2 :]
+    xa, xb, own_rest, sib_rest, out_ref, buffer, sems = refs
     core = where_ref[0]
     copies = [
-        pltpu.make_async_copy(ref, buffer.at[i], sems.at[i])
-        for i, ref in enumerate((left_own, left_sib))
+        pltpu.make_async_copy(ref, buffer.at[i], sems.at[i]) for i, ref in enumerate(weights)
     ]
     for copy in copies:
         copy.start()
     points = xa.shape[1]
-    halves = [(core, xa[...]), (1 - core, xb[...])]
-    copies[0].wait()
-    own = own_rest[:, :points] - weigh(buffer.at[0], None, halves)
-    copies[1].wait()
-    sib = sib_rest[:, :points] - weigh(buffer.at[1], None, halves)
-    out_ref[...] = weigh(inv_hi, inv_lo, [(core, own), (1 - core, sib)])
-
-
-def turn(where, lefts, inverse, xa, xb, own_rest, sib_rest):
+    n = own_rest.shape[0]
+    own, sib = own_rest[:, :points], sib_rest[:, :points]
+    for i in range(count):
+        halves = [(core, xa[i * n : (i + 1) * n]), (1 - core, xb[i * n : (i + 1) * n])]
+        copies[2 * i].wait()
+        own -= weigh(buffer.at[2 * i], None, halves)
+        copies[2 * i + 1].wait()
+        sib -= weigh(buffer.at[2 * i + 1], None, halves)
+    copies[-2].wait()
+    copies[-1].wait()
+    solved = weigh(
+        buffer.at[2 * count], buffer.at[2 * count + 1], [(core, own), (1 - core, sib)]
+    )
+    if out_ref.shape[0] > n:
+        out_ref[: count * n] = xa[...]
+    out_ref[out_ref.shape[0] - n :] = solved
+
+
+def turn(where, lefts, inverse, xa, xb, own_rest, sib_rest, keep):
     vmem = pl.BlockSpec(memory_space=pltpu.VMEM)
-    return pl.pallas_call(
-        turn_kernel,
+    weights = [*lefts, *inverse]
+    n, points = own_rest.shape[0], xa.shape[1]
+    count = len(lefts) // 2
+    return pl.pallas_call(
+        functools.partial(turn_kernel, count),
         in_specs=[pl.BlockSpec(memory_space=pltpu.SMEM)]
-        + [pl.BlockSpec(memory_space=pl.ANY)] * 2
-        + [vmem] * 6,
+        + [pl.BlockSpec(memory_space=pltpu.HBM)] * len(weights)
+        + [vmem] * 4,
         out_specs=vmem,
-        out_shape=jax.ShapeDtypeStruct(xa.shape, F32),
+        out_shape=jax.ShapeDtypeStruct(((count + 1) * n if keep else n, points), F32),
         scratch_shapes=[
-            pltpu.VMEM((2,) + lefts[0].shape, BF16),
-            pltpu.SemaphoreType.DMA((2,)),
+            pltpu.VMEM((len(weights),) + weights[0].shape, BF16),
+            pltpu.SemaphoreType.DMA((len(weights),)),
         ],
-        compiler_params=pltpu.CompilerParams(vmem_limit_bytes=16 << 20),
-        cost_estimate=pl.CostEstimate(flops=2 << 30, transcendentals=0, bytes_accessed=1 << 22),
+        compiler_params=pltpu.CompilerParams(vmem_limit_bytes=32 << 20),
+        cost_estimate=pl.CostEstimate(flops=1 << 20, transcendentals=0, bytes_accessed=1 << 16),
         name="turn",
-    )(where, *lefts, *inverse, xa, xb, own_rest, sib_rest)
+    )(where, *weights, xa, xb, own_rest, sib_rest)
 
 
 def combine_kernel(count, turn_ref, inverse_ref, *refs):
     x_refs, out_refs = refs[:count], refs[count:]
     x = jnp.zeros(x_refs[0].shape, F32)
     for t, ref in enumerate(x_refs):
-        x = jnp.where(turn_ref[0] == t, ref[...], x)
+        x = jnp.where(turn_ref[0] == t, ref[ref.shape[0] - x.shape[0] :], x)
     rows = out_refs[0].shape[0]
     for k, ref in enumerate(out_refs):
         inverse = inverse_ref[pl.ds(turn_ref[1 + k] * rows, rows), :]
@@ -382,8 +395,6 @@
     for k in range(gen_count):
         piece = lax.dynamic_index_in_dim(spread, gen_index ^ chip ^ k, 0, keepdims=False)
         own_parts.append(move(piece, across(k)) if k else piece)
-    own_parts, sibling, metric_late = lax.optimization_barrier((own_parts, sibling, metric_late))
-
     own_raw = raw_columns.transpose(1, 0, 2)
     sib_raw = sibling.transpose(1, 0, 2)
     pivot_rows = pivot_pairs // NORB - gen_index * orb_block
@@ -424,10 +435,12 @@
         )
     )
 
-    all_parts, first_side, entries, inverse_rows = lax.optimization_barrier(
-        (all_parts, first_side, entries, inverse_rows)
-    )
-    left_sib = move(left_own, swap)
+    all_parts, first_side, entries, inverse_rows, left_rows = lax.optimization_barrier(
+        (all_parts, first_side, entries, inverse_rows, own_rows)
+    )
+    left_own, left_sib = {1: left_own}, {1: move(left_own, swap)}
+    for d in range(2, gen_count - 1):
+        left_own[d] = move(left_rows, lambda g, j, c: (j, j, c) if g >= 1 and j == g + d else None)
 
     own_raw = own_raw.reshape(orb_block * vec_total, pair_block)
     sib_raw = sib_raw.reshape(orb_block * vec_total, pair_block)
@@ -444,7 +457,7 @@
             [k if part % 128 == 0 else 0 for k in group],
         )
         if group[0] == 0:
-            shares, left_sib = lax.optimization_barrier((shares, left_sib))
+            shares, left_sib[1] = lax.optimization_barrier((shares, left_sib[1]))
         for k, share in zip(group, shares):
             if k:
                 share = move(share, across(k))
@@ -456,25 +469,31 @@
     rest, sib_rest = total, move(total, swap)
     solved = apply_weights(at_core, inverse_rows, rest, sib_rest)
     turns = [solved]
-    far = {}
-    for t in range(gen_count - 1):
-        near = move(solved, lambda g, j, c: (t + 1, t + 1, c) if g == j == t else None)
-        near_sib = move(solved, lambda g, j, c: (t + 1, t + 1, 1 - c) if g == j == t else None)
-        for z in range(t + 2, gen_count):
-            one = move(solved, lambda g, j, c: (t, z, c) if g == j == t else None)
-            far[t] = far[t] + one if t in far else one
-        if t == 0:
-            near, inverse_factor = lax.optimization_barrier((near, inverse_factor))
-        if t - 1 in far:
-            gone, _ = lax.optimization_barrier((far[t - 1], solved))
-            brought = apply_weights(at_core, [own_rows], gone, move(gone, swap))
-            brought = move(
-                brought, lambda g, j, c: (j, j, c) if g == t - 1 and j >= t + 1 else None
-            )
+    for t in range(1, gen_count):
+        near = move(solved, lambda g, j, c: (t, t, c) if g == j == t - 1 else None)
+        near_sib = move(solved, lambda g, j, c: (t, t, 1 - c) if g == j == t - 1 else None)
+        if t == 1 and gen_count > 2:
+            far = [
+                move(solved, lambda g, j, c: (0, z, c) if g == j == 0 else None)
+                for z in range(2, gen_count)
+            ]
+            far = sum(far[1:], far[0])
+            acted = apply_weights(at_core, [own_rows], far, move(far, swap))
+            brought = move(acted, lambda g, j, c: (j, j, c) if g == 0 and j >= 2 else None)
+            near, near_sib, acted = lax.optimization_barrier((near, near_sib, acted))
+        if t == 2:
             rest = rest[:, :points] - brought
             sib_rest = move(rest, swap)
-        solved = turn(at_core, (left_own, left_sib), inverse_rows, near, near_sib, rest, sib_rest)
+            near, inverse_factor = lax.optimization_barrier((near, inverse_factor))
+        lefts = []
+        for g in range(min(1, t - 1), t):
+            lefts += [left_own[t - g], left_sib[t - g]]
+        solved = turn(at_core, lefts, inverse_rows, near, near_sib, rest, sib_rest, t > 1)
         turns.append(solved)
+        if t == 1:
+            for d in range(2, gen_count - 1):
+                _, left_own[d] = lax.optimization_barrier((solved, left_own[d]))
+                left_sib[d] = move(left_own[d], swap)
 
     which = jnp.stack([jnp.where(diagonal, gen_index, -1)] + [gen_index ^ k for k in range(gen_count)])
     shares = combine(which, inverse_factor, turns, vec_dev)

time: 164 us -> 157 us (0.957)
  starting transfers between devices: 42 us -> 38.5 us
  Pallas kernels: 35 us -> 32.6 us
  waiting for transfers between devices: 63.9 us -> 61.9 us
    ppermute x42 -> x40, starting transfers between devices: 42 us -> 38.5 us  [move(): return lax.ppermute(value, BOTH, pairs)]
    unnamed x36 -> x30, local copies, waits for them, and re-layouts: 6.26 us -> 4.05 us
    ppermute x42 -> x40, waiting for transfers between devices: 63.9 us -> 61.9 us  [move(): return lax.ppermute(value, BOTH, pairs)]
    squeeze x1, local copies, waits for them, and re-layouts: 0.04 us -> 1.88 us  [on_device(): lax.dynamic_index_in_dim(spread, gen_index ^ chip ^ k, 0, keepdims=False)]
    pallas_call x3 -> x2, Pallas kernels: 3.85 us -> 2.25 us  [apply_weights(): pl.pallas_call(apply_kernel, in_specs=[pl.BlockSpec(memory_space=pltpu.SM...]
  transfers between devices with their start and end apart: 42 -> 40, of which waited for: 21 -> 18; matrix products, arithmetic and copies ran while one was open for 8% -> 10% of each run, Pallas kernels for 15% -> 18%
where the time goes in v8:
time: 157 us; the launch traced here: 156 us
  waiting for transfers between devices  61.9 us (39%)
  starting transfers between devices  38.5 us (25%)
  Pallas kernels  32.6 us (21%)
  local copies, waits for them, and re-layouts  9.85 us (6%)
  matrix products  6.62 us (4%)
  other arithmetic  5.64 us (4%)
    ppermute x40, waiting for transfers between devices, move(): return lax.ppermute(value, BOTH, pairs)  61.9 us
    ppermute x40, starting transfers between devices, move(): return lax.ppermute(value, BOTH, pairs)  38.5 us
    pallas_call x1, Pallas kernels, project(): pl.pallas_call(kernel, grid_spec=pltpu.PrefetchScalarGridSpec(num_scalar_...  11.6 us
    pallas_call x3, Pallas kernels, turn(): pl.pallas_call(functools.partial(turn_kernel, count), in_specs=[pl.BlockS...  7.06 us
    pallas_call x1, Pallas kernels, invert_block(): pl.pallas_call(invert_kernel, grid_spec=pltpu.PrefetchScalarGridSpec(num_...  5.34 us
    dot_general x1, matrix products, on_device(): corner = jnp.dot(metric_factor[:, :points], upper, precision=HIGHEST)  4.72 us
    unnamed x30, local copies, waits for them, and re-layouts  4.05 us
  transfers between devices with their start and end apart: 40, of which 18 were waited for; matrix products, arithmetic and copies ran while one was open for 10% of the time, Pallas kernels for 18%

profile of v8, /device:TPU:24, one launch (start us, length us, event | category | flops | bytes accessed | tf_op | source)
XLA Modules:
  0.0 155.7 jit_solution(7377777125032311644)
XLA Ops:
  0.0 2.0 %fusion.5 = (bf16[500,256]{1,0:T(8,128)(2,1)}, bf16[500,256]{1,0:T(8,128)(2,1)S(1)}) fusion(bf16[500,512]{1,0:T(8,128)(2,1)} %rest_0_), kind=kLoop, calls=%fused_computation.29 | loop fusion | bytes 1024000 | tf_op jit(solution)/shard_map/slice | solution.py:387
  3.6 1.6 collective-permute-start
  7.1 2.3 %collective-permute-done = bf16[2,250,128]{2,1,0:T(8,128)(2,1)S(1)} collective-permute-done((bf16[2,250,128]{2,1,0:T(8,128)(2,1)S(1)}, bf16[2,250,128]{2,1,0:T(8,128)(2,1)S(1)}, u32[]{:S(2)}, u32[]{:S(2)}) %collective-permute-start) | collective-permute-done | bytes 128032 | tf_op jit(solution)/shard_map/ppermute | solution.py:30
  9.5 3.7 %collective-permute-done.1 = bf16[2,250,128]{2,1,0:T(8,128)(2,1)S(1)} collective-permute-done((bf16[2,250,128]{2,1,0:T(8,128)(2,1)S(1)}, bf16[2,250,128]{2,1,0:T(8,128)(2,1)S(1)}, u32[]{:S(2)}, u32[]{:S(2)}) %collective-permute-start.1) | collective-permute-done | bytes 128032 | tf_op jit(solution)/shard_map/ppermute | solution.py:30
  14.0 2.8 %collective-permute-done.4.rest_2_ = bf16[500,256]{1,0:T(8,128)(2,1)S(1)} collective-permute-done((bf16[500,256]{1,0:T(8,128)(2,1)S(1)}, bf16[500,256]{1,0:T(8,128)(2,1)S(1)}, u32[]{:S(2)}, u32[]{:S(2)}) %collective-permute-start.4) | collective-permute-done | bytes 256032 | tf_op jit(solution)/shard_map/ppermute | solution.py:30
  19.4 1.9 %dynamic-slice_bitcast_fusion = (bf16[2,250,128]{2,1,0:T(8,128)(2,1)}, bf16[2,250,128]{2,1,0:T(8,128)(2,1)}, bf16[2,250,128]{2,1,0:T(8,128)(2,1)}, bf16[2,250,128]{2,1,0:T(8,128)(2,1)S(1)}) fusion(bf16[4,2,250,128]{3,2,1,0:T(8,128)(2,1)} %pad_maximum_fusion.1, s32[]{:T(128)S(6)} %select_n.75, s32[]{:T(128)S(6)} %select_n.74, s32[]{:T(128)S(6)} %select_n.73, ...), kind=kLoop, calls=%fused_computation.11 | loop fusion | bytes 1024016 | tf_op jit(solution)/shard_map/jit(dynamic_index_in_dim)/squeeze | solution.py:396
  21.2 2.3 %collective-permute-start.6 = (bf16[2,250,128]{2,1,0:T(8,128)(2,1)}, bf16[2,250,128]{2,1,0:T(8,128)(2,1)}, u32[]{:S(2)}, u32[]{:S(2)}) collective-permute-start(bf16[2,250,128]{2,1,0:T(8,128)(2,1)} %get-tuple-element.100), channel_id=1, source_target_pairs={{0,4},{1,5},{2,6},{3,7},{4,0},{5,1},{6,2},{7,3},{8,12},{9,13},{10,... | collective-permute-start | bytes 384008 | tf_op jit(solution)/shard_map/ppermute | solution.py:30
  23.5 2.1 %collective-permute-start.7 = (bf16[2,250,128]{2,1,0:T(8,128)(2,1)}, bf16[2,250,128]{2,1,0:T(8,128)(2,1)}, u32[]{:S(2)}, u32[]{:S(2)}) collective-permute-start(bf16[2,250,128]{2,1,0:T(8,128)(2,1)} %get-tuple-element.99), channel_id=1, source_target_pairs={{0,6},{1,7},{2,4},{3,5},{4,2},{5,3},{6,0},{7,1},{8,14},{9,15},{10,... | collective-permute-start | bytes 384008 | tf_op jit(solution)/shard_map/ppermute | solution.py:30
  27.0 5.3 %invert_block.1 = f32[512,512]{1,0:T(8,128)S(1)} custom-call(s32[2]{0:T(128)S(1)} %pad_add_fusion.where_ref, f32[512,1024]{1,0:T(8,128)S(1)} %copy-done.3), custom_call_target="tpu_custom_call" | custom-call | flops 4294967296 | bytes 4194304 | tf_op jit(solution)/shard_map/invert_block/pallas_call | solution.py:230
  33.4 2.8 %pivot_entries.1.entries_ref = f32[8,8]{1,0:T(8,128)} custom-call(s32[8]{0:T(128)} %get-tuple-element.110.row_ref, bf16[500,8,250]{2,1,0:T(8,128)(2,1)} %bitcast.33, bf16[500,8,250]{2,1,0:T(8,128)(2,1)} %bitcast.16.sib_ref, s32[8]{0:T(128)} %get-tuple-element.111.own_col_ref, s32[8]{0:T(128)} %get-tuple-element.109.sib_col_ref), custom_call_target="tpu_custom_call" | custom-call | tf_op jit(solution)/shard_map/pivot_entries/pallas_call | solution.py:63
  36.2 3.8 %collective-permute-done.6 = bf16[2,250,128]{2,1,0:T(8,128)(2,1)} collective-permute-done((bf16[2,250,128]{2,1,0:T(8,128)(2,1)}, bf16[2,250,128]{2,1,0:T(8,128)(2,1)}, u32[]{:S(2)}, u32[]{:S(2)}) %collective-permute-start.6) | collective-permute-done | bytes 128032 | tf_op jit(solution)/shard_map/ppermute | solution.py:30
  39.9 7.5 %collective-permute-done.8.rest_3_ = bf16[500,256]{1,0:T(8,128)(2,1)} collective-permute-done((bf16[500,256]{1,0:T(8,128)(2,1)}, bf16[500,256]{1,0:T(8,128)(2,1)}, u32[]{:S(2)}, u32[]{:S(2)}) %collective-permute-start.8) | collective-permute-done | bytes 256032 | tf_op jit(solution)/shard_map/ppermute | solution.py:30
  50.3 2.6 %collective-permute-start.11 = (bf16[4,2,250,128]{3,2,1,0:T(8,128)(2,1)S(1)}, bf16[4,2,250,128]{3,2,1,0:T(8,128)(2,1)S(1)}, u32[]{:S(2)}, u32[]{:S(2)}) collective-permute-start(bf16[4,2,250,128]{3,2,1,0:T(8,128)(2,1)S(1)} %pad_maximum_fusion.2.rest_5_.rest_9_.rest_13_.rest_17_), channel_id=1, source_target_pairs={{0,16},{1,17},{2,18},{3,19},{4,20},{5,21},{6,22},{7,23},{8,24},{9,... | collective-permute-start | bytes 1536008 | tf_op jit(solution)/shard_map/ppermute | solution.py:30
  55.8 4.7 %fusion.2 = f32[512,512]{1,0:T(8,128)S(1)} fusion(f32[512,512]{1,0:T(8,128)} %collective-permute-done.15, f32[512,1024]{1,0:T(8,128)S(1)} %copy-done.3), kind=kOutput, calls=%fused_computation.6 | convolution fusion | flops 1610612736 | bytes 3145728 | tf_op jit(solution)/shard_map/dot_general | solution.py:426
  60.5 2.9 %collective-permute-done.10.rest_6_.rest_10_.rest_14_.rest_18_ = bf16[4,2,250,128]{3,2,1,0:T(8,128)(2,1)S(1)} collective-permute-done((bf16[4,2,250,128]{3,2,1,0:T(8,128)(2,1)S(1)}, bf16[4,2,250,128]{3,2,1,0:T(8,128)(2,1)S(1)}, u32[]{:S(2)}, u32[]{:S(2)}) %collective-permute-start.10) | collective-permute-done | bytes 512032 | tf_op jit(solution)/shard_map/ppermute | solution.py:30
  63.5 1.9 %fusion.1 = f32[512,512]{1,0:T(8,128)S(1)} fusion(f32[512,512]{1,0:T(8,128)S(1)} %copy-done.5, f32[512,512]{1,0:T(8,128)S(1)} %fusion.2, pred[]{:T(512)S(6)} %eq.13), kind=kOutput, calls=%fused_computation.5 | convolution fusion | flops 1611137024 | bytes 3145729 | tf_op jit(solution)/shard_map/dot_general | solution.py:427
  65.9 10.1 %collective-permute-done.11.rest_7_.rest_11_.rest_15_.rest_19_ = bf16[4,2,250,128]{3,2,1,0:T(8,128)(2,1)S(1)} collective-permute-done((bf16[4,2,250,128]{3,2,1,0:T(8,128)(2,1)S(1)}, bf16[4,2,250,128]{3,2,1,0:T(8,128)(2,1)S(1)}, u32[]{:S(2)}, u32[]{:S(2)}) %collective-permute-start.11) | collective-permute-done | bytes 512032 | tf_op jit(solution)/shard_map/ppermute | solution.py:30
  75.9 1.8 %collective-permute-done.12.rest_8_.rest_12_.rest_16_.rest_20_ = bf16[4,2,250,128]{3,2,1,0:T(8,128)(2,1)S(1)} collective-permute-done((bf16[4,2,250,128]{3,2,1,0:T(8,128)(2,1)S(1)}, bf16[4,2,250,128]{3,2,1,0:T(8,128)(2,1)S(1)}, u32[]{:S(2)}, u32[]{:S(2)}) %collective-permute-start.12) | collective-permute-done | bytes 512032 | tf_op jit(solution)/shard_map/ppermute | solution.py:30
  79.1 1.6 %collective-permute-start.33 = (bf16[512,1024]{1,0:T(8,128)(2,1)}, bf16[512,1024]{1,0:T(8,128)(2,1)}, u32[]{:S(2)}, u32[]{:S(2)}) collective-permute-start(bf16[512,1024]{1,0:T(8,128)(2,1)} %convert_element_type.10.refs_0_), channel_id=1, source_target_pairs={{14,30},{15,31}} | collective-permute-start | bytes 3145736 | tf_op jit(solution)/shard_map/ppermute | solution.py:30
  80.7 11.6 %project.1 = (f32[8,640]{1,0:T(8,128)S(1)}, f32[8,640]{1,0:T(8,128)S(1)}, f32[8,640]{1,0:T(8,128)S(1)}, f32[8,640]{1,0:T(8,128)S(1)}) custom-call(s32[5]{0:T(128)S(1)} %stack.80.where_ref, bf16[4000,250]{1,0:T(8,128)(2,1)S(1)} %bitcast.34, bf16[4000,250]{1,0:T(8,128)(2,1)} %bitcast.18.sib_ref, f32[8,8]{1,0:T(8,128)S(1)} %copy-done.13, ...), custom_call_target="tpu_custom_call" | custom-call | flops 8192000000 | bytes 1048576 | tf_op jit(solution)/shard_map/project/pallas_call | solution.py:170
  92.4 3.0 %collective-permute-start.17 = (f32[8,640]{1,0:T(8,128)S(1)}, f32[8,640]{1,0:T(8,128)S(1)}, u32[]{:S(2)}, u32[]{:S(2)}) collective-permute-start(f32[8,640]{1,0:T(8,128)S(1)} %get-tuple-element.84), channel_id=1, source_target_pairs={{0,2},{1,3},{2,0},{3,1},{4,6},{5,7},{6,4},{7,5},{8,10},{9,11},{10,... | collective-permute-start | bytes 61448 | tf_op jit(solution)/shard_map/ppermute | solution.py:30
  95.4 2.4 %collective-permute-start.19 = (f32[8,640]{1,0:T(8,128)S(1)}, f32[8,640]{1,0:T(8,128)S(1)}, u32[]{:S(2)}, u32[]{:S(2)}) collective-permute-start(f32[8,640]{1,0:T(8,128)S(1)} %get-tuple-element.86), channel_id=1, source_target_pairs={{0,6},{1,7},{2,4},{3,5},{4,2},{5,3},{6,0},{7,1},{8,14},{9,15},{10,... | collective-permute-start | bytes 61448 | tf_op jit(solution)/shard_map/ppermute | solution.py:30
  97.8 2.2 %collective-permute-done.18 = f32[8,640]{1,0:T(8,128)S(1)} collective-permute-done((f32[8,640]{1,0:T(8,128)S(1)}, f32[8,640]{1,0:T(8,128)S(1)}, u32[]{:S(2)}, u32[]{:S(2)}) %collective-permute-start.18) | collective-permute-done | bytes 20512 | tf_op jit(solution)/shard_map/ppermute | solution.py:30
  106.0 1.8 %collective-permute-done.22 = f32[8,640]{1,0:T(8,128)S(1)} collective-permute-done((f32[8,640]{1,0:T(8,128)S(1)}, f32[8,640]{1,0:T(8,128)S(1)}, u32[]{:S(2)}, u32[]{:S(2)}) %collective-permute-start.22) | collective-permute-done | bytes 20512 | tf_op jit(solution)/shard_map/ppermute | solution.py:30
  111.8 6.1 %collective-permute-done.27 = f32[8,512]{1,0:T(8,128)S(1)} collective-permute-done((f32[8,512]{1,0:T(8,128)S(1)}, f32[8,512]{1,0:T(8,128)S(1)}, u32[]{:S(2)}, u32[]{:S(2)}) %collective-permute-start.27) | collective-permute-done | bytes 16416 | tf_op jit(solution)/shard_map/ppermute | solution.py:30
  119.3 1.6 %apply_weights.3 = f32[8,512]{1,0:T(8,128)S(1)} custom-call(s32[1]{0:T(128)} %bitcast.5.where_ref, bf16[512,1024]{1,0:T(8,128)(2,1)} %convert_element_type.10.refs_0_, f32[8,512]{1,0:T(8,128)S(1)} %add.85.refs_1_, f32[8,512]{1,0:T(8,128)S(1)} %collective-permute-done.28.refs_2_), custom_call_target="tpu_custom_call" | custom-call | flops 1073741824 | bytes 2097152 | tf_op jit(solution)/shard_map/apply_weights/pallas_call | solution.py:274
  120.9 1.8 %turn.3.refs_1_ = f32[8,512]{1,0:T(8,128)S(1)} custom-call(s32[1]{0:T(128)} %bitcast.5.where_ref, bf16[512,1024]{1,0:T(8,128)(2,1)S(1)} %collective-permute-done.9.refs_0_.refs_2_, bf16[512,1024]{1,0:T(8,128)(2,1)S(1)} %collective-permute-done.16.refs_1_.refs_3_, bf16[512,1024]{1,0:T(8,128)(2,1)S(1)} %get-tuple-element.81.refs_0_.refs_2_.refs_4_, ...), custom_call_target="tpu_custom_call" | custom-call | flops 1048576 | bytes 65536 | tf_op jit(solution)/shard_map/turn/pallas_call | solution.py:319
  126.0 2.0 %factor_inverse.1.inverse_ref = f32[8,8]{1,0:T(8,128)} custom-call(f32[8,640]{1,0:T(8,128)} %copy-done.8), custom_call_target="tpu_custom_call" | custom-call | tf_op jit(solution)/shard_map/factor_inverse/pallas_call | solution.py:98
  129.2 1.8 %turn.4.refs_2_ = f32[16,512]{1,0:T(8,128)S(1)} custom-call(s32[1]{0:T(128)} %bitcast.5.where_ref, bf16[512,1024]{1,0:T(8,128)(2,1)S(1)} %collective-permute-done.9.refs_0_.refs_2_, bf16[512,1024]{1,0:T(8,128)(2,1)S(1)} %copy-done.1, bf16[512,1024]{1,0:T(8,128)(2,1)S(1)} %get-tuple-element.81.refs_0_.refs_2_.refs_4_, ...), custom_call_target="tpu_custom_call" | custom-call | flops 1048576 | bytes 65536 | tf_op jit(solution)/shard_map/turn/pallas_call | solution.py:319
  134.3 3.5 %turn.5.refs_3_ = f32[24,512]{1,0:T(8,128)S(1)} custom-call(s32[1]{0:T(128)} %bitcast.5.where_ref, bf16[512,1024]{1,0:T(8,128)(2,1)} %collective-permute-done.33.refs_0_, bf16[512,1024]{1,0:T(8,128)(2,1)} %collective-permute-done.34.refs_1_, bf16[512,1024]{1,0:T(8,128)(2,1)S(1)} %collective-permute-done.9.refs_0_.refs_2_, bf16[512,1024]{1,0:T(8,128)(2,1)S(1)} %copy-done.2, ...), custom_call_target="tpu_custom_call" | custom-call | flops 1048576 | bytes 65536 | tf_op jit(solution)/shard_map/turn/pallas_call | solution.py:319
  138.4 1.6 %combine.1 = (f32[2,512]{1,0:T(2,128)}, f32[2,512]{1,0:T(2,128)}, f32[2,512]{1,0:T(2,128)}, f32[2,512]{1,0:T(2,128)}) custom-call(s32[5]{0:T(128)} %stack.71.turn_ref, f32[8,8]{1,0:T(8,128)} %factor_inverse.1.inverse_ref, f32[8,512]{1,0:T(8,128)} %copy-done.12, f32[8,512]{1,0:T(8,128)} %copy-done.11, f32[16,512]{1,0:T(8,128)} %copy-done.10, f32[24,512]{1,0:T(8,128)} %copy-done.9), custom_call_target="tpu_custom_call" | custom-call | tf_op jit(solution)/shard_map/combine/pallas_call | solution.py:353
  142.6 11.8 %collective-permute-done.39 = f32[2,512]{1,0:T(2,128)S(1)} collective-permute-done((f32[2,512]{1,0:T(2,128)}, f32[2,512]{1,0:T(2,128)S(1)}, u32[]{:S(2)}, u32[]{:S(2)}) %collective-permute-start.39) | collective-permute-done | bytes 4128 | tf_op jit(solution)/shard_map/ppermute | solution.py:30
  (108 shorter events, 40.3 us)
Async XLA Ops:
  0.0 16.8 %collective-permute-start.3 = (bf16[8,500,250]{2,0,1:T(8,128)(2,1)}, bf16[8,500,250]{2,0,1:T(8,128)(2,1)}, u32[]{:S(2)}, u32[]{:S(2)}) collective-permute-start(bf16[8,500,250]{2,0,1:T(8,128)(2,1)} %param.4), channel_id=1, source_target_pairs={{0,1},{1,0},{2,3},{3,2},{4,5},{5,4},{6,7},{7,6},{8,9},{9,8},{10,11... | collective-permute-start | bytes 6000008 | tf_op jit(solution)/shard_map/ppermute | solution.py:30
  2.0 14.8 %collective-permute-start.4 = (bf16[500,256]{1,0:T(8,128)(2,1)S(1)}, bf16[500,256]{1,0:T(8,128)(2,1)S(1)}, u32[]{:S(2)}, u32[]{:S(2)}) collective-permute-start(bf16[500,256]{1,0:T(8,128)(2,1)S(1)} %get-tuple-element.108), channel_id=1, source_target_pairs={{0,4},{1,5},{2,6},{3,7},{4,0},{5,1},{6,2},{7,3},{8,12},{9,13},{10,... | collective-permute-start | bytes 768008 | tf_op jit(solution)/shard_map/ppermute | solution.py:30
  3.6 5.9 %collective-permute-start = (bf16[2,250,128]{2,1,0:T(8,128)(2,1)S(1)}, bf16[2,250,128]{2,1,0:T(8,128)(2,1)S(1)}, u32[]{:S(2)}, u32[]{:S(2)}) collective-permute-start(bf16[2,250,128]{2,1,0:T(8,128)(2,1)S(1)} %get-tuple-element.106), channel_id=1, source_target_pairs={{0,8},{1,9},{2,10},{3,11},{4,12},{5,13},{6,14},{7,15},{8,0},{9,1},... | collective-permute-start | bytes 384008 | tf_op jit(solution)/shard_map/ppermute | solution.py:30
  5.1 8.0 %collective-permute-start.1 = (bf16[2,250,128]{2,1,0:T(8,128)(2,1)S(1)}, bf16[2,250,128]{2,1,0:T(8,128)(2,1)S(1)}, u32[]{:S(2)}, u32[]{:S(2)}) collective-permute-start(bf16[2,250,128]{2,1,0:T(8,128)(2,1)S(1)} %get-tuple-element.105), channel_id=1, source_target_pairs={{0,16},{1,17},{2,18},{3,19},{4,20},{5,21},{6,22},{7,23},{8,24},{9,... | collective-permute-start | bytes 384008 | tf_op jit(solution)/shard_map/ppermute | solution.py:30
  6.7 6.5 %collective-permute-start.2 = (bf16[2,250,128]{2,1,0:T(8,128)(2,1)S(1)}, bf16[2,250,128]{2,1,0:T(8,128)(2,1)S(1)}, u32[]{:S(2)}, u32[]{:S(2)}) collective-permute-start(bf16[2,250,128]{2,1,0:T(8,128)(2,1)S(1)} %get-tuple-element.104), channel_id=1, source_target_pairs={{0,24},{1,25},{2,26},{3,27},{4,28},{5,29},{6,30},{7,31},{8,16},{9,... | collective-permute-start | bytes 384008 | tf_op jit(solution)/shard_map/ppermute | solution.py:30
  17.9 29.5 %collective-permute-start.9 = (bf16[512,1024]{1,0:T(8,128)(2,1)}, bf16[512,1024]{1,0:T(8,128)(2,1)S(1)}, u32[]{:S(2)}, u32[]{:S(2)}) collective-permute-start(bf16[512,1024]{1,0:T(8,128)(2,1)} %convert_element_type.10.refs_0_), channel_id=1, source_target_pairs={{2,10},{3,11},{12,20},{13,21},{22,30},{23,31}} | collective-permute-start | bytes 3145736 | tf_op jit(solution)/shard_map/ppermute | solution.py:30
  21.2 14.9 %collective-permute-start.5 = (bf16[2,250,128]{2,1,0:T(8,128)(2,1)}, bf16[2,250,128]{2,1,0:T(8,128)(2,1)}, u32[]{:S(2)}, u32[]{:S(2)}) collective-permute-start(bf16[2,250,128]{2,1,0:T(8,128)(2,1)} %get-tuple-element.101), channel_id=1, source_target_pairs={{0,2},{1,3},{2,0},{3,1},{4,6},{5,7},{6,4},{7,5},{8,10},{9,11},{10,... | collective-permute-start | bytes 384008 | tf_op jit(solution)/shard_map/ppermute | solution.py:30
  21.2 18.7 %collective-permute-start.6 = (bf16[2,250,128]{2,1,0:T(8,128)(2,1)}, bf16[2,250,128]{2,1,0:T(8,128)(2,1)}, u32[]{:S(2)}, u32[]{:S(2)}) collective-permute-start(bf16[2,250,128]{2,1,0:T(8,128)(2,1)} %get-tuple-element.100), channel_id=1, source_target_pairs={{0,4},{1,5},{2,6},{3,7},{4,0},{5,1},{6,2},{7,3},{8,12},{9,13},{10,... | collective-permute-start | bytes 384008 | tf_op jit(solution)/shard_map/ppermute | solution.py:30
  23.5 16.4 %collective-permute-start.7 = (bf16[2,250,128]{2,1,0:T(8,128)(2,1)}, bf16[2,250,128]{2,1,0:T(8,128)(2,1)}, u32[]{:S(2)}, u32[]{:S(2)}) collective-permute-start(bf16[2,250,128]{2,1,0:T(8,128)(2,1)} %get-tuple-element.99), channel_id=1, source_target_pairs={{0,6},{1,7},{2,4},{3,5},{4,2},{5,3},{6,0},{7,1},{8,14},{9,15},{10,... | collective-permute-start | bytes 384008 | tf_op jit(solution)/shard_map/ppermute | solution.py:30
  25.6 21.8 %collective-permute-start.8 = (bf16[500,256]{1,0:T(8,128)(2,1)}, bf16[500,256]{1,0:T(8,128)(2,1)}, u32[]{:S(2)}, u32[]{:S(2)}) collective-permute-start(bf16[500,256]{1,0:T(8,128)(2,1)} %get-tuple-element.53), channel_id=1, source_target_pairs={{0,4},{1,5},{2,6},{3,7},{4,0},{5,1},{6,2},{7,3},{8,12},{9,13},{10,... | collective-permute-start | bytes 768008 | tf_op jit(solution)/shard_map/ppermute | solution.py:30
  47.4 6.9 %collective-permute-start.15 = (f32[512,512]{1,0:T(8,128)}, f32[512,512]{1,0:T(8,128)}, u32[]{:S(2)}, u32[]{:S(2)}) collective-permute-start(f32[512,512]{1,0:T(8,128)} %copy-done.4), channel_id=1, source_target_pairs={{0,1},{1,0},{2,3},{3,2},{4,5},{5,4},{6,7},{7,6},{8,9},{9,8},{10,11... | collective-permute-start | bytes 3145736 | tf_op jit(solution)/shard_map/ppermute | solution.py:30
  48.7 14.8 %collective-permute-start.10 = (bf16[4,2,250,128]{3,2,1,0:T(8,128)(2,1)S(1)}, bf16[4,2,250,128]{3,2,1,0:T(8,128)(2,1)S(1)}, u32[]{:S(2)}, u32[]{:S(2)}) collective-permute-start(bf16[4,2,250,128]{3,2,1,0:T(8,128)(2,1)S(1)} %pad_maximum_fusion.2.rest_5_.rest_9_.rest_13_.rest_17_), channel_id=1, source_target_pairs={{0,8},{1,9},{2,10},{3,11},{4,12},{5,13},{6,14},{7,15},{8,0},{9,1},... | collective-permute-start | bytes 1536008 | tf_op jit(solution)/shard_map/ppermute | solution.py:30
  50.3 25.6 %collective-permute-start.11 = (bf16[4,2,250,128]{3,2,1,0:T(8,128)(2,1)S(1)}, bf16[4,2,250,128]{3,2,1,0:T(8,128)(2,1)S(1)}, u32[]{:S(2)}, u32[]{:S(2)}) collective-permute-start(bf16[4,2,250,128]{3,2,1,0:T(8,128)(2,1)S(1)} %pad_maximum_fusion.2.rest_5_.rest_9_.rest_13_.rest_17_), channel_id=1, source_target_pairs={{0,16},{1,17},{2,18},{3,19},{4,20},{5,21},{6,22},{7,23},{8,24},{9,... | collective-permute-start | bytes 1536008 | tf_op jit(solution)/shard_map/ppermute | solution.py:30
  52.8 24.9 %collective-permute-start.12 = (bf16[4,2,250,128]{3,2,1,0:T(8,128)(2,1)S(1)}, bf16[4,2,250,128]{3,2,1,0:T(8,128)(2,1)S(1)}, u32[]{:S(2)}, u32[]{:S(2)}) collective-permute-start(bf16[4,2,250,128]{3,2,1,0:T(8,128)(2,1)S(1)} %pad_maximum_fusion.2.rest_5_.rest_9_.rest_13_.rest_17_), channel_id=1, source_target_pairs={{0,24},{1,25},{2,26},{3,27},{4,28},{5,29},{6,30},{7,31},{8,16},{9,... | collective-permute-start | bytes 1536008 | tf_op jit(solution)/shard_map/ppermute | solution.py:30
  54.2 24.9 %collective-permute-start.13 = (bf16[500,512]{1,0:T(8,128)(2,1)}, bf16[500,512]{1,0:T(8,128)(2,1)S(1)}, u32[]{:S(2)}, u32[]{:S(2)}) collective-permute-start(bf16[500,512]{1,0:T(8,128)(2,1)} %rest_0_), channel_id=1, source_target_pairs={{0,2},{1,3},{2,0},{3,1},{4,6},{5,7},{6,4},{7,5},{8,10},{9,11},{10,... | collective-permute-start | bytes 1536008 | tf_op jit(solution)/shard_map/ppermute | solution.py:30
  54.3 24.7 %collective-permute-start.14 = (bf16[500,512]{1,0:T(8,128)(2,1)S(1)}, bf16[500,512]{1,0:T(8,128)(2,1)S(1)}, u32[]{:S(2)}, u32[]{:S(2)}) collective-permute-start(bf16[500,512]{1,0:T(8,128)(2,1)S(1)} %copy-done.6), channel_id=1, source_target_pairs={{0,6},{1,7},{2,4},{3,5},{4,2},{5,3},{6,0},{7,1},{8,14},{9,15},{10,... | collective-permute-start | bytes 1536008 | tf_op jit(solution)/shard_map/ppermute | solution.py:30
  63.5 28.9 %collective-permute-start.16 = (bf16[512,1024]{1,0:T(8,128)(2,1)S(1)}, bf16[512,1024]{1,0:T(8,128)(2,1)S(1)}, u32[]{:S(2)}, u32[]{:S(2)}) collective-permute-start(bf16[512,1024]{1,0:T(8,128)(2,1)S(1)} %collective-permute-done.9.refs_0_.refs_2_), channel_id=1, source_target_pairs={{0,1},{1,0},{2,3},{3,2},{4,5},{5,4},{6,7},{7,6},{8,9},{9,8},{10,11... | collective-permute-start | bytes 3145736 | tf_op jit(solution)/shard_map/ppermute | solution.py:30
  79.1 43.6 %collective-permute-start.33 = (bf16[512,1024]{1,0:T(8,128)(2,1)}, bf16[512,1024]{1,0:T(8,128)(2,1)}, u32[]{:S(2)}, u32[]{:S(2)}) collective-permute-start(bf16[512,1024]{1,0:T(8,128)(2,1)} %convert_element_type.10.refs_0_), channel_id=1, source_target_pairs={{14,30},{15,31}} | collective-permute-start | bytes 3145736 | tf_op jit(solution)/shard_map/ppermute | solution.py:30
  92.4 5.5 %collective-permute-start.17 = (f32[8,640]{1,0:T(8,128)S(1)}, f32[8,640]{1,0:T(8,128)S(1)}, u32[]{:S(2)}, u32[]{:S(2)}) collective-permute-start(f32[8,640]{1,0:T(8,128)S(1)} %get-tuple-element.84), channel_id=1, source_target_pairs={{0,2},{1,3},{2,0},{3,1},{4,6},{5,7},{6,4},{7,5},{8,10},{9,11},{10,... | collective-permute-start | bytes 61448 | tf_op jit(solution)/shard_map/ppermute | solution.py:30
  95.4 4.7 %collective-permute-start.18 = (f32[8,640]{1,0:T(8,128)S(1)}, f32[8,640]{1,0:T(8,128)S(1)}, u32[]{:S(2)}, u32[]{:S(2)}) collective-permute-start(f32[8,640]{1,0:T(8,128)S(1)} %get-tuple-element.85), channel_id=1, source_target_pairs={{0,4},{1,5},{2,6},{3,7},{4,0},{5,1},{6,2},{7,3},{8,12},{9,13},{10,... | collective-permute-start | bytes 61448 | tf_op jit(solution)/shard_map/ppermute | solution.py:30
  95.4 5.6 %collective-permute-start.19 = (f32[8,640]{1,0:T(8,128)S(1)}, f32[8,640]{1,0:T(8,128)S(1)}, u32[]{:S(2)}, u32[]{:S(2)}) collective-permute-start(f32[8,640]{1,0:T(8,128)S(1)} %get-tuple-element.86), channel_id=1, source_target_pairs={{0,6},{1,7},{2,4},{3,5},{4,2},{5,3},{6,0},{7,1},{8,14},{9,15},{10,... | collective-permute-start | bytes 61448 | tf_op jit(solution)/shard_map/ppermute | solution.py:30
  101.0 3.8 %collective-permute-start.20 = (f32[8,640]{1,0:T(8,128)S(1)}, f32[8,640]{1,0:T(8,128)S(1)}, u32[]{:S(2)}, u32[]{:S(2)}) collective-permute-start(f32[8,640]{1,0:T(8,128)S(1)} %add_add_fusion.1), channel_id=1, source_target_pairs={{0,8},{1,9},{2,10},{3,11},{4,12},{5,13},{6,14},{7,15},{8,0},{9,1},... | collective-permute-start | bytes 61448 | tf_op jit(solution)/shard_map/ppermute | solution.py:30
  102.2 3.8 %collective-permute-start.21 = (f32[8,640]{1,0:T(8,128)S(1)}, f32[8,640]{1,0:T(8,128)S(1)}, u32[]{:S(2)}, u32[]{:S(2)}) collective-permute-start(f32[8,640]{1,0:T(8,128)S(1)} %add_add_fusion.1), channel_id=1, source_target_pairs={{0,16},{1,17},{2,18},{3,19},{4,20},{5,21},{6,22},{7,23},{8,24},{9,... | collective-permute-start | bytes 61448 | tf_op jit(solution)/shard_map/ppermute | solution.py:30
  103.2 4.7 %collective-permute-start.22 = (f32[8,640]{1,0:T(8,128)S(1)}, f32[8,640]{1,0:T(8,128)S(1)}, u32[]{:S(2)}, u32[]{:S(2)}) collective-permute-start(f32[8,640]{1,0:T(8,128)S(1)} %add_add_fusion.1), channel_id=1, source_target_pairs={{0,24},{1,25},{2,26},{3,27},{4,28},{5,29},{6,30},{7,31},{8,16},{9,... | collective-permute-start | bytes 61448 | tf_op jit(solution)/shard_map/ppermute | solution.py:30
  110.5 7.4 %collective-permute-start.27 = (f32[8,512]{1,0:T(8,128)S(1)}, f32[8,512]{1,0:T(8,128)S(1)}, u32[]{:S(2)}, u32[]{:S(2)}) collective-permute-start(f32[8,512]{1,0:T(8,128)S(1)} %apply_weights.2.refs_0_), channel_id=1, source_target_pairs={{0,6},{1,7}} | collective-permute-start | bytes 49160 | tf_op jit(solution)/shard_map/ppermute | solution.py:30
  117.9 3.0 %collective-permute-start.24 = (f32[8,512]{1,0:T(8,128)S(1)}, f32[8,512]{1,0:T(8,128)S(1)}, u32[]{:S(2)}, u32[]{:S(2)}) collective-permute-start(f32[8,512]{1,0:T(8,128)S(1)} %apply_weights.2.refs_0_), channel_id=1, source_target_pairs={{0,10},{1,11}} | collective-permute-start | bytes 49160 | tf_op jit(solution)/shard_map/ppermute | solution.py:30
  122.7 10.3 %collective-permute-start.34 = (bf16[512,1024]{1,0:T(8,128)(2,1)}, bf16[512,1024]{1,0:T(8,128)(2,1)}, u32[]{:S(2)}, u32[]{:S(2)}) collective-permute-start(bf16[512,1024]{1,0:T(8,128)(2,1)} %collective-permute-done.33.refs_0_), channel_id=1, source_target_pairs={{0,1},{1,0},{2,3},{3,2},{4,5},{5,4},{6,7},{7,6},{8,9},{9,8},{10,11... | collective-permute-start | bytes 3145736 | tf_op jit(solution)/shard_map/ppermute | solution.py:30
  123.3 2.7 %collective-permute-start.31 = (f32[8,512]{1,0:T(8,128)S(1)}, f32[8,512]{1,0:T(8,128)S(1)}, u32[]{:S(2)}, u32[]{:S(2)}) collective-permute-start(f32[8,512]{1,0:T(8,128)S(1)} %apply_weights.3), channel_id=1, source_target_pairs={{4,20},{5,21},{6,30},{7,31}} | collective-permute-start | bytes 49160 | tf_op jit(solution)/shard_map/ppermute | solution.py:30
  124.6 3.4 %collective-permute-start.29 = (f32[8,512]{1,0:T(8,128)S(1)}, f32[8,512]{1,0:T(8,128)S(1)}, u32[]{:S(2)}, u32[]{:S(2)}) collective-permute-start(f32[8,512]{1,0:T(8,128)S(1)} %turn.3.refs_1_), channel_id=1, source_target_pairs={{10,20},{11,21}} | collective-permute-start | bytes 49160 | tf_op jit(solution)/shard_map/ppermute | solution.py:30
  125.2 2.8 %collective-permute-start.30 = (f32[8,512]{1,0:T(8,128)S(1)}, f32[8,512]{1,0:T(8,128)S(1)}, u32[]{:S(2)}, u32[]{:S(2)}) collective-permute-start(f32[8,512]{1,0:T(8,128)S(1)} %turn.3.refs_1_), channel_id=1, source_target_pairs={{10,21},{11,20}} | collective-permute-start | bytes 49160 | tf_op jit(solution)/shard_map/ppermute | solution.py:30
  140.0 2.6 %collective-permute-start.37 = (f32[2,512]{1,0:T(2,128)}, f32[2,512]{1,0:T(2,128)S(1)}, u32[]{:S(2)}, u32[]{:S(2)}) collective-permute-start(f32[2,512]{1,0:T(2,128)} %get-tuple-element.94), channel_id=1, source_target_pairs={{0,8},{1,9},{10,2},{11,3},{20,28},{21,29},{30,22},{31,23}} | collective-permute-start | bytes 12296 | tf_op jit(solution)/shard_map/ppermute | solution.py:30
  141.3 13.1 %collective-permute-start.39 = (f32[2,512]{1,0:T(2,128)}, f32[2,512]{1,0:T(2,128)S(1)}, u32[]{:S(2)}, u32[]{:S(2)}) collective-permute-start(f32[2,512]{1,0:T(2,128)} %get-tuple-element.96), channel_id=1, source_target_pairs={{0,24},{1,25},{10,18},{11,19},{20,12},{21,13},{30,6},{31,7}} | collective-permute-start | bytes 12296 | tf_op jit(solution)/shard_map/ppermute | solution.py:30
  (23 other events, 161.8 us)

commit v9 on v8

--- a/solution.py
+++ b/solution.py
@@ -319,7 +319,7 @@
     return pl.pallas_call(
         functools.partial(turn_kernel, count),
         in_specs=[pl.BlockSpec(memory_space=pltpu.SMEM)]
-        + [pl.BlockSpec(memory_space=pltpu.HBM)] * len(weights)
+        + [pl.BlockSpec(memory_space=pl.ANY)] * len(weights)
         + [vmem] * 4,
         out_specs=vmem,
         out_shape=jax.ShapeDtypeStruct(((count + 1) * n if keep else n, points), F32),
@@ -477,13 +477,15 @@
                 move(solved, lambda g, j, c: (0, z, c) if g == j == 0 else None)
                 for z in range(2, gen_count)
             ]
+            near, near_sib, far = lax.optimization_barrier((near, near_sib, far))
+        if t == 2:
             far = sum(far[1:], far[0])
             acted = apply_weights(at_core, [own_rows], far, move(far, swap))
             brought = move(acted, lambda g, j, c: (j, j, c) if g == 0 and j >= 2 else None)
-            near, near_sib, acted = lax.optimization_barrier((near, near_sib, acted))
-        if t == 2:
+            near, near_sib, brought = lax.optimization_barrier((near, near_sib, brought))
             rest = rest[:, :points] - brought
             sib_rest = move(rest, swap)
+        if t == gen_count - 1:
             near, inverse_factor = lax.optimization_barrier((near, inverse_factor))
         lefts = []
         for g in range(min(1, t - 1), t):

time: 157 us -> 158 us (level)
  waiting for transfers between devices: 61.9 us -> 64.6 us
    ppermute x40, waiting for transfers between devices: 61.9 us -> 64.6 us  [move(): return lax.ppermute(value, BOTH, pairs)]
    unnamed x30 -> x28, local copies, waits for them, and re-layouts: 4.05 us -> 2.85 us
  transfers between devices with their start and end apart: 40 -> 40, of which waited for: 18 -> 20; matrix products, arithmetic and copies ran while one was open for 10% -> 10% of each run, Pallas kernels for 18% -> 18%
where the time goes in v9:
time: 158 us; the launch traced here: 157 us
  waiting for transfers between devices  64.6 us (41%)
  starting transfers between devices  38.5 us (24%)
  Pallas kernels  32.6 us (21%)
  local copies, waits for them, and re-layouts  8.56 us (5%)
  matrix products  6.62 us (4%)
  other arithmetic  5.65 us (4%)
    ppermute x40, waiting for transfers between devices, move(): return lax.ppermute(value, BOTH, pairs)  64.6 us
    ppermute x40, starting transfers between devices, move(): return lax.ppermute(value, BOTH, pairs)  38.5 us
    pallas_call x1, Pallas kernels, project(): pl.pallas_call(kernel, grid_spec=pltpu.PrefetchScalarGridSpec(num_scalar_...  11.6 us
    pallas_call x3, Pallas kernels, turn(): pl.pallas_call(functools.partial(turn_kernel, count), in_specs=[pl.BlockS...  7.06 us
    pallas_call x1, Pallas kernels, invert_block(): pl.pallas_call(invert_kernel, grid_spec=pltpu.PrefetchScalarGridSpec(num_...  5.34 us
    dot_general x1, matrix products, on_device(): corner = jnp.dot(metric_factor[:, :points], upper, precision=HIGHEST)  4.72 us
  transfers between devices with their start and end apart: 40, of which 20 were waited for; matrix products, arithmetic and copies ran while one was open for 10% of the time, Pallas kernels for 18%

profile of v9, /device:TPU:24, one launch (start us, length us, event | category | flops | bytes accessed | tf_op | source)
XLA Modules:
  0.0 157.1 jit_solution(10227718326680257658)
XLA Ops:
  0.0 1.9 %fusion.5 = (bf16[500,256]{1,0:T(8,128)(2,1)}, bf16[500,256]{1,0:T(8,128)(2,1)S(1)}) fusion(bf16[500,512]{1,0:T(8,128)(2,1)} %rest_0_), kind=kLoop, calls=%fused_computation.29 | loop fusion | bytes 1024000 | tf_op jit(solution)/shard_map/slice | solution.py:387
  3.6 1.6 collective-permute-start
  7.1 2.3 %collective-permute-done = bf16[2,250,128]{2,1,0:T(8,128)(2,1)S(1)} collective-permute-done((bf16[2,250,128]{2,1,0:T(8,128)(2,1)S(1)}, bf16[2,250,128]{2,1,0:T(8,128)(2,1)S(1)}, u32[]{:S(2)}, u32[]{:S(2)}) %collective-permute-start) | collective-permute-done | bytes 128032 | tf_op jit(solution)/shard_map/ppermute | solution.py:30
  9.5 3.7 %collective-permute-done.1 = bf16[2,250,128]{2,1,0:T(8,128)(2,1)S(1)} collective-permute-done((bf16[2,250,128]{2,1,0:T(8,128)(2,1)S(1)}, bf16[2,250,128]{2,1,0:T(8,128)(2,1)S(1)}, u32[]{:S(2)}, u32[]{:S(2)}) %collective-permute-start.1) | collective-permute-done | bytes 128032 | tf_op jit(solution)/shard_map/ppermute | solution.py:30
  14.0 2.8 %collective-permute-done.4.rest_2_ = bf16[500,256]{1,0:T(8,128)(2,1)S(1)} collective-permute-done((bf16[500,256]{1,0:T(8,128)(2,1)S(1)}, bf16[500,256]{1,0:T(8,128)(2,1)S(1)}, u32[]{:S(2)}, u32[]{:S(2)}) %collective-permute-start.4) | collective-permute-done | bytes 256032 | tf_op jit(solution)/shard_map/ppermute | solution.py:30
  19.4 1.9 %dynamic-slice_bitcast_fusion = (bf16[2,250,128]{2,1,0:T(8,128)(2,1)}, bf16[2,250,128]{2,1,0:T(8,128)(2,1)}, bf16[2,250,128]{2,1,0:T(8,128)(2,1)}, bf16[2,250,128]{2,1,0:T(8,128)(2,1)S(1)}) fusion(bf16[4,2,250,128]{3,2,1,0:T(8,128)(2,1)} %pad_maximum_fusion.1, s32[]{:T(128)S(6)} %select_n.75, s32[]{:T(128)S(6)} %select_n.74, s32[]{:T(128)S(6)} %select_n.73, ...), kind=kLoop, calls=%fused_computation.11 | loop fusion | bytes 1024016 | tf_op jit(solution)/shard_map/jit(dynamic_index_in_dim)/squeeze | solution.py:396
  21.2 2.3 %collective-permute-start.6 = (bf16[2,250,128]{2,1,0:T(8,128)(2,1)}, bf16[2,250,128]{2,1,0:T(8,128)(2,1)}, u32[]{:S(2)}, u32[]{:S(2)}) collective-permute-start(bf16[2,250,128]{2,1,0:T(8,128)(2,1)} %get-tuple-element.110), channel_id=1, source_target_pairs={{0,4},{1,5},{2,6},{3,7},{4,0},{5,1},{6,2},{7,3},{8,12},{9,13},{10,... | collective-permute-start | bytes 384008 | tf_op jit(solution)/shard_map/ppermute | solution.py:30
  23.5 2.1 %collective-permute-start.7 = (bf16[2,250,128]{2,1,0:T(8,128)(2,1)}, bf16[2,250,128]{2,1,0:T(8,128)(2,1)}, u32[]{:S(2)}, u32[]{:S(2)}) collective-permute-start(bf16[2,250,128]{2,1,0:T(8,128)(2,1)} %get-tuple-element.109), channel_id=1, source_target_pairs={{0,6},{1,7},{2,4},{3,5},{4,2},{5,3},{6,0},{7,1},{8,14},{9,15},{10,... | collective-permute-start | bytes 384008 | tf_op jit(solution)/shard_map/ppermute | solution.py:30
  27.0 5.3 %invert_block.1 = f32[512,512]{1,0:T(8,128)S(1)} custom-call(s32[2]{0:T(128)S(1)} %pad_add_fusion.where_ref, f32[512,1024]{1,0:T(8,128)S(1)} %copy-done.2), custom_call_target="tpu_custom_call" | custom-call | flops 4294967296 | bytes 4194304 | tf_op jit(solution)/shard_map/invert_block/pallas_call | solution.py:230
  33.3 2.8 %pivot_entries.1.entries_ref = f32[8,8]{1,0:T(8,128)} custom-call(s32[8]{0:T(128)} %get-tuple-element.120.row_ref, bf16[500,8,250]{2,1,0:T(8,128)(2,1)} %bitcast.33, bf16[500,8,250]{2,1,0:T(8,128)(2,1)} %bitcast.16.sib_ref, s32[8]{0:T(128)} %get-tuple-element.121.own_col_ref, s32[8]{0:T(128)} %get-tuple-element.119.sib_col_ref), custom_call_target="tpu_custom_call" | custom-call | tf_op jit(solution)/shard_map/pivot_entries/pallas_call | solution.py:63
  36.1 3.8 %collective-permute-done.6 = bf16[2,250,128]{2,1,0:T(8,128)(2,1)} collective-permute-done((bf16[2,250,128]{2,1,0:T(8,128)(2,1)}, bf16[2,250,128]{2,1,0:T(8,128)(2,1)}, u32[]{:S(2)}, u32[]{:S(2)}) %collective-permute-start.6) | collective-permute-done | bytes 128032 | tf_op jit(solution)/shard_map/ppermute | solution.py:30
  39.9 7.5 %collective-permute-done.8.rest_3_ = bf16[500,256]{1,0:T(8,128)(2,1)} collective-permute-done((bf16[500,256]{1,0:T(8,128)(2,1)}, bf16[500,256]{1,0:T(8,128)(2,1)}, u32[]{:S(2)}, u32[]{:S(2)}) %collective-permute-start.8) | collective-permute-done | bytes 256032 | tf_op jit(solution)/shard_map/ppermute | solution.py:30
  50.2 2.6 %collective-permute-start.11 = (bf16[4,2,250,128]{3,2,1,0:T(8,128)(2,1)S(1)}, bf16[4,2,250,128]{3,2,1,0:T(8,128)(2,1)S(1)}, u32[]{:S(2)}, u32[]{:S(2)}) collective-permute-start(bf16[4,2,250,128]{3,2,1,0:T(8,128)(2,1)S(1)} %pad_maximum_fusion.2.rest_5_.rest_9_.rest_13_.rest_17_), channel_id=1, source_target_pairs={{0,16},{1,17},{2,18},{3,19},{4,20},{5,21},{6,22},{7,23},{8,24},{9,... | collective-permute-start | bytes 1536008 | tf_op jit(solution)/shard_map/ppermute | solution.py:30
  55.8 4.7 %fusion.2 = f32[512,512]{1,0:T(8,128)S(1)} fusion(f32[512,512]{1,0:T(8,128)} %collective-permute-done.15, f32[512,1024]{1,0:T(8,128)S(1)} %copy-done.2), kind=kOutput, calls=%fused_computation.6 | convolution fusion | flops 1610612736 | bytes 3145728 | tf_op jit(solution)/shard_map/dot_general | solution.py:426
  60.5 2.9 %collective-permute-done.10.rest_6_.rest_10_.rest_14_.rest_18_ = bf16[4,2,250,128]{3,2,1,0:T(8,128)(2,1)S(1)} collective-permute-done((bf16[4,2,250,128]{3,2,1,0:T(8,128)(2,1)S(1)}, bf16[4,2,250,128]{3,2,1,0:T(8,128)(2,1)S(1)}, u32[]{:S(2)}, u32[]{:S(2)}) %collective-permute-start.10) | collective-permute-done | bytes 512032 | tf_op jit(solution)/shard_map/ppermute | solution.py:30
  63.5 1.9 %fusion.1 = f32[512,512]{1,0:T(8,128)S(1)} fusion(f32[512,512]{1,0:T(8,128)S(1)} %copy-done.4, f32[512,512]{1,0:T(8,128)S(1)} %fusion.2, pred[]{:T(512)S(6)} %eq.13), kind=kOutput, calls=%fused_computation.5 | convolution fusion | flops 1611137024 | bytes 3145729 | tf_op jit(solution)/shard_map/dot_general | solution.py:427
  65.8 10.1 %collective-permute-done.11.rest_7_.rest_11_.rest_15_.rest_19_ = bf16[4,2,250,128]{3,2,1,0:T(8,128)(2,1)S(1)} collective-permute-done((bf16[4,2,250,128]{3,2,1,0:T(8,128)(2,1)S(1)}, bf16[4,2,250,128]{3,2,1,0:T(8,128)(2,1)S(1)}, u32[]{:S(2)}, u32[]{:S(2)}) %collective-permute-start.11) | collective-permute-done | bytes 512032 | tf_op jit(solution)/shard_map/ppermute | solution.py:30
  75.9 1.8 %collective-permute-done.12.rest_8_.rest_12_.rest_16_.rest_20_ = bf16[4,2,250,128]{3,2,1,0:T(8,128)(2,1)S(1)} collective-permute-done((bf16[4,2,250,128]{3,2,1,0:T(8,128)(2,1)S(1)}, bf16[4,2,250,128]{3,2,1,0:T(8,128)(2,1)S(1)}, u32[]{:S(2)}, u32[]{:S(2)}) %collective-permute-start.12) | collective-permute-done | bytes 512032 | tf_op jit(solution)/shard_map/ppermute | solution.py:30
  79.1 1.6 %collective-permute-start.34 = (bf16[512,1024]{1,0:T(8,128)(2,1)}, bf16[512,1024]{1,0:T(8,128)(2,1)}, u32[]{:S(2)}, u32[]{:S(2)}) collective-permute-start(bf16[512,1024]{1,0:T(8,128)(2,1)} %convert_element_type.10.refs_0_), channel_id=1, source_target_pairs={{14,30},{15,31}} | collective-permute-start | bytes 3145736 | tf_op jit(solution)/shard_map/ppermute | solution.py:30
  80.7 11.6 %project.1 = (f32[8,640]{1,0:T(8,128)S(1)}, f32[8,640]{1,0:T(8,128)S(1)}, f32[8,640]{1,0:T(8,128)S(1)}, f32[8,640]{1,0:T(8,128)S(1)}) custom-call(s32[5]{0:T(128)S(1)} %stack.80.where_ref, bf16[4000,250]{1,0:T(8,128)(2,1)S(1)} %bitcast.34, bf16[4000,250]{1,0:T(8,128)(2,1)} %bitcast.18.sib_ref, f32[8,8]{1,0:T(8,128)S(1)} %copy-done.12, ...), custom_call_target="tpu_custom_call" | custom-call | flops 8192000000 | bytes 1048576 | tf_op jit(solution)/shard_map/project/pallas_call | solution.py:170
  92.4 3.0 %collective-permute-start.17 = (f32[8,640]{1,0:T(8,128)S(1)}, f32[8,640]{1,0:T(8,128)S(1)}, u32[]{:S(2)}, u32[]{:S(2)}) collective-permute-start(f32[8,640]{1,0:T(8,128)S(1)} %get-tuple-element.89), channel_id=1, source_target_pairs={{0,2},{1,3},{2,0},{3,1},{4,6},{5,7},{6,4},{7,5},{8,10},{9,11},{10,... | collective-permute-start | bytes 61448 | tf_op jit(solution)/shard_map/ppermute | solution.py:30
  95.4 2.4 %collective-permute-start.19 = (f32[8,640]{1,0:T(8,128)S(1)}, f32[8,640]{1,0:T(8,128)S(1)}, u32[]{:S(2)}, u32[]{:S(2)}) collective-permute-start(f32[8,640]{1,0:T(8,128)S(1)} %get-tuple-element.91), channel_id=1, source_target_pairs={{0,6},{1,7},{2,4},{3,5},{4,2},{5,3},{6,0},{7,1},{8,14},{9,15},{10,... | collective-permute-start | bytes 61448 | tf_op jit(solution)/shard_map/ppermute | solution.py:30
  97.8 2.2 %collective-permute-done.18 = f32[8,640]{1,0:T(8,128)S(1)} collective-permute-done((f32[8,640]{1,0:T(8,128)S(1)}, f32[8,640]{1,0:T(8,128)S(1)}, u32[]{:S(2)}, u32[]{:S(2)}) %collective-permute-start.18) | collective-permute-done | bytes 20512 | tf_op jit(solution)/shard_map/ppermute | solution.py:30
  106.0 1.8 %collective-permute-done.22 = f32[8,640]{1,0:T(8,128)S(1)} collective-permute-done((f32[8,640]{1,0:T(8,128)S(1)}, f32[8,640]{1,0:T(8,128)S(1)}, u32[]{:S(2)}, u32[]{:S(2)}) %collective-permute-start.22) | collective-permute-done | bytes 20512 | tf_op jit(solution)/shard_map/ppermute | solution.py:30
  113.1 7.8 %collective-permute-done.27 = f32[8,512]{1,0:T(8,128)S(1)} collective-permute-done((f32[8,512]{1,0:T(8,128)S(1)}, f32[8,512]{1,0:T(8,128)S(1)}, u32[]{:S(2)}, u32[]{:S(2)}) %collective-permute-start.27) | collective-permute-done | bytes 16416 | tf_op jit(solution)/shard_map/ppermute | solution.py:30
  121.0 1.8 %turn.3.refs_1_ = f32[8,512]{1,0:T(8,128)S(1)} custom-call(s32[1]{0:T(128)} %bitcast.5.where_ref, bf16[512,1024]{1,0:T(8,128)(2,1)S(1)} %collective-permute-done.9.refs_0_.refs_2_, bf16[512,1024]{1,0:T(8,128)(2,1)S(1)} %collective-permute-done.16.refs_1_.refs_3_, bf16[512,1024]{1,0:T(8,128)(2,1)S(1)} %get-tuple-element.86.refs_0_.refs_2_.refs_4_, ...), custom_call_target="tpu_custom_call" | custom-call | flops 1048576 | bytes 65536 | tf_op jit(solution)/shard_map/turn/pallas_call | solution.py:319
  125.1 1.6 %apply_weights.3 = f32[8,512]{1,0:T(8,128)S(1)} custom-call(s32[1]{0:T(128)} %bitcast.5.where_ref, bf16[512,1024]{1,0:T(8,128)(2,1)} %convert_element_type.10.refs_0_, f32[8,512]{1,0:T(8,128)S(1)} %add.85.refs_1_, f32[8,512]{1,0:T(8,128)S(1)} %collective-permute-done.30.refs_2_), custom_call_target="tpu_custom_call" | custom-call | flops 1073741824 | bytes 2097152 | tf_op jit(solution)/shard_map/apply_weights/pallas_call | solution.py:274
  130.7 1.8 %turn.4.refs_2_ = f32[16,512]{1,0:T(8,128)S(1)} custom-call(s32[1]{0:T(128)} %bitcast.5.where_ref, bf16[512,1024]{1,0:T(8,128)(2,1)S(1)} %collective-permute-done.9.refs_0_.refs_2_, bf16[512,1024]{1,0:T(8,128)(2,1)S(1)} %collective-permute-done.16.refs_1_.refs_3_, bf16[512,1024]{1,0:T(8,128)(2,1)S(1)} %get-tuple-element.86.refs_0_.refs_2_.refs_4_, ...), custom_call_target="tpu_custom_call" | custom-call | flops 1048576 | bytes 65536 | tf_op jit(solution)/shard_map/turn/pallas_call | solution.py:319
  134.4 2.0 %factor_inverse.1.inverse_ref = f32[8,8]{1,0:T(8,128)} custom-call(f32[8,640]{1,0:T(8,128)} %copy-done.7), custom_call_target="tpu_custom_call" | custom-call | tf_op jit(solution)/shard_map/factor_inverse/pallas_call | solution.py:98
  137.6 3.5 %turn.5.refs_3_ = f32[24,512]{1,0:T(8,128)S(1)} custom-call(s32[1]{0:T(128)} %bitcast.5.where_ref, bf16[512,1024]{1,0:T(8,128)(2,1)} %collective-permute-done.34.refs_0_, bf16[512,1024]{1,0:T(8,128)(2,1)} %collective-permute-done.35.refs_1_, bf16[512,1024]{1,0:T(8,128)(2,1)S(1)} %collective-permute-done.9.refs_0_.refs_2_, bf16[512,1024]{1,0:T(8,128)(2,1)S(1)} %copy-done.1, ...), custom_call_target="tpu_custom_call" | custom-call | flops 1048576 | bytes 65536 | tf_op jit(solution)/shard_map/turn/pallas_call | solution.py:319
  141.7 1.6 %combine.1 = (f32[2,512]{1,0:T(2,128)}, f32[2,512]{1,0:T(2,128)}, f32[2,512]{1,0:T(2,128)}, f32[2,512]{1,0:T(2,128)}) custom-call(s32[5]{0:T(128)} %stack.71.turn_ref, f32[8,8]{1,0:T(8,128)} %factor_inverse.1.inverse_ref, f32[8,512]{1,0:T(8,128)} %copy-done.11, f32[8,512]{1,0:T(8,128)} %copy-done.10, f32[16,512]{1,0:T(8,128)} %copy-done.9, f32[24,512]{1,0:T(8,128)} %copy-done.8), custom_call_target="tpu_custom_call" | custom-call | tf_op jit(solution)/shard_map/combine/pallas_call | solution.py:353
  146.0 9.8 %collective-permute-done.39 = f32[2,512]{1,0:T(2,128)S(1)} collective-permute-done((f32[2,512]{1,0:T(2,128)}, f32[2,512]{1,0:T(2,128)S(1)}, u32[]{:S(2)}, u32[]{:S(2)}) %collective-permute-start.39) | collective-permute-done | bytes 4128 | tf_op jit(solution)/shard_map/ppermute | solution.py:30
  (106 shorter events, 42.0 us)
Async XLA Ops:
  0.0 16.7 %collective-permute-start.3 = (bf16[8,500,250]{2,0,1:T(8,128)(2,1)}, bf16[8,500,250]{2,0,1:T(8,128)(2,1)}, u32[]{:S(2)}, u32[]{:S(2)}) collective-permute-start(bf16[8,500,250]{2,0,1:T(8,128)(2,1)} %param.4), channel_id=1, source_target_pairs={{0,1},{1,0},{2,3},{3,2},{4,5},{5,4},{6,7},{7,6},{8,9},{9,8},{10,11... | collective-permute-start | bytes 6000008 | tf_op jit(solution)/shard_map/ppermute | solution.py:30
  2.0 14.8 %collective-permute-start.4 = (bf16[500,256]{1,0:T(8,128)(2,1)S(1)}, bf16[500,256]{1,0:T(8,128)(2,1)S(1)}, u32[]{:S(2)}, u32[]{:S(2)}) collective-permute-start(bf16[500,256]{1,0:T(8,128)(2,1)S(1)} %get-tuple-element.118), channel_id=1, source_target_pairs={{0,4},{1,5},{2,6},{3,7},{4,0},{5,1},{6,2},{7,3},{8,12},{9,13},{10,... | collective-permute-start | bytes 768008 | tf_op jit(solution)/shard_map/ppermute | solution.py:30
  3.6 5.9 %collective-permute-start = (bf16[2,250,128]{2,1,0:T(8,128)(2,1)S(1)}, bf16[2,250,128]{2,1,0:T(8,128)(2,1)S(1)}, u32[]{:S(2)}, u32[]{:S(2)}) collective-permute-start(bf16[2,250,128]{2,1,0:T(8,128)(2,1)S(1)} %get-tuple-element.116), channel_id=1, source_target_pairs={{0,8},{1,9},{2,10},{3,11},{4,12},{5,13},{6,14},{7,15},{8,0},{9,1},... | collective-permute-start | bytes 384008 | tf_op jit(solution)/shard_map/ppermute | solution.py:30
  5.1 8.0 %collective-permute-start.1 = (bf16[2,250,128]{2,1,0:T(8,128)(2,1)S(1)}, bf16[2,250,128]{2,1,0:T(8,128)(2,1)S(1)}, u32[]{:S(2)}, u32[]{:S(2)}) collective-permute-start(bf16[2,250,128]{2,1,0:T(8,128)(2,1)S(1)} %get-tuple-element.115), channel_id=1, source_target_pairs={{0,16},{1,17},{2,18},{3,19},{4,20},{5,21},{6,22},{7,23},{8,24},{9,... | collective-permute-start | bytes 384008 | tf_op jit(solution)/shard_map/ppermute | solution.py:30
  6.7 6.5 %collective-permute-start.2 = (bf16[2,250,128]{2,1,0:T(8,128)(2,1)S(1)}, bf16[2,250,128]{2,1,0:T(8,128)(2,1)S(1)}, u32[]{:S(2)}, u32[]{:S(2)}) collective-permute-start(bf16[2,250,128]{2,1,0:T(8,128)(2,1)S(1)} %get-tuple-element.114), channel_id=1, source_target_pairs={{0,24},{1,25},{2,26},{3,27},{4,28},{5,29},{6,30},{7,31},{8,16},{9,... | collective-permute-start | bytes 384008 | tf_op jit(solution)/shard_map/ppermute | solution.py:30
  17.9 29.5 %collective-permute-start.9 = (bf16[512,1024]{1,0:T(8,128)(2,1)}, bf16[512,1024]{1,0:T(8,128)(2,1)S(1)}, u32[]{:S(2)}, u32[]{:S(2)}) collective-permute-start(bf16[512,1024]{1,0:T(8,128)(2,1)} %convert_element_type.10.refs_0_), channel_id=1, source_target_pairs={{2,10},{3,11},{12,20},{13,21},{22,30},{23,31}} | collective-permute-start | bytes 3145736 | tf_op jit(solution)/shard_map/ppermute | solution.py:30
  21.2 14.9 %collective-permute-start.5 = (bf16[2,250,128]{2,1,0:T(8,128)(2,1)}, bf16[2,250,128]{2,1,0:T(8,128)(2,1)}, u32[]{:S(2)}, u32[]{:S(2)}) collective-permute-start(bf16[2,250,128]{2,1,0:T(8,128)(2,1)} %get-tuple-element.111), channel_id=1, source_target_pairs={{0,2},{1,3},{2,0},{3,1},{4,6},{5,7},{6,4},{7,5},{8,10},{9,11},{10,... | collective-permute-start | bytes 384008 | tf_op jit(solution)/shard_map/ppermute | solution.py:30
  21.2 18.7 %collective-permute-start.6 = (bf16[2,250,128]{2,1,0:T(8,128)(2,1)}, bf16[2,250,128]{2,1,0:T(8,128)(2,1)}, u32[]{:S(2)}, u32[]{:S(2)}) collective-permute-start(bf16[2,250,128]{2,1,0:T(8,128)(2,1)} %get-tuple-element.110), channel_id=1, source_target_pairs={{0,4},{1,5},{2,6},{3,7},{4,0},{5,1},{6,2},{7,3},{8,12},{9,13},{10,... | collective-permute-start | bytes 384008 | tf_op jit(solution)/shard_map/ppermute | solution.py:30
  23.5 16.4 %collective-permute-start.7 = (bf16[2,250,128]{2,1,0:T(8,128)(2,1)}, bf16[2,250,128]{2,1,0:T(8,128)(2,1)}, u32[]{:S(2)}, u32[]{:S(2)}) collective-permute-start(bf16[2,250,128]{2,1,0:T(8,128)(2,1)} %get-tuple-element.109), channel_id=1, source_target_pairs={{0,6},{1,7},{2,4},{3,5},{4,2},{5,3},{6,0},{7,1},{8,14},{9,15},{10,... | collective-permute-start | bytes 384008 | tf_op jit(solution)/shard_map/ppermute | solution.py:30
  25.6 21.8 %collective-permute-start.8 = (bf16[500,256]{1,0:T(8,128)(2,1)}, bf16[500,256]{1,0:T(8,128)(2,1)}, u32[]{:S(2)}, u32[]{:S(2)}) collective-permute-start(bf16[500,256]{1,0:T(8,128)(2,1)} %get-tuple-element.58), channel_id=1, source_target_pairs={{0,4},{1,5},{2,6},{3,7},{4,0},{5,1},{6,2},{7,3},{8,12},{9,13},{10,... | collective-permute-start | bytes 768008 | tf_op jit(solution)/shard_map/ppermute | solution.py:30
  47.4 6.9 %collective-permute-start.15 = (f32[512,512]{1,0:T(8,128)}, f32[512,512]{1,0:T(8,128)}, u32[]{:S(2)}, u32[]{:S(2)}) collective-permute-start(f32[512,512]{1,0:T(8,128)} %copy-done.3), channel_id=1, source_target_pairs={{0,1},{1,0},{2,3},{3,2},{4,5},{5,4},{6,7},{7,6},{8,9},{9,8},{10,11... | collective-permute-start | bytes 3145736 | tf_op jit(solution)/shard_map/ppermute | solution.py:30
  48.7 14.8 %collective-permute-start.10 = (bf16[4,2,250,128]{3,2,1,0:T(8,128)(2,1)S(1)}, bf16[4,2,250,128]{3,2,1,0:T(8,128)(2,1)S(1)}, u32[]{:S(2)}, u32[]{:S(2)}) collective-permute-start(bf16[4,2,250,128]{3,2,1,0:T(8,128)(2,1)S(1)} %pad_maximum_fusion.2.rest_5_.rest_9_.rest_13_.rest_17_), channel_id=1, source_target_pairs={{0,8},{1,9},{2,10},{3,11},{4,12},{5,13},{6,14},{7,15},{8,0},{9,1},... | collective-permute-start | bytes 1536008 | tf_op jit(solution)/shard_map/ppermute | solution.py:30
  50.2 25.6 %collective-permute-start.11 = (bf16[4,2,250,128]{3,2,1,0:T(8,128)(2,1)S(1)}, bf16[4,2,250,128]{3,2,1,0:T(8,128)(2,1)S(1)}, u32[]{:S(2)}, u32[]{:S(2)}) collective-permute-start(bf16[4,2,250,128]{3,2,1,0:T(8,128)(2,1)S(1)} %pad_maximum_fusion.2.rest_5_.rest_9_.rest_13_.rest_17_), channel_id=1, source_target_pairs={{0,16},{1,17},{2,18},{3,19},{4,20},{5,21},{6,22},{7,23},{8,24},{9,... | collective-permute-start | bytes 1536008 | tf_op jit(solution)/shard_map/ppermute | solution.py:30
  52.8 24.9 %collective-permute-start.12 = (bf16[4,2,250,128]{3,2,1,0:T(8,128)(2,1)S(1)}, bf16[4,2,250,128]{3,2,1,0:T(8,128)(2,1)S(1)}, u32[]{:S(2)}, u32[]{:S(2)}) collective-permute-start(bf16[4,2,250,128]{3,2,1,0:T(8,128)(2,1)S(1)} %pad_maximum_fusion.2.rest_5_.rest_9_.rest_13_.rest_17_), channel_id=1, source_target_pairs={{0,24},{1,25},{2,26},{3,27},{4,28},{5,29},{6,30},{7,31},{8,16},{9,... | collective-permute-start | bytes 1536008 | tf_op jit(solution)/shard_map/ppermute | solution.py:30
  54.2 24.9 %collective-permute-start.13 = (bf16[500,512]{1,0:T(8,128)(2,1)}, bf16[500,512]{1,0:T(8,128)(2,1)S(1)}, u32[]{:S(2)}, u32[]{:S(2)}) collective-permute-start(bf16[500,512]{1,0:T(8,128)(2,1)} %rest_0_), channel_id=1, source_target_pairs={{0,2},{1,3},{2,0},{3,1},{4,6},{5,7},{6,4},{7,5},{8,10},{9,11},{10,... | collective-permute-start | bytes 1536008 | tf_op jit(solution)/shard_map/ppermute | solution.py:30
  54.3 24.7 %collective-permute-start.14 = (bf16[500,512]{1,0:T(8,128)(2,1)S(1)}, bf16[500,512]{1,0:T(8,128)(2,1)S(1)}, u32[]{:S(2)}, u32[]{:S(2)}) collective-permute-start(bf16[500,512]{1,0:T(8,128)(2,1)S(1)} %copy-done.5), channel_id=1, source_target_pairs={{0,6},{1,7},{2,4},{3,5},{4,2},{5,3},{6,0},{7,1},{8,14},{9,15},{10,... | collective-permute-start | bytes 1536008 | tf_op jit(solution)/shard_map/ppermute | solution.py:30
  63.5 28.9 %collective-permute-start.16 = (bf16[512,1024]{1,0:T(8,128)(2,1)S(1)}, bf16[512,1024]{1,0:T(8,128)(2,1)S(1)}, u32[]{:S(2)}, u32[]{:S(2)}) collective-permute-start(bf16[512,1024]{1,0:T(8,128)(2,1)S(1)} %collective-permute-done.9.refs_0_.refs_2_), channel_id=1, source_target_pairs={{0,1},{1,0},{2,3},{3,2},{4,5},{5,4},{6,7},{7,6},{8,9},{9,8},{10,11... | collective-permute-start | bytes 3145736 | tf_op jit(solution)/shard_map/ppermute | solution.py:30
  79.1 43.7 %collective-permute-start.34 = (bf16[512,1024]{1,0:T(8,128)(2,1)}, bf16[512,1024]{1,0:T(8,128)(2,1)}, u32[]{:S(2)}, u32[]{:S(2)}) collective-permute-start(bf16[512,1024]{1,0:T(8,128)(2,1)} %convert_element_type.10.refs_0_), channel_id=1, source_target_pairs={{14,30},{15,31}} | collective-permute-start | bytes 3145736 | tf_op jit(solution)/shard_map/ppermute | solution.py:30
  92.4 5.5 %collective-permute-start.17 = (f32[8,640]{1,0:T(8,128)S(1)}, f32[8,640]{1,0:T(8,128)S(1)}, u32[]{:S(2)}, u32[]{:S(2)}) collective-permute-start(f32[8,640]{1,0:T(8,128)S(1)} %get-tuple-element.89), channel_id=1, source_target_pairs={{0,2},{1,3},{2,0},{3,1},{4,6},{5,7},{6,4},{7,5},{8,10},{9,11},{10,... | collective-permute-start | bytes 61448 | tf_op jit(solution)/shard_map/ppermute | solution.py:30
  95.4 4.7 %collective-permute-start.18 = (f32[8,640]{1,0:T(8,128)S(1)}, f32[8,640]{1,0:T(8,128)S(1)}, u32[]{:S(2)}, u32[]{:S(2)}) collective-permute-start(f32[8,640]{1,0:T(8,128)S(1)} %get-tuple-element.90), channel_id=1, source_target_pairs={{0,4},{1,5},{2,6},{3,7},{4,0},{5,1},{6,2},{7,3},{8,12},{9,13},{10,... | collective-permute-start | bytes 61448 | tf_op jit(solution)/shard_map/ppermute | solution.py:30
  95.4 5.6 %collective-permute-start.19 = (f32[8,640]{1,0:T(8,128)S(1)}, f32[8,640]{1,0:T(8,128)S(1)}, u32[]{:S(2)}, u32[]{:S(2)}) collective-permute-start(f32[8,640]{1,0:T(8,128)S(1)} %get-tuple-element.91), channel_id=1, source_target_pairs={{0,6},{1,7},{2,4},{3,5},{4,2},{5,3},{6,0},{7,1},{8,14},{9,15},{10,... | collective-permute-start | bytes 61448 | tf_op jit(solution)/shard_map/ppermute | solution.py:30
  101.0 3.8 %collective-permute-start.20 = (f32[8,640]{1,0:T(8,128)S(1)}, f32[8,640]{1,0:T(8,128)S(1)}, u32[]{:S(2)}, u32[]{:S(2)}) collective-permute-start(f32[8,640]{1,0:T(8,128)S(1)} %add_add_fusion.1), channel_id=1, source_target_pairs={{0,8},{1,9},{2,10},{3,11},{4,12},{5,13},{6,14},{7,15},{8,0},{9,1},... | collective-permute-start | bytes 61448 | tf_op jit(solution)/shard_map/ppermute | solution.py:30
  102.2 3.8 %collective-permute-start.21 = (f32[8,640]{1,0:T(8,128)S(1)}, f32[8,640]{1,0:T(8,128)S(1)}, u32[]{:S(2)}, u32[]{:S(2)}) collective-permute-start(f32[8,640]{1,0:T(8,128)S(1)} %add_add_fusion.1), channel_id=1, source_target_pairs={{0,16},{1,17},{2,18},{3,19},{4,20},{5,21},{6,22},{7,23},{8,24},{9,... | collective-permute-start | bytes 61448 | tf_op jit(solution)/shard_map/ppermute | solution.py:30
  103.2 4.7 %collective-permute-start.22 = (f32[8,640]{1,0:T(8,128)S(1)}, f32[8,640]{1,0:T(8,128)S(1)}, u32[]{:S(2)}, u32[]{:S(2)}) collective-permute-start(f32[8,640]{1,0:T(8,128)S(1)} %add_add_fusion.1), channel_id=1, source_target_pairs={{0,24},{1,25},{2,26},{3,27},{4,28},{5,29},{6,30},{7,31},{8,16},{9,... | collective-permute-start | bytes 61448 | tf_op jit(solution)/shard_map/ppermute | solution.py:30
  109.8 3.3 %collective-permute-start.24 = (f32[8,512]{1,0:T(8,128)S(1)}, f32[8,512]{1,0:T(8,128)S(1)}, u32[]{:S(2)}, u32[]{:S(2)}) collective-permute-start(f32[8,512]{1,0:T(8,128)S(1)} %apply_weights.2.refs_0_), channel_id=1, source_target_pairs={{0,10},{1,11}} | collective-permute-start | bytes 49160 | tf_op jit(solution)/shard_map/ppermute | solution.py:30
  111.8 9.2 %collective-permute-start.27 = (f32[8,512]{1,0:T(8,128)S(1)}, f32[8,512]{1,0:T(8,128)S(1)}, u32[]{:S(2)}, u32[]{:S(2)}) collective-permute-start(f32[8,512]{1,0:T(8,128)S(1)} %apply_weights.2.refs_0_), channel_id=1, source_target_pairs={{0,6},{1,7}} | collective-permute-start | bytes 49160 | tf_op jit(solution)/shard_map/ppermute | solution.py:30
  122.8 13.6 %collective-permute-start.35 = (bf16[512,1024]{1,0:T(8,128)(2,1)}, bf16[512,1024]{1,0:T(8,128)(2,1)}, u32[]{:S(2)}, u32[]{:S(2)}) collective-permute-start(bf16[512,1024]{1,0:T(8,128)(2,1)} %collective-permute-done.34.refs_0_), channel_id=1, source_target_pairs={{0,1},{1,0},{2,3},{3,2},{4,5},{5,4},{6,7},{7,6},{8,9},{9,8},{10,11... | collective-permute-start | bytes 3145736 | tf_op jit(solution)/shard_map/ppermute | solution.py:30
  123.3 4.7 %collective-permute-start.28 = (f32[8,512]{1,0:T(8,128)S(1)}, f32[8,512]{1,0:T(8,128)S(1)}, u32[]{:S(2)}, u32[]{:S(2)}) collective-permute-start(f32[8,512]{1,0:T(8,128)S(1)} %turn.3.refs_1_), channel_id=1, source_target_pairs={{10,20},{11,21}} | collective-permute-start | bytes 49160 | tf_op jit(solution)/shard_map/ppermute | solution.py:30
  124.0 4.1 %collective-permute-start.29 = (f32[8,512]{1,0:T(8,128)S(1)}, f32[8,512]{1,0:T(8,128)S(1)}, u32[]{:S(2)}, u32[]{:S(2)}) collective-permute-start(f32[8,512]{1,0:T(8,128)S(1)} %turn.3.refs_1_), channel_id=1, source_target_pairs={{10,21},{11,20}} | collective-permute-start | bytes 49160 | tf_op jit(solution)/shard_map/ppermute | solution.py:30
  132.5 3.9 %collective-permute-start.33 = (f32[16,512]{1,0:T(8,128)S(1)}, f32[16,512]{1,0:T(8,128)S(1)}, u32[]{:S(2)}, u32[]{:S(2)}) collective-permute-start(f32[16,512]{1,0:T(8,128)S(1)} %turn.4.refs_2_), channel_id=1, source_target_pairs={{20,30},{21,31}} | collective-permute-start | bytes 98312 | tf_op jit(solution)/shard_map/ppermute | solution.py:30
  133.1 3.2 %collective-permute-start.36 = (f32[16,512]{1,0:T(8,128)S(1)}, f32[16,512]{1,0:T(8,128)S(1)}, u32[]{:S(2)}, u32[]{:S(2)}) collective-permute-start(f32[16,512]{1,0:T(8,128)S(1)} %turn.4.refs_2_), channel_id=1, source_target_pairs={{20,31},{21,30}} | collective-permute-start | bytes 98312 | tf_op jit(solution)/shard_map/ppermute | solution.py:30
  144.7 11.1 %collective-permute-start.39 = (f32[2,512]{1,0:T(2,128)}, f32[2,512]{1,0:T(2,128)S(1)}, u32[]{:S(2)}, u32[]{:S(2)}) collective-permute-start(f32[2,512]{1,0:T(2,128)} %get-tuple-element.106), channel_id=1, source_target_pairs={{0,24},{1,25},{10,18},{11,19},{20,12},{21,13},{30,6},{31,7}} | collective-permute-start | bytes 12296 | tf_op jit(solution)/shard_map/ppermute | solution.py:30
  (22 other events, 179.8 us)

commit v10 on v9

--- a/solution.py
+++ b/solution.py
@@ -481,9 +481,14 @@
         if t == 2:
             far = sum(far[1:], far[0])
             acted = apply_weights(at_core, [own_rows], far, move(far, swap))
-            brought = move(acted, lambda g, j, c: (j, j, c) if g == 0 and j >= 2 else None)
-            near, near_sib, brought = lax.optimization_barrier((near, near_sib, brought))
-            rest = rest[:, :points] - brought
+            brought = {
+                z: move(acted, lambda g, j, c: (j, j, c) if g == 0 and j == z else None)
+                for z in range(2, gen_count)
+            }
+        if t >= 2:
+            if t == 2:
+                near, near_sib, brought[t] = lax.optimization_barrier((near, near_sib, brought[t]))
+            rest = rest[:, :points] - brought[t]
             sib_rest = move(rest, swap)
         if t == gen_count - 1:
             near, inverse_factor = lax.optimization_barrier((near, inverse_factor))

time: 158 us -> 159 us (level)
    ppermute x40 -> x42, starting transfers between devices: 38.5 us -> 39.5 us  [move(): return lax.ppermute(value, BOTH, pairs)]
    ppermute x40 -> x42, waiting for transfers between devices: 64.6 us -> 64.2 us  [move(): return lax.ppermute(value, BOTH, pairs)]
  transfers between devices with their start and end apart: 40 -> 42, of which waited for: 20 -> 20; matrix products, arithmetic and copies ran while one was open for 10% -> 10% of each run, Pallas kernels for 18% -> 17%
where the time goes in v10:
time: 159 us; the launch traced here: 158 us
  waiting for transfers between devices  64.2 us (40%)
  starting transfers between devices  39.5 us (25%)
  Pallas kernels  32.6 us (21%)
  local copies, waits for them, and re-layouts  8.66 us (5%)
  matrix products  6.6 us (4%)
  other arithmetic  5.65 us (4%)
    ppermute x42, waiting for transfers between devices, move(): return lax.ppermute(value, BOTH, pairs)  64.2 us
    ppermute x42, starting transfers between devices, move(): return lax.ppermute(value, BOTH, pairs)  39.5 us
    pallas_call x1, Pallas kernels, project(): pl.pallas_call(kernel, grid_spec=pltpu.PrefetchScalarGridSpec(num_scalar_...  11.7 us
    pallas_call x3, Pallas kernels, turn(): pl.pallas_call(functools.partial(turn_kernel, count), in_specs=[pl.BlockS...  7.06 us
    pallas_call x1, Pallas kernels, invert_block(): pl.pallas_call(invert_kernel, grid_spec=pltpu.PrefetchScalarGridSpec(num_...  5.34 us
    dot_general x1, matrix products, on_device(): corner = jnp.dot(metric_factor[:, :points], upper, precision=HIGHEST)  4.71 us
  transfers between devices with their start and end apart: 42, of which 20 were waited for; matrix products, arithmetic and copies ran while one was open for 10% of the time, Pallas kernels for 17%

profile of v10, /device:TPU:24, one launch (start us, length us, event | category | flops | bytes accessed | tf_op | source)
XLA Modules:
  0.0 157.8 jit_solution(12837872146708943266)
XLA Ops:
  0.0 2.0 %fusion.6 = (bf16[500,256]{1,0:T(8,128)(2,1)}, bf16[500,256]{1,0:T(8,128)(2,1)S(1)}) fusion(bf16[500,512]{1,0:T(8,128)(2,1)} %rest_0_), kind=kLoop, calls=%fused_computation.30 | loop fusion | bytes 1024000 | tf_op jit(solution)/shard_map/slice | solution.py:387
  3.6 1.6 collective-permute-start
  7.1 2.3 %collective-permute-done = bf16[2,250,128]{2,1,0:T(8,128)(2,1)S(1)} collective-permute-done((bf16[2,250,128]{2,1,0:T(8,128)(2,1)S(1)}, bf16[2,250,128]{2,1,0:T(8,128)(2,1)S(1)}, u32[]{:S(2)}, u32[]{:S(2)}) %collective-permute-start) | collective-permute-done | bytes 128032 | tf_op jit(solution)/shard_map/ppermute | solution.py:30
  9.5 3.7 %collective-permute-done.1 = bf16[2,250,128]{2,1,0:T(8,128)(2,1)S(1)} collective-permute-done((bf16[2,250,128]{2,1,0:T(8,128)(2,1)S(1)}, bf16[2,250,128]{2,1,0:T(8,128)(2,1)S(1)}, u32[]{:S(2)}, u32[]{:S(2)}) %collective-permute-start.1) | collective-permute-done | bytes 128032 | tf_op jit(solution)/shard_map/ppermute | solution.py:30
  14.0 2.8 %collective-permute-done.4.rest_2_ = bf16[500,256]{1,0:T(8,128)(2,1)S(1)} collective-permute-done((bf16[500,256]{1,0:T(8,128)(2,1)S(1)}, bf16[500,256]{1,0:T(8,128)(2,1)S(1)}, u32[]{:S(2)}, u32[]{:S(2)}) %collective-permute-start.4) | collective-permute-done | bytes 256032 | tf_op jit(solution)/shard_map/ppermute | solution.py:30
  19.4 1.9 %dynamic-slice_bitcast_fusion = (bf16[2,250,128]{2,1,0:T(8,128)(2,1)}, bf16[2,250,128]{2,1,0:T(8,128)(2,1)}, bf16[2,250,128]{2,1,0:T(8,128)(2,1)}, bf16[2,250,128]{2,1,0:T(8,128)(2,1)S(1)}) fusion(bf16[4,2,250,128]{3,2,1,0:T(8,128)(2,1)} %pad_maximum_fusion.1, s32[]{:T(128)S(6)} %select_n.75, s32[]{:T(128)S(6)} %select_n.74, s32[]{:T(128)S(6)} %select_n.73, ...), kind=kLoop, calls=%fused_computation.11 | loop fusion | bytes 1024016 | tf_op jit(solution)/shard_map/jit(dynamic_index_in_dim)/squeeze | solution.py:396
  21.2 2.3 %collective-permute-start.6 = (bf16[2,250,128]{2,1,0:T(8,128)(2,1)}, bf16[2,250,128]{2,1,0:T(8,128)(2,1)}, u32[]{:S(2)}, u32[]{:S(2)}) collective-permute-start(bf16[2,250,128]{2,1,0:T(8,128)(2,1)} %get-tuple-element.112), channel_id=1, source_target_pairs={{0,4},{1,5},{2,6},{3,7},{4,0},{5,1},{6,2},{7,3},{8,12},{9,13},{10,... | collective-permute-start | bytes 384008 | tf_op jit(solution)/shard_map/ppermute | solution.py:30
  23.5 2.1 %collective-permute-start.7 = (bf16[2,250,128]{2,1,0:T(8,128)(2,1)}, bf16[2,250,128]{2,1,0:T(8,128)(2,1)}, u32[]{:S(2)}, u32[]{:S(2)}) collective-permute-start(bf16[2,250,128]{2,1,0:T(8,128)(2,1)} %get-tuple-element.111), channel_id=1, source_target_pairs={{0,6},{1,7},{2,4},{3,5},{4,2},{5,3},{6,0},{7,1},{8,14},{9,15},{10,... | collective-permute-start | bytes 384008 | tf_op jit(solution)/shard_map/ppermute | solution.py:30
  27.0 5.3 %invert_block.1 = f32[512,512]{1,0:T(8,128)S(1)} custom-call(s32[2]{0:T(128)S(1)} %pad_add_fusion.where_ref, f32[512,1024]{1,0:T(8,128)S(1)} %copy-done.2), custom_call_target="tpu_custom_call" | custom-call | flops 4294967296 | bytes 4194304 | tf_op jit(solution)/shard_map/invert_block/pallas_call | solution.py:230
  33.4 2.8 %pivot_entries.1.entries_ref = f32[8,8]{1,0:T(8,128)} custom-call(s32[8]{0:T(128)} %get-tuple-element.122.row_ref, bf16[500,8,250]{2,1,0:T(8,128)(2,1)} %bitcast.33, bf16[500,8,250]{2,1,0:T(8,128)(2,1)} %bitcast.16.sib_ref, s32[8]{0:T(128)} %get-tuple-element.123.own_col_ref, s32[8]{0:T(128)} %get-tuple-element.121.sib_col_ref), custom_call_target="tpu_custom_call" | custom-call | tf_op jit(solution)/shard_map/pivot_entries/pallas_call | solution.py:63
  36.2 3.8 %collective-permute-done.6 = bf16[2,250,128]{2,1,0:T(8,128)(2,1)} collective-permute-done((bf16[2,250,128]{2,1,0:T(8,128)(2,1)}, bf16[2,250,128]{2,1,0:T(8,128)(2,1)}, u32[]{:S(2)}, u32[]{:S(2)}) %collective-permute-start.6) | collective-permute-done | bytes 128032 | tf_op jit(solution)/shard_map/ppermute | solution.py:30
  39.9 7.5 %collective-permute-done.8.rest_3_ = bf16[500,256]{1,0:T(8,128)(2,1)} collective-permute-done((bf16[500,256]{1,0:T(8,128)(2,1)}, bf16[500,256]{1,0:T(8,128)(2,1)}, u32[]{:S(2)}, u32[]{:S(2)}) %collective-permute-start.8) | collective-permute-done | bytes 256032 | tf_op jit(solution)/shard_map/ppermute | solution.py:30
  50.2 2.6 %collective-permute-start.11 = (bf16[4,2,250,128]{3,2,1,0:T(8,128)(2,1)S(1)}, bf16[4,2,250,128]{3,2,1,0:T(8,128)(2,1)S(1)}, u32[]{:S(2)}, u32[]{:S(2)}) collective-permute-start(bf16[4,2,250,128]{3,2,1,0:T(8,128)(2,1)S(1)} %pad_maximum_fusion.2.rest_5_.rest_9_.rest_13_.rest_17_), channel_id=1, source_target_pairs={{0,16},{1,17},{2,18},{3,19},{4,20},{5,21},{6,22},{7,23},{8,24},{9,... | collective-permute-start | bytes 1536008 | tf_op jit(solution)/shard_map/ppermute | solution.py:30
  55.8 4.7 %fusion.2 = f32[512,512]{1,0:T(8,128)S(1)} fusion(f32[512,512]{1,0:T(8,128)} %collective-permute-done.15, f32[512,1024]{1,0:T(8,128)S(1)} %copy-done.2), kind=kOutput, calls=%fused_computation.6 | convolution fusion | flops 1610612736 | bytes 3145728 | tf_op jit(solution)/shard_map/dot_general | solution.py:426
  60.5 2.9 %collective-permute-done.10.rest_6_.rest_10_.rest_14_.rest_18_ = bf16[4,2,250,128]{3,2,1,0:T(8,128)(2,1)S(1)} collective-permute-done((bf16[4,2,250,128]{3,2,1,0:T(8,128)(2,1)S(1)}, bf16[4,2,250,128]{3,2,1,0:T(8,128)(2,1)S(1)}, u32[]{:S(2)}, u32[]{:S(2)}) %collective-permute-start.10) | collective-permute-done | bytes 512032 | tf_op jit(solution)/shard_map/ppermute | solution.py:30
  63.5 1.9 %fusion.1 = f32[512,512]{1,0:T(8,128)S(1)} fusion(f32[512,512]{1,0:T(8,128)S(1)} %copy-done.4, f32[512,512]{1,0:T(8,128)S(1)} %fusion.2, pred[]{:T(512)S(6)} %eq.13), kind=kOutput, calls=%fused_computation.5 | convolution fusion | flops 1611137024 | bytes 3145729 | tf_op jit(solution)/shard_map/dot_general | solution.py:427
  65.8 10.1 %collective-permute-done.11.rest_7_.rest_11_.rest_15_.rest_19_ = bf16[4,2,250,128]{3,2,1,0:T(8,128)(2,1)S(1)} collective-permute-done((bf16[4,2,250,128]{3,2,1,0:T(8,128)(2,1)S(1)}, bf16[4,2,250,128]{3,2,1,0:T(8,128)(2,1)S(1)}, u32[]{:S(2)}, u32[]{:S(2)}) %collective-permute-start.11) | collective-permute-done | bytes 512032 | tf_op jit(solution)/shard_map/ppermute | solution.py:30
  75.9 1.8 %collective-permute-done.12.rest_8_.rest_12_.rest_16_.rest_20_ = bf16[4,2,250,128]{3,2,1,0:T(8,128)(2,1)S(1)} collective-permute-done((bf16[4,2,250,128]{3,2,1,0:T(8,128)(2,1)S(1)}, bf16[4,2,250,128]{3,2,1,0:T(8,128)(2,1)S(1)}, u32[]{:S(2)}, u32[]{:S(2)}) %collective-permute-start.12) | collective-permute-done | bytes 512032 | tf_op jit(solution)/shard_map/ppermute | solution.py:30
  79.1 1.6 %collective-permute-start.34 = (bf16[512,1024]{1,0:T(8,128)(2,1)}, bf16[512,1024]{1,0:T(8,128)(2,1)}, u32[]{:S(2)}, u32[]{:S(2)}) collective-permute-start(bf16[512,1024]{1,0:T(8,128)(2,1)} %convert_element_type.10.refs_0_), channel_id=1, source_target_pairs={{14,30},{15,31}} | collective-permute-start | bytes 3145736 | tf_op jit(solution)/shard_map/ppermute | solution.py:30
  80.7 11.7 %project.1 = (f32[8,640]{1,0:T(8,128)S(1)}, f32[8,640]{1,0:T(8,128)S(1)}, f32[8,640]{1,0:T(8,128)S(1)}, f32[8,640]{1,0:T(8,128)S(1)}) custom-call(s32[5]{0:T(128)S(1)} %stack.80.where_ref, bf16[4000,250]{1,0:T(8,128)(2,1)S(1)} %bitcast.34, bf16[4000,250]{1,0:T(8,128)(2,1)} %bitcast.18.sib_ref, f32[8,8]{1,0:T(8,128)S(1)} %copy-done.12, ...), custom_call_target="tpu_custom_call" | custom-call | flops 8192000000 | bytes 1048576 | tf_op jit(solution)/shard_map/project/pallas_call | solution.py:170
  92.4 3.0 %collective-permute-start.17 = (f32[8,640]{1,0:T(8,128)S(1)}, f32[8,640]{1,0:T(8,128)S(1)}, u32[]{:S(2)}, u32[]{:S(2)}) collective-permute-start(f32[8,640]{1,0:T(8,128)S(1)} %get-tuple-element.89), channel_id=1, source_target_pairs={{0,2},{1,3},{2,0},{3,1},{4,6},{5,7},{6,4},{7,5},{8,10},{9,11},{10,... | collective-permute-start | bytes 61448 | tf_op jit(solution)/shard_map/ppermute | solution.py:30
  95.4 2.4 %collective-permute-start.19 = (f32[8,640]{1,0:T(8,128)S(1)}, f32[8,640]{1,0:T(8,128)S(1)}, u32[]{:S(2)}, u32[]{:S(2)}) collective-permute-start(f32[8,640]{1,0:T(8,128)S(1)} %get-tuple-element.91), channel_id=1, source_target_pairs={{0,6},{1,7},{2,4},{3,5},{4,2},{5,3},{6,0},{7,1},{8,14},{9,15},{10,... | collective-permute-start | bytes 61448 | tf_op jit(solution)/shard_map/ppermute | solution.py:30
  97.8 2.2 %collective-permute-done.18 = f32[8,640]{1,0:T(8,128)S(1)} collective-permute-done((f32[8,640]{1,0:T(8,128)S(1)}, f32[8,640]{1,0:T(8,128)S(1)}, u32[]{:S(2)}, u32[]{:S(2)}) %collective-permute-start.18) | collective-permute-done | bytes 20512 | tf_op jit(solution)/shard_map/ppermute | solution.py:30
  106.0 1.8 %collective-permute-done.22 = f32[8,640]{1,0:T(8,128)S(1)} collective-permute-done((f32[8,640]{1,0:T(8,128)S(1)}, f32[8,640]{1,0:T(8,128)S(1)}, u32[]{:S(2)}, u32[]{:S(2)}) %collective-permute-start.22) | collective-permute-done | bytes 20512 | tf_op jit(solution)/shard_map/ppermute | solution.py:30
  113.1 7.8 %collective-permute-done.27 = f32[8,512]{1,0:T(8,128)S(1)} collective-permute-done((f32[8,512]{1,0:T(8,128)S(1)}, f32[8,512]{1,0:T(8,128)S(1)}, u32[]{:S(2)}, u32[]{:S(2)}) %collective-permute-start.27) | collective-permute-done | bytes 16416 | tf_op jit(solution)/shard_map/ppermute | solution.py:30
  121.0 1.8 %turn.3.refs_1_ = f32[8,512]{1,0:T(8,128)S(1)} custom-call(s32[1]{0:T(128)} %bitcast.5.where_ref, bf16[512,1024]{1,0:T(8,128)(2,1)S(1)} %collective-permute-done.9.refs_0_.refs_2_, bf16[512,1024]{1,0:T(8,128)(2,1)S(1)} %collective-permute-done.16.refs_1_.refs_3_, bf16[512,1024]{1,0:T(8,128)(2,1)S(1)} %get-tuple-element.86.refs_0_.refs_2_.refs_4_, ...), custom_call_target="tpu_custom_call" | custom-call | flops 1048576 | bytes 65536 | tf_op jit(solution)/shard_map/turn/pallas_call | solution.py:319
  125.2 1.6 %apply_weights.3 = f32[8,512]{1,0:T(8,128)S(1)} custom-call(s32[1]{0:T(128)} %bitcast.5.where_ref, bf16[512,1024]{1,0:T(8,128)(2,1)} %convert_element_type.10.refs_0_, f32[8,512]{1,0:T(8,128)S(1)} %add.85.refs_1_, f32[8,512]{1,0:T(8,128)S(1)} %collective-permute-done.30.refs_2_), custom_call_target="tpu_custom_call" | custom-call | flops 1073741824 | bytes 2097152 | tf_op jit(solution)/shard_map/apply_weights/pallas_call | solution.py:274
  131.4 1.8 %turn.4.refs_2_ = f32[16,512]{1,0:T(8,128)S(1)} custom-call(s32[1]{0:T(128)} %bitcast.5.where_ref, bf16[512,1024]{1,0:T(8,128)(2,1)S(1)} %collective-permute-done.9.refs_0_.refs_2_, bf16[512,1024]{1,0:T(8,128)(2,1)S(1)} %collective-permute-done.16.refs_1_.refs_3_, bf16[512,1024]{1,0:T(8,128)(2,1)S(1)} %get-tuple-element.86.refs_0_.refs_2_.refs_4_, ...), custom_call_target="tpu_custom_call" | custom-call | flops 1048576 | bytes 65536 | tf_op jit(solution)/shard_map/turn/pallas_call | solution.py:319
  135.5 2.0 %factor_inverse.1.inverse_ref = f32[8,8]{1,0:T(8,128)} custom-call(f32[8,640]{1,0:T(8,128)} %copy-done.7), custom_call_target="tpu_custom_call" | custom-call | tf_op jit(solution)/shard_map/factor_inverse/pallas_call | solution.py:98
  138.7 3.5 %turn.5.refs_3_ = f32[24,512]{1,0:T(8,128)S(1)} custom-call(s32[1]{0:T(128)} %bitcast.5.where_ref, bf16[512,1024]{1,0:T(8,128)(2,1)} %collective-permute-done.34.refs_0_, bf16[512,1024]{1,0:T(8,128)(2,1)} %collective-permute-done.35.refs_1_, bf16[512,1024]{1,0:T(8,128)(2,1)S(1)} %collective-permute-done.9.refs_0_.refs_2_, bf16[512,1024]{1,0:T(8,128)(2,1)S(1)} %copy-done.1, ...), custom_call_target="tpu_custom_call" | custom-call | flops 1048576 | bytes 65536 | tf_op jit(solution)/shard_map/turn/pallas_call | solution.py:319
  142.8 1.6 %combine.1 = (f32[2,512]{1,0:T(2,128)}, f32[2,512]{1,0:T(2,128)}, f32[2,512]{1,0:T(2,128)}, f32[2,512]{1,0:T(2,128)}) custom-call(s32[5]{0:T(128)} %stack.71.turn_ref, f32[8,8]{1,0:T(8,128)} %factor_inverse.1.inverse_ref, f32[8,512]{1,0:T(8,128)} %copy-done.11, f32[8,512]{1,0:T(8,128)} %copy-done.10, f32[16,512]{1,0:T(8,128)} %copy-done.9, f32[24,512]{1,0:T(8,128)} %copy-done.8), custom_call_target="tpu_custom_call" | custom-call | tf_op jit(solution)/shard_map/combine/pallas_call | solution.py:353
  147.1 9.4 %collective-permute-done.41 = f32[2,512]{1,0:T(2,128)S(1)} collective-permute-done((f32[2,512]{1,0:T(2,128)}, f32[2,512]{1,0:T(2,128)S(1)}, u32[]{:S(2)}, u32[]{:S(2)}) %collective-permute-start.41) | collective-permute-done | bytes 4128 | tf_op jit(solution)/shard_map/ppermute | solution.py:30
  (110 shorter events, 43.0 us)
Async XLA Ops:
  0.0 16.8 %collective-permute-start.3 = (bf16[8,500,250]{2,0,1:T(8,128)(2,1)}, bf16[8,500,250]{2,0,1:T(8,128)(2,1)}, u32[]{:S(2)}, u32[]{:S(2)}) collective-permute-start(bf16[8,500,250]{2,0,1:T(8,128)(2,1)} %param.4), channel_id=1, source_target_pairs={{0,1},{1,0},{2,3},{3,2},{4,5},{5,4},{6,7},{7,6},{8,9},{9,8},{10,11... | collective-permute-start | bytes 6000008 | tf_op jit(solution)/shard_map/ppermute | solution.py:30
  2.0 14.8 %collective-permute-start.4 = (bf16[500,256]{1,0:T(8,128)(2,1)S(1)}, bf16[500,256]{1,0:T(8,128)(2,1)S(1)}, u32[]{:S(2)}, u32[]{:S(2)}) collective-permute-start(bf16[500,256]{1,0:T(8,128)(2,1)S(1)} %get-tuple-element.120), channel_id=1, source_target_pairs={{0,4},{1,5},{2,6},{3,7},{4,0},{5,1},{6,2},{7,3},{8,12},{9,13},{10,... | collective-permute-start | bytes 768008 | tf_op jit(solution)/shard_map/ppermute | solution.py:30
  3.6 5.9 %collective-permute-start = (bf16[2,250,128]{2,1,0:T(8,128)(2,1)S(1)}, bf16[2,250,128]{2,1,0:T(8,128)(2,1)S(1)}, u32[]{:S(2)}, u32[]{:S(2)}) collective-permute-start(bf16[2,250,128]{2,1,0:T(8,128)(2,1)S(1)} %get-tuple-element.118), channel_id=1, source_target_pairs={{0,8},{1,9},{2,10},{3,11},{4,12},{5,13},{6,14},{7,15},{8,0},{9,1},... | collective-permute-start | bytes 384008 | tf_op jit(solution)/shard_map/ppermute | solution.py:30
  5.1 8.0 %collective-permute-start.1 = (bf16[2,250,128]{2,1,0:T(8,128)(2,1)S(1)}, bf16[2,250,128]{2,1,0:T(8,128)(2,1)S(1)}, u32[]{:S(2)}, u32[]{:S(2)}) collective-permute-start(bf16[2,250,128]{2,1,0:T(8,128)(2,1)S(1)} %get-tuple-element.117), channel_id=1, source_target_pairs={{0,16},{1,17},{2,18},{3,19},{4,20},{5,21},{6,22},{7,23},{8,24},{9,... | collective-permute-start | bytes 384008 | tf_op jit(solution)/shard_map/ppermute | solution.py:30
  6.7 6.5 %collective-permute-start.2 = (bf16[2,250,128]{2,1,0:T(8,128)(2,1)S(1)}, bf16[2,250,128]{2,1,0:T(8,128)(2,1)S(1)}, u32[]{:S(2)}, u32[]{:S(2)}) collective-permute-start(bf16[2,250,128]{2,1,0:T(8,128)(2,1)S(1)} %get-tuple-element.116), channel_id=1, source_target_pairs={{0,24},{1,25},{2,26},{3,27},{4,28},{5,29},{6,30},{7,31},{8,16},{9,... | collective-permute-start | bytes 384008 | tf_op jit(solution)/shard_map/ppermute | solution.py:30
  17.9 29.5 %collective-permute-start.9 = (bf16[512,1024]{1,0:T(8,128)(2,1)}, bf16[512,1024]{1,0:T(8,128)(2,1)S(1)}, u32[]{:S(2)}, u32[]{:S(2)}) collective-permute-start(bf16[512,1024]{1,0:T(8,128)(2,1)} %convert_element_type.10.refs_0_), channel_id=1, source_target_pairs={{2,10},{3,11},{12,20},{13,21},{22,30},{23,31}} | collective-permute-start | bytes 3145736 | tf_op jit(solution)/shard_map/ppermute | solution.py:30
  21.2 14.9 %collective-permute-start.5 = (bf16[2,250,128]{2,1,0:T(8,128)(2,1)}, bf16[2,250,128]{2,1,0:T(8,128)(2,1)}, u32[]{:S(2)}, u32[]{:S(2)}) collective-permute-start(bf16[2,250,128]{2,1,0:T(8,128)(2,1)} %get-tuple-element.113), channel_id=1, source_target_pairs={{0,2},{1,3},{2,0},{3,1},{4,6},{5,7},{6,4},{7,5},{8,10},{9,11},{10,... | collective-permute-start | bytes 384008 | tf_op jit(solution)/shard_map/ppermute | solution.py:30
  21.2 18.7 %collective-permute-start.6 = (bf16[2,250,128]{2,1,0:T(8,128)(2,1)}, bf16[2,250,128]{2,1,0:T(8,128)(2,1)}, u32[]{:S(2)}, u32[]{:S(2)}) collective-permute-start(bf16[2,250,128]{2,1,0:T(8,128)(2,1)} %get-tuple-element.112), channel_id=1, source_target_pairs={{0,4},{1,5},{2,6},{3,7},{4,0},{5,1},{6,2},{7,3},{8,12},{9,13},{10,... | collective-permute-start | bytes 384008 | tf_op jit(solution)/shard_map/ppermute | solution.py:30
  23.5 16.4 %collective-permute-start.7 = (bf16[2,250,128]{2,1,0:T(8,128)(2,1)}, bf16[2,250,128]{2,1,0:T(8,128)(2,1)}, u32[]{:S(2)}, u32[]{:S(2)}) collective-permute-start(bf16[2,250,128]{2,1,0:T(8,128)(2,1)} %get-tuple-element.111), channel_id=1, source_target_pairs={{0,6},{1,7},{2,4},{3,5},{4,2},{5,3},{6,0},{7,1},{8,14},{9,15},{10,... | collective-permute-start | bytes 384008 | tf_op jit(solution)/shard_map/ppermute | solution.py:30
  25.6 21.8 %collective-permute-start.8 = (bf16[500,256]{1,0:T(8,128)(2,1)}, bf16[500,256]{1,0:T(8,128)(2,1)}, u32[]{:S(2)}, u32[]{:S(2)}) collective-permute-start(bf16[500,256]{1,0:T(8,128)(2,1)} %get-tuple-element.58), channel_id=1, source_target_pairs={{0,4},{1,5},{2,6},{3,7},{4,0},{5,1},{6,2},{7,3},{8,12},{9,13},{10,... | collective-permute-start | bytes 768008 | tf_op jit(solution)/shard_map/ppermute | solution.py:30
  47.4 6.9 %collective-permute-start.15 = (f32[512,512]{1,0:T(8,128)}, f32[512,512]{1,0:T(8,128)}, u32[]{:S(2)}, u32[]{:S(2)}) collective-permute-start(f32[512,512]{1,0:T(8,128)} %copy-done.3), channel_id=1, source_target_pairs={{0,1},{1,0},{2,3},{3,2},{4,5},{5,4},{6,7},{7,6},{8,9},{9,8},{10,11... | collective-permute-start | bytes 3145736 | tf_op jit(solution)/shard_map/ppermute | solution.py:30
  48.7 14.8 %collective-permute-start.10 = (bf16[4,2,250,128]{3,2,1,0:T(8,128)(2,1)S(1)}, bf16[4,2,250,128]{3,2,1,0:T(8,128)(2,1)S(1)}, u32[]{:S(2)}, u32[]{:S(2)}) collective-permute-start(bf16[4,2,250,128]{3,2,1,0:T(8,128)(2,1)S(1)} %pad_maximum_fusion.2.rest_5_.rest_9_.rest_13_.rest_17_), channel_id=1, source_target_pairs={{0,8},{1,9},{2,10},{3,11},{4,12},{5,13},{6,14},{7,15},{8,0},{9,1},... | collective-permute-start | bytes 1536008 | tf_op jit(solution)/shard_map/ppermute | solution.py:30
  50.2 25.6 %collective-permute-start.11 = (bf16[4,2,250,128]{3,2,1,0:T(8,128)(2,1)S(1)}, bf16[4,2,250,128]{3,2,1,0:T(8,128)(2,1)S(1)}, u32[]{:S(2)}, u32[]{:S(2)}) collective-permute-start(bf16[4,2,250,128]{3,2,1,0:T(8,128)(2,1)S(1)} %pad_maximum_fusion.2.rest_5_.rest_9_.rest_13_.rest_17_), channel_id=1, source_target_pairs={{0,16},{1,17},{2,18},{3,19},{4,20},{5,21},{6,22},{7,23},{8,24},{9,... | collective-permute-start | bytes 1536008 | tf_op jit(solution)/shard_map/ppermute | solution.py:30
  52.8 24.9 %collective-permute-start.12 = (bf16[4,2,250,128]{3,2,1,0:T(8,128)(2,1)S(1)}, bf16[4,2,250,128]{3,2,1,0:T(8,128)(2,1)S(1)}, u32[]{:S(2)}, u32[]{:S(2)}) collective-permute-start(bf16[4,2,250,128]{3,2,1,0:T(8,128)(2,1)S(1)} %pad_maximum_fusion.2.rest_5_.rest_9_.rest_13_.rest_17_), channel_id=1, source_target_pairs={{0,24},{1,25},{2,26},{3,27},{4,28},{5,29},{6,30},{7,31},{8,16},{9,... | collective-permute-start | bytes 1536008 | tf_op jit(solution)/shard_map/ppermute | solution.py:30
  54.2 24.9 %collective-permute-start.13 = (bf16[500,512]{1,0:T(8,128)(2,1)}, bf16[500,512]{1,0:T(8,128)(2,1)S(1)}, u32[]{:S(2)}, u32[]{:S(2)}) collective-permute-start(bf16[500,512]{1,0:T(8,128)(2,1)} %rest_0_), channel_id=1, source_target_pairs={{0,2},{1,3},{2,0},{3,1},{4,6},{5,7},{6,4},{7,5},{8,10},{9,11},{10,... | collective-permute-start | bytes 1536008 | tf_op jit(solution)/shard_map/ppermute | solution.py:30
  54.3 24.7 %collective-permute-start.14 = (bf16[500,512]{1,0:T(8,128)(2,1)S(1)}, bf16[500,512]{1,0:T(8,128)(2,1)S(1)}, u32[]{:S(2)}, u32[]{:S(2)}) collective-permute-start(bf16[500,512]{1,0:T(8,128)(2,1)S(1)} %copy-done.5), channel_id=1, source_target_pairs={{0,6},{1,7},{2,4},{3,5},{4,2},{5,3},{6,0},{7,1},{8,14},{9,15},{10,... | collective-permute-start | bytes 1536008 | tf_op jit(solution)/shard_map/ppermute | solution.py:30
  63.5 28.9 %collective-permute-start.16 = (bf16[512,1024]{1,0:T(8,128)(2,1)S(1)}, bf16[512,1024]{1,0:T(8,128)(2,1)S(1)}, u32[]{:S(2)}, u32[]{:S(2)}) collective-permute-start(bf16[512,1024]{1,0:T(8,128)(2,1)S(1)} %collective-permute-done.9.refs_0_.refs_2_), channel_id=1, source_target_pairs={{0,1},{1,0},{2,3},{3,2},{4,5},{5,4},{6,7},{7,6},{8,9},{9,8},{10,11... | collective-permute-start | bytes 3145736 | tf_op jit(solution)/shard_map/ppermute | solution.py:30
  79.1 43.7 %collective-permute-start.34 = (bf16[512,1024]{1,0:T(8,128)(2,1)}, bf16[512,1024]{1,0:T(8,128)(2,1)}, u32[]{:S(2)}, u32[]{:S(2)}) collective-permute-start(bf16[512,1024]{1,0:T(8,128)(2,1)} %convert_element_type.10.refs_0_), channel_id=1, source_target_pairs={{14,30},{15,31}} | collective-permute-start | bytes 3145736 | tf_op jit(solution)/shard_map/ppermute | solution.py:30
  92.4 5.5 %collective-permute-start.17 = (f32[8,640]{1,0:T(8,128)S(1)}, f32[8,640]{1,0:T(8,128)S(1)}, u32[]{:S(2)}, u32[]{:S(2)}) collective-permute-start(f32[8,640]{1,0:T(8,128)S(1)} %get-tuple-element.89), channel_id=1, source_target_pairs={{0,2},{1,3},{2,0},{3,1},{4,6},{5,7},{6,4},{7,5},{8,10},{9,11},{10,... | collective-permute-start | bytes 61448 | tf_op jit(solution)/shard_map/ppermute | solution.py:30
  95.4 4.7 %collective-permute-start.18 = (f32[8,640]{1,0:T(8,128)S(1)}, f32[8,640]{1,0:T(8,128)S(1)}, u32[]{:S(2)}, u32[]{:S(2)}) collective-permute-start(f32[8,640]{1,0:T(8,128)S(1)} %get-tuple-element.90), channel_id=1, source_target_pairs={{0,4},{1,5},{2,6},{3,7},{4,0},{5,1},{6,2},{7,3},{8,12},{9,13},{10,... | collective-permute-start | bytes 61448 | tf_op jit(solution)/shard_map/ppermute | solution.py:30
  95.4 5.6 %collective-permute-start.19 = (f32[8,640]{1,0:T(8,128)S(1)}, f32[8,640]{1,0:T(8,128)S(1)}, u32[]{:S(2)}, u32[]{:S(2)}) collective-permute-start(f32[8,640]{1,0:T(8,128)S(1)} %get-tuple-element.91), channel_id=1, source_target_pairs={{0,6},{1,7},{2,4},{3,5},{4,2},{5,3},{6,0},{7,1},{8,14},{9,15},{10,... | collective-permute-start | bytes 61448 | tf_op jit(solution)/shard_map/ppermute | solution.py:30
  101.0 3.8 %collective-permute-start.20 = (f32[8,640]{1,0:T(8,128)S(1)}, f32[8,640]{1,0:T(8,128)S(1)}, u32[]{:S(2)}, u32[]{:S(2)}) collective-permute-start(f32[8,640]{1,0:T(8,128)S(1)} %add_add_fusion.1), channel_id=1, source_target_pairs={{0,8},{1,9},{2,10},{3,11},{4,12},{5,13},{6,14},{7,15},{8,0},{9,1},... | collective-permute-start | bytes 61448 | tf_op jit(solution)/shard_map/ppermute | solution.py:30
  102.2 3.8 %collective-permute-start.21 = (f32[8,640]{1,0:T(8,128)S(1)}, f32[8,640]{1,0:T(8,128)S(1)}, u32[]{:S(2)}, u32[]{:S(2)}) collective-permute-start(f32[8,640]{1,0:T(8,128)S(1)} %add_add_fusion.1), channel_id=1, source_target_pairs={{0,16},{1,17},{2,18},{3,19},{4,20},{5,21},{6,22},{7,23},{8,24},{9,... | collective-permute-start | bytes 61448 | tf_op jit(solution)/shard_map/ppermute | solution.py:30
  103.2 4.7 %collective-permute-start.22 = (f32[8,640]{1,0:T(8,128)S(1)}, f32[8,640]{1,0:T(8,128)S(1)}, u32[]{:S(2)}, u32[]{:S(2)}) collective-permute-start(f32[8,640]{1,0:T(8,128)S(1)} %add_add_fusion.1), channel_id=1, source_target_pairs={{0,24},{1,25},{2,26},{3,27},{4,28},{5,29},{6,30},{7,31},{8,16},{9,... | collective-permute-start | bytes 61448 | tf_op jit(solution)/shard_map/ppermute | solution.py:30
  109.8 3.3 %collective-permute-start.24 = (f32[8,512]{1,0:T(8,128)S(1)}, f32[8,512]{1,0:T(8,128)S(1)}, u32[]{:S(2)}, u32[]{:S(2)}) collective-permute-start(f32[8,512]{1,0:T(8,128)S(1)} %apply_weights.2.refs_0_), channel_id=1, source_target_pairs={{0,10},{1,11}} | collective-permute-start | bytes 49160 | tf_op jit(solution)/shard_map/ppermute | solution.py:30
  111.8 9.2 %collective-permute-start.27 = (f32[8,512]{1,0:T(8,128)S(1)}, f32[8,512]{1,0:T(8,128)S(1)}, u32[]{:S(2)}, u32[]{:S(2)}) collective-permute-start(f32[8,512]{1,0:T(8,128)S(1)} %apply_weights.2.refs_0_), channel_id=1, source_target_pairs={{0,6},{1,7}} | collective-permute-start | bytes 49160 | tf_op jit(solution)/shard_map/ppermute | solution.py:30
  122.8 14.7 %collective-permute-start.35 = (bf16[512,1024]{1,0:T(8,128)(2,1)}, bf16[512,1024]{1,0:T(8,128)(2,1)}, u32[]{:S(2)}, u32[]{:S(2)}) collective-permute-start(bf16[512,1024]{1,0:T(8,128)(2,1)} %collective-permute-done.34.refs_0_), channel_id=1, source_target_pairs={{0,1},{1,0},{2,3},{3,2},{4,5},{5,4},{6,7},{7,6},{8,9},{9,8},{10,11... | collective-permute-start | bytes 3145736 | tf_op jit(solution)/shard_map/ppermute | solution.py:30
  123.4 5.4 %collective-permute-start.28 = (f32[8,512]{1,0:T(8,128)S(1)}, f32[8,512]{1,0:T(8,128)S(1)}, u32[]{:S(2)}, u32[]{:S(2)}) collective-permute-start(f32[8,512]{1,0:T(8,128)S(1)} %turn.3.refs_1_), channel_id=1, source_target_pairs={{10,20},{11,21}} | collective-permute-start | bytes 49160 | tf_op jit(solution)/shard_map/ppermute | solution.py:30
  124.0 4.7 %collective-permute-start.29 = (f32[8,512]{1,0:T(8,128)S(1)}, f32[8,512]{1,0:T(8,128)S(1)}, u32[]{:S(2)}, u32[]{:S(2)}) collective-permute-start(f32[8,512]{1,0:T(8,128)S(1)} %turn.3.refs_1_), channel_id=1, source_target_pairs={{10,21},{11,20}} | collective-permute-start | bytes 49160 | tf_op jit(solution)/shard_map/ppermute | solution.py:30
  133.2 4.2 %collective-permute-start.33 = (f32[16,512]{1,0:T(8,128)S(1)}, f32[16,512]{1,0:T(8,128)S(1)}, u32[]{:S(2)}, u32[]{:S(2)}) collective-permute-start(f32[16,512]{1,0:T(8,128)S(1)} %turn.4.refs_2_), channel_id=1, source_target_pairs={{20,30},{21,31}} | collective-permute-start | bytes 98312 | tf_op jit(solution)/shard_map/ppermute | solution.py:30
  133.9 3.5 %collective-permute-start.36 = (f32[16,512]{1,0:T(8,128)S(1)}, f32[16,512]{1,0:T(8,128)S(1)}, u32[]{:S(2)}, u32[]{:S(2)}) collective-permute-start(f32[16,512]{1,0:T(8,128)S(1)} %turn.4.refs_2_), channel_id=1, source_target_pairs={{20,31},{21,30}} | collective-permute-start | bytes 98312 | tf_op jit(solution)/shard_map/ppermute | solution.py:30
  145.7 10.7 %collective-permute-start.41 = (f32[2,512]{1,0:T(2,128)}, f32[2,512]{1,0:T(2,128)S(1)}, u32[]{:S(2)}, u32[]{:S(2)}) collective-permute-start(f32[2,512]{1,0:T(2,128)} %get-tuple-element.106), channel_id=1, source_target_pairs={{0,24},{1,25},{10,18},{11,19},{20,12},{21,13},{30,6},{31,7}} | collective-permute-start | bytes 12296 | tf_op jit(solution)/shard_map/ppermute | solution.py:30
  (24 other events, 187.2 us)

commit v11 on v10

--- a/solution.py
+++ b/solution.py
@@ -488,6 +488,8 @@
         if t >= 2:
             if t == 2:
                 near, near_sib, brought[t] = lax.optimization_barrier((near, near_sib, brought[t]))
+            else:
+                brought[t], _ = lax.optimization_barrier((brought[t], solved))
             rest = rest[:, :points] - brought[t]
             sib_rest = move(rest, swap)
         if t == gen_count - 1:

time: 159 us -> 154 us (0.969)
  waiting for transfers between devices: 64.2 us -> 58.9 us
    ppermute x42, waiting for transfers between devices: 64.2 us -> 58.9 us  [move(): return lax.ppermute(value, BOTH, pairs)]
  transfers between devices with their start and end apart: 42 -> 42, of which waited for: 20 -> 18; matrix products, arithmetic and copies ran while one was open for 10% -> 10% of each run, Pallas kernels for 17% -> 18%
where the time goes in v11:
time: 154 us; the launch traced here: 153 us
  waiting for transfers between devices  58.9 us (38%)
  starting transfers between devices  39.8 us (26%)
  Pallas kernels  32.7 us (21%)
  local copies, waits for them, and re-layouts  8.59 us (6%)
  matrix products  6.6 us (4%)
  other arithmetic  5.66 us (4%)
    ppermute x42, waiting for transfers between devices, move(): return lax.ppermute(value, BOTH, pairs)  58.9 us
    ppermute x42, starting transfers between devices, move(): return lax.ppermute(value, BOTH, pairs)  39.8 us
    pallas_call x1, Pallas kernels, project(): pl.pallas_call(kernel, grid_spec=pltpu.PrefetchScalarGridSpec(num_scalar_...  11.6 us
    pallas_call x3, Pallas kernels, turn(): pl.pallas_call(functools.partial(turn_kernel, count), in_specs=[pl.BlockS...  7.06 us
    pallas_call x1, Pallas kernels, invert_block(): pl.pallas_call(invert_kernel, grid_spec=pltpu.PrefetchScalarGridSpec(num_...  5.35 us
    dot_general x1, matrix products, on_device(): corner = jnp.dot(metric_factor[:, :points], upper, precision=HIGHEST)  4.71 us
  transfers between devices with their start and end apart: 42, of which 18 were waited for; matrix products, arithmetic and copies ran while one was open for 10% of the time, Pallas kernels for 18%

profile of v11, /device:TPU:24, one launch (start us, length us, event | category | flops | bytes accessed | tf_op | source)
XLA Modules:
  0.0 152.8 jit_solution(8011729854599799816)
XLA Ops:
  0.0 2.0 %fusion.5 = (bf16[500,256]{1,0:T(8,128)(2,1)}, bf16[500,256]{1,0:T(8,128)(2,1)S(1)}) fusion(bf16[500,512]{1,0:T(8,128)(2,1)} %rest_0_), kind=kLoop, calls=%fused_computation.29 | loop fusion | bytes 1024000 | tf_op jit(solution)/shard_map/slice | solution.py:387
  3.6 1.6 %collective-permute-start = (bf16[2,250,128]{2,1,0:T(8,128)(2,1)S(1)}, bf16[2,250,128]{2,1,0:T(8,128)(2,1)S(1)}, u32[]{:S(2)}, u32[]{:S(2)}) collective-permute-start(bf16[2,250,128]{2,1,0:T(8,128)(2,1)S(1)} %get-tuple-element.118), channel_id=1, source_target_pairs={{0,8},{1,9},{2,10},{3,11},{4,12},{5,13},{6,14},{7,15},{8,0},{9,1},... | collective-permute-start | bytes 384008 | tf_op jit(solution)/shard_map/ppermute | solution.py:30
  7.1 2.3 %collective-permute-done = bf16[2,250,128]{2,1,0:T(8,128)(2,1)S(1)} collective-permute-done((bf16[2,250,128]{2,1,0:T(8,128)(2,1)S(1)}, bf16[2,250,128]{2,1,0:T(8,128)(2,1)S(1)}, u32[]{:S(2)}, u32[]{:S(2)}) %collective-permute-start) | collective-permute-done | bytes 128032 | tf_op jit(solution)/shard_map/ppermute | solution.py:30
  9.5 3.7 %collective-permute-done.1 = bf16[2,250,128]{2,1,0:T(8,128)(2,1)S(1)} collective-permute-done((bf16[2,250,128]{2,1,0:T(8,128)(2,1)S(1)}, bf16[2,250,128]{2,1,0:T(8,128)(2,1)S(1)}, u32[]{:S(2)}, u32[]{:S(2)}) %collective-permute-start.1) | collective-permute-done | bytes 128032 | tf_op jit(solution)/shard_map/ppermute | solution.py:30
  14.0 2.8 %collective-permute-done.4.rest_2_ = bf16[500,256]{1,0:T(8,128)(2,1)S(1)} collective-permute-done((bf16[500,256]{1,0:T(8,128)(2,1)S(1)}, bf16[500,256]{1,0:T(8,128)(2,1)S(1)}, u32[]{:S(2)}, u32[]{:S(2)}) %collective-permute-start.4) | collective-permute-done | bytes 256032 | tf_op jit(solution)/shard_map/ppermute | solution.py:30
  19.4 1.9 %dynamic-slice_bitcast_fusion = (bf16[2,250,128]{2,1,0:T(8,128)(2,1)}, bf16[2,250,128]{2,1,0:T(8,128)(2,1)}, bf16[2,250,128]{2,1,0:T(8,128)(2,1)}, bf16[2,250,128]{2,1,0:T(8,128)(2,1)S(1)}) fusion(bf16[4,2,250,128]{3,2,1,0:T(8,128)(2,1)} %pad_maximum_fusion.1, s32[]{:T(128)S(6)} %select_n.75, s32[]{:T(128)S(6)} %select_n.74, s32[]{:T(128)S(6)} %select_n.73, ...), kind=kLoop, calls=%fused_computation.11 | loop fusion | bytes 1024016 | tf_op jit(solution)/shard_map/jit(dynamic_index_in_dim)/squeeze | solution.py:396
  21.2 2.3 %collective-permute-start.6 = (bf16[2,250,128]{2,1,0:T(8,128)(2,1)}, bf16[2,250,128]{2,1,0:T(8,128)(2,1)}, u32[]{:S(2)}, u32[]{:S(2)}) collective-permute-start(bf16[2,250,128]{2,1,0:T(8,128)(2,1)} %get-tuple-element.112), channel_id=1, source_target_pairs={{0,4},{1,5},{2,6},{3,7},{4,0},{5,1},{6,2},{7,3},{8,12},{9,13},{10,... | collective-permute-start | bytes 384008 | tf_op jit(solution)/shard_map/ppermute | solution.py:30
  23.5 2.1 %collective-permute-start.7 = (bf16[2,250,128]{2,1,0:T(8,128)(2,1)}, bf16[2,250,128]{2,1,0:T(8,128)(2,1)}, u32[]{:S(2)}, u32[]{:S(2)}) collective-permute-start(bf16[2,250,128]{2,1,0:T(8,128)(2,1)} %get-tuple-element.111), channel_id=1, source_target_pairs={{0,6},{1,7},{2,4},{3,5},{4,2},{5,3},{6,0},{7,1},{8,14},{9,15},{10,... | collective-permute-start | bytes 384008 | tf_op jit(solution)/shard_map/ppermute | solution.py:30
  27.0 5.3 %invert_block.1 = f32[512,512]{1,0:T(8,128)S(1)} custom-call(s32[2]{0:T(128)S(1)} %pad_add_fusion.where_ref, f32[512,1024]{1,0:T(8,128)S(1)} %copy-done.2), custom_call_target="tpu_custom_call" | custom-call | flops 4294967296 | bytes 4194304 | tf_op jit(solution)/shard_map/invert_block/pallas_call | solution.py:230
  33.3 2.8 %pivot_entries.1.entries_ref = f32[8,8]{1,0:T(8,128)} custom-call(s32[8]{0:T(128)} %get-tuple-element.122.row_ref, bf16[500,8,250]{2,1,0:T(8,128)(2,1)} %bitcast.33, bf16[500,8,250]{2,1,0:T(8,128)(2,1)} %bitcast.16.sib_ref, s32[8]{0:T(128)} %get-tuple-element.123.own_col_ref, s32[8]{0:T(128)} %get-tuple-element.121.sib_col_ref), custom_call_target="tpu_custom_call" | custom-call | tf_op jit(solution)/shard_map/pivot_entries/pallas_call | solution.py:63
  36.2 3.8 %collective-permute-done.6 = bf16[2,250,128]{2,1,0:T(8,128)(2,1)} collective-permute-done((bf16[2,250,128]{2,1,0:T(8,128)(2,1)}, bf16[2,250,128]{2,1,0:T(8,128)(2,1)}, u32[]{:S(2)}, u32[]{:S(2)}) %collective-permute-start.6) | collective-permute-done | bytes 128032 | tf_op jit(solution)/shard_map/ppermute | solution.py:30
  39.9 7.5 %collective-permute-done.8.rest_3_ = bf16[500,256]{1,0:T(8,128)(2,1)} collective-permute-done((bf16[500,256]{1,0:T(8,128)(2,1)}, bf16[500,256]{1,0:T(8,128)(2,1)}, u32[]{:S(2)}, u32[]{:S(2)}) %collective-permute-start.8) | collective-permute-done | bytes 256032 | tf_op jit(solution)/shard_map/ppermute | solution.py:30
  50.2 2.6 %collective-permute-start.11 = (bf16[4,2,250,128]{3,2,1,0:T(8,128)(2,1)S(1)}, bf16[4,2,250,128]{3,2,1,0:T(8,128)(2,1)S(1)}, u32[]{:S(2)}, u32[]{:S(2)}) collective-permute-start(bf16[4,2,250,128]{3,2,1,0:T(8,128)(2,1)S(1)} %pad_maximum_fusion.2.rest_5_.rest_9_.rest_13_.rest_17_), channel_id=1, source_target_pairs={{0,16},{1,17},{2,18},{3,19},{4,20},{5,21},{6,22},{7,23},{8,24},{9,... | collective-permute-start | bytes 1536008 | tf_op jit(solution)/shard_map/ppermute | solution.py:30
  55.8 4.7 %fusion.2 = f32[512,512]{1,0:T(8,128)S(1)} fusion(f32[512,512]{1,0:T(8,128)} %collective-permute-done.15, f32[512,1024]{1,0:T(8,128)S(1)} %copy-done.2), kind=kOutput, calls=%fused_computation.6 | convolution fusion | flops 1610612736 | bytes 3145728 | tf_op jit(solution)/shard_map/dot_general | solution.py:426
  60.5 2.9 %collective-permute-done.10.rest_6_.rest_10_.rest_14_.rest_18_ = bf16[4,2,250,128]{3,2,1,0:T(8,128)(2,1)S(1)} collective-permute-done((bf16[4,2,250,128]{3,2,1,0:T(8,128)(2,1)S(1)}, bf16[4,2,250,128]{3,2,1,0:T(8,128)(2,1)S(1)}, u32[]{:S(2)}, u32[]{:S(2)}) %collective-permute-start.10) | collective-permute-done | bytes 512032 | tf_op jit(solution)/shard_map/ppermute | solution.py:30
  63.5 1.9 %fusion.1 = f32[512,512]{1,0:T(8,128)S(1)} fusion(f32[512,512]{1,0:T(8,128)S(1)} %copy-done.4, f32[512,512]{1,0:T(8,128)S(1)} %fusion.2, pred[]{:T(512)S(6)} %eq.13), kind=kOutput, calls=%fused_computation.5 | convolution fusion | flops 1611137024 | bytes 3145729 | tf_op jit(solution)/shard_map/dot_general | solution.py:427
  65.8 10.1 %collective-permute-done.11.rest_7_.rest_11_.rest_15_.rest_19_ = bf16[4,2,250,128]{3,2,1,0:T(8,128)(2,1)S(1)} collective-permute-done((bf16[4,2,250,128]{3,2,1,0:T(8,128)(2,1)S(1)}, bf16[4,2,250,128]{3,2,1,0:T(8,128)(2,1)S(1)}, u32[]{:S(2)}, u32[]{:S(2)}) %collective-permute-start.11) | collective-permute-done | bytes 512032 | tf_op jit(solution)/shard_map/ppermute | solution.py:30
  75.9 1.8 %collective-permute-done.12.rest_8_.rest_12_.rest_16_.rest_20_ = bf16[4,2,250,128]{3,2,1,0:T(8,128)(2,1)S(1)} collective-permute-done((bf16[4,2,250,128]{3,2,1,0:T(8,128)(2,1)S(1)}, bf16[4,2,250,128]{3,2,1,0:T(8,128)(2,1)S(1)}, u32[]{:S(2)}, u32[]{:S(2)}) %collective-permute-start.12) | collective-permute-done | bytes 512032 | tf_op jit(solution)/shard_map/ppermute | solution.py:30
  79.1 1.6 %collective-permute-start.34 = (bf16[512,1024]{1,0:T(8,128)(2,1)}, bf16[512,1024]{1,0:T(8,128)(2,1)}, u32[]{:S(2)}, u32[]{:S(2)}) collective-permute-start(bf16[512,1024]{1,0:T(8,128)(2,1)} %convert_element_type.10.refs_0_), channel_id=1, source_target_pairs={{14,30},{15,31}} | collective-permute-start | bytes 3145736 | tf_op jit(solution)/shard_map/ppermute | solution.py:30
  80.7 11.6 %project.1 = (f32[8,640]{1,0:T(8,128)S(1)}, f32[8,640]{1,0:T(8,128)S(1)}, f32[8,640]{1,0:T(8,128)S(1)}, f32[8,640]{1,0:T(8,128)S(1)}) custom-call(s32[5]{0:T(128)S(1)} %stack.80.where_ref, bf16[4000,250]{1,0:T(8,128)(2,1)S(1)} %bitcast.34, bf16[4000,250]{1,0:T(8,128)(2,1)} %bitcast.18.sib_ref, f32[8,8]{1,0:T(8,128)S(1)} %copy-done.12, ...), custom_call_target="tpu_custom_call" | custom-call | flops 8192000000 | bytes 1048576 | tf_op jit(solution)/shard_map/project/pallas_call | solution.py:170
  92.4 3.0 %collective-permute-start.17 = (f32[8,640]{1,0:T(8,128)S(1)}, f32[8,640]{1,0:T(8,128)S(1)}, u32[]{:S(2)}, u32[]{:S(2)}) collective-permute-start(f32[8,640]{1,0:T(8,128)S(1)} %get-tuple-element.90), channel_id=1, source_target_pairs={{0,2},{1,3},{2,0},{3,1},{4,6},{5,7},{6,4},{7,5},{8,10},{9,11},{10,... | collective-permute-start | bytes 61448 | tf_op jit(solution)/shard_map/ppermute | solution.py:30
  95.4 2.4 %collective-permute-start.19 = (f32[8,640]{1,0:T(8,128)S(1)}, f32[8,640]{1,0:T(8,128)S(1)}, u32[]{:S(2)}, u32[]{:S(2)}) collective-permute-start(f32[8,640]{1,0:T(8,128)S(1)} %get-tuple-element.92), channel_id=1, source_target_pairs={{0,6},{1,7},{2,4},{3,5},{4,2},{5,3},{6,0},{7,1},{8,14},{9,15},{10,... | collective-permute-start | bytes 61448 | tf_op jit(solution)/shard_map/ppermute | solution.py:30
  97.8 2.2 %collective-permute-done.18 = f32[8,640]{1,0:T(8,128)S(1)} collective-permute-done((f32[8,640]{1,0:T(8,128)S(1)}, f32[8,640]{1,0:T(8,128)S(1)}, u32[]{:S(2)}, u32[]{:S(2)}) %collective-permute-start.18) | collective-permute-done | bytes 20512 | tf_op jit(solution)/shard_map/ppermute | solution.py:30
  106.0 1.8 %collective-permute-done.22 = f32[8,640]{1,0:T(8,128)S(1)} collective-permute-done((f32[8,640]{1,0:T(8,128)S(1)}, f32[8,640]{1,0:T(8,128)S(1)}, u32[]{:S(2)}, u32[]{:S(2)}) %collective-permute-start.22) | collective-permute-done | bytes 20512 | tf_op jit(solution)/shard_map/ppermute | solution.py:30
  113.1 7.8 %collective-permute-done.27 = f32[8,512]{1,0:T(8,128)S(1)} collective-permute-done((f32[8,512]{1,0:T(8,128)S(1)}, f32[8,512]{1,0:T(8,128)S(1)}, u32[]{:S(2)}, u32[]{:S(2)}) %collective-permute-start.27) | collective-permute-done | bytes 16416 | tf_op jit(solution)/shard_map/ppermute | solution.py:30
  121.0 1.8 %turn.3.refs_1_ = f32[8,512]{1,0:T(8,128)S(1)} custom-call(s32[1]{0:T(128)} %bitcast.5.where_ref, bf16[512,1024]{1,0:T(8,128)(2,1)S(1)} %collective-permute-done.9.refs_0_.refs_2_, bf16[512,1024]{1,0:T(8,128)(2,1)S(1)} %collective-permute-done.16.refs_1_.refs_3_, bf16[512,1024]{1,0:T(8,128)(2,1)S(1)} %get-tuple-element.87.refs_0_.refs_2_.refs_4_, ...), custom_call_target="tpu_custom_call" | custom-call | flops 1048576 | bytes 65536 | tf_op jit(solution)/shard_map/turn/pallas_call | solution.py:319
  125.1 1.6 %apply_weights.3 = f32[8,512]{1,0:T(8,128)S(1)} custom-call(s32[1]{0:T(128)} %bitcast.5.where_ref, bf16[512,1024]{1,0:T(8,128)(2,1)} %convert_element_type.10.refs_0_, f32[8,512]{1,0:T(8,128)S(1)} %add.85.refs_1_, f32[8,512]{1,0:T(8,128)S(1)} %collective-permute-done.30.refs_2_), custom_call_target="tpu_custom_call" | custom-call | flops 1073741824 | bytes 2097152 | tf_op jit(solution)/shard_map/apply_weights/pallas_call | solution.py:274
  129.2 1.8 %turn.4.refs_2_ = f32[16,512]{1,0:T(8,128)S(1)} custom-call(s32[1]{0:T(128)} %bitcast.5.where_ref, bf16[512,1024]{1,0:T(8,128)(2,1)S(1)} %collective-permute-done.9.refs_0_.refs_2_, bf16[512,1024]{1,0:T(8,128)(2,1)S(1)} %collective-permute-done.16.refs_1_.refs_3_, bf16[512,1024]{1,0:T(8,128)(2,1)S(1)} %get-tuple-element.87.refs_0_.refs_2_.refs_4_, ...), custom_call_target="tpu_custom_call" | custom-call | flops 1048576 | bytes 65536 | tf_op jit(solution)/shard_map/turn/pallas_call | solution.py:319
  133.2 2.0 %factor_inverse.1.inverse_ref = f32[8,8]{1,0:T(8,128)} custom-call(f32[8,640]{1,0:T(8,128)} %copy-done.7), custom_call_target="tpu_custom_call" | custom-call | tf_op jit(solution)/shard_map/factor_inverse/pallas_call | solution.py:98
  136.4 3.5 %turn.5.refs_3_ = f32[24,512]{1,0:T(8,128)S(1)} custom-call(s32[1]{0:T(128)} %bitcast.5.where_ref, bf16[512,1024]{1,0:T(8,128)(2,1)} %collective-permute-done.34.refs_0_, bf16[512,1024]{1,0:T(8,128)(2,1)} %collective-permute-done.35.refs_1_, bf16[512,1024]{1,0:T(8,128)(2,1)S(1)} %collective-permute-done.9.refs_0_.refs_2_, bf16[512,1024]{1,0:T(8,128)(2,1)S(1)} %copy-done.1, ...), custom_call_target="tpu_custom_call" | custom-call | flops 1048576 | bytes 65536 | tf_op jit(solution)/shard_map/turn/pallas_call | solution.py:319
  140.6 1.6 %combine.1 = (f32[2,512]{1,0:T(2,128)}, f32[2,512]{1,0:T(2,128)}, f32[2,512]{1,0:T(2,128)}, f32[2,512]{1,0:T(2,128)}) custom-call(s32[5]{0:T(128)} %stack.71.turn_ref, f32[8,8]{1,0:T(8,128)} %factor_inverse.1.inverse_ref, f32[8,512]{1,0:T(8,128)} %copy-done.11, f32[8,512]{1,0:T(8,128)} %copy-done.10, f32[16,512]{1,0:T(8,128)} %copy-done.9, f32[24,512]{1,0:T(8,128)} %copy-done.8), custom_call_target="tpu_custom_call" | custom-call | tf_op jit(solution)/shard_map/combine/pallas_call | solution.py:353
  144.8 6.7 %collective-permute-done.41 = f32[2,512]{1,0:T(2,128)S(1)} collective-permute-done((f32[2,512]{1,0:T(2,128)}, f32[2,512]{1,0:T(2,128)S(1)}, u32[]{:S(2)}, u32[]{:S(2)}) %collective-permute-start.41) | collective-permute-done | bytes 4128 | tf_op jit(solution)/shard_map/ppermute | solution.py:30
  (111 shorter events, 40.7 us)
Async XLA Ops:
  0.0 16.8 %collective-permute-start.3 = (bf16[8,500,250]{2,0,1:T(8,128)(2,1)}, bf16[8,500,250]{2,0,1:T(8,128)(2,1)}, u32[]{:S(2)}, u32[]{:S(2)}) collective-permute-start(bf16[8,500,250]{2,0,1:T(8,128)(2,1)} %param.4), channel_id=1, source_target_pairs={{0,1},{1,0},{2,3},{3,2},{4,5},{5,4},{6,7},{7,6},{8,9},{9,8},{10,11... | collective-permute-start | bytes 6000008 | tf_op jit(solution)/shard_map/ppermute | solution.py:30
  2.0 14.8 %collective-permute-start.4 = (bf16[500,256]{1,0:T(8,128)(2,1)S(1)}, bf16[500,256]{1,0:T(8,128)(2,1)S(1)}, u32[]{:S(2)}, u32[]{:S(2)}) collective-permute-start(bf16[500,256]{1,0:T(8,128)(2,1)S(1)} %get-tuple-element.120), channel_id=1, source_target_pairs={{0,4},{1,5},{2,6},{3,7},{4,0},{5,1},{6,2},{7,3},{8,12},{9,13},{10,... | collective-permute-start | bytes 768008 | tf_op jit(solution)/shard_map/ppermute | solution.py:30
  3.6 5.9 %collective-permute-start = (bf16[2,250,128]{2,1,0:T(8,128)(2,1)S(1)}, bf16[2,250,128]{2,1,0:T(8,128)(2,1)S(1)}, u32[]{:S(2)}, u32[]{:S(2)}) collective-permute-start(bf16[2,250,128]{2,1,0:T(8,128)(2,1)S(1)} %get-tuple-element.118), channel_id=1, source_target_pairs={{0,8},{1,9},{2,10},{3,11},{4,12},{5,13},{6,14},{7,15},{8,0},{9,1},... | collective-permute-start | bytes 384008 | tf_op jit(solution)/shard_map/ppermute | solution.py:30
  5.1 8.0 %collective-permute-start.1 = (bf16[2,250,128]{2,1,0:T(8,128)(2,1)S(1)}, bf16[2,250,128]{2,1,0:T(8,128)(2,1)S(1)}, u32[]{:S(2)}, u32[]{:S(2)}) collective-permute-start(bf16[2,250,128]{2,1,0:T(8,128)(2,1)S(1)} %get-tuple-element.117), channel_id=1, source_target_pairs={{0,16},{1,17},{2,18},{3,19},{4,20},{5,21},{6,22},{7,23},{8,24},{9,... | collective-permute-start | bytes 384008 | tf_op jit(solution)/shard_map/ppermute | solution.py:30
  6.7 6.5 %collective-permute-start.2 = (bf16[2,250,128]{2,1,0:T(8,128)(2,1)S(1)}, bf16[2,250,128]{2,1,0:T(8,128)(2,1)S(1)}, u32[]{:S(2)}, u32[]{:S(2)}) collective-permute-start(bf16[2,250,128]{2,1,0:T(8,128)(2,1)S(1)} %get-tuple-element.116), channel_id=1, source_target_pairs={{0,24},{1,25},{2,26},{3,27},{4,28},{5,29},{6,30},{7,31},{8,16},{9,... | collective-permute-start | bytes 384008 | tf_op jit(solution)/shard_map/ppermute | solution.py:30
  17.9 29.5 %collective-permute-start.9 = (bf16[512,1024]{1,0:T(8,128)(2,1)}, bf16[512,1024]{1,0:T(8,128)(2,1)S(1)}, u32[]{:S(2)}, u32[]{:S(2)}) collective-permute-start(bf16[512,1024]{1,0:T(8,128)(2,1)} %convert_element_type.10.refs_0_), channel_id=1, source_target_pairs={{2,10},{3,11},{12,20},{13,21},{22,30},{23,31}} | collective-permute-start | bytes 3145736 | tf_op jit(solution)/shard_map/ppermute | solution.py:30
  21.2 14.9 %collective-permute-start.5 = (bf16[2,250,128]{2,1,0:T(8,128)(2,1)}, bf16[2,250,128]{2,1,0:T(8,128)(2,1)}, u32[]{:S(2)}, u32[]{:S(2)}) collective-permute-start(bf16[2,250,128]{2,1,0:T(8,128)(2,1)} %get-tuple-element.113), channel_id=1, source_target_pairs={{0,2},{1,3},{2,0},{3,1},{4,6},{5,7},{6,4},{7,5},{8,10},{9,11},{10,... | collective-permute-start | bytes 384008 | tf_op jit(solution)/shard_map/ppermute | solution.py:30
  21.2 18.7 %collective-permute-start.6 = (bf16[2,250,128]{2,1,0:T(8,128)(2,1)}, bf16[2,250,128]{2,1,0:T(8,128)(2,1)}, u32[]{:S(2)}, u32[]{:S(2)}) collective-permute-start(bf16[2,250,128]{2,1,0:T(8,128)(2,1)} %get-tuple-element.112), channel_id=1, source_target_pairs={{0,4},{1,5},{2,6},{3,7},{4,0},{5,1},{6,2},{7,3},{8,12},{9,13},{10,... | collective-permute-start | bytes 384008 | tf_op jit(solution)/shard_map/ppermute | solution.py:30
  23.5 16.4 %collective-permute-start.7 = (bf16[2,250,128]{2,1,0:T(8,128)(2,1)}, bf16[2,250,128]{2,1,0:T(8,128)(2,1)}, u32[]{:S(2)}, u32[]{:S(2)}) collective-permute-start(bf16[2,250,128]{2,1,0:T(8,128)(2,1)} %get-tuple-element.111), channel_id=1, source_target_pairs={{0,6},{1,7},{2,4},{3,5},{4,2},{5,3},{6,0},{7,1},{8,14},{9,15},{10,... | collective-permute-start | bytes 384008 | tf_op jit(solution)/shard_map/ppermute | solution.py:30
  25.6 21.8 %collective-permute-start.8 = (bf16[500,256]{1,0:T(8,128)(2,1)}, bf16[500,256]{1,0:T(8,128)(2,1)}, u32[]{:S(2)}, u32[]{:S(2)}) collective-permute-start(bf16[500,256]{1,0:T(8,128)(2,1)} %get-tuple-element.59), channel_id=1, source_target_pairs={{0,4},{1,5},{2,6},{3,7},{4,0},{5,1},{6,2},{7,3},{8,12},{9,13},{10,... | collective-permute-start | bytes 768008 | tf_op jit(solution)/shard_map/ppermute | solution.py:30
  47.4 6.9 %collective-permute-start.15 = (f32[512,512]{1,0:T(8,128)}, f32[512,512]{1,0:T(8,128)}, u32[]{:S(2)}, u32[]{:S(2)}) collective-permute-start(f32[512,512]{1,0:T(8,128)} %copy-done.3), channel_id=1, source_target_pairs={{0,1},{1,0},{2,3},{3,2},{4,5},{5,4},{6,7},{7,6},{8,9},{9,8},{10,11... | collective-permute-start | bytes 3145736 | tf_op jit(solution)/shard_map/ppermute | solution.py:30
  48.7 14.8 %collective-permute-start.10 = (bf16[4,2,250,128]{3,2,1,0:T(8,128)(2,1)S(1)}, bf16[4,2,250,128]{3,2,1,0:T(8,128)(2,1)S(1)}, u32[]{:S(2)}, u32[]{:S(2)}) collective-permute-start(bf16[4,2,250,128]{3,2,1,0:T(8,128)(2,1)S(1)} %pad_maximum_fusion.2.rest_5_.rest_9_.rest_13_.rest_17_), channel_id=1, source_target_pairs={{0,8},{1,9},{2,10},{3,11},{4,12},{5,13},{6,14},{7,15},{8,0},{9,1},... | collective-permute-start | bytes 1536008 | tf_op jit(solution)/shard_map/ppermute | solution.py:30
  50.2 25.6 %collective-permute-start.11 = (bf16[4,2,250,128]{3,2,1,0:T(8,128)(2,1)S(1)}, bf16[4,2,250,128]{3,2,1,0:T(8,128)(2,1)S(1)}, u32[]{:S(2)}, u32[]{:S(2)}) collective-permute-start(bf16[4,2,250,128]{3,2,1,0:T(8,128)(2,1)S(1)} %pad_maximum_fusion.2.rest_5_.rest_9_.rest_13_.rest_17_), channel_id=1, source_target_pairs={{0,16},{1,17},{2,18},{3,19},{4,20},{5,21},{6,22},{7,23},{8,24},{9,... | collective-permute-start | bytes 1536008 | tf_op jit(solution)/shard_map/ppermute | solution.py:30
  52.8 24.9 %collective-permute-start.12 = (bf16[4,2,250,128]{3,2,1,0:T(8,128)(2,1)S(1)}, bf16[4,2,250,128]{3,2,1,0:T(8,128)(2,1)S(1)}, u32[]{:S(2)}, u32[]{:S(2)}) collective-permute-start(bf16[4,2,250,128]{3,2,1,0:T(8,128)(2,1)S(1)} %pad_maximum_fusion.2.rest_5_.rest_9_.rest_13_.rest_17_), channel_id=1, source_target_pairs={{0,24},{1,25},{2,26},{3,27},{4,28},{5,29},{6,30},{7,31},{8,16},{9,... | collective-permute-start | bytes 1536008 | tf_op jit(solution)/shard_map/ppermute | solution.py:30
  54.2 24.9 %collective-permute-start.13 = (bf16[500,512]{1,0:T(8,128)(2,1)}, bf16[500,512]{1,0:T(8,128)(2,1)S(1)}, u32[]{:S(2)}, u32[]{:S(2)}) collective-permute-start(bf16[500,512]{1,0:T(8,128)(2,1)} %rest_0_), channel_id=1, source_target_pairs={{0,2},{1,3},{2,0},{3,1},{4,6},{5,7},{6,4},{7,5},{8,10},{9,11},{10,... | collective-permute-start | bytes 1536008 | tf_op jit(solution)/shard_map/ppermute | solution.py:30
  54.3 24.7 %collective-permute-start.14 = (bf16[500,512]{1,0:T(8,128)(2,1)S(1)}, bf16[500,512]{1,0:T(8,128)(2,1)S(1)}, u32[]{:S(2)}, u32[]{:S(2)}) collective-permute-start(bf16[500,512]{1,0:T(8,128)(2,1)S(1)} %copy-done.5), channel_id=1, source_target_pairs={{0,6},{1,7},{2,4},{3,5},{4,2},{5,3},{6,0},{7,1},{8,14},{9,15},{10,... | collective-permute-start | bytes 1536008 | tf_op jit(solution)/shard_map/ppermute | solution.py:30
  63.5 28.9 %collective-permute-start.16 = (bf16[512,1024]{1,0:T(8,128)(2,1)S(1)}, bf16[512,1024]{1,0:T(8,128)(2,1)S(1)}, u32[]{:S(2)}, u32[]{:S(2)}) collective-permute-start(bf16[512,1024]{1,0:T(8,128)(2,1)S(1)} %collective-permute-done.9.refs_0_.refs_2_), channel_id=1, source_target_pairs={{0,1},{1,0},{2,3},{3,2},{4,5},{5,4},{6,7},{7,6},{8,9},{9,8},{10,11... | collective-permute-start | bytes 3145736 | tf_op jit(solution)/shard_map/ppermute | solution.py:30
  79.1 43.7 %collective-permute-start.34 = (bf16[512,1024]{1,0:T(8,128)(2,1)}, bf16[512,1024]{1,0:T(8,128)(2,1)}, u32[]{:S(2)}, u32[]{:S(2)}) collective-permute-start(bf16[512,1024]{1,0:T(8,128)(2,1)} %convert_element_type.10.refs_0_), channel_id=1, source_target_pairs={{14,30},{15,31}} | collective-permute-start | bytes 3145736 | tf_op jit(solution)/shard_map/ppermute | solution.py:30
  92.4 5.5 %collective-permute-start.17 = (f32[8,640]{1,0:T(8,128)S(1)}, f32[8,640]{1,0:T(8,128)S(1)}, u32[]{:S(2)}, u32[]{:S(2)}) collective-permute-start(f32[8,640]{1,0:T(8,128)S(1)} %get-tuple-element.90), channel_id=1, source_target_pairs={{0,2},{1,3},{2,0},{3,1},{4,6},{5,7},{6,4},{7,5},{8,10},{9,11},{10,... | collective-permute-start | bytes 61448 | tf_op jit(solution)/shard_map/ppermute | solution.py:30
  95.4 4.7 %collective-permute-start.18 = (f32[8,640]{1,0:T(8,128)S(1)}, f32[8,640]{1,0:T(8,128)S(1)}, u32[]{:S(2)}, u32[]{:S(2)}) collective-permute-start(f32[8,640]{1,0:T(8,128)S(1)} %get-tuple-element.91), channel_id=1, source_target_pairs={{0,4},{1,5},{2,6},{3,7},{4,0},{5,1},{6,2},{7,3},{8,12},{9,13},{10,... | collective-permute-start | bytes 61448 | tf_op jit(solution)/shard_map/ppermute | solution.py:30
  95.4 5.6 %collective-permute-start.19 = (f32[8,640]{1,0:T(8,128)S(1)}, f32[8,640]{1,0:T(8,128)S(1)}, u32[]{:S(2)}, u32[]{:S(2)}) collective-permute-start(f32[8,640]{1,0:T(8,128)S(1)} %get-tuple-element.92), channel_id=1, source_target_pairs={{0,6},{1,7},{2,4},{3,5},{4,2},{5,3},{6,0},{7,1},{8,14},{9,15},{10,... | collective-permute-start | bytes 61448 | tf_op jit(solution)/shard_map/ppermute | solution.py:30
  101.0 3.8 %collective-permute-start.20 = (f32[8,640]{1,0:T(8,128)S(1)}, f32[8,640]{1,0:T(8,128)S(1)}, u32[]{:S(2)}, u32[]{:S(2)}) collective-permute-start(f32[8,640]{1,0:T(8,128)S(1)} %add_add_fusion.1), channel_id=1, source_target_pairs={{0,8},{1,9},{2,10},{3,11},{4,12},{5,13},{6,14},{7,15},{8,0},{9,1},... | collective-permute-start | bytes 61448 | tf_op jit(solution)/shard_map/ppermute | solution.py:30
  102.2 3.8 %collective-permute-start.21 = (f32[8,640]{1,0:T(8,128)S(1)}, f32[8,640]{1,0:T(8,128)S(1)}, u32[]{:S(2)}, u32[]{:S(2)}) collective-permute-start(f32[8,640]{1,0:T(8,128)S(1)} %add_add_fusion.1), channel_id=1, source_target_pairs={{0,16},{1,17},{2,18},{3,19},{4,20},{5,21},{6,22},{7,23},{8,24},{9,... | collective-permute-start | bytes 61448 | tf_op jit(solution)/shard_map/ppermute | solution.py:30
  103.2 4.7 %collective-permute-start.22 = (f32[8,640]{1,0:T(8,128)S(1)}, f32[8,640]{1,0:T(8,128)S(1)}, u32[]{:S(2)}, u32[]{:S(2)}) collective-permute-start(f32[8,640]{1,0:T(8,128)S(1)} %add_add_fusion.1), channel_id=1, source_target_pairs={{0,24},{1,25},{2,26},{3,27},{4,28},{5,29},{6,30},{7,31},{8,16},{9,... | collective-permute-start | bytes 61448 | tf_op jit(solution)/shard_map/ppermute | solution.py:30
  111.8 9.2 %collective-permute-start.27 = (f32[8,512]{1,0:T(8,128)S(1)}, f32[8,512]{1,0:T(8,128)S(1)}, u32[]{:S(2)}, u32[]{:S(2)}) collective-permute-start(f32[8,512]{1,0:T(8,128)S(1)} %apply_weights.2.refs_0_), channel_id=1, source_target_pairs={{0,6},{1,7}} | collective-permute-start | bytes 49160 | tf_op jit(solution)/shard_map/ppermute | solution.py:30
  122.8 12.4 %collective-permute-start.35 = (bf16[512,1024]{1,0:T(8,128)(2,1)}, bf16[512,1024]{1,0:T(8,128)(2,1)}, u32[]{:S(2)}, u32[]{:S(2)}) collective-permute-start(bf16[512,1024]{1,0:T(8,128)(2,1)} %collective-permute-done.34.refs_0_), channel_id=1, source_target_pairs={{0,1},{1,0},{2,3},{3,2},{4,5},{5,4},{6,7},{7,6},{8,9},{9,8},{10,11... | collective-permute-start | bytes 3145736 | tf_op jit(solution)/shard_map/ppermute | solution.py:30
  123.3 4.1 %collective-permute-start.28 = (f32[8,512]{1,0:T(8,128)S(1)}, f32[8,512]{1,0:T(8,128)S(1)}, u32[]{:S(2)}, u32[]{:S(2)}) collective-permute-start(f32[8,512]{1,0:T(8,128)S(1)} %turn.3.refs_1_), channel_id=1, source_target_pairs={{10,20},{11,21}} | collective-permute-start | bytes 49160 | tf_op jit(solution)/shard_map/ppermute | solution.py:30
  124.0 3.4 %collective-permute-start.29 = (f32[8,512]{1,0:T(8,128)S(1)}, f32[8,512]{1,0:T(8,128)S(1)}, u32[]{:S(2)}, u32[]{:S(2)}) collective-permute-start(f32[8,512]{1,0:T(8,128)S(1)} %turn.3.refs_1_), channel_id=1, source_target_pairs={{10,21},{11,20}} | collective-permute-start | bytes 49160 | tf_op jit(solution)/shard_map/ppermute | solution.py:30
  127.9 4.5 %collective-permute-start.37 = (f32[8,512]{1,0:T(8,128)S(1)}, f32[8,512]{1,0:T(8,128)S(1)}, u32[]{:S(2)}, u32[]{:S(2)}) collective-permute-start(f32[8,512]{1,0:T(8,128)S(1)} %apply_weights.3), channel_id=1, source_target_pairs={{6,30},{7,31}} | collective-permute-start | bytes 49160 | tf_op jit(solution)/shard_map/ppermute | solution.py:30
  131.0 4.2 %collective-permute-start.33 = (f32[16,512]{1,0:T(8,128)S(1)}, f32[16,512]{1,0:T(8,128)S(1)}, u32[]{:S(2)}, u32[]{:S(2)}) collective-permute-start(f32[16,512]{1,0:T(8,128)S(1)} %turn.4.refs_2_), channel_id=1, source_target_pairs={{20,30},{21,31}} | collective-permute-start | bytes 98312 | tf_op jit(solution)/shard_map/ppermute | solution.py:30
  131.7 3.5 %collective-permute-start.36 = (f32[16,512]{1,0:T(8,128)S(1)}, f32[16,512]{1,0:T(8,128)S(1)}, u32[]{:S(2)}, u32[]{:S(2)}) collective-permute-start(f32[16,512]{1,0:T(8,128)S(1)} %turn.4.refs_2_), channel_id=1, source_target_pairs={{20,31},{21,30}} | collective-permute-start | bytes 98312 | tf_op jit(solution)/shard_map/ppermute | solution.py:30
  143.5 8.1 %collective-permute-start.41 = (f32[2,512]{1,0:T(2,128)}, f32[2,512]{1,0:T(2,128)S(1)}, u32[]{:S(2)}, u32[]{:S(2)}) collective-permute-start(f32[2,512]{1,0:T(2,128)} %get-tuple-element.108), channel_id=1, source_target_pairs={{0,24},{1,25},{10,18},{11,19},{20,12},{21,13},{30,6},{31,7}} | collective-permute-start | bytes 12296 | tf_op jit(solution)/shard_map/ppermute | solution.py:30
  (24 other events, 179.7 us)

commit v12 on v11

--- a/solution.py
+++ b/solution.py
@@ -384,12 +384,10 @@
     early, half = 2, points // 2
     sibling = move(raw_columns, swap)
     early_parts = [move(collocation[:, :half], across(early))]
-    second_half = collocation[:, half:]
-    spread, sibling, early_parts, second_half, metric_late = lax.optimization_barrier(
-        (spread, sibling, early_parts, second_half, metric_factor)
-    )
-    early_parts.append(move(second_half, across(early)))
-    own_rows = metric_late.astype(BF16)
+    spread, sibling, early_parts, own_rows, first, metric_late = lax.optimization_barrier(
+        (spread, sibling, early_parts, metric_factor.astype(BF16), collocation, metric_factor)
+    )
+    early_parts.append(move(first[:, half:], across(early)))
     left_own = move(own_rows, lambda g, j, c: (g + 1, j, c) if j == g + 1 else None)
     own_parts = []
     for k in range(gen_count):

time: 154 us -> 152 us (0.987)
  waiting for transfers between devices: 58.9 us -> 56.1 us
    ppermute x42, waiting for transfers between devices: 58.9 us -> 56.1 us  [move(): return lax.ppermute(value, BOTH, pairs)]
  transfers between devices with their start and end apart: 42 -> 42, of which waited for: 18 -> 18; matrix products, arithmetic and copies ran while one was open for 10% -> 12% of each run, Pallas kernels for 18% -> 18%
where the time goes in v12:
time: 152 us; the launch traced here: 151 us
  waiting for transfers between devices  56.1 us (37%)
  starting transfers between devices  39.8 us (26%)
  Pallas kernels  32.6 us (21%)
  local copies, waits for them, and re-layouts  9.49 us (6%)
  matrix products  6.61 us (4%)
  other arithmetic  5.64 us (4%)
    ppermute x42, waiting for transfers between devices, move(): return lax.ppermute(value, BOTH, pairs)  56.1 us
    ppermute x42, starting transfers between devices, move(): return lax.ppermute(value, BOTH, pairs)  39.8 us
    pallas_call x1, Pallas kernels, project(): pl.pallas_call(kernel, grid_spec=pltpu.PrefetchScalarGridSpec(num_scalar_...  11.6 us
    pallas_call x3, Pallas kernels, turn(): pl.pallas_call(functools.partial(turn_kernel, count), in_specs=[pl.BlockS...  7.06 us
    pallas_call x1, Pallas kernels, invert_block(): pl.pallas_call(invert_kernel, grid_spec=pltpu.PrefetchScalarGridSpec(num_...  5.35 us
    dot_general x1, matrix products, on_device(): corner = jnp.dot(metric_factor[:, :points], upper, precision=HIGHEST)  4.71 us
  transfers between devices with their start and end apart: 42, of which 18 were waited for; matrix products, arithmetic and copies ran while one was open for 12% of the time, Pallas kernels for 18%

profile of v12, /device:TPU:24, one launch (start us, length us, event | category | flops | bytes accessed | tf_op | source)
XLA Modules:
  0.0 150.9 jit_solution(9049402310355220906)
XLA Ops:
  2.8 1.6 %collective-permute-start = (bf16[2,250,128]{2,1,0:T(8,128)(2,1)S(1)}, bf16[2,250,128]{2,1,0:T(8,128)(2,1)S(1)}, u32[]{:S(2)}, u32[]{:S(2)}) collective-permute-start(bf16[2,250,128]{2,1,0:T(8,128)(2,1)S(1)} %get-tuple-element.120), channel_id=1, source_target_pairs={{0,8},{1,9},{2,10},{3,11},{4,12},{5,13},{6,14},{7,15},{8,0},{9,1},... | collective-permute-start | bytes 384008 | tf_op jit(solution)/shard_map/ppermute | solution.py:30
  8.7 3.7 %collective-permute-done.1 = bf16[2,250,128]{2,1,0:T(8,128)(2,1)S(1)} collective-permute-done((bf16[2,250,128]{2,1,0:T(8,128)(2,1)S(1)}, bf16[2,250,128]{2,1,0:T(8,128)(2,1)S(1)}, u32[]{:S(2)}, u32[]{:S(2)}) %collective-permute-start.1) | collective-permute-done | bytes 128032 | tf_op jit(solution)/shard_map/ppermute | solution.py:30
  13.2 2.8 %collective-permute-done.4.rest_2_ = bf16[500,256]{1,0:T(8,128)(2,1)S(1)} collective-permute-done((bf16[500,256]{1,0:T(8,128)(2,1)S(1)}, bf16[500,256]{1,0:T(8,128)(2,1)S(1)}, u32[]{:S(2)}, u32[]{:S(2)}) %collective-permute-start.4) | collective-permute-done | bytes 256032 | tf_op jit(solution)/shard_map/ppermute | solution.py:30
  17.4 1.9 %dynamic-slice_bitcast_fusion = (bf16[2,250,128]{2,1,0:T(8,128)(2,1)}, bf16[2,250,128]{2,1,0:T(8,128)(2,1)}, bf16[2,250,128]{2,1,0:T(8,128)(2,1)}, bf16[2,250,128]{2,1,0:T(8,128)(2,1)S(1)}) fusion(bf16[4,2,250,128]{3,2,1,0:T(8,128)(2,1)} %pad_maximum_fusion.1, s32[]{:T(128)S(6)} %select_n.75, s32[]{:T(128)S(6)} %select_n.74, s32[]{:T(128)S(6)} %select_n.73, ...), kind=kLoop, calls=%fused_computation.11 | loop fusion | bytes 1024016 | tf_op jit(solution)/shard_map/jit(dynamic_index_in_dim)/squeeze | solution.py:394
  19.3 2.3 %collective-permute-start.6 = (bf16[2,250,128]{2,1,0:T(8,128)(2,1)}, bf16[2,250,128]{2,1,0:T(8,128)(2,1)}, u32[]{:S(2)}, u32[]{:S(2)}) collective-permute-start(bf16[2,250,128]{2,1,0:T(8,128)(2,1)} %get-tuple-element.114), channel_id=1, source_target_pairs={{0,4},{1,5},{2,6},{3,7},{4,0},{5,1},{6,2},{7,3},{8,12},{9,13},{10,... | collective-permute-start | bytes 384008 | tf_op jit(solution)/shard_map/ppermute | solution.py:30
  21.6 2.1 %collective-permute-start.7 = (bf16[2,250,128]{2,1,0:T(8,128)(2,1)}, bf16[2,250,128]{2,1,0:T(8,128)(2,1)}, u32[]{:S(2)}, u32[]{:S(2)}) collective-permute-start(bf16[2,250,128]{2,1,0:T(8,128)(2,1)} %get-tuple-element.113), channel_id=1, source_target_pairs={{0,6},{1,7},{2,4},{3,5},{4,2},{5,3},{6,0},{7,1},{8,14},{9,15},{10,... | collective-permute-start | bytes 384008 | tf_op jit(solution)/shard_map/ppermute | solution.py:30
  23.7 1.7 %slice.13 = bf16[500,256]{1,0:T(8,128)(2,1)} slice(bf16[500,512]{1,0:T(8,128)(2,1)} %rest_0_), slice={[0:500], [256:512]} | slice | bytes 512000 | tf_op jit(solution)/shard_map/slice | solution.py:390
  26.8 5.3 %invert_block.1 = f32[512,512]{1,0:T(8,128)S(1)} custom-call(s32[2]{0:T(128)S(1)} %pad_add_fusion.where_ref, f32[512,1024]{1,0:T(8,128)S(1)} %copy-done.2), custom_call_target="tpu_custom_call" | custom-call | flops 4294967296 | bytes 4194304 | tf_op jit(solution)/shard_map/invert_block/pallas_call | solution.py:230
  33.1 2.8 %pivot_entries.1.entries_ref = f32[8,8]{1,0:T(8,128)} custom-call(s32[8]{0:T(128)} %get-tuple-element.122.row_ref, bf16[500,8,250]{2,1,0:T(8,128)(2,1)} %bitcast.33, bf16[500,8,250]{2,1,0:T(8,128)(2,1)} %bitcast.16.sib_ref, s32[8]{0:T(128)} %get-tuple-element.123.own_col_ref, s32[8]{0:T(128)} %get-tuple-element.121.sib_col_ref), custom_call_target="tpu_custom_call" | custom-call | tf_op jit(solution)/shard_map/pivot_entries/pallas_call | solution.py:63
  35.9 2.1 %collective-permute-done.6 = bf16[2,250,128]{2,1,0:T(8,128)(2,1)} collective-permute-done((bf16[2,250,128]{2,1,0:T(8,128)(2,1)}, bf16[2,250,128]{2,1,0:T(8,128)(2,1)}, u32[]{:S(2)}, u32[]{:S(2)}) %collective-permute-start.6) | collective-permute-done | bytes 128032 | tf_op jit(solution)/shard_map/ppermute | solution.py:30
  38.0 7.5 %collective-permute-done.8.rest_3_ = bf16[500,256]{1,0:T(8,128)(2,1)} collective-permute-done((bf16[500,256]{1,0:T(8,128)(2,1)}, bf16[500,256]{1,0:T(8,128)(2,1)}, u32[]{:S(2)}, u32[]{:S(2)}) %collective-permute-start.8) | collective-permute-done | bytes 256032 | tf_op jit(solution)/shard_map/ppermute | solution.py:30
  46.8 1.6 %collective-permute-start.10 = (bf16[4,2,250,128]{3,2,1,0:T(8,128)(2,1)S(1)}, bf16[4,2,250,128]{3,2,1,0:T(8,128)(2,1)S(1)}, u32[]{:S(2)}, u32[]{:S(2)}) collective-permute-start(bf16[4,2,250,128]{3,2,1,0:T(8,128)(2,1)S(1)} %pad_maximum_fusion.2.rest_5_.rest_9_.rest_13_.rest_17_), channel_id=1, source_target_pairs={{0,8},{1,9},{2,10},{3,11},{4,12},{5,13},{6,14},{7,15},{8,0},{9,1},... | collective-permute-start | bytes 1536008 | tf_op jit(solution)/shard_map/ppermute | solution.py:30
  48.3 2.6 %collective-permute-start.11 = (bf16[4,2,250,128]{3,2,1,0:T(8,128)(2,1)S(1)}, bf16[4,2,250,128]{3,2,1,0:T(8,128)(2,1)S(1)}, u32[]{:S(2)}, u32[]{:S(2)}) collective-permute-start(bf16[4,2,250,128]{3,2,1,0:T(8,128)(2,1)S(1)} %pad_maximum_fusion.2.rest_5_.rest_9_.rest_13_.rest_17_), channel_id=1, source_target_pairs={{0,16},{1,17},{2,18},{3,19},{4,20},{5,21},{6,22},{7,23},{8,24},{9,... | collective-permute-start | bytes 1536008 | tf_op jit(solution)/shard_map/ppermute | solution.py:30
  53.9 4.7 %fusion.2 = f32[512,512]{1,0:T(8,128)S(1)} fusion(f32[512,512]{1,0:T(8,128)} %collective-permute-done.15, f32[512,1024]{1,0:T(8,128)S(1)} %copy-done.2), kind=kOutput, calls=%fused_computation.6 | convolution fusion | flops 1610612736 | bytes 3145728 | tf_op jit(solution)/shard_map/dot_general | solution.py:424
  58.6 2.9 %collective-permute-done.10.rest_6_.rest_10_.rest_14_.rest_18_ = bf16[4,2,250,128]{3,2,1,0:T(8,128)(2,1)S(1)} collective-permute-done((bf16[4,2,250,128]{3,2,1,0:T(8,128)(2,1)S(1)}, bf16[4,2,250,128]{3,2,1,0:T(8,128)(2,1)S(1)}, u32[]{:S(2)}, u32[]{:S(2)}) %collective-permute-start.10) | collective-permute-done | bytes 512032 | tf_op jit(solution)/shard_map/ppermute | solution.py:30
  61.6 1.9 %fusion.1 = f32[512,512]{1,0:T(8,128)S(1)} fusion(f32[512,512]{1,0:T(8,128)S(1)} %copy-done.4, f32[512,512]{1,0:T(8,128)S(1)} %fusion.2, pred[]{:T(512)S(6)} %eq.13), kind=kOutput, calls=%fused_computation.5 | convolution fusion | flops 1611137024 | bytes 3145729 | tf_op jit(solution)/shard_map/dot_general | solution.py:425
  63.9 10.1 %collective-permute-done.11.rest_7_.rest_11_.rest_15_.rest_19_ = bf16[4,2,250,128]{3,2,1,0:T(8,128)(2,1)S(1)} collective-permute-done((bf16[4,2,250,128]{3,2,1,0:T(8,128)(2,1)S(1)}, bf16[4,2,250,128]{3,2,1,0:T(8,128)(2,1)S(1)}, u32[]{:S(2)}, u32[]{:S(2)}) %collective-permute-start.11) | collective-permute-done | bytes 512032 | tf_op jit(solution)/shard_map/ppermute | solution.py:30
  74.0 1.8 %collective-permute-done.12.rest_8_.rest_12_.rest_16_.rest_20_ = bf16[4,2,250,128]{3,2,1,0:T(8,128)(2,1)S(1)} collective-permute-done((bf16[4,2,250,128]{3,2,1,0:T(8,128)(2,1)S(1)}, bf16[4,2,250,128]{3,2,1,0:T(8,128)(2,1)S(1)}, u32[]{:S(2)}, u32[]{:S(2)}) %collective-permute-start.12) | collective-permute-done | bytes 512032 | tf_op jit(solution)/shard_map/ppermute | solution.py:30
  77.2 1.6 %collective-permute-start.34 = (bf16[512,1024]{1,0:T(8,128)(2,1)}, bf16[512,1024]{1,0:T(8,128)(2,1)}, u32[]{:S(2)}, u32[]{:S(2)}) collective-permute-start(bf16[512,1024]{1,0:T(8,128)(2,1)} %convert_element_type.10.refs_0_), channel_id=1, source_target_pairs={{14,30},{15,31}} | collective-permute-start | bytes 3145736 | tf_op jit(solution)/shard_map/ppermute | solution.py:30
  78.8 11.6 %project.1 = (f32[8,640]{1,0:T(8,128)S(1)}, f32[8,640]{1,0:T(8,128)S(1)}, f32[8,640]{1,0:T(8,128)S(1)}, f32[8,640]{1,0:T(8,128)S(1)}) custom-call(s32[5]{0:T(128)S(1)} %stack.80.where_ref, bf16[4000,250]{1,0:T(8,128)(2,1)S(1)} %bitcast.34, bf16[4000,250]{1,0:T(8,128)(2,1)} %bitcast.18.sib_ref, f32[8,8]{1,0:T(8,128)S(1)} %copy-done.12, ...), custom_call_target="tpu_custom_call" | custom-call | flops 8192000000 | bytes 1048576 | tf_op jit(solution)/shard_map/project/pallas_call | solution.py:170
  90.5 3.0 %collective-permute-start.17 = (f32[8,640]{1,0:T(8,128)S(1)}, f32[8,640]{1,0:T(8,128)S(1)}, u32[]{:S(2)}, u32[]{:S(2)}) collective-permute-start(f32[8,640]{1,0:T(8,128)S(1)} %get-tuple-element.92), channel_id=1, source_target_pairs={{0,2},{1,3},{2,0},{3,1},{4,6},{5,7},{6,4},{7,5},{8,10},{9,11},{10,... | collective-permute-start | bytes 61448 | tf_op jit(solution)/shard_map/ppermute | solution.py:30
  93.5 2.4 %collective-permute-start.19 = (f32[8,640]{1,0:T(8,128)S(1)}, f32[8,640]{1,0:T(8,128)S(1)}, u32[]{:S(2)}, u32[]{:S(2)}) collective-permute-start(f32[8,640]{1,0:T(8,128)S(1)} %get-tuple-element.94), channel_id=1, source_target_pairs={{0,6},{1,7},{2,4},{3,5},{4,2},{5,3},{6,0},{7,1},{8,14},{9,15},{10,... | collective-permute-start | bytes 61448 | tf_op jit(solution)/shard_map/ppermute | solution.py:30
  95.9 2.2 %collective-permute-done.18 = f32[8,640]{1,0:T(8,128)S(1)} collective-permute-done((f32[8,640]{1,0:T(8,128)S(1)}, f32[8,640]{1,0:T(8,128)S(1)}, u32[]{:S(2)}, u32[]{:S(2)}) %collective-permute-start.18) | collective-permute-done | bytes 20512 | tf_op jit(solution)/shard_map/ppermute | solution.py:30
  104.1 1.9 %collective-permute-done.22 = f32[8,640]{1,0:T(8,128)S(1)} collective-permute-done((f32[8,640]{1,0:T(8,128)S(1)}, f32[8,640]{1,0:T(8,128)S(1)}, u32[]{:S(2)}, u32[]{:S(2)}) %collective-permute-start.22) | collective-permute-done | bytes 20512 | tf_op jit(solution)/shard_map/ppermute | solution.py:30
  111.2 7.8 %collective-permute-done.27 = f32[8,512]{1,0:T(8,128)S(1)} collective-permute-done((f32[8,512]{1,0:T(8,128)S(1)}, f32[8,512]{1,0:T(8,128)S(1)}, u32[]{:S(2)}, u32[]{:S(2)}) %collective-permute-start.27) | collective-permute-done | bytes 16416 | tf_op jit(solution)/shard_map/ppermute | solution.py:30
  119.0 1.8 %turn.3.refs_1_ = f32[8,512]{1,0:T(8,128)S(1)} custom-call(s32[1]{0:T(128)} %bitcast.5.where_ref, bf16[512,1024]{1,0:T(8,128)(2,1)S(1)} %collective-permute-done.9.refs_0_.refs_2_, bf16[512,1024]{1,0:T(8,128)(2,1)S(1)} %collective-permute-done.16.refs_1_.refs_3_, bf16[512,1024]{1,0:T(8,128)(2,1)S(1)} %get-tuple-element.89.refs_0_.refs_2_.refs_4_, ...), custom_call_target="tpu_custom_call" | custom-call | flops 1048576 | bytes 65536 | tf_op jit(solution)/shard_map/turn/pallas_call | solution.py:319
  123.2 1.6 %apply_weights.3 = f32[8,512]{1,0:T(8,128)S(1)} custom-call(s32[1]{0:T(128)} %bitcast.5.where_ref, bf16[512,1024]{1,0:T(8,128)(2,1)} %convert_element_type.10.refs_0_, f32[8,512]{1,0:T(8,128)S(1)} %add.85.refs_1_, f32[8,512]{1,0:T(8,128)S(1)} %collective-permute-done.30.refs_2_), custom_call_target="tpu_custom_call" | custom-call | flops 1073741824 | bytes 2097152 | tf_op jit(solution)/shard_map/apply_weights/pallas_call | solution.py:274
  127.3 1.8 %turn.4.refs_2_ = f32[16,512]{1,0:T(8,128)S(1)} custom-call(s32[1]{0:T(128)} %bitcast.5.where_ref, bf16[512,1024]{1,0:T(8,128)(2,1)S(1)} %collective-permute-done.9.refs_0_.refs_2_, bf16[512,1024]{1,0:T(8,128)(2,1)S(1)} %collective-permute-done.16.refs_1_.refs_3_, bf16[512,1024]{1,0:T(8,128)(2,1)S(1)} %get-tuple-element.89.refs_0_.refs_2_.refs_4_, ...), custom_call_target="tpu_custom_call" | custom-call | flops 1048576 | bytes 65536 | tf_op jit(solution)/shard_map/turn/pallas_call | solution.py:319
  131.4 2.0 %factor_inverse.1.inverse_ref = f32[8,8]{1,0:T(8,128)} custom-call(f32[8,640]{1,0:T(8,128)} %copy-done.7), custom_call_target="tpu_custom_call" | custom-call | tf_op jit(solution)/shard_map/factor_inverse/pallas_call | solution.py:98
  134.6 3.5 %turn.5.refs_3_ = f32[24,512]{1,0:T(8,128)S(1)} custom-call(s32[1]{0:T(128)} %bitcast.5.where_ref, bf16[512,1024]{1,0:T(8,128)(2,1)} %collective-permute-done.34.refs_0_, bf16[512,1024]{1,0:T(8,128)(2,1)} %collective-permute-done.35.refs_1_, bf16[512,1024]{1,0:T(8,128)(2,1)S(1)} %collective-permute-done.9.refs_0_.refs_2_, bf16[512,1024]{1,0:T(8,128)(2,1)S(1)} %copy-done.1, ...), custom_call_target="tpu_custom_call" | custom-call | flops 1048576 | bytes 65536 | tf_op jit(solution)/shard_map/turn/pallas_call | solution.py:319
  138.7 1.6 %combine.1 = (f32[2,512]{1,0:T(2,128)}, f32[2,512]{1,0:T(2,128)}, f32[2,512]{1,0:T(2,128)}, f32[2,512]{1,0:T(2,128)}) custom-call(s32[5]{0:T(128)} %stack.71.turn_ref, f32[8,8]{1,0:T(8,128)} %factor_inverse.1.inverse_ref, f32[8,512]{1,0:T(8,128)} %copy-done.11, f32[8,512]{1,0:T(8,128)} %copy-done.10, f32[16,512]{1,0:T(8,128)} %copy-done.9, f32[24,512]{1,0:T(8,128)} %copy-done.8), custom_call_target="tpu_custom_call" | custom-call | tf_op jit(solution)/shard_map/combine/pallas_call | solution.py:353
  142.9 6.7 %collective-permute-done.41 = f32[2,512]{1,0:T(2,128)S(1)} collective-permute-done((f32[2,512]{1,0:T(2,128)}, f32[2,512]{1,0:T(2,128)S(1)}, u32[]{:S(2)}, u32[]{:S(2)}) %collective-permute-start.41) | collective-permute-done | bytes 4128 | tf_op jit(solution)/shard_map/ppermute | solution.py:30
  (112 shorter events, 41.6 us)
Async XLA Ops:
  0.0 16.0 %collective-permute-start.3 = (bf16[8,500,250]{2,0,1:T(8,128)(2,1)}, bf16[8,500,250]{2,0,1:T(8,128)(2,1)}, u32[]{:S(2)}, u32[]{:S(2)}) collective-permute-start(bf16[8,500,250]{2,0,1:T(8,128)(2,1)} %param.4), channel_id=1, source_target_pairs={{0,1},{1,0},{2,3},{3,2},{4,5},{5,4},{6,7},{7,6},{8,9},{9,8},{10,11... | collective-permute-start | bytes 6000008 | tf_op jit(solution)/shard_map/ppermute | solution.py:30
  1.1 14.9 %collective-permute-start.4 = (bf16[500,256]{1,0:T(8,128)(2,1)S(1)}, bf16[500,256]{1,0:T(8,128)(2,1)S(1)}, u32[]{:S(2)}, u32[]{:S(2)}) collective-permute-start(bf16[500,256]{1,0:T(8,128)(2,1)S(1)} %slice.12), channel_id=1, source_target_pairs={{0,4},{1,5},{2,6},{3,7},{4,0},{5,1},{6,2},{7,3},{8,12},{9,13},{10,... | collective-permute-start | bytes 768008 | tf_op jit(solution)/shard_map/ppermute | solution.py:30
  2.8 5.9 %collective-permute-start = (bf16[2,250,128]{2,1,0:T(8,128)(2,1)S(1)}, bf16[2,250,128]{2,1,0:T(8,128)(2,1)S(1)}, u32[]{:S(2)}, u32[]{:S(2)}) collective-permute-start(bf16[2,250,128]{2,1,0:T(8,128)(2,1)S(1)} %get-tuple-element.120), channel_id=1, source_target_pairs={{0,8},{1,9},{2,10},{3,11},{4,12},{5,13},{6,14},{7,15},{8,0},{9,1},... | collective-permute-start | bytes 384008 | tf_op jit(solution)/shard_map/ppermute | solution.py:30
  4.4 8.0 %collective-permute-start.1 = (bf16[2,250,128]{2,1,0:T(8,128)(2,1)S(1)}, bf16[2,250,128]{2,1,0:T(8,128)(2,1)S(1)}, u32[]{:S(2)}, u32[]{:S(2)}) collective-permute-start(bf16[2,250,128]{2,1,0:T(8,128)(2,1)S(1)} %get-tuple-element.119), channel_id=1, source_target_pairs={{0,16},{1,17},{2,18},{3,19},{4,20},{5,21},{6,22},{7,23},{8,24},{9,... | collective-permute-start | bytes 384008 | tf_op jit(solution)/shard_map/ppermute | solution.py:30
  5.9 6.5 %collective-permute-start.2 = (bf16[2,250,128]{2,1,0:T(8,128)(2,1)S(1)}, bf16[2,250,128]{2,1,0:T(8,128)(2,1)S(1)}, u32[]{:S(2)}, u32[]{:S(2)}) collective-permute-start(bf16[2,250,128]{2,1,0:T(8,128)(2,1)S(1)} %get-tuple-element.118), channel_id=1, source_target_pairs={{0,24},{1,25},{2,26},{3,27},{4,28},{5,29},{6,30},{7,31},{8,16},{9,... | collective-permute-start | bytes 384008 | tf_op jit(solution)/shard_map/ppermute | solution.py:30
  16.0 29.5 %collective-permute-start.9 = (bf16[512,1024]{1,0:T(8,128)(2,1)}, bf16[512,1024]{1,0:T(8,128)(2,1)S(1)}, u32[]{:S(2)}, u32[]{:S(2)}) collective-permute-start(bf16[512,1024]{1,0:T(8,128)(2,1)} %convert_element_type.10.refs_0_), channel_id=1, source_target_pairs={{2,10},{3,11},{12,20},{13,21},{22,30},{23,31}} | collective-permute-start | bytes 3145736 | tf_op jit(solution)/shard_map/ppermute | solution.py:30
  19.3 16.6 %collective-permute-start.5 = (bf16[2,250,128]{2,1,0:T(8,128)(2,1)}, bf16[2,250,128]{2,1,0:T(8,128)(2,1)}, u32[]{:S(2)}, u32[]{:S(2)}) collective-permute-start(bf16[2,250,128]{2,1,0:T(8,128)(2,1)} %get-tuple-element.115), channel_id=1, source_target_pairs={{0,2},{1,3},{2,0},{3,1},{4,6},{5,7},{6,4},{7,5},{8,10},{9,11},{10,... | collective-permute-start | bytes 384008 | tf_op jit(solution)/shard_map/ppermute | solution.py:30
  19.3 18.7 %collective-permute-start.6 = (bf16[2,250,128]{2,1,0:T(8,128)(2,1)}, bf16[2,250,128]{2,1,0:T(8,128)(2,1)}, u32[]{:S(2)}, u32[]{:S(2)}) collective-permute-start(bf16[2,250,128]{2,1,0:T(8,128)(2,1)} %get-tuple-element.114), channel_id=1, source_target_pairs={{0,4},{1,5},{2,6},{3,7},{4,0},{5,1},{6,2},{7,3},{8,12},{9,13},{10,... | collective-permute-start | bytes 384008 | tf_op jit(solution)/shard_map/ppermute | solution.py:30
  21.6 16.4 %collective-permute-start.7 = (bf16[2,250,128]{2,1,0:T(8,128)(2,1)}, bf16[2,250,128]{2,1,0:T(8,128)(2,1)}, u32[]{:S(2)}, u32[]{:S(2)}) collective-permute-start(bf16[2,250,128]{2,1,0:T(8,128)(2,1)} %get-tuple-element.113), channel_id=1, source_target_pairs={{0,6},{1,7},{2,4},{3,5},{4,2},{5,3},{6,0},{7,1},{8,14},{9,15},{10,... | collective-permute-start | bytes 384008 | tf_op jit(solution)/shard_map/ppermute | solution.py:30
  25.4 20.2 %collective-permute-start.8 = (bf16[500,256]{1,0:T(8,128)(2,1)}, bf16[500,256]{1,0:T(8,128)(2,1)}, u32[]{:S(2)}, u32[]{:S(2)}) collective-permute-start(bf16[500,256]{1,0:T(8,128)(2,1)} %slice.13), channel_id=1, source_target_pairs={{0,4},{1,5},{2,6},{3,7},{4,0},{5,1},{6,2},{7,3},{8,12},{9,13},{10,... | collective-permute-start | bytes 768008 | tf_op jit(solution)/shard_map/ppermute | solution.py:30
  45.5 6.9 %collective-permute-start.15 = (f32[512,512]{1,0:T(8,128)}, f32[512,512]{1,0:T(8,128)}, u32[]{:S(2)}, u32[]{:S(2)}) collective-permute-start(f32[512,512]{1,0:T(8,128)} %copy-done.3), channel_id=1, source_target_pairs={{0,1},{1,0},{2,3},{3,2},{4,5},{5,4},{6,7},{7,6},{8,9},{9,8},{10,11... | collective-permute-start | bytes 3145736 | tf_op jit(solution)/shard_map/ppermute | solution.py:30
  46.8 14.8 %collective-permute-start.10 = (bf16[4,2,250,128]{3,2,1,0:T(8,128)(2,1)S(1)}, bf16[4,2,250,128]{3,2,1,0:T(8,128)(2,1)S(1)}, u32[]{:S(2)}, u32[]{:S(2)}) collective-permute-start(bf16[4,2,250,128]{3,2,1,0:T(8,128)(2,1)S(1)} %pad_maximum_fusion.2.rest_5_.rest_9_.rest_13_.rest_17_), channel_id=1, source_target_pairs={{0,8},{1,9},{2,10},{3,11},{4,12},{5,13},{6,14},{7,15},{8,0},{9,1},... | collective-permute-start | bytes 1536008 | tf_op jit(solution)/shard_map/ppermute | solution.py:30
  48.3 25.6 %collective-permute-start.11 = (bf16[4,2,250,128]{3,2,1,0:T(8,128)(2,1)S(1)}, bf16[4,2,250,128]{3,2,1,0:T(8,128)(2,1)S(1)}, u32[]{:S(2)}, u32[]{:S(2)}) collective-permute-start(bf16[4,2,250,128]{3,2,1,0:T(8,128)(2,1)S(1)} %pad_maximum_fusion.2.rest_5_.rest_9_.rest_13_.rest_17_), channel_id=1, source_target_pairs={{0,16},{1,17},{2,18},{3,19},{4,20},{5,21},{6,22},{7,23},{8,24},{9,... | collective-permute-start | bytes 1536008 | tf_op jit(solution)/shard_map/ppermute | solution.py:30
  50.9 24.9 %collective-permute-start.12 = (bf16[4,2,250,128]{3,2,1,0:T(8,128)(2,1)S(1)}, bf16[4,2,250,128]{3,2,1,0:T(8,128)(2,1)S(1)}, u32[]{:S(2)}, u32[]{:S(2)}) collective-permute-start(bf16[4,2,250,128]{3,2,1,0:T(8,128)(2,1)S(1)} %pad_maximum_fusion.2.rest_5_.rest_9_.rest_13_.rest_17_), channel_id=1, source_target_pairs={{0,24},{1,25},{2,26},{3,27},{4,28},{5,29},{6,30},{7,31},{8,16},{9,... | collective-permute-start | bytes 1536008 | tf_op jit(solution)/shard_map/ppermute | solution.py:30
  52.3 24.9 %collective-permute-start.13 = (bf16[500,512]{1,0:T(8,128)(2,1)}, bf16[500,512]{1,0:T(8,128)(2,1)S(1)}, u32[]{:S(2)}, u32[]{:S(2)}) collective-permute-start(bf16[500,512]{1,0:T(8,128)(2,1)} %rest_0_), channel_id=1, source_target_pairs={{0,2},{1,3},{2,0},{3,1},{4,6},{5,7},{6,4},{7,5},{8,10},{9,11},{10,... | collective-permute-start | bytes 1536008 | tf_op jit(solution)/shard_map/ppermute | solution.py:30
  52.4 24.7 %collective-permute-start.14 = (bf16[500,512]{1,0:T(8,128)(2,1)S(1)}, bf16[500,512]{1,0:T(8,128)(2,1)S(1)}, u32[]{:S(2)}, u32[]{:S(2)}) collective-permute-start(bf16[500,512]{1,0:T(8,128)(2,1)S(1)} %copy-done.5), channel_id=1, source_target_pairs={{0,6},{1,7},{2,4},{3,5},{4,2},{5,3},{6,0},{7,1},{8,14},{9,15},{10,... | collective-permute-start | bytes 1536008 | tf_op jit(solution)/shard_map/ppermute | solution.py:30
  61.6 28.9 %collective-permute-start.16 = (bf16[512,1024]{1,0:T(8,128)(2,1)S(1)}, bf16[512,1024]{1,0:T(8,128)(2,1)S(1)}, u32[]{:S(2)}, u32[]{:S(2)}) collective-permute-start(bf16[512,1024]{1,0:T(8,128)(2,1)S(1)} %collective-permute-done.9.refs_0_.refs_2_), channel_id=1, source_target_pairs={{0,1},{1,0},{2,3},{3,2},{4,5},{5,4},{6,7},{7,6},{8,9},{9,8},{10,11... | collective-permute-start | bytes 3145736 | tf_op jit(solution)/shard_map/ppermute | solution.py:30
  77.2 43.7 %collective-permute-start.34 = (bf16[512,1024]{1,0:T(8,128)(2,1)}, bf16[512,1024]{1,0:T(8,128)(2,1)}, u32[]{:S(2)}, u32[]{:S(2)}) collective-permute-start(bf16[512,1024]{1,0:T(8,128)(2,1)} %convert_element_type.10.refs_0_), channel_id=1, source_target_pairs={{14,30},{15,31}} | collective-permute-start | bytes 3145736 | tf_op jit(solution)/shard_map/ppermute | solution.py:30
  90.5 5.5 %collective-permute-start.17 = (f32[8,640]{1,0:T(8,128)S(1)}, f32[8,640]{1,0:T(8,128)S(1)}, u32[]{:S(2)}, u32[]{:S(2)}) collective-permute-start(f32[8,640]{1,0:T(8,128)S(1)} %get-tuple-element.92), channel_id=1, source_target_pairs={{0,2},{1,3},{2,0},{3,1},{4,6},{5,7},{6,4},{7,5},{8,10},{9,11},{10,... | collective-permute-start | bytes 61448 | tf_op jit(solution)/shard_map/ppermute | solution.py:30
  93.5 4.7 %collective-permute-start.18 = (f32[8,640]{1,0:T(8,128)S(1)}, f32[8,640]{1,0:T(8,128)S(1)}, u32[]{:S(2)}, u32[]{:S(2)}) collective-permute-start(f32[8,640]{1,0:T(8,128)S(1)} %get-tuple-element.93), channel_id=1, source_target_pairs={{0,4},{1,5},{2,6},{3,7},{4,0},{5,1},{6,2},{7,3},{8,12},{9,13},{10,... | collective-permute-start | bytes 61448 | tf_op jit(solution)/shard_map/ppermute | solution.py:30
  93.5 5.6 %collective-permute-start.19 = (f32[8,640]{1,0:T(8,128)S(1)}, f32[8,640]{1,0:T(8,128)S(1)}, u32[]{:S(2)}, u32[]{:S(2)}) collective-permute-start(f32[8,640]{1,0:T(8,128)S(1)} %get-tuple-element.94), channel_id=1, source_target_pairs={{0,6},{1,7},{2,4},{3,5},{4,2},{5,3},{6,0},{7,1},{8,14},{9,15},{10,... | collective-permute-start | bytes 61448 | tf_op jit(solution)/shard_map/ppermute | solution.py:30
  99.1 3.8 %collective-permute-start.20 = (f32[8,640]{1,0:T(8,128)S(1)}, f32[8,640]{1,0:T(8,128)S(1)}, u32[]{:S(2)}, u32[]{:S(2)}) collective-permute-start(f32[8,640]{1,0:T(8,128)S(1)} %add_add_fusion.1), channel_id=1, source_target_pairs={{0,8},{1,9},{2,10},{3,11},{4,12},{5,13},{6,14},{7,15},{8,0},{9,1},... | collective-permute-start | bytes 61448 | tf_op jit(solution)/shard_map/ppermute | solution.py:30
  100.3 3.8 %collective-permute-start.21 = (f32[8,640]{1,0:T(8,128)S(1)}, f32[8,640]{1,0:T(8,128)S(1)}, u32[]{:S(2)}, u32[]{:S(2)}) collective-permute-start(f32[8,640]{1,0:T(8,128)S(1)} %add_add_fusion.1), channel_id=1, source_target_pairs={{0,16},{1,17},{2,18},{3,19},{4,20},{5,21},{6,22},{7,23},{8,24},{9,... | collective-permute-start | bytes 61448 | tf_op jit(solution)/shard_map/ppermute | solution.py:30
  101.3 4.7 %collective-permute-start.22 = (f32[8,640]{1,0:T(8,128)S(1)}, f32[8,640]{1,0:T(8,128)S(1)}, u32[]{:S(2)}, u32[]{:S(2)}) collective-permute-start(f32[8,640]{1,0:T(8,128)S(1)} %add_add_fusion.1), channel_id=1, source_target_pairs={{0,24},{1,25},{2,26},{3,27},{4,28},{5,29},{6,30},{7,31},{8,16},{9,... | collective-permute-start | bytes 61448 | tf_op jit(solution)/shard_map/ppermute | solution.py:30
  109.9 9.2 %collective-permute-start.27 = (f32[8,512]{1,0:T(8,128)S(1)}, f32[8,512]{1,0:T(8,128)S(1)}, u32[]{:S(2)}, u32[]{:S(2)}) collective-permute-start(f32[8,512]{1,0:T(8,128)S(1)} %apply_weights.2.refs_0_), channel_id=1, source_target_pairs={{0,6},{1,7}} | collective-permute-start | bytes 49160 | tf_op jit(solution)/shard_map/ppermute | solution.py:30
  120.9 12.5 %collective-permute-start.35 = (bf16[512,1024]{1,0:T(8,128)(2,1)}, bf16[512,1024]{1,0:T(8,128)(2,1)}, u32[]{:S(2)}, u32[]{:S(2)}) collective-permute-start(bf16[512,1024]{1,0:T(8,128)(2,1)} %collective-permute-done.34.refs_0_), channel_id=1, source_target_pairs={{0,1},{1,0},{2,3},{3,2},{4,5},{5,4},{6,7},{7,6},{8,9},{9,8},{10,11... | collective-permute-start | bytes 3145736 | tf_op jit(solution)/shard_map/ppermute | solution.py:30
  121.4 4.1 %collective-permute-start.28 = (f32[8,512]{1,0:T(8,128)S(1)}, f32[8,512]{1,0:T(8,128)S(1)}, u32[]{:S(2)}, u32[]{:S(2)}) collective-permute-start(f32[8,512]{1,0:T(8,128)S(1)} %turn.3.refs_1_), channel_id=1, source_target_pairs={{10,20},{11,21}} | collective-permute-start | bytes 49160 | tf_op jit(solution)/shard_map/ppermute | solution.py:30
  122.1 3.4 %collective-permute-start.29 = (f32[8,512]{1,0:T(8,128)S(1)}, f32[8,512]{1,0:T(8,128)S(1)}, u32[]{:S(2)}, u32[]{:S(2)}) collective-permute-start(f32[8,512]{1,0:T(8,128)S(1)} %turn.3.refs_1_), channel_id=1, source_target_pairs={{10,21},{11,20}} | collective-permute-start | bytes 49160 | tf_op jit(solution)/shard_map/ppermute | solution.py:30
  126.0 4.5 %collective-permute-start.37 = (f32[8,512]{1,0:T(8,128)S(1)}, f32[8,512]{1,0:T(8,128)S(1)}, u32[]{:S(2)}, u32[]{:S(2)}) collective-permute-start(f32[8,512]{1,0:T(8,128)S(1)} %apply_weights.3), channel_id=1, source_target_pairs={{6,30},{7,31}} | collective-permute-start | bytes 49160 | tf_op jit(solution)/shard_map/ppermute | solution.py:30
  129.1 4.2 %collective-permute-start.33 = (f32[16,512]{1,0:T(8,128)S(1)}, f32[16,512]{1,0:T(8,128)S(1)}, u32[]{:S(2)}, u32[]{:S(2)}) collective-permute-start(f32[16,512]{1,0:T(8,128)S(1)} %turn.4.refs_2_), channel_id=1, source_target_pairs={{20,30},{21,31}} | collective-permute-start | bytes 98312 | tf_op jit(solution)/shard_map/ppermute | solution.py:30
  129.8 3.5 %collective-permute-start.36 = (f32[16,512]{1,0:T(8,128)S(1)}, f32[16,512]{1,0:T(8,128)S(1)}, u32[]{:S(2)}, u32[]{:S(2)}) collective-permute-start(f32[16,512]{1,0:T(8,128)S(1)} %turn.4.refs_2_), channel_id=1, source_target_pairs={{20,31},{21,30}} | collective-permute-start | bytes 98312 | tf_op jit(solution)/shard_map/ppermute | solution.py:30
  141.6 8.0 %collective-permute-start.41 = (f32[2,512]{1,0:T(2,128)}, f32[2,512]{1,0:T(2,128)S(1)}, u32[]{:S(2)}, u32[]{:S(2)}) collective-permute-start(f32[2,512]{1,0:T(2,128)} %get-tuple-element.110), channel_id=1, source_target_pairs={{0,24},{1,25},{10,18},{11,19},{20,12},{21,13},{30,6},{31,7}} | collective-permute-start | bytes 12296 | tf_op jit(solution)/shard_map/ppermute | solution.py:30
  (24 other events, 174.8 us)

commit v13 on v12

--- a/solution.py
+++ b/solution.py
@@ -433,19 +433,11 @@
         )
     )
 
-    all_parts, first_side, entries, inverse_rows, left_rows = lax.optimization_barrier(
-        (all_parts, first_side, entries, inverse_rows, own_rows)
-    )
-    left_own, left_sib = {1: left_own}, {1: move(left_own, swap)}
-    for d in range(2, gen_count - 1):
-        left_own[d] = move(left_rows, lambda g, j, c: (j, j, c) if g >= 1 and j == g + d else None)
-
     own_raw = own_raw.reshape(orb_block * vec_total, pair_block)
     sib_raw = sib_raw.reshape(orb_block * vec_total, pair_block)
     where = jnp.stack([core] + [gen_index ^ k for k in range(gen_count)])
-    total = None
-    for group in [list(range(i, min(i + 4, gen_count))) for i in range(0, gen_count, 4)]:
-        shares = project(
+    def shares_of(group):
+        return project(
             where,
             own_raw,
             sib_raw,
@@ -454,12 +446,22 @@
             [second_side(k) for k in group],
             [k if part % 128 == 0 else 0 for k in group],
         )
-        if group[0] == 0:
-            shares, left_sib[1] = lax.optimization_barrier((shares, left_sib[1]))
-        for k, share in zip(group, shares):
-            if k:
-                share = move(share, across(k))
-            total = share if total is None else total + share
+
+    all_parts, entries, inverse_rows = lax.optimization_barrier((all_parts, entries, inverse_rows))
+    shares = []
+    for i in range(0, gen_count - 1, 3):
+        shares += shares_of(list(range(i, min(i + 3, gen_count - 1))))
+    shares, first_side, left_own, left_rows = lax.optimization_barrier(
+        (shares, first_side, left_own, own_rows)
+    )
+    left_own, left_sib = {1: left_own}, {1: move(left_own, swap)}
+    for d in range(2, gen_count - 1):
+        left_own[d] = move(left_rows, lambda g, j, c: (j, j, c) if g >= 1 and j == g + d else None)
+    shares += shares_of([gen_count - 1])
+    shares, left_sib[1] = lax.optimization_barrier((shares, left_sib[1]))
+    total = shares[0]
+    for k in others:
+        total += move(shares[k], across(k))
     total = sum([move(total, lambda g, j, c, k=k: (g ^ k, j, c)) for k in others], total)
 
     at_core = core[None]

time: 152 us -> 154 us (1.013)
  waiting for transfers between devices: 56.1 us -> 52.8 us
  Pallas kernels: 32.6 us -> 35.5 us
  starting transfers between devices: 39.8 us -> 42.4 us
    ppermute x42, waiting for transfers between devices: 56.1 us -> 52.8 us  [move(): return lax.ppermute(value, BOTH, pairs)]
    pallas_call x1 -> x2, Pallas kernels: 11.6 us -> 14.5 us  [project(): pl.pallas_call(kernel, grid_spec=pltpu.PrefetchScalarGridSpec(num_scalar_...]
    ppermute x42, starting transfers between devices: 39.8 us -> 42.4 us  [move(): return lax.ppermute(value, BOTH, pairs)]
  transfers between devices with their start and end apart: 42 -> 42, of which waited for: 18 -> 19; matrix products, arithmetic and copies ran while one was open for 12% -> 12% of each run, Pallas kernels for 18% -> 20%
where the time goes in v13:
time: 154 us; the launch traced here: 153 us
  waiting for transfers between devices  52.8 us (34%)
  starting transfers between devices  42.4 us (28%)
  Pallas kernels  35.5 us (23%)
  local copies, waits for them, and re-layouts  9.49 us (6%)
  matrix products  6.61 us (4%)
  other arithmetic  5.64 us (4%)
    ppermute x42, waiting for transfers between devices, move(): return lax.ppermute(value, BOTH, pairs)  52.8 us
    ppermute x42, starting transfers between devices, move(): return lax.ppermute(value, BOTH, pairs)  42.4 us
    pallas_call x2, Pallas kernels, project(): pl.pallas_call(kernel, grid_spec=pltpu.PrefetchScalarGridSpec(num_scalar_...  14.5 us
    pallas_call x3, Pallas kernels, turn(): pl.pallas_call(functools.partial(turn_kernel, count), in_specs=[pl.BlockS...  7.06 us
    pallas_call x1, Pallas kernels, invert_block(): pl.pallas_call(invert_kernel, grid_spec=pltpu.PrefetchScalarGridSpec(num_...  5.34 us
    dot_general x1, matrix products, on_device(): corner = jnp.dot(metric_factor[:, :points], upper, precision=HIGHEST)  4.71 us
  transfers between devices with their start and end apart: 42, of which 19 were waited for; matrix products, arithmetic and copies ran while one was open for 12% of the time, Pallas kernels for 20%

profile of v13, /device:TPU:24, one launch (start us, length us, event | category | flops | bytes accessed | tf_op | source)
XLA Modules:
  0.0 153.1 jit_solution(13510298569085444004)
XLA Ops:
  7.5 3.1 %collective-permute-done.1 = bf16[2,250,128]{2,1,0:T(8,128)(2,1)S(1)} collective-permute-done((bf16[2,250,128]{2,1,0:T(8,128)(2,1)S(1)}, bf16[2,250,128]{2,1,0:T(8,128)(2,1)S(1)}, u32[]{:S(2)}, u32[]{:S(2)}) %collective-permute-start.1) | collective-permute-done | bytes 128032 | tf_op jit(solution)/shard_map/ppermute | solution.py:30
  13.2 2.8 %collective-permute-done.4.rest_2_ = bf16[500,256]{1,0:T(8,128)(2,1)S(1)} collective-permute-done((bf16[500,256]{1,0:T(8,128)(2,1)S(1)}, bf16[500,256]{1,0:T(8,128)(2,1)S(1)}, u32[]{:S(2)}, u32[]{:S(2)}) %collective-permute-start.4) | collective-permute-done | bytes 256032 | tf_op jit(solution)/shard_map/ppermute | solution.py:30
  17.4 1.9 %dynamic-slice_bitcast_fusion = (bf16[2,250,128]{2,1,0:T(8,128)(2,1)}, bf16[2,250,128]{2,1,0:T(8,128)(2,1)}, bf16[2,250,128]{2,1,0:T(8,128)(2,1)}, bf16[2,250,128]{2,1,0:T(8,128)(2,1)S(1)}) fusion(bf16[4,2,250,128]{3,2,1,0:T(8,128)(2,1)} %pad_maximum_fusion.1, s32[]{:T(128)S(6)} %select_n.75, s32[]{:T(128)S(6)} %select_n.74, s32[]{:T(128)S(6)} %select_n.73, ...), kind=kLoop, calls=%fused_computation.11 | loop fusion | bytes 1024016 | tf_op jit(solution)/shard_map/jit(dynamic_index_in_dim)/squeeze | solution.py:394
  19.3 2.6 %collective-permute-start.6 = (bf16[2,250,128]{2,1,0:T(8,128)(2,1)}, bf16[2,250,128]{2,1,0:T(8,128)(2,1)}, u32[]{:S(2)}, u32[]{:S(2)}) collective-permute-start(bf16[2,250,128]{2,1,0:T(8,128)(2,1)} %get-tuple-element.112), channel_id=1, source_target_pairs={{0,4},{1,5},{2,6},{3,7},{4,0},{5,1},{6,2},{7,3},{8,12},{9,13},{10,... | collective-permute-start | bytes 384008 | tf_op jit(solution)/shard_map/ppermute | solution.py:30
  21.9 1.8 %collective-permute-start.7 = (bf16[2,250,128]{2,1,0:T(8,128)(2,1)}, bf16[2,250,128]{2,1,0:T(8,128)(2,1)}, u32[]{:S(2)}, u32[]{:S(2)}) collective-permute-start(bf16[2,250,128]{2,1,0:T(8,128)(2,1)} %get-tuple-element.111), channel_id=1, source_target_pairs={{0,6},{1,7},{2,4},{3,5},{4,2},{5,3},{6,0},{7,1},{8,14},{9,15},{10,... | collective-permute-start | bytes 384008 | tf_op jit(solution)/shard_map/ppermute | solution.py:30
  23.7 1.7 %slice.13 = bf16[500,256]{1,0:T(8,128)(2,1)} slice(bf16[500,512]{1,0:T(8,128)(2,1)} %rest_0_.1), slice={[0:500], [256:512]} | slice | bytes 512000 | tf_op jit(solution)/shard_map/slice | solution.py:390
  25.4 1.7 %collective-permute-start.8 = (bf16[500,256]{1,0:T(8,128)(2,1)}, bf16[500,256]{1,0:T(8,128)(2,1)}, u32[]{:S(2)}, u32[]{:S(2)}) collective-permute-start(bf16[500,256]{1,0:T(8,128)(2,1)} %slice.13), channel_id=1, source_target_pairs={{0,4},{1,5},{2,6},{3,7},{4,0},{5,1},{6,2},{7,3},{8,12},{9,13},{10,... | collective-permute-start | bytes 768008 | tf_op jit(solution)/shard_map/ppermute | solution.py:30
  27.0 5.3 %invert_block.1 = f32[512,512]{1,0:T(8,128)S(1)} custom-call(s32[2]{0:T(128)S(1)} %pad_add_fusion.where_ref, f32[512,1024]{1,0:T(8,128)S(1)} %copy-done.2), custom_call_target="tpu_custom_call" | custom-call | flops 4294967296 | bytes 4194304 | tf_op jit(solution)/shard_map/invert_block/pallas_call | solution.py:230
  33.4 2.8 %pivot_entries.1.entries_ref = f32[8,8]{1,0:T(8,128)} custom-call(s32[8]{0:T(128)} %get-tuple-element.120.row_ref, bf16[500,8,250]{2,1,0:T(8,128)(2,1)} %bitcast.33, bf16[500,8,250]{2,1,0:T(8,128)(2,1)} %bitcast.12.sib_ref, s32[8]{0:T(128)} %get-tuple-element.121.own_col_ref, s32[8]{0:T(128)} %get-tuple-element.119.sib_col_ref), custom_call_target="tpu_custom_call" | custom-call | tf_op jit(solution)/shard_map/pivot_entries/pallas_call | solution.py:63
  36.2 1.9 %collective-permute-done.6 = bf16[2,250,128]{2,1,0:T(8,128)(2,1)} collective-permute-done((bf16[2,250,128]{2,1,0:T(8,128)(2,1)}, bf16[2,250,128]{2,1,0:T(8,128)(2,1)}, u32[]{:S(2)}, u32[]{:S(2)}) %collective-permute-start.6) | collective-permute-done | bytes 128032 | tf_op jit(solution)/shard_map/ppermute | solution.py:30
  38.0 7.5 %collective-permute-done.8.rest_3_ = bf16[500,256]{1,0:T(8,128)(2,1)} collective-permute-done((bf16[500,256]{1,0:T(8,128)(2,1)}, bf16[500,256]{1,0:T(8,128)(2,1)}, u32[]{:S(2)}, u32[]{:S(2)}) %collective-permute-start.8) | collective-permute-done | bytes 256032 | tf_op jit(solution)/shard_map/ppermute | solution.py:30
  48.3 2.6 %collective-permute-start.11 = (bf16[4,2,250,128]{3,2,1,0:T(8,128)(2,1)S(1)}, bf16[4,2,250,128]{3,2,1,0:T(8,128)(2,1)S(1)}, u32[]{:S(2)}, u32[]{:S(2)}) collective-permute-start(bf16[4,2,250,128]{3,2,1,0:T(8,128)(2,1)S(1)} %pad_maximum_fusion.2.rest_4_.rest_8_.rest_12_.rest_1_), channel_id=1, source_target_pairs={{0,16},{1,17},{2,18},{3,19},{4,20},{5,21},{6,22},{7,23},{8,24},{9,... | collective-permute-start | bytes 1536008 | tf_op jit(solution)/shard_map/ppermute | solution.py:30
  53.9 4.7 %fusion.2 = f32[512,512]{1,0:T(8,128)S(1)} fusion(f32[512,512]{1,0:T(8,128)} %collective-permute-done.13, f32[512,1024]{1,0:T(8,128)S(1)} %copy-done.2), kind=kOutput, calls=%fused_computation.6 | convolution fusion | flops 1610612736 | bytes 3145728 | tf_op jit(solution)/shard_map/dot_general | solution.py:424
  58.6 1.9 %fusion.1 = f32[512,512]{1,0:T(8,128)S(1)} fusion(f32[512,512]{1,0:T(8,128)S(1)} %copy-done.4, f32[512,512]{1,0:T(8,128)S(1)} %fusion.2, pred[]{:T(512)S(6)} %eq.13), kind=kOutput, calls=%fused_computation.5 | convolution fusion | flops 1611137024 | bytes 3145729 | tf_op jit(solution)/shard_map/dot_general | solution.py:425
  61.6 12.4 %collective-permute-done.11.rest_6_.rest_10_.rest_14_.rest_3_ = bf16[4,2,250,128]{3,2,1,0:T(8,128)(2,1)S(1)} collective-permute-done((bf16[4,2,250,128]{3,2,1,0:T(8,128)(2,1)S(1)}, bf16[4,2,250,128]{3,2,1,0:T(8,128)(2,1)S(1)}, u32[]{:S(2)}, u32[]{:S(2)}) %collective-permute-start.11) | collective-permute-done | bytes 512032 | tf_op jit(solution)/shard_map/ppermute | solution.py:30
  74.0 1.8 %collective-permute-done.12.rest_7_.rest_11_.rest_15_.rest_4_ = bf16[4,2,250,128]{3,2,1,0:T(8,128)(2,1)S(1)} collective-permute-done((bf16[4,2,250,128]{3,2,1,0:T(8,128)(2,1)S(1)}, bf16[4,2,250,128]{3,2,1,0:T(8,128)(2,1)S(1)}, u32[]{:S(2)}, u32[]{:S(2)}) %collective-permute-start.12) | collective-permute-done | bytes 512032 | tf_op jit(solution)/shard_map/ppermute | solution.py:30
  77.2 9.5 %project.2 = (f32[8,640]{1,0:T(8,128)S(1)}, f32[8,640]{1,0:T(8,128)S(1)}, f32[8,640]{1,0:T(8,128)S(1)}) custom-call(s32[5]{0:T(128)S(1)} %stack.72.where_ref, bf16[4000,250]{1,0:T(8,128)(2,1)S(1)} %bitcast.34, bf16[4000,250]{1,0:T(8,128)(2,1)} %bitcast.13.sib_ref, f32[8,8]{1,0:T(8,128)S(1)} %copy-done.12, bf16[500,512]{1,0:T(8,128)(2,1)S(1)} %copy-done.5, ...), custom_call_target="tpu_custom_call" | custom-call | flops 6144000000 | bytes 1048576 | tf_op jit(solution)/shard_map/project/pallas_call | solution.py:170
  86.8 1.6 %collective-permute-start.34 = (bf16[512,1024]{1,0:T(8,128)(2,1)}, bf16[512,1024]{1,0:T(8,128)(2,1)}, u32[]{:S(2)}, u32[]{:S(2)}) collective-permute-start(bf16[512,1024]{1,0:T(8,128)(2,1)} %convert_element_type.10.refs_0_), channel_id=1, source_target_pairs={{14,30},{15,31}} | collective-permute-start | bytes 3145736 | tf_op jit(solution)/shard_map/ppermute | solution.py:30
  88.4 5.0 %project.3 = f32[8,640]{1,0:T(8,128)S(1)} custom-call(s32[5]{0:T(128)S(1)} %stack.72.where_ref, bf16[4000,250]{1,0:T(8,128)(2,1)S(1)} %bitcast.35, bf16[4000,250]{1,0:T(8,128)(2,1)} %bitcast.13.sib_ref, f32[8,8]{1,0:T(8,128)S(1)} %copy-done.12, bf16[500,512]{1,0:T(8,128)(2,1)S(1)} %collective-permute-done.15.rest_0_, ...), custom_call_target="tpu_custom_call" | custom-call | flops 2048000000 | bytes 1048576 | tf_op jit(solution)/shard_map/project/pallas_call | solution.py:170
  94.2 3.7 %collective-permute-start.19 = (f32[8,640]{1,0:T(8,128)S(1)}, f32[8,640]{1,0:T(8,128)S(1)}, u32[]{:S(2)}, u32[]{:S(2)}) collective-permute-start(f32[8,640]{1,0:T(8,128)S(1)} %project.3), channel_id=1, source_target_pairs={{0,6},{1,7},{2,4},{3,5},{4,2},{5,3},{6,0},{7,1},{8,14},{9,15},{10,... | collective-permute-start | bytes 61448 | tf_op jit(solution)/shard_map/ppermute | solution.py:30
  98.3 1.6 %collective-permute-done.19 = f32[8,640]{1,0:T(8,128)S(1)} collective-permute-done((f32[8,640]{1,0:T(8,128)S(1)}, f32[8,640]{1,0:T(8,128)S(1)}, u32[]{:S(2)}, u32[]{:S(2)}) %collective-permute-start.19) | collective-permute-done | bytes 20512 | tf_op jit(solution)/shard_map/ppermute | solution.py:30
  99.9 3.4 %collective-permute-start.20 = (f32[8,640]{1,0:T(8,128)S(1)}, f32[8,640]{1,0:T(8,128)S(1)}, u32[]{:S(2)}, u32[]{:S(2)}) collective-permute-start(f32[8,640]{1,0:T(8,128)S(1)} %add_add_fusion.1), channel_id=1, source_target_pairs={{0,8},{1,9},{2,10},{3,11},{4,12},{5,13},{6,14},{7,15},{8,0},{9,1},... | collective-permute-start | bytes 61448 | tf_op jit(solution)/shard_map/ppermute | solution.py:30
  105.0 2.0 %collective-permute-done.21 = f32[8,640]{1,0:T(8,128)S(1)} collective-permute-done((f32[8,640]{1,0:T(8,128)S(1)}, f32[8,640]{1,0:T(8,128)S(1)}, u32[]{:S(2)}, u32[]{:S(2)}) %collective-permute-start.21) | collective-permute-done | bytes 20512 | tf_op jit(solution)/shard_map/ppermute | solution.py:30
  113.2 7.2 %collective-permute-done.27 = f32[8,512]{1,0:T(8,128)S(1)} collective-permute-done((f32[8,512]{1,0:T(8,128)S(1)}, f32[8,512]{1,0:T(8,128)S(1)}, u32[]{:S(2)}, u32[]{:S(2)}) %collective-permute-start.27) | collective-permute-done | bytes 16416 | tf_op jit(solution)/shard_map/ppermute | solution.py:30
  120.4 1.8 %turn.3.refs_1_ = f32[8,512]{1,0:T(8,128)S(1)} custom-call(s32[1]{0:T(128)} %bitcast.5.where_ref, bf16[512,1024]{1,0:T(8,128)(2,1)S(1)} %collective-permute-done.9.refs_0_.refs_2_, bf16[512,1024]{1,0:T(8,128)(2,1)S(1)} %collective-permute-done.16.refs_1_.refs_3_, bf16[512,1024]{1,0:T(8,128)(2,1)S(1)} %get-tuple-element.87.refs_0_.refs_2_.refs_4_, ...), custom_call_target="tpu_custom_call" | custom-call | flops 1048576 | bytes 65536 | tf_op jit(solution)/shard_map/turn/pallas_call | solution.py:319
  124.6 1.6 %apply_weights.3 = f32[8,512]{1,0:T(8,128)S(1)} custom-call(s32[1]{0:T(128)} %bitcast.5.where_ref, bf16[512,1024]{1,0:T(8,128)(2,1)} %convert_element_type.10.refs_0_, f32[8,512]{1,0:T(8,128)S(1)} %add.85.refs_1_, f32[8,512]{1,0:T(8,128)S(1)} %collective-permute-done.30.refs_2_), custom_call_target="tpu_custom_call" | custom-call | flops 1073741824 | bytes 2097152 | tf_op jit(solution)/shard_map/apply_weights/pallas_call | solution.py:274
  127.4 3.2 %collective-permute-start.37 = (f32[8,512]{1,0:T(8,128)S(1)}, f32[8,512]{1,0:T(8,128)S(1)}, u32[]{:S(2)}, u32[]{:S(2)}) collective-permute-start(f32[8,512]{1,0:T(8,128)S(1)} %apply_weights.3), channel_id=1, source_target_pairs={{6,30},{7,31}} | collective-permute-start | bytes 49160 | tf_op jit(solution)/shard_map/ppermute | solution.py:30
  130.5 1.8 %turn.4.refs_2_ = f32[16,512]{1,0:T(8,128)S(1)} custom-call(s32[1]{0:T(128)} %bitcast.5.where_ref, bf16[512,1024]{1,0:T(8,128)(2,1)S(1)} %collective-permute-done.9.refs_0_.refs_2_, bf16[512,1024]{1,0:T(8,128)(2,1)S(1)} %collective-permute-done.16.refs_1_.refs_3_, bf16[512,1024]{1,0:T(8,128)(2,1)S(1)} %get-tuple-element.87.refs_0_.refs_2_.refs_4_, ...), custom_call_target="tpu_custom_call" | custom-call | flops 1048576 | bytes 65536 | tf_op jit(solution)/shard_map/turn/pallas_call | solution.py:319
  134.5 2.0 %factor_inverse.1.inverse_ref = f32[8,8]{1,0:T(8,128)} custom-call(f32[8,640]{1,0:T(8,128)} %copy-done.7), custom_call_target="tpu_custom_call" | custom-call | tf_op jit(solution)/shard_map/factor_inverse/pallas_call | solution.py:98
  137.7 3.5 %turn.5.refs_3_ = f32[24,512]{1,0:T(8,128)S(1)} custom-call(s32[1]{0:T(128)} %bitcast.5.where_ref, bf16[512,1024]{1,0:T(8,128)(2,1)} %collective-permute-done.34.refs_0_, bf16[512,1024]{1,0:T(8,128)(2,1)} %collective-permute-done.35.refs_1_, bf16[512,1024]{1,0:T(8,128)(2,1)S(1)} %collective-permute-done.9.refs_0_.refs_2_, bf16[512,1024]{1,0:T(8,128)(2,1)S(1)} %copy-done.1, ...), custom_call_target="tpu_custom_call" | custom-call | flops 1048576 | bytes 65536 | tf_op jit(solution)/shard_map/turn/pallas_call | solution.py:319
  141.9 1.6 %combine.1 = (f32[2,512]{1,0:T(2,128)}, f32[2,512]{1,0:T(2,128)}, f32[2,512]{1,0:T(2,128)}, f32[2,512]{1,0:T(2,128)}) custom-call(s32[5]{0:T(128)} %stack.71.turn_ref, f32[8,8]{1,0:T(8,128)} %factor_inverse.1.inverse_ref, f32[8,512]{1,0:T(8,128)} %copy-done.11, f32[8,512]{1,0:T(8,128)} %copy-done.10, f32[16,512]{1,0:T(8,128)} %copy-done.9, f32[24,512]{1,0:T(8,128)} %copy-done.8), custom_call_target="tpu_custom_call" | custom-call | tf_op jit(solution)/shard_map/combine/pallas_call | solution.py:353
  146.1 5.7 %collective-permute-done.41 = f32[2,512]{1,0:T(2,128)S(1)} collective-permute-done((f32[2,512]{1,0:T(2,128)}, f32[2,512]{1,0:T(2,128)S(1)}, u32[]{:S(2)}, u32[]{:S(2)}) %collective-permute-start.41) | collective-permute-done | bytes 4128 | tf_op jit(solution)/shard_map/ppermute | solution.py:30
  (113 shorter events, 41.0 us)
Async XLA Ops:
  0.0 16.0 %collective-permute-start.3 = (bf16[8,500,250]{2,0,1:T(8,128)(2,1)}, bf16[8,500,250]{2,0,1:T(8,128)(2,1)}, u32[]{:S(2)}, u32[]{:S(2)}) collective-permute-start(bf16[8,500,250]{2,0,1:T(8,128)(2,1)} %param.4), channel_id=1, source_target_pairs={{0,1},{1,0},{2,3},{3,2},{4,5},{5,4},{6,7},{7,6},{8,9},{9,8},{10,11... | collective-permute-start | bytes 6000008 | tf_op jit(solution)/shard_map/ppermute | solution.py:30
  1.1 14.9 %collective-permute-start.4 = (bf16[500,256]{1,0:T(8,128)(2,1)S(1)}, bf16[500,256]{1,0:T(8,128)(2,1)S(1)}, u32[]{:S(2)}, u32[]{:S(2)}) collective-permute-start(bf16[500,256]{1,0:T(8,128)(2,1)S(1)} %slice.12), channel_id=1, source_target_pairs={{0,4},{1,5},{2,6},{3,7},{4,0},{5,1},{6,2},{7,3},{8,12},{9,13},{10,... | collective-permute-start | bytes 768008 | tf_op jit(solution)/shard_map/ppermute | solution.py:30
  2.8 7.8 %collective-permute-start.1 = (bf16[2,250,128]{2,1,0:T(8,128)(2,1)S(1)}, bf16[2,250,128]{2,1,0:T(8,128)(2,1)S(1)}, u32[]{:S(2)}, u32[]{:S(2)}) collective-permute-start(bf16[2,250,128]{2,1,0:T(8,128)(2,1)S(1)} %get-tuple-element.117), channel_id=1, source_target_pairs={{0,16},{1,17},{2,18},{3,19},{4,20},{5,21},{6,22},{7,23},{8,24},{9,... | collective-permute-start | bytes 384008 | tf_op jit(solution)/shard_map/ppermute | solution.py:30
  4.4 7.3 %collective-permute-start.2 = (bf16[2,250,128]{2,1,0:T(8,128)(2,1)S(1)}, bf16[2,250,128]{2,1,0:T(8,128)(2,1)S(1)}, u32[]{:S(2)}, u32[]{:S(2)}) collective-permute-start(bf16[2,250,128]{2,1,0:T(8,128)(2,1)S(1)} %get-tuple-element.116), channel_id=1, source_target_pairs={{0,24},{1,25},{2,26},{3,27},{4,28},{5,29},{6,30},{7,31},{8,16},{9,... | collective-permute-start | bytes 384008 | tf_op jit(solution)/shard_map/ppermute | solution.py:30
  5.8 6.5 %collective-permute-start = (bf16[2,250,128]{2,1,0:T(8,128)(2,1)S(1)}, bf16[2,250,128]{2,1,0:T(8,128)(2,1)S(1)}, u32[]{:S(2)}, u32[]{:S(2)}) collective-permute-start(bf16[2,250,128]{2,1,0:T(8,128)(2,1)S(1)} %get-tuple-element.118), channel_id=1, source_target_pairs={{0,8},{1,9},{2,10},{3,11},{4,12},{5,13},{6,14},{7,15},{8,0},{9,1},... | collective-permute-start | bytes 384008 | tf_op jit(solution)/shard_map/ppermute | solution.py:30
  16.0 29.5 %collective-permute-start.9 = (bf16[512,1024]{1,0:T(8,128)(2,1)}, bf16[512,1024]{1,0:T(8,128)(2,1)S(1)}, u32[]{:S(2)}, u32[]{:S(2)}) collective-permute-start(bf16[512,1024]{1,0:T(8,128)(2,1)} %convert_element_type.10.refs_0_), channel_id=1, source_target_pairs={{2,10},{3,11},{12,20},{13,21},{22,30},{23,31}} | collective-permute-start | bytes 3145736 | tf_op jit(solution)/shard_map/ppermute | solution.py:30
  19.3 16.9 %collective-permute-start.5 = (bf16[2,250,128]{2,1,0:T(8,128)(2,1)}, bf16[2,250,128]{2,1,0:T(8,128)(2,1)}, u32[]{:S(2)}, u32[]{:S(2)}) collective-permute-start(bf16[2,250,128]{2,1,0:T(8,128)(2,1)} %get-tuple-element.113), channel_id=1, source_target_pairs={{0,2},{1,3},{2,0},{3,1},{4,6},{5,7},{6,4},{7,5},{8,10},{9,11},{10,... | collective-permute-start | bytes 384008 | tf_op jit(solution)/shard_map/ppermute | solution.py:30
  19.3 18.7 %collective-permute-start.6 = (bf16[2,250,128]{2,1,0:T(8,128)(2,1)}, bf16[2,250,128]{2,1,0:T(8,128)(2,1)}, u32[]{:S(2)}, u32[]{:S(2)}) collective-permute-start(bf16[2,250,128]{2,1,0:T(8,128)(2,1)} %get-tuple-element.112), channel_id=1, source_target_pairs={{0,4},{1,5},{2,6},{3,7},{4,0},{5,1},{6,2},{7,3},{8,12},{9,13},{10,... | collective-permute-start | bytes 384008 | tf_op jit(solution)/shard_map/ppermute | solution.py:30
  21.9 16.1 %collective-permute-start.7 = (bf16[2,250,128]{2,1,0:T(8,128)(2,1)}, bf16[2,250,128]{2,1,0:T(8,128)(2,1)}, u32[]{:S(2)}, u32[]{:S(2)}) collective-permute-start(bf16[2,250,128]{2,1,0:T(8,128)(2,1)} %get-tuple-element.111), channel_id=1, source_target_pairs={{0,6},{1,7},{2,4},{3,5},{4,2},{5,3},{6,0},{7,1},{8,14},{9,15},{10,... | collective-permute-start | bytes 384008 | tf_op jit(solution)/shard_map/ppermute | solution.py:30
  25.4 20.2 %collective-permute-start.8 = (bf16[500,256]{1,0:T(8,128)(2,1)}, bf16[500,256]{1,0:T(8,128)(2,1)}, u32[]{:S(2)}, u32[]{:S(2)}) collective-permute-start(bf16[500,256]{1,0:T(8,128)(2,1)} %slice.13), channel_id=1, source_target_pairs={{0,4},{1,5},{2,6},{3,7},{4,0},{5,1},{6,2},{7,3},{8,12},{9,13},{10,... | collective-permute-start | bytes 768008 | tf_op jit(solution)/shard_map/ppermute | solution.py:30
  45.5 6.9 %collective-permute-start.13 = (f32[512,512]{1,0:T(8,128)}, f32[512,512]{1,0:T(8,128)}, u32[]{:S(2)}, u32[]{:S(2)}) collective-permute-start(f32[512,512]{1,0:T(8,128)} %copy-done.3), channel_id=1, source_target_pairs={{0,1},{1,0},{2,3},{3,2},{4,5},{5,4},{6,7},{7,6},{8,9},{9,8},{10,11... | collective-permute-start | bytes 3145736 | tf_op jit(solution)/shard_map/ppermute | solution.py:30
  46.8 14.8 %collective-permute-start.10 = (bf16[4,2,250,128]{3,2,1,0:T(8,128)(2,1)S(1)}, bf16[4,2,250,128]{3,2,1,0:T(8,128)(2,1)S(1)}, u32[]{:S(2)}, u32[]{:S(2)}) collective-permute-start(bf16[4,2,250,128]{3,2,1,0:T(8,128)(2,1)S(1)} %pad_maximum_fusion.2.rest_4_.rest_8_.rest_12_.rest_1_), channel_id=1, source_target_pairs={{0,8},{1,9},{2,10},{3,11},{4,12},{5,13},{6,14},{7,15},{8,0},{9,1},... | collective-permute-start | bytes 1536008 | tf_op jit(solution)/shard_map/ppermute | solution.py:30
  48.3 25.6 %collective-permute-start.11 = (bf16[4,2,250,128]{3,2,1,0:T(8,128)(2,1)S(1)}, bf16[4,2,250,128]{3,2,1,0:T(8,128)(2,1)S(1)}, u32[]{:S(2)}, u32[]{:S(2)}) collective-permute-start(bf16[4,2,250,128]{3,2,1,0:T(8,128)(2,1)S(1)} %pad_maximum_fusion.2.rest_4_.rest_8_.rest_12_.rest_1_), channel_id=1, source_target_pairs={{0,16},{1,17},{2,18},{3,19},{4,20},{5,21},{6,22},{7,23},{8,24},{9,... | collective-permute-start | bytes 1536008 | tf_op jit(solution)/shard_map/ppermute | solution.py:30
  50.9 24.9 %collective-permute-start.12 = (bf16[4,2,250,128]{3,2,1,0:T(8,128)(2,1)S(1)}, bf16[4,2,250,128]{3,2,1,0:T(8,128)(2,1)S(1)}, u32[]{:S(2)}, u32[]{:S(2)}) collective-permute-start(bf16[4,2,250,128]{3,2,1,0:T(8,128)(2,1)S(1)} %pad_maximum_fusion.2.rest_4_.rest_8_.rest_12_.rest_1_), channel_id=1, source_target_pairs={{0,24},{1,25},{2,26},{3,27},{4,28},{5,29},{6,30},{7,31},{8,16},{9,... | collective-permute-start | bytes 1536008 | tf_op jit(solution)/shard_map/ppermute | solution.py:30
  52.3 24.9 %collective-permute-start.14 = (bf16[500,512]{1,0:T(8,128)(2,1)}, bf16[500,512]{1,0:T(8,128)(2,1)S(1)}, u32[]{:S(2)}, u32[]{:S(2)}) collective-permute-start(bf16[500,512]{1,0:T(8,128)(2,1)} %rest_0_.1), channel_id=1, source_target_pairs={{0,2},{1,3},{2,0},{3,1},{4,6},{5,7},{6,4},{7,5},{8,10},{9,11},{10,... | collective-permute-start | bytes 1536008 | tf_op jit(solution)/shard_map/ppermute | solution.py:30
  52.4 34.3 %collective-permute-start.15 = (bf16[500,512]{1,0:T(8,128)(2,1)S(1)}, bf16[500,512]{1,0:T(8,128)(2,1)S(1)}, u32[]{:S(2)}, u32[]{:S(2)}) collective-permute-start(bf16[500,512]{1,0:T(8,128)(2,1)S(1)} %copy-done.5), channel_id=1, source_target_pairs={{0,6},{1,7},{2,4},{3,5},{4,2},{5,3},{6,0},{7,1},{8,14},{9,15},{10,... | collective-permute-start | bytes 1536008 | tf_op jit(solution)/shard_map/ppermute | solution.py:30
  86.7 6.7 %collective-permute-start.16 = (bf16[512,1024]{1,0:T(8,128)(2,1)S(1)}, bf16[512,1024]{1,0:T(8,128)(2,1)S(1)}, u32[]{:S(2)}, u32[]{:S(2)}) collective-permute-start(bf16[512,1024]{1,0:T(8,128)(2,1)S(1)} %collective-permute-done.9.refs_0_.refs_2_), channel_id=1, source_target_pairs={{0,1},{1,0},{2,3},{3,2},{4,5},{5,4},{6,7},{7,6},{8,9},{9,8},{10,11... | collective-permute-start | bytes 3145736 | tf_op jit(solution)/shard_map/ppermute | solution.py:30
  86.8 35.4 %collective-permute-start.34 = (bf16[512,1024]{1,0:T(8,128)(2,1)}, bf16[512,1024]{1,0:T(8,128)(2,1)}, u32[]{:S(2)}, u32[]{:S(2)}) collective-permute-start(bf16[512,1024]{1,0:T(8,128)(2,1)} %convert_element_type.10.refs_0_), channel_id=1, source_target_pairs={{14,30},{15,31}} | collective-permute-start | bytes 3145736 | tf_op jit(solution)/shard_map/ppermute | solution.py:30
  93.4 4.5 %collective-permute-start.17 = (f32[8,640]{1,0:T(8,128)S(1)}, f32[8,640]{1,0:T(8,128)S(1)}, u32[]{:S(2)}, u32[]{:S(2)}) collective-permute-start(f32[8,640]{1,0:T(8,128)S(1)} %get-tuple-element.90), channel_id=1, source_target_pairs={{0,2},{1,3},{2,0},{3,1},{4,6},{5,7},{6,4},{7,5},{8,10},{9,11},{10,... | collective-permute-start | bytes 61448 | tf_op jit(solution)/shard_map/ppermute | solution.py:30
  93.5 4.7 %collective-permute-start.18 = (f32[8,640]{1,0:T(8,128)S(1)}, f32[8,640]{1,0:T(8,128)S(1)}, u32[]{:S(2)}, u32[]{:S(2)}) collective-permute-start(f32[8,640]{1,0:T(8,128)S(1)} %get-tuple-element.91), channel_id=1, source_target_pairs={{0,4},{1,5},{2,6},{3,7},{4,0},{5,1},{6,2},{7,3},{8,12},{9,13},{10,... | collective-permute-start | bytes 61448 | tf_op jit(solution)/shard_map/ppermute | solution.py:30
  94.2 5.7 %collective-permute-start.19 = (f32[8,640]{1,0:T(8,128)S(1)}, f32[8,640]{1,0:T(8,128)S(1)}, u32[]{:S(2)}, u32[]{:S(2)}) collective-permute-start(f32[8,640]{1,0:T(8,128)S(1)} %project.3), channel_id=1, source_target_pairs={{0,6},{1,7},{2,4},{3,5},{4,2},{5,3},{6,0},{7,1},{8,14},{9,15},{10,... | collective-permute-start | bytes 61448 | tf_op jit(solution)/shard_map/ppermute | solution.py:30
  99.9 5.2 %collective-permute-start.20 = (f32[8,640]{1,0:T(8,128)S(1)}, f32[8,640]{1,0:T(8,128)S(1)}, u32[]{:S(2)}, u32[]{:S(2)}) collective-permute-start(f32[8,640]{1,0:T(8,128)S(1)} %add_add_fusion.1), channel_id=1, source_target_pairs={{0,8},{1,9},{2,10},{3,11},{4,12},{5,13},{6,14},{7,15},{8,0},{9,1},... | collective-permute-start | bytes 61448 | tf_op jit(solution)/shard_map/ppermute | solution.py:30
  103.3 3.8 %collective-permute-start.21 = (f32[8,640]{1,0:T(8,128)S(1)}, f32[8,640]{1,0:T(8,128)S(1)}, u32[]{:S(2)}, u32[]{:S(2)}) collective-permute-start(f32[8,640]{1,0:T(8,128)S(1)} %add_add_fusion.1), channel_id=1, source_target_pairs={{0,16},{1,17},{2,18},{3,19},{4,20},{5,21},{6,22},{7,23},{8,24},{9,... | collective-permute-start | bytes 61448 | tf_op jit(solution)/shard_map/ppermute | solution.py:30
  103.3 4.7 %collective-permute-start.22 = (f32[8,640]{1,0:T(8,128)S(1)}, f32[8,640]{1,0:T(8,128)S(1)}, u32[]{:S(2)}, u32[]{:S(2)}) collective-permute-start(f32[8,640]{1,0:T(8,128)S(1)} %add_add_fusion.1), channel_id=1, source_target_pairs={{0,24},{1,25},{2,26},{3,27},{4,28},{5,29},{6,30},{7,31},{8,16},{9,... | collective-permute-start | bytes 61448 | tf_op jit(solution)/shard_map/ppermute | solution.py:30
  111.9 8.5 %collective-permute-start.27 = (f32[8,512]{1,0:T(8,128)S(1)}, f32[8,512]{1,0:T(8,128)S(1)}, u32[]{:S(2)}, u32[]{:S(2)}) collective-permute-start(f32[8,512]{1,0:T(8,128)S(1)} %apply_weights.2.refs_0_), channel_id=1, source_target_pairs={{0,6},{1,7}} | collective-permute-start | bytes 49160 | tf_op jit(solution)/shard_map/ppermute | solution.py:30
  122.2 14.3 %collective-permute-start.35 = (bf16[512,1024]{1,0:T(8,128)(2,1)}, bf16[512,1024]{1,0:T(8,128)(2,1)}, u32[]{:S(2)}, u32[]{:S(2)}) collective-permute-start(bf16[512,1024]{1,0:T(8,128)(2,1)} %collective-permute-done.34.refs_0_), channel_id=1, source_target_pairs={{0,1},{1,0},{2,3},{3,2},{4,5},{5,4},{6,7},{7,6},{8,9},{9,8},{10,11... | collective-permute-start | bytes 3145736 | tf_op jit(solution)/shard_map/ppermute | solution.py:30
  122.8 4.1 %collective-permute-start.28 = (f32[8,512]{1,0:T(8,128)S(1)}, f32[8,512]{1,0:T(8,128)S(1)}, u32[]{:S(2)}, u32[]{:S(2)}) collective-permute-start(f32[8,512]{1,0:T(8,128)S(1)} %turn.3.refs_1_), channel_id=1, source_target_pairs={{10,20},{11,21}} | collective-permute-start | bytes 49160 | tf_op jit(solution)/shard_map/ppermute | solution.py:30
  126.9 3.6 %collective-permute-start.32 = (f32[8,512]{1,0:T(8,128)S(1)}, f32[8,512]{1,0:T(8,128)S(1)}, u32[]{:S(2)}, u32[]{:S(2)}) collective-permute-start(f32[8,512]{1,0:T(8,128)S(1)} %slice_subtract_fusion.refs_6_), channel_id=1, source_target_pairs={{0,1},{1,0},{2,3},{3,2},{4,5},{5,4},{6,7},{7,6},{8,9},{9,8},{10,11... | collective-permute-start | bytes 49160 | tf_op jit(solution)/shard_map/ppermute | solution.py:30
  127.4 6.3 %collective-permute-start.37 = (f32[8,512]{1,0:T(8,128)S(1)}, f32[8,512]{1,0:T(8,128)S(1)}, u32[]{:S(2)}, u32[]{:S(2)}) collective-permute-start(f32[8,512]{1,0:T(8,128)S(1)} %apply_weights.3), channel_id=1, source_target_pairs={{6,30},{7,31}} | collective-permute-start | bytes 49160 | tf_op jit(solution)/shard_map/ppermute | solution.py:30
  132.3 4.1 %collective-permute-start.33 = (f32[16,512]{1,0:T(8,128)S(1)}, f32[16,512]{1,0:T(8,128)S(1)}, u32[]{:S(2)}, u32[]{:S(2)}) collective-permute-start(f32[16,512]{1,0:T(8,128)S(1)} %turn.4.refs_2_), channel_id=1, source_target_pairs={{20,30},{21,31}} | collective-permute-start | bytes 98312 | tf_op jit(solution)/shard_map/ppermute | solution.py:30
  133.0 3.5 %collective-permute-start.36 = (f32[16,512]{1,0:T(8,128)S(1)}, f32[16,512]{1,0:T(8,128)S(1)}, u32[]{:S(2)}, u32[]{:S(2)}) collective-permute-start(f32[16,512]{1,0:T(8,128)S(1)} %turn.4.refs_2_), channel_id=1, source_target_pairs={{20,31},{21,30}} | collective-permute-start | bytes 98312 | tf_op jit(solution)/shard_map/ppermute | solution.py:30
  144.8 7.0 %collective-permute-start.41 = (f32[2,512]{1,0:T(2,128)}, f32[2,512]{1,0:T(2,128)S(1)}, u32[]{:S(2)}, u32[]{:S(2)}) collective-permute-start(f32[2,512]{1,0:T(2,128)} %get-tuple-element.108), channel_id=1, source_target_pairs={{0,24},{1,25},{10,18},{11,19},{20,12},{21,13},{30,6},{31,7}} | collective-permute-start | bytes 12296 | tf_op jit(solution)/shard_map/ppermute | solution.py:30
  (24 other events, 176.9 us)
